TPU v7x, 128 devices: a whole 4x4x4 slice. The times are simulated.
128 devices in a mesh: quad: 8 (over z, x_lo), row: 16 (over x_hi, y, core).
Axes of the slice: x: 4 (x_hi: 2, x_lo: 2; x = x_hi * 2 + x_lo), y: 4, z: 4, core: 2. Of those that a mesh axis runs over, the one named last changes fastest.
Arguments:
- hamiltonian: bfloat16 [1024, 64, 1536], P('row'), may hold values from -0.15625 to 0.15625
- columns: int32 [1024, 24], P('row'), may hold values from 0 to 1023, as said below
- counts: int32 [1024], P('row'), may hold values from 2 to 24, as said below
- precond: bfloat16 [16, 1024, 64, 128], P('quad', 'row'), may hold values from -0.5 to 0.5
- rhs: bfloat16 [65536, 128], P('row'), may hold values from -6 to 6
Outputs:
- moments_out: float32 [8, 65536, 128], P('quad', 'row')
- blocks_out: float32 [8, 128, 128], P('quad')
Inputs may be any that keep to these rules, and one draw needn't show every extreme that they name: `columns`: slot 0 of row block b holds b itself; slot 1 holds b - 64 for even b and b + 64 for odd b, reflected at the ends (an index -m becomes m, an index 1023 + m becomes 1024 - 1 - m); every column block lies within 64 blocks of its row block. `counts`: every run of 64 row blocks starting at a multiple of 64 holds a row block with all 24 slots live.
All inputs are finite; a program needn't handle non-finite values.
Results may differ from a plain program's by a relative error of at most 0.02.
Values may be sent and summed in bfloat16 or wider, within the bound.
No kernel may reach another device: no remote copies, remote signals or barrier semaphores. Data moves between devices by JAX's collectives and lax.ppermute only.
A program may use at most 128 MiB of HBM per device.

v0:
```python
import math

import jax
import jax.numpy as jnp
from jax import lax
from jax.sharding import PartitionSpec as P

ITERS = 2
MOMENTS = 8


def extended_2(x, sides, width):
    for axis, dim in sides:
        peers, length = (lax.axis_size(axis), x.shape[dim])
        up = [(i, (i + 1) % peers) for i in range(peers - 1)]
        down = [(j, i) for i, j in up]
        last = lax.slice_in_dim(x, length - width, length, axis=dim)
        first = lax.slice_in_dim(x, 0, width, axis=dim)
        before = lax.ppermute(last, axis, up)
        after = lax.ppermute(first, axis, down)
        x = jnp.concatenate([before, x, after], axis=dim)
    return x


def rotate(values):
    half_cols = values.shape[-1] // 2
    return jnp.concatenate([-values[..., half_cols:], values[..., :half_cols]], axis=-1)


def precondition(blocks_pre, resid):
    stacked = jnp.concatenate([resid, rotate(resid)], axis=1)
    return jnp.einsum("bij,bjc->bic", blocks_pre, stacked, preferred_element_type=jnp.float32)


def shards(hamiltonian, columns, counts, precond, rhs):
    row_blocks = hamiltonian.shape[0]
    block_size = hamiltonian.shape[1]
    slots = columns.shape[1]
    width = rhs.shape[1]
    per_quad = precond.shape[0]
    quad_count = lax.axis_size("quad")
    row_count = lax.axis_size("row")
    quads_total = per_quad * quad_count
    per_device = MOMENTS // quad_count
    local_rows = row_blocks * block_size
    row_index = lax.axis_index("row")
    quad_index = lax.axis_index("quad")
    first_block = (row_index - 1) * row_blocks
    live = jnp.arange(slots)[None, :] < counts[:, None]
    local_index = jnp.where(live, columns - first_block, 3 * row_blocks)
    rhs_blocks = rhs.reshape(row_blocks, block_size, width)
    rhs_float = rhs_blocks.astype(jnp.float32)
    thetas = []
    solutions = []
    for which in range(per_quad):
        theta = (
            2.0 * jnp.pi * ((quad_index * per_quad + which).astype(jnp.float32) + 0.5) / quads_total
        )
        thetas.append(theta)
        zreal = jnp.cos(theta)
        zimag = jnp.sin(theta)
        iterate = precondition(precond[which], rhs_blocks).astype(jnp.bfloat16)
        for sweep in range(ITERS):
            flat = iterate.reshape(local_rows, width)
            extended = extended_2(flat, (("row", 0),), local_rows)
            stacked = jnp.concatenate(
                [
                    extended.reshape(3 * row_blocks, block_size, width),
                    jnp.zeros((1, block_size, width), jnp.bfloat16),
                ],
                axis=0,
            )
            gathered = stacked[local_index].reshape(row_blocks, slots * block_size, width)
            product = jnp.einsum(
                "bij,bjc->bic", hamiltonian, gathered, preferred_element_type=jnp.float32
            )
            current = iterate.astype(jnp.float32)
            shifted = zreal * current + zimag * rotate(current)
            resid = (rhs_float - (shifted - product)).astype(jnp.bfloat16)
            iterate = (current + precondition(precond[which], resid)).astype(jnp.bfloat16)
        solutions.append(iterate.reshape(local_rows, width))
    orders = jnp.arange(lax.axis_size("quad") * per_device).astype(jnp.float32) + 1.0
    total = jnp.zeros((lax.axis_size("quad") * per_device, local_rows, width), jnp.float32)
    for which in range(per_quad):
        phase = orders * thetas[which]
        coef_a = jnp.cos(phase) / quads_total
        coef_b = jnp.sin(phase) / quads_total
        current = solutions[which].astype(jnp.float32)
        total = (
            total
            + coef_a[:, None, None] * current[None]
            + coef_b[:, None, None] * rotate(current)[None]
        )
    held = lax.optimization_barrier(total.astype(jnp.bfloat16))
    moments_out = lax.psum_scatter(
        held.astype(jnp.float32).astype(jnp.bfloat16), "quad", scatter_dimension=0, tiled=True
    ).astype(jnp.float32)
    scale = 1.0 / math.sqrt(local_rows * row_count)
    flat_rhs = rhs.astype(jnp.float32)
    local_blocks = (
        jnp.einsum("rc,krd->kcd", flat_rhs, moments_out, precision=lax.Precision.HIGHEST) * scale
    )
    blocks_out = lax.psum(local_blocks.astype(jnp.bfloat16), "row").astype(jnp.float32)
    return (moments_out, blocks_out)


def solution(mesh):
    return jax.shard_map(
        shards,
        mesh=mesh,
        in_specs=(
            P("row", None, None),
            P("row", None),
            P("row"),
            P("quad", "row", None, None),
            P("row", None),
        ),
        out_specs=(P("quad", "row", None), P("quad", None, None)),
        check_vma=False,
    )
```

profile of v0, /device:TPU:4, one launch (start us, length us, event | category | flops | bytes accessed | tf_op | source)
XLA Modules:
  0.0 559.1 jit_solution(10902191708547151597)
XLA Ops:
  12.6 7.3 %collective-permute-start.5 = (bf16[4096,128]{1,0:T(8,128)(2,1)S(1)}, bf16[4096,128]{1,0:T(8,128)(2,1)}, u32[]{:S(2)}, u32[]{:S(2)}) collective-permute-start(bf16[4096,128]{1,0:T(8,128)(2,1)S(1)} %bitcast.107), channel_id=1, source_target_pairs={{1,0},{2,1},{3,2},{4,3},{5,4},{6,5},{7,6},{8,7},{9,8},{10,9},{11,1... | collective-permute-start | bytes 3145736 | tf_op jit(solution)/shard_map/ppermute | solution.py:20
  24.3 7.3 %collective-permute-start.1 = (bf16[4096,128]{1,0:T(8,128)(2,1)}, bf16[4096,128]{1,0:T(8,128)(2,1)}, u32[]{:S(2)}, u32[]{:S(2)}) collective-permute-start(bf16[4096,128]{1,0:T(8,128)(2,1)} %bitcast.3), channel_id=1, source_target_pairs={{1,0},{2,1},{3,2},{4,3},{5,4},{6,5},{7,6},{8,7},{9,8},{10,9},{11,1... | collective-permute-start | bytes 3145736 | tf_op jit(solution)/shard_map/ppermute | solution.py:20
  33.3 2.8 slice_negate_fusion.2
  36.1 2.8 slice_negate_fusion.5
  39.0 8.6 %pad_maximum_fusion.2 = bf16[12288,128]{1,0:T(8,128)(2,1)S(1)} fusion(bf16[4096,128]{1,0:T(8,128)(2,1)} %collective-permute-done.5, bf16[4096,128]{1,0:T(8,128)(2,1)S(1)} %bitcast.108, bf16[4096,128]{1,0:T(8,128)(2,1)} %collective-permute-done.4), kind=kLoop, calls=%fused_computation.11 | loop fusion | flops 9437184 | bytes 6291456 | tf_op jit(solution)/shard_map/concatenate | solution.py:21
  48.3 31.8 %gather_fusion.2 = bf16[1536,64,128]{2,1,0:T(8,128)(2,1)} fusion(bf16[193,64,128]{2,1,0:T(8,128)(2,1)S(1)} %concatenate.89, s32[2048]{0:T(1024)S(1)} %pad_clamp_fusion), kind=kCustom, calls=%fused_computation.2 | custom fusion | bytes 50337792 | tf_op jit(solution)/shard_map/gather | solution.py:73
  80.0 16.3 %fusion.2 = bf16[64,64,128]{2,1,0:T(8,128)(2,1)S(1)} fusion(bf16[64,64,128]{2,1,0:T(8,128)(2,1)} %bitcast.100, f32[64,64,64]{2,1,0:T(8,128)} %get-tuple-element.13, f32[64,64,64]{2,1,0:T(8,128)} %get-tuple-element.12, bf16[64,64,1536]{2,1,0:T(8,128)(2,1)} %param.5, bf16[64,1536,128]{2,1,0:T(8,128)(2,1)} %bitcast.97, bf16[64,128,64]{1,2,0:T(8,128)(2,1)} %copy-done.5, ...), kind=kOutput, calls=%fused_computation.15 | convolution fusion | flops 1615331328 | bytes 42991624 | tf_op jit(solution)/shard_map/bij,bjc->bic/dot_general | solution.py:74
  102.8 7.3 %collective-permute-start.7 = (bf16[4096,128]{1,0:T(8,128)(2,1)}, bf16[4096,128]{1,0:T(8,128)(2,1)}, u32[]{:S(2)}, u32[]{:S(2)}) collective-permute-start(bf16[4096,128]{1,0:T(8,128)(2,1)} %bitcast.24), channel_id=1, source_target_pairs={{1,0},{2,1},{3,2},{4,3},{5,4},{6,5},{7,6},{8,7},{9,8},{10,9},{11,1... | collective-permute-start | bytes 3145736 | tf_op jit(solution)/shard_map/ppermute | solution.py:20
  110.0 4.1 pad_maximum_fusion
  114.9 31.7 %gather_fusion = bf16[1536,64,128]{2,1,0:T(8,128)(2,1)} fusion(bf16[193,64,128]{2,1,0:T(8,128)(2,1)S(1)} %concatenate.78, s32[2048]{0:T(1024)S(1)} %pad_clamp_fusion), kind=kCustom, calls=%fused_computation | custom fusion | bytes 50337792 | tf_op jit(solution)/shard_map/gather | solution.py:73
  146.6 16.1 %fusion = bf16[64,64,128]{2,1,0:T(8,128)(2,1)S(1)} fusion(bf16[64,64,128]{2,1,0:T(8,128)(2,1)} %bitcast.101, f32[64,64,64]{2,1,0:T(8,128)} %get-tuple-element.9, f32[64,64,64]{2,1,0:T(8,128)} %get-tuple-element.8, bf16[64,64,1536]{2,1,0:T(8,128)(2,1)} %param.5, bf16[64,1536,128]{2,1,0:T(8,128)(2,1)} %bitcast.98, ...), kind=kOutput, calls=%fused_computation.13 | convolution fusion | flops 1615331328 | bytes 42991624 | tf_op jit(solution)/shard_map/bij,bjc->bic/dot_general | solution.py:74
  163.2 3.0 slice.127
  166.2 3.1 fusion.72
  171.3 7.6 %collective-permute-start.3 = (bf16[4096,128]{1,0:T(8,128)(2,1)}, bf16[4096,128]{1,0:T(8,128)(2,1)}, u32[]{:S(2)}, u32[]{:S(2)}) collective-permute-start(bf16[4096,128]{1,0:T(8,128)(2,1)} %bitcast.9), channel_id=1, source_target_pairs={{1,0},{2,1},{3,2},{4,3},{5,4},{6,5},{7,6},{8,7},{9,8},{10,9},{11,1... | collective-permute-start | bytes 3145736 | tf_op jit(solution)/shard_map/ppermute | solution.py:20
  179.0 2.8 slice.117
  185.7 4.1 pad_maximum_fusion.3
  190.5 31.8 %gather_fusion.3 = bf16[1536,64,128]{2,1,0:T(8,128)(2,1)} fusion(bf16[193,64,128]{2,1,0:T(8,128)(2,1)S(1)} %concatenate.94, s32[2048]{0:T(1024)S(1)} %pad_clamp_fusion), kind=kCustom, calls=%fused_computation.3 | custom fusion | bytes 50337792 | tf_op jit(solution)/shard_map/gather | solution.py:73
  222.3 16.1 %fusion.3 = bf16[64,64,128]{2,1,0:T(8,128)(2,1)S(1)} fusion(bf16[64,64,128]{2,1,0:T(8,128)(2,1)} %bitcast.102, f32[64,64,64]{2,1,0:T(8,128)} %slice.127, f32[64,64,64]{2,1,0:T(8,128)} %slice_negate_fusion.1, bf16[64,64,1536]{2,1,0:T(8,128)(2,1)} %param.5, bf16[64,1536,128]{2,1,0:T(8,128)(2,1)} %bitcast.96, bf16[64,64,128]{2,1,0:T(8,128)(2,1)} %get-tuple-element.27, ...), kind=kOutput, calls=%fused_computation.16 | convolution fusion | flops 1615331328 | bytes 42991624 | tf_op jit(solution)/shard_map/bij,bjc->bic/dot_general | solution.py:74
  245.0 4.3 pad_maximum_fusion.1
  250.1 31.8 %gather_fusion.1 = bf16[1536,64,128]{2,1,0:T(8,128)(2,1)} fusion(bf16[193,64,128]{2,1,0:T(8,128)(2,1)S(1)} %concatenate.83, s32[2048]{0:T(1024)S(1)} %pad_clamp_fusion), kind=kCustom, calls=%fused_computation.1 | custom fusion | bytes 50337792 | tf_op jit(solution)/shard_map/gather | solution.py:73
  281.8 16.4 %fusion.1 = bf16[64,64,128]{2,1,0:T(8,128)(2,1)S(1)} fusion(bf16[64,64,128]{2,1,0:T(8,128)(2,1)} %bitcast.103, f32[64,64,64]{2,1,0:T(8,128)} %slice.117, f32[64,64,64]{2,1,0:T(8,128)} %slice_negate_fusion.4, bf16[64,64,1536]{2,1,0:T(8,128)(2,1)} %param.5, bf16[64,1536,128]{2,1,0:T(8,128)(2,1)} %bitcast.95, bf16[64,64,128]{2,1,0:T(8,128)(2,1)} %get-tuple-element.31, ...), kind=kOutput, calls=%fused_computation.14 | convolution fusion | flops 1615331328 | bytes 42991624 | tf_op jit(solution)/shard_map/bij,bjc->bic/dot_general | solution.py:74
  306.0 6.1 %add_convert_fusion = bf16[8,4096,128]{2,1,0:T(8,128)(2,1)} fusion(f32[4096,128]{1,0:T(8,128)S(1)} %get-tuple-element.37, f32[8]{0:T(128)S(1)} %copy-done.17, f32[4096,128]{1,0:T(8,128)S(1)} %copy-done.3, f32[8]{0:T(128)S(1)} %copy-done.18, f32[4096,128]{1,0:T(8,128)S(1)} %get-tuple-element.36, f32[8]{0:T(128)S(1)} %copy-done.19, ...), kind=kLoop, calls=%fused_computation.4 | loop fusion | flops 33554432 | bytes 16777344 | tf_op jit(solution)/shard_map/convert_element_type | solution.py:94
  312.1 168.7 %reduce-scatter.2.cloned.1.call-done = bf16[1,4096,128]{2,1,0:T(8,128)(2,1)} async-done(((bf16[8,4096,128]{2,1,0:T(8,128)(2,1)}), bf16[1,4096,128]{2,1,0:T(8,128)(2,1)}) %reduce-scatter.2.cloned.1.call-update) | async-done | bytes 1048592 | tf_op jit(solution)/shard_map/reduce_scatter | solution.py:95
  482.6 67.3 %psum.7 = bf16[1,128,128]{1,2,0:T(8,128)(2,1)S(1)} all-reduce(bf16[1,128,128]{1,2,0:T(8,128)(2,1)S(1)} %fusion.49), channel_id=1, replica_groups=mesh['quad'=8,'row'=16] {'row'}, use_global_device_ids=true, to_apply=%region_1.2 | all-reduce | flops 16384 | bytes 65536 | tf_op jit(solution)/shard_map/psum | solution.py:103
  (88 shorter events, 45.0 us)
Async XLA Ops:
  7.2 473.7 %reduce-scatter.2.cloned.1.call-start = ((), (), s32[]{:S(2)}) async-start(), calls=%async_computation.1 | async-start | bytes 9437184 | tf_op jit(solution)/shard_map/reduce_scatter | solution.py:95
  7.2 2.2 copy-start
  7.2 2.5 copy-start.8
  10.5 28.4 %copy-start.5 = (bf16[64,128,64]{1,2,0:T(8,128)(2,1)}, bf16[64,128,64]{1,2,0:T(8,128)(2,1)S(1)}, u32[]{:S(2)}) copy-start(bf16[64,128,64]{1,2,0:T(8,128)(2,1)S(1)} %get-tuple-element.25) | copy-start | bytes 3145732
  10.5 21.3 %copy-start.16 = (s32[64,24]{0,1:T(8,128)S(1)}, s32[64,24]{0,1:T(8,128)}, u32[]{:S(2)}) copy-start(s32[64,24]{0,1:T(8,128)} %param.6) | copy-start | bytes 18436
  10.5 21.3 %copy-start.21 = (s32[64]{0:T(128)S(1)}, s32[64]{0:T(128)}, u32[]{:S(2)}) copy-start(s32[64]{0:T(128)} %param.7) | copy-start | bytes 772
  10.5 28.4 %collective-permute-start.4 = (bf16[4096,128]{1,0:T(8,128)(2,1)S(1)}, bf16[4096,128]{1,0:T(8,128)(2,1)}, u32[]{:S(2)}, u32[]{:S(2)}) collective-permute-start(bf16[4096,128]{1,0:T(8,128)(2,1)S(1)} %bitcast.106), channel_id=1, source_target_pairs={{0,1},{1,2},{2,3},{3,4},{4,5},{5,6},{6,7},{7,8},{8,9},{9,10},{10,1... | collective-permute-start | bytes 3145736 | tf_op jit(solution)/shard_map/ppermute | solution.py:19
  12.6 26.3 %collective-permute-start.5 = (bf16[4096,128]{1,0:T(8,128)(2,1)S(1)}, bf16[4096,128]{1,0:T(8,128)(2,1)}, u32[]{:S(2)}, u32[]{:S(2)}) collective-permute-start(bf16[4096,128]{1,0:T(8,128)(2,1)S(1)} %bitcast.107), channel_id=1, source_target_pairs={{1,0},{2,1},{3,2},{4,3},{5,4},{6,5},{7,6},{8,7},{9,8},{10,9},{11,1... | collective-permute-start | bytes 3145736 | tf_op jit(solution)/shard_map/ppermute | solution.py:20
  22.3 87.7 %collective-permute-start = (bf16[4096,128]{1,0:T(8,128)(2,1)}, bf16[4096,128]{1,0:T(8,128)(2,1)}, u32[]{:S(2)}, u32[]{:S(2)}) collective-permute-start(bf16[4096,128]{1,0:T(8,128)(2,1)} %bitcast.3), channel_id=1, source_target_pairs={{0,1},{1,2},{2,3},{3,4},{4,5},{5,6},{6,7},{7,8},{8,9},{9,10},{10,1... | collective-permute-start | bytes 3145736 | tf_op jit(solution)/shard_map/ppermute | solution.py:19
  24.3 85.8 %collective-permute-start.1 = (bf16[4096,128]{1,0:T(8,128)(2,1)}, bf16[4096,128]{1,0:T(8,128)(2,1)}, u32[]{:S(2)}, u32[]{:S(2)}) collective-permute-start(bf16[4096,128]{1,0:T(8,128)(2,1)} %bitcast.3), channel_id=1, source_target_pairs={{1,0},{2,1},{3,2},{4,3},{5,4},{6,5},{7,6},{8,7},{9,8},{10,9},{11,1... | collective-permute-start | bytes 3145736 | tf_op jit(solution)/shard_map/ppermute | solution.py:20
  33.3 2.8 copy-start.4
  96.4 1.9 copy-start.9
  100.8 84.9 %collective-permute-start.6 = (bf16[4096,128]{1,0:T(8,128)(2,1)}, bf16[4096,128]{1,0:T(8,128)(2,1)}, u32[]{:S(2)}, u32[]{:S(2)}) collective-permute-start(bf16[4096,128]{1,0:T(8,128)(2,1)} %bitcast.24), channel_id=1, source_target_pairs={{0,1},{1,2},{2,3},{3,4},{4,5},{5,6},{6,7},{7,8},{8,9},{9,10},{10,1... | collective-permute-start | bytes 3145736 | tf_op jit(solution)/shard_map/ppermute | solution.py:19
  102.8 82.9 %collective-permute-start.7 = (bf16[4096,128]{1,0:T(8,128)(2,1)}, bf16[4096,128]{1,0:T(8,128)(2,1)}, u32[]{:S(2)}, u32[]{:S(2)}) collective-permute-start(bf16[4096,128]{1,0:T(8,128)(2,1)} %bitcast.24), channel_id=1, source_target_pairs={{1,0},{2,1},{3,2},{4,3},{5,4},{6,5},{7,6},{8,7},{9,8},{10,9},{11,1... | collective-permute-start | bytes 3145736 | tf_op jit(solution)/shard_map/ppermute | solution.py:20
  163.1 3.0 copy-start.10
  169.3 12.5 %copy-start.7 = (f32[64,64,128]{2,1,0:T(8,128)S(1)}, f32[64,64,128]{2,1,0:T(8,128)}, u32[]{:S(2)}) copy-start(f32[64,64,128]{2,1,0:T(8,128)} %get-tuple-element.26) | copy-start | bytes 6291460
  169.3 75.8 %collective-permute-start.2 = (bf16[4096,128]{1,0:T(8,128)(2,1)}, bf16[4096,128]{1,0:T(8,128)(2,1)}, u32[]{:S(2)}, u32[]{:S(2)}) collective-permute-start(bf16[4096,128]{1,0:T(8,128)(2,1)} %bitcast.9), channel_id=1, source_target_pairs={{0,1},{1,2},{2,3},{3,4},{4,5},{5,6},{6,7},{7,8},{8,9},{9,10},{10,1... | collective-permute-start | bytes 3145736 | tf_op jit(solution)/shard_map/ppermute | solution.py:19
  171.3 73.7 %collective-permute-start.3 = (bf16[4096,128]{1,0:T(8,128)(2,1)}, bf16[4096,128]{1,0:T(8,128)(2,1)}, u32[]{:S(2)}, u32[]{:S(2)}) collective-permute-start(bf16[4096,128]{1,0:T(8,128)(2,1)} %bitcast.9), channel_id=1, source_target_pairs={{1,0},{2,1},{3,2},{4,3},{5,4},{6,5},{7,6},{8,7},{9,8},{10,9},{11,1... | collective-permute-start | bytes 3145736 | tf_op jit(solution)/shard_map/ppermute | solution.py:20
  238.4 1.6 copy-start.11
  242.3 2.7 copy-start.2
  298.2 1.6 copy-start.12
  302.1 2.2 copy-start.14
  312.1 168.8 %copy-start.1 = (bf16[4096,128]{1,0:T(8,128)(2,1)S(1)}, bf16[4096,128]{1,0:T(8,128)(2,1)}, u32[]{:S(2)}) copy-start(bf16[4096,128]{1,0:T(8,128)(2,1)} %param.9) | copy-start | bytes 3145732
  480.8 69.8 %copy-start.15 = (bf16[1,4096,128]{2,1,0:T(8,128)(2,1)S(1)}, bf16[1,4096,128]{2,1,0:T(8,128)(2,1)}, u32[]{:S(2)}) copy-start(bf16[1,4096,128]{2,1,0:T(8,128)(2,1)} %reduce-scatter.2.cloned.1.call-done) | copy-start | bytes 3145732
  (7 other events, 10.8 us)
Sparse Core Ops, SparseCore 0:
  312.2 168.5 reduce-scatter.1
where the time goes:
time: 566 us; the launch traced here: 559 us
  waiting for transfers between devices  169 us (30%)
  local copies, waits for them, and re-layouts  143 us (25%)
  matrix products  79.8 us (14%)
  blocking collectives  67.3 us (12%)
  other arithmetic  48.4 us (9%)
  starting transfers between devices  37.4 us (7%)
  between operations  15 us (3%)
    reduce_scatter x1, waiting for transfers between devices, shards(): lax.psum_scatter(held.astype(jnp.float32).astype(jnp.bfloat16), 'quad', s...  169 us
    gather x4, local copies, waits for them, and re-layouts, shards(): stacked[local_index].reshape(row_blocks, slots * block_size, width)  127 us
    psum x1, blocking collectives, shards(): lax.psum(local_blocks.astype(jnp.bfloat16), 'row').astype(jnp.float32)  67.3 us
    dot_general x4, matrix products, shards(): jnp.einsum('bij,bjc->bic', hamiltonian, gathered, preferred_element_type=...  64.9 us
    ppermute x4, starting transfers between devices, extended_2(): after = lax.ppermute(first, axis, down)  29.4 us
    concatenate x4, other arithmetic, extended_2(): x = jnp.concatenate([before, x, after], axis=dim)  21.2 us
    neg x11, other arithmetic, rotate(): -values[..., half_cols:]  16.8 us
    dot_general x6, matrix products, precondition(): jnp.einsum('bij,bjc->bic', blocks_pre, stacked, preferred_element_type=jn...  13.1 us
  transfers between devices with their start and end apart: 9, of which 1 were waited for; matrix products, arithmetic and copies ran while one was open for 35% of the time, Pallas kernels for 0%

commit v1 on v0

v1 whole, which is shorter than its diff:
```python
import math

import jax
import jax.numpy as jnp
import numpy as np
from jax import lax
from jax.experimental import pallas as pl
from jax.experimental.pallas import tpu as pltpu
from jax.sharding import PartitionSpec as P

ITERS = 2
MOMENTS = 8
POINTS = 16
BS = 64
SLOTS = 24
RB = 64
LANES = 128
GROUP = 64
HALF = 32
STEP = 8
F32 = jnp.float32
BF16 = jnp.bfloat16


def unit_lanes():
    table = np.zeros((LANES, 4 * LANES), np.float32)
    for unit in range(2):
        for lane in range(LANES):
            part, col = (lane // HALF) % 2, lane % HALF
            src = unit * HALF + col
            table[part * GROUP + src, unit * LANES + lane] = 1.0
            sign = -1.0 if part == 0 else 1.0
            table[(1 - part) * GROUP + src, (2 + unit) * LANES + lane] = sign
    return table


def lane_ids(shape):
    return lax.broadcasted_iota(jnp.int32, shape, len(shape) - 1)


def split_points(top, bottom):
    lane = lane_ids(top.shape) % LANES
    first = lane < GROUP
    zero = jnp.zeros_like(top)
    return jnp.concatenate(
        [
            jnp.where(first, top, zero),
            jnp.where(first, bottom, zero),
            jnp.where(first, zero, top),
            jnp.where(first, zero, bottom),
        ],
        axis=0,
    )


def init_kernel(x_ref, pre_ref, map_ref, rhs_a_ref, rhs_b_ref, y_a_ref, y_b_ref):
    spread = jnp.dot(x_ref[...], map_ref[...], preferred_element_type=F32)
    rhs_a_ref[...] = spread[:, :LANES].astype(BF16).reshape(STEP, BS, LANES)
    rhs_b_ref[...] = spread[:, LANES : 2 * LANES].astype(BF16).reshape(STEP, BS, LANES)
    for b in range(STEP):
        rows = slice(b * BS, (b + 1) * BS)
        right = split_points(spread[rows, : 2 * LANES], spread[rows, 2 * LANES :]).astype(BF16)
        left = jnp.concatenate([pre_ref[0, b], pre_ref[1, b]], axis=1)
        out = jnp.dot(left, right, preferred_element_type=F32)
        y_a_ref[b] = out[:, :LANES].astype(BF16)
        y_b_ref[b] = out[:, LANES:].astype(BF16)


def initial(rhs, precond):
    block = jax.ShapeDtypeStruct((RB, BS, LANES), BF16)
    out_spec = pl.BlockSpec((STEP, BS, LANES), lambda i: (i, 0, 0))
    return pl.pallas_call(
        init_kernel,
        grid=(RB // STEP,),
        in_specs=[
            pl.BlockSpec((STEP * BS, LANES), lambda i: (i, 0)),
            pl.BlockSpec((2, STEP, BS, LANES), lambda i: (0, i, 0, 0)),
            pl.BlockSpec((LANES, 4 * LANES), lambda i: (0, 0)),
        ],
        out_specs=[out_spec] * 4,
        out_shape=[block] * 4,
        name="initial",
    )(rhs, precond, jnp.asarray(unit_lanes(), BF16))


def rotate_lanes(x):
    lane = lane_ids(x.shape) % GROUP
    up = pltpu.roll(x, LANES - HALF, axis=x.ndim - 1)
    down = pltpu.roll(x, HALF, axis=x.ndim - 1)
    return jnp.where(lane < HALF, -up, down)


def sweep_kernel(
    last, index_ref, ham_ref, pre_ref, rhs_ref, z_ref, local_ref, before_ref, after_ref, x_ref,
    out_ref, *rest
):
    if last:
        gram_ref, held, sems = rest
    else:
        held, sems = rest
    step = pl.program_id(0)

    @pl.when(step == 0)
    def _():
        copies = []
        for n, ref in enumerate((before_ref, local_ref, after_ref)):
            copies.append(
                pltpu.make_async_copy(ref, held.at[pl.ds(n * RB, RB)], sems.at[n])
            )
            copies[-1].start()
        held[3 * RB] = jnp.zeros((BS, LANES), BF16)
        if last:
            gram_ref[...] = jnp.zeros_like(gram_ref)
        for copy in copies:
            copy.wait()

    zreal = z_ref[0:1, :]
    zimag = z_ref[1:2, :]
    for b in range(STEP):
        row = step * STEP + b
        total = jnp.zeros((BS, LANES), F32)
        for g in range(SLOTS // 4):
            right = jnp.concatenate(
                [held[index_ref[row * SLOTS + g * 4 + s]] for s in range(4)], axis=0
            )
            left = ham_ref[b, :, g * 4 * BS : (g + 1) * 4 * BS]
            total = total + jnp.dot(left, right, preferred_element_type=F32)
        current = held[RB + row].astype(F32)
        shifted = zreal * current + zimag * rotate_lanes(current)
        resid = (rhs_ref[b].astype(F32) - (shifted - total)).astype(BF16).astype(F32)
        right = split_points(resid, rotate_lanes(resid)).astype(BF16)
        left = jnp.concatenate([pre_ref[0, b], pre_ref[1, b]], axis=1)
        out_ref[b] = (current + jnp.dot(left, right, preferred_element_type=F32)).astype(BF16)
    if last:
        gram_ref[...] += lax.dot_general(
            x_ref[...],
            out_ref[...].reshape(STEP * BS, LANES),
            (((0,), (0,)), ((), ())),
            preferred_element_type=F32,
        )


def sweep(index, ham, precond, rhs_unit, z, local, before, after, rhs, last):
    block = pl.BlockSpec((STEP, BS, LANES), lambda i, n: (i, 0, 0))
    anywhere = pl.BlockSpec(memory_space=pl.ANY)
    out_specs = [block]
    out_shape = [jax.ShapeDtypeStruct((RB, BS, LANES), BF16)]
    if last:
        out_specs.append(pl.BlockSpec((LANES, LANES), lambda i, n: (0, 0)))
        out_shape.append(jax.ShapeDtypeStruct((LANES, LANES), F32))

    def kernel(*refs):
        sweep_kernel(last, *refs)

    return pl.pallas_call(
        kernel,
        grid_spec=pltpu.PrefetchScalarGridSpec(
            num_scalar_prefetch=1,
            grid=(RB // STEP,),
            in_specs=[
                pl.BlockSpec((STEP, BS, SLOTS * BS), lambda i, n: (i, 0, 0)),
                pl.BlockSpec((2, STEP, BS, LANES), lambda i, n: (0, i, 0, 0)),
                block,
                pl.BlockSpec((8, LANES), lambda i, n: (0, 0)),
                anywhere,
                anywhere,
                anywhere,
                pl.BlockSpec((STEP * BS, LANES), lambda i, n: (i, 0)),
            ],
            out_specs=out_specs,
            scratch_shapes=[
                pltpu.VMEM((3 * RB + 1, BS, LANES), BF16),
                pltpu.SemaphoreType.DMA((3,)),
            ],
        ),
        out_shape=out_shape,
        cost_estimate=pl.CostEstimate(
            flops=2 * RB * BS * SLOTS * BS * LANES, bytes_accessed=20 << 20, transcendentals=0
        ),
        name="sweep_last" if last else "sweep",
    )(index, ham, precond, rhs_unit, z, local, before, after, rhs)


def combine_kernel(own_ref, peer_ref, hi_ref, lo_ref, send_ref, keep_ref):
    both = jnp.concatenate([own_ref[...], peer_ref[...]], axis=1)
    out = jnp.dot(both, hi_ref[...], preferred_element_type=F32)
    out = out + jnp.dot(both, lo_ref[...], preferred_element_type=F32)
    send_ref[...] = out[:, :LANES].astype(BF16)
    keep_ref[...] = out[:, LANES:]


def combine(own, peer, weights, rows_step, offset):
    rows = peer.shape[0]
    hi, lo = weights
    base = offset // rows_step
    row_spec = pl.BlockSpec((rows_step, LANES), lambda i: (i, 0))
    mat = pl.BlockSpec((2 * LANES, 2 * LANES), lambda i: (0, 0))
    return pl.pallas_call(
        combine_kernel,
        grid=(rows // rows_step,),
        in_specs=[pl.BlockSpec((rows_step, LANES), lambda i: (i + base, 0)), row_spec, mat, mat],
        out_specs=[row_spec, row_spec],
        out_shape=[
            jax.ShapeDtypeStruct((rows, LANES), BF16),
            jax.ShapeDtypeStruct((rows, LANES), F32),
        ],
        cost_estimate=pl.CostEstimate(
            flops=2 * rows * 256 * 512, bytes_accessed=rows * LANES * 12, transcendentals=0
        ),
        name="combine",
    )(own, peer, hi, lo)


def fold_kernel(keep1_ref, got1_ref, keep2_ref, got2_ref, send_ref, own_ref):
    top = keep1_ref[...] + got1_ref[...].astype(F32)
    bottom = keep2_ref[...] + got2_ref[...].astype(F32)
    first = lane_ids(top.shape) < GROUP
    send_ref[...] = jnp.where(first, pltpu.roll(top, GROUP, axis=1), bottom).astype(BF16)
    own_ref[...] = jnp.where(first, top, pltpu.roll(bottom, GROUP, axis=1))


def fold(keep1, got1, keep2, got2, rows_step):
    rows = keep1.shape[0]
    spec = pl.BlockSpec((rows_step, LANES), lambda i: (i, 0))
    return pl.pallas_call(
        fold_kernel,
        grid=(rows // rows_step,),
        in_specs=[spec] * 4,
        out_specs=[spec, spec],
        out_shape=[
            jax.ShapeDtypeStruct((rows, LANES), BF16),
            jax.ShapeDtypeStruct((rows, LANES), F32),
        ],
        cost_estimate=pl.CostEstimate(
            flops=rows * LANES * 8, bytes_accessed=rows * LANES * 18, transcendentals=0
        ),
        name="fold",
    )(keep1, got1, keep2, got2)


def finish_kernel(own_a_ref, got_a_ref, own_b_ref, got_b_ref, out_ref):
    unit_a = own_a_ref[...] + got_a_ref[...].astype(F32)
    unit_b = own_b_ref[...] + got_b_ref[...].astype(F32)
    quarter = lane_ids(unit_a.shape) // HALF

    def turn(x, shift):
        return pltpu.roll(x, shift, axis=1)

    def merge(first, second, third, fourth):
        low = jnp.where(quarter == 0, first, second)
        high = jnp.where(quarter == 2, third, fourth)
        return jnp.where(quarter < 2, low, high)

    out_ref[0, 0] = merge(unit_a, turn(unit_b, HALF), turn(unit_a, HALF), turn(unit_b, GROUP))
    out_ref[0, 1] = merge(turn(unit_a, GROUP), turn(unit_b, 96), turn(unit_a, 96), unit_b)


def finish(own_a, got_a, own_b, got_b, rows_step):
    rows = own_a.shape[0]
    spec = pl.BlockSpec((rows_step, LANES), lambda i: (i, 0))
    return pl.pallas_call(
        finish_kernel,
        grid=(rows // rows_step,),
        in_specs=[spec] * 4,
        out_specs=pl.BlockSpec((1, 2, rows_step, LANES), lambda i: (0, 0, i, 0)),
        out_shape=jax.ShapeDtypeStruct((1, 2, rows, LANES), F32),
        name="finish",
    )(own_a, got_a, own_b, got_b)


def moment_weights(owners, orders):
    shape = (2 * LANES, 2 * LANES)
    r = lax.broadcasted_iota(jnp.int32, shape, 0)
    c = lax.broadcasted_iota(jnp.int32, shape, 1)
    owner = jnp.where(r < LANES, owners[0], owners[1])
    point = owner * 2 + (r // GROUP) % 2
    slot = c // GROUP
    order = jnp.where(
        slot < 2,
        jnp.where(slot == 0, orders[0], orders[1]),
        jnp.where(slot == 2, orders[2], orders[3]),
    )
    turns = ((order + 1) * (2 * point + 1)) % (2 * POINTS)
    phase = turns.astype(F32) * (math.pi / POINTS)
    part_in, part_out = (r // HALF) % 2, (c // HALF) % 2
    sine = jnp.where(part_out == 0, -1.0, 1.0) * jnp.sin(phase)
    value = jnp.where(part_in == part_out, jnp.cos(phase), sine) / POINTS
    value = jnp.where(r % HALF == c % HALF, value, 0.0)
    high = lax.reduce_precision(value, 8, 7)
    return high.astype(BF16), (value - high).astype(BF16)


def shards(hamiltonian, columns, counts, precond, rhs):
    row_index = lax.axis_index("row")
    quad_index = lax.axis_index("quad")
    z_at, x_at = quad_index // 2, quad_index % 2

    def swap(x, axis, peer_of):
        size = lax.axis_size(axis)
        return lax.ppermute(x, axis, [(i, peer_of(i)) for i in range(size)])

    def by_pair(i):
        return (((i // 2) ^ 1) * 2) + i % 2

    def by_mirror(i):
        return ((3 - i // 2) * 2) + i % 2

    def by_x(i):
        return i ^ 1

    up = [(i, i + 1) for i in range(15)]
    down = [(i + 1, i) for i in range(15)]

    rhs_a, rhs_b, y_a, y_b = initial(rhs, precond)

    live = jnp.arange(SLOTS)[None, :] < counts[:, None]
    index = jnp.where(live, columns - (row_index - 1) * RB, 3 * RB).reshape(RB * SLOTS)
    lane = jnp.arange(LANES)[None, :]
    theta = 2.0 * jnp.pi * ((quad_index * 2 + lane // GROUP).astype(F32) + 0.5) / POINTS
    z = jnp.concatenate([jnp.cos(theta), jnp.sin(theta), jnp.zeros((6, LANES), F32)], axis=0)

    units = [y_a, y_b]
    rhs_units = [rhs_a, rhs_b]
    grams = [None, None]
    for unit in range(2):
        for it in range(ITERS):
            y = units[unit]
            before = lax.ppermute(y, "row", up)
            after = lax.ppermute(y, "row", down)
            last = it == ITERS - 1
            got = sweep(
                index, hamiltonian, precond, rhs_units[unit], z, y, before, after, rhs, last
            )
            units[unit] = got[0]
            if last:
                grams[unit] = got[1]

    mine, other = quad_index, quad_index ^ 1
    pair, mirror = by_pair(quad_index), by_mirror(quad_index)
    w_pair = moment_weights((mine, pair), (mirror, mirror ^ 1, mine, other))
    w_mirror = moment_weights((mine, mirror), (pair, pair ^ 1, mine, other))

    half_rows = RB * BS // 2
    sums = []
    for unit in range(2):
        flat = units[unit].reshape(RB * BS, LANES)
        got1 = swap(flat[:half_rows], "quad", by_pair)
        got2 = swap(flat[half_rows:], "quad", by_mirror)
        send1, keep1 = combine(flat, got1, w_pair, 512, 0)
        send2, keep2 = combine(flat, got2, w_mirror, 512, half_rows)
        back1 = swap(send1, "quad", by_mirror)
        back2 = swap(send2, "quad", by_pair)
        send3, own = fold(keep1, back1, keep2, back2, 512)
        sums.append((send3, own))

    gram = jnp.concatenate(grams, axis=0)
    for bit in (1, 2, 4, 8):
        gram = gram + swap(gram, "row", lambda i, bit=bit: i ^ bit)
    gram = gram.astype(BF16)
    send_g, keep_g = combine(gram, swap(gram, "quad", by_pair), w_pair, 256, 0)
    gram_sum = keep_g + swap(send_g, "quad", by_mirror).astype(F32)
    gram_got = swap(gram_sum[:, GROUP:].astype(BF16), "quad", by_x)
    blocks = gram_sum[:, :GROUP] + gram_got.astype(F32)
    blocks = blocks.reshape(2, LANES, 2, HALF).transpose(1, 2, 0, 3).reshape(1, LANES, LANES)
    blocks = blocks * (1.0 / math.sqrt(RB * BS * 16))

    got_a = swap(sums[0][0], "quad", by_x)
    got_b = swap(sums[1][0], "quad", by_x)
    moments = finish(sums[0][1], got_a, sums[1][1], got_b, 512)
    return moments.reshape(1, RB * BS, LANES), blocks


def solution(mesh):
    return jax.shard_map(
        shards,
        mesh=mesh,
        in_specs=(
            P("row", None, None),
            P("row", None),
            P("row"),
            P("quad", "row", None, None),
            P("row", None),
        ),
        out_specs=(P("quad", "row", None), P("quad", None, None)),
        check_vma=False,
    )
```

time: 566 us -> 247 us (0.44)
  Pallas kernels: 0 us -> 134 us
  local copies, waits for them, and re-layouts: 143 us -> 13.4 us
  waiting for transfers between devices: 169 us -> 43.2 us
  matrix products: 79.8 us -> 0 us
  blocking collectives: 67.3 us -> 0 us
  other arithmetic: 48.4 us -> 4.49 us
  between operations: 15 us -> 1.07 us
  starting transfers between devices: 37.4 us -> 49.2 us
    reduce_scatter x1 -> x0, waiting for transfers between devices: 169 us -> none  [shards(): lax.psum_scatter(held.astype(jnp.float32).astype(jnp.bfloat16), 'quad', s...]
    pallas_call x0 -> x13, Pallas kernels: none -> 134 us  [the longest x4 95.1 us: sweep(): pl.pallas_call(kernel, grid_spec=pltpu.PrefetchScalarGridSpec(num_scalar_...]
    gather x4 -> x0, local copies, waits for them, and re-layouts: 127 us -> none  [shards(): stacked[local_index].reshape(row_blocks, slots * block_size, width)]
    dot_general x11 -> x0, matrix products: 79.8 us -> none  [the longest x4 64.9 us: shards(): jnp.einsum('bij,bjc->bic', hamiltonian, gathered, preferred_element_type=...]
    psum x1 -> x0, blocking collectives: 67.3 us -> none  [shards(): lax.psum(local_blocks.astype(jnp.bfloat16), 'row').astype(jnp.float32)]
    ppermute x8 -> x25, waiting for transfers between devices: 0.02 us -> 43.2 us  [the longest x17 36.5 us: swap(): return lax.ppermute(x, axis, [(i, peer_of(i)) for i in range(size)])]
    concatenate x5 -> x1, other arithmetic: 22.4 us -> 0.67 us  [shards(): jnp.concatenate([jnp.cos(theta), jnp.sin(theta), jnp.zeros((6, LANES), F3...]
    neg x11 -> x0, other arithmetic: 16.8 us -> none  [rotate(): -values[..., half_cols:]]
  transfers between devices with their start and end apart: 9 -> 25, of which waited for: 1 -> 7; matrix products, arithmetic and copies ran while one was open for 35% -> 3% of each run, Pallas kernels for 0% -> 40%
where the time goes in v1:
time: 247 us; the launch traced here: 246 us
  Pallas kernels  134 us (54%)
  starting transfers between devices  49.2 us (20%)
  waiting for transfers between devices  43.2 us (17%)
  local copies, waits for them, and re-layouts  13.4 us (5%)
  other arithmetic  4.49 us (2%)
    pallas_call x4, Pallas kernels, sweep(): pl.pallas_call(kernel, grid_spec=pltpu.PrefetchScalarGridSpec(num_scalar_...  95.1 us
    ppermute x17, waiting for transfers between devices, swap(): return lax.ppermute(x, axis, [(i, peer_of(i)) for i in range(size)])  36.5 us
    ppermute x4, starting transfers between devices, shards(): after = lax.ppermute(y, 'row', down)  23.8 us
    pallas_call x5, Pallas kernels, combine(): pl.pallas_call(combine_kernel, grid=(rows // rows_step,), in_specs=[pl.Bl...  18.8 us
    ppermute x17, starting transfers between devices, swap(): return lax.ppermute(x, axis, [(i, peer_of(i)) for i in range(size)])  17.3 us
    unnamed x38, local copies, waits for them, and re-layouts  10 us
    ppermute x4, starting transfers between devices, shards(): before = lax.ppermute(y, 'row', up)  8.16 us
    pallas_call x2, Pallas kernels, fold(): pl.pallas_call(fold_kernel, grid=(rows // rows_step,), in_specs=[spec] *...  8.14 us
  transfers between devices with their start and end apart: 25, of which 7 were waited for; matrix products, arithmetic and copies ran while one was open for 3% of the time, Pallas kernels for 40%

profile of v1, /device:TPU:4, one launch (start us, length us, event | category | flops | bytes accessed | tf_op | source)
XLA Modules:
  0.0 245.8 jit_solution(883148594677628182)
XLA Ops:
  0.6 7.6 %initial.1 = (bf16[64,64,128]{2,1,0:T(8,128)(2,1)}, bf16[64,64,128]{2,1,0:T(8,128)(2,1)}, bf16[64,64,128]{2,1,0:T(8,128)(2,1)}, bf16[64,64,128]{2,1,0:T(8,128)(2,1)}) custom-call(bf16[4096,128]{1,0:T(8,128)(2,1)} %refs_8_.7, bf16[2,64,64,128]{3,2,1,0:T(8,128)(2,1)} %refs_2_.7, bf16[128,512]{1,0:T(8,128)(2,1)} %constant.196.clone.map_ref), custom_call_target="tpu_custom_call" | custom-call | tf_op jit(solution)/shard_map/initial/pallas_call | solution.py:72
  10.2 7.3 %collective-permute-start.1 = (bf16[64,64,128]{2,1,0:T(8,128)(2,1)}, bf16[64,64,128]{2,1,0:T(8,128)(2,1)S(1)}, u32[]{:S(2)}, u32[]{:S(2)}) collective-permute-start(bf16[64,64,128]{2,1,0:T(8,128)(2,1)} %get-tuple-element.25.refs_5_), channel_id=1, source_target_pairs={{1,0},{2,1},{3,2},{4,3},{5,4},{6,5},{7,6},{8,7},{9,8},{10,9},{11,1... | collective-permute-start | bytes 3145736 | tf_op jit(solution)/shard_map/ppermute | solution.py:329
  19.4 2.4 collective-permute-start.9
  23.4 4.8 %collective-permute-done.refs_6_ = bf16[64,64,128]{2,1,0:T(8,128)(2,1)S(1)} collective-permute-done((bf16[64,64,128]{2,1,0:T(8,128)(2,1)}, bf16[64,64,128]{2,1,0:T(8,128)(2,1)S(1)}, u32[]{:S(2)}, u32[]{:S(2)}) %collective-permute-start) | collective-permute-done | bytes 1048608 | tf_op jit(solution)/shard_map/ppermute | solution.py:328
  31.0 23.1 %sweep.2.refs_5_ = bf16[64,64,128]{2,1,0:T(8,128)(2,1)} custom-call(s32[1536]{0:T(1024)} %reshape.121.refs_0_, bf16[64,64,1536]{2,1,0:T(8,128)(2,1)} %refs_1_.7, bf16[2,64,64,128]{3,2,1,0:T(8,128)(2,1)} %refs_2_.7, bf16[64,64,128]{2,1,0:T(8,128)(2,1)} %get-tuple-element.24.refs_3_, f32[8,128]{1,0:T(8,128)} %maximum_maximum_fusion.refs_4_, ...), custom_call_target="tpu_custom_call" | custom-call | flops 1610612736 | bytes 20971520 | tf_op jit(solution)/shard_map/sweep/pallas_call | solution.py:155
  56.1 7.3 %collective-permute-start.3 = (bf16[64,64,128]{2,1,0:T(8,128)(2,1)}, bf16[64,64,128]{2,1,0:T(8,128)(2,1)S(1)}, u32[]{:S(2)}, u32[]{:S(2)}) collective-permute-start(bf16[64,64,128]{2,1,0:T(8,128)(2,1)} %sweep.2.refs_5_), channel_id=1, source_target_pairs={{1,0},{2,1},{3,2},{4,3},{5,4},{6,5},{7,6},{8,7},{9,8},{10,9},{11,1... | collective-permute-start | bytes 3145736 | tf_op jit(solution)/shard_map/ppermute | solution.py:329
  64.4 23.1 %sweep.3.refs_5_ = bf16[64,64,128]{2,1,0:T(8,128)(2,1)} custom-call(s32[1536]{0:T(1024)} %reshape.121.refs_0_, bf16[64,64,1536]{2,1,0:T(8,128)(2,1)} %refs_1_.7, bf16[2,64,64,128]{3,2,1,0:T(8,128)(2,1)} %refs_2_.7, bf16[64,64,128]{2,1,0:T(8,128)(2,1)} %get-tuple-element.33.refs_3_, f32[8,128]{1,0:T(8,128)} %maximum_maximum_fusion.refs_4_, ...), custom_call_target="tpu_custom_call" | custom-call | flops 1610612736 | bytes 20971520 | tf_op jit(solution)/shard_map/sweep/pallas_call | solution.py:155
  89.5 7.3 %collective-permute-start.12 = (bf16[64,64,128]{2,1,0:T(8,128)(2,1)}, bf16[64,64,128]{2,1,0:T(8,128)(2,1)}, u32[]{:S(2)}, u32[]{:S(2)}) collective-permute-start(bf16[64,64,128]{2,1,0:T(8,128)(2,1)} %sweep.3.refs_5_), channel_id=1, source_target_pairs={{1,0},{2,1},{3,2},{4,3},{5,4},{6,5},{7,6},{8,7},{9,8},{10,9},{11,1... | collective-permute-start | bytes 3145736 | tf_op jit(solution)/shard_map/ppermute | solution.py:329
  98.8 24.4 %sweep_last.2 = (bf16[64,64,128]{2,1,0:T(8,128)(2,1)}, f32[128,128]{1,0:T(8,128)}) custom-call(s32[1536]{0:T(1024)} %reshape.121.refs_0_, bf16[64,64,1536]{2,1,0:T(8,128)(2,1)} %refs_1_.7, bf16[2,64,64,128]{3,2,1,0:T(8,128)(2,1)} %refs_2_.7, bf16[64,64,128]{2,1,0:T(8,128)(2,1)} %get-tuple-element.24.refs_3_, f32[8,128]{1,0:T(8,128)} %maximum_maximum_fusion.refs_4_, ...), custom_call_target="tpu_custom_call" | custom-call | flops 1610612736 | bytes 20971520 | tf_op jit(solution)/shard_map/sweep_last/pallas_call | solution.py:155
  125.1 24.4 %sweep_last.3 = (bf16[64,64,128]{2,1,0:T(8,128)(2,1)}, f32[128,128]{1,0:T(8,128)}) custom-call(s32[1536]{0:T(1024)} %reshape.121.refs_0_, bf16[64,64,1536]{2,1,0:T(8,128)(2,1)} %refs_1_.7, bf16[2,64,64,128]{3,2,1,0:T(8,128)(2,1)} %refs_2_.7, bf16[64,64,128]{2,1,0:T(8,128)(2,1)} %get-tuple-element.33.refs_3_, f32[8,128]{1,0:T(8,128)} %maximum_maximum_fusion.refs_4_, ...), custom_call_target="tpu_custom_call" | custom-call | flops 1610612736 | bytes 20971520 | tf_op jit(solution)/shard_map/sweep_last/pallas_call | solution.py:155
  151.7 4.1 %collective-permute-start.15 = (bf16[2048,128]{1,0:T(8,128)(2,1)S(1)}, bf16[2048,128]{1,0:T(8,128)(2,1)}, u32[]{:S(2)}, u32[]{:S(2)}) collective-permute-start(bf16[2048,128]{1,0:T(8,128)(2,1)S(1)} %bitcast.19), channel_id=1, source_target_pairs={{0,96},{16,112},{32,64},{48,80},{64,32},{80,48},{96,0},{112,16},{1... | collective-permute-start | bytes 1572872 | tf_op jit(solution)/shard_map/ppermute | solution.py:300
  158.2 3.6 %fusion.13 = (bf16[256,256]{1,0:T(8,128)(2,1)}, bf16[256,256]{1,0:T(8,128)(2,1)}, bf16[256,256]{1,0:T(8,128)(2,1)}, bf16[256,256]{1,0:T(8,128)(2,1)}) fusion(s32[256]{0:T(256)S(1)} %get-tuple-element.64, s32[256]{0:T(256)S(1)} %get-tuple-element.68, pred[256]{0:T(512)(128)(4,1)S(1)} %get-tuple-element.62, s32[256]{0:T(256)S(1)} %get-tuple-element.58, ...), kind=kLoop, calls=%fused_computation.45 | loop fusion | flops 6750208 | bytes 533272 | tf_op jit(solution)/shard_map/convert_element_type | solution.py:290
  163.4 5.3 %collective-permute-done.15.peer_ref = bf16[2048,128]{1,0:T(8,128)(2,1)} collective-permute-done((bf16[2048,128]{1,0:T(8,128)(2,1)S(1)}, bf16[2048,128]{1,0:T(8,128)(2,1)}, u32[]{:S(2)}, u32[]{:S(2)}) %collective-permute-start.15) | collective-permute-done | bytes 524320 | tf_op jit(solution)/shard_map/ppermute | solution.py:300
  168.7 4.2 %combine.8 = (bf16[2048,128]{1,0:T(8,128)(2,1)}, f32[2048,128]{1,0:T(8,128)}) custom-call(bf16[4096,128]{1,0:T(8,128)(2,1)} %bitcast.14, bf16[2048,128]{1,0:T(8,128)(2,1)} %collective-permute-done.15.peer_ref, bf16[256,256]{1,0:T(8,128)(2,1)} %get-tuple-element.53.hi_ref, bf16[256,256]{1,0:T(8,128)(2,1)} %get-tuple-element.52.lo_ref), custom_call_target="tpu_custom_call" | custom-call | flops 536870912 | bytes 3145728 | tf_op jit(solution)/shard_map/combine/pallas_call | solution.py:198
  172.9 4.2 %combine.7 = (bf16[2048,128]{1,0:T(8,128)(2,1)}, f32[2048,128]{1,0:T(8,128)}) custom-call(bf16[4096,128]{1,0:T(8,128)(2,1)} %bitcast.15, bf16[2048,128]{1,0:T(8,128)(2,1)} %collective-permute-done.13.peer_ref, bf16[256,256]{1,0:T(8,128)(2,1)} %get-tuple-element.56.hi_ref, bf16[256,256]{1,0:T(8,128)(2,1)} %get-tuple-element.57.lo_ref), custom_call_target="tpu_custom_call" | custom-call | flops 536870912 | bytes 3145728 | tf_op jit(solution)/shard_map/combine/pallas_call | solution.py:198
  177.1 3.2 %collective-permute-start.14 = (bf16[2048,128]{1,0:T(8,128)(2,1)}, bf16[2048,128]{1,0:T(8,128)(2,1)S(1)}, u32[]{:S(2)}, u32[]{:S(2)}) collective-permute-start(bf16[2048,128]{1,0:T(8,128)(2,1)} %get-tuple-element.37), channel_id=1, source_target_pairs={{0,96},{16,112},{32,64},{48,80},{64,32},{80,48},{96,0},{112,16},{1... | collective-permute-start | bytes 1572872 | tf_op jit(solution)/shard_map/ppermute | solution.py:300
  180.4 4.3 %combine.6 = (bf16[2048,128]{1,0:T(8,128)(2,1)}, f32[2048,128]{1,0:T(8,128)}) custom-call(bf16[4096,128]{1,0:T(8,128)(2,1)} %bitcast.12, bf16[2048,128]{1,0:T(8,128)(2,1)} %collective-permute-done.6.peer_ref, bf16[256,256]{1,0:T(8,128)(2,1)} %get-tuple-element.53.hi_ref, bf16[256,256]{1,0:T(8,128)(2,1)} %get-tuple-element.52.lo_ref), custom_call_target="tpu_custom_call" | custom-call | flops 536870912 | bytes 3145728 | tf_op jit(solution)/shard_map/combine/pallas_call | solution.py:198
  186.1 4.2 %combine.5 = (bf16[2048,128]{1,0:T(8,128)(2,1)}, f32[2048,128]{1,0:T(8,128)}) custom-call(bf16[4096,128]{1,0:T(8,128)(2,1)} %bitcast.13, bf16[2048,128]{1,0:T(8,128)(2,1)} %collective-permute-done.4.peer_ref, bf16[256,256]{1,0:T(8,128)(2,1)} %get-tuple-element.56.hi_ref, bf16[256,256]{1,0:T(8,128)(2,1)} %get-tuple-element.57.lo_ref), custom_call_target="tpu_custom_call" | custom-call | flops 536870912 | bytes 3145728 | tf_op jit(solution)/shard_map/combine/pallas_call | solution.py:198
  191.3 6.5 %collective-permute-done.21 = f32[256,128]{1,0:T(8,128)S(1)} collective-permute-done((f32[256,128]{1,0:T(8,128)S(1)}, f32[256,128]{1,0:T(8,128)S(1)}, u32[]{:S(2)}, u32[]{:S(2)}) %collective-permute-start.21) | collective-permute-done | bytes 131104 | tf_op jit(solution)/shard_map/ppermute | solution.py:300
  199.3 5.7 %collective-permute-done.22.peer_ref = bf16[256,128]{1,0:T(8,128)(2,1)S(1)} collective-permute-done((bf16[256,128]{1,0:T(8,128)(2,1)S(1)}, bf16[256,128]{1,0:T(8,128)(2,1)S(1)}, u32[]{:S(2)}, u32[]{:S(2)}) %collective-permute-start.22) | collective-permute-done | bytes 65568 | tf_op jit(solution)/shard_map/ppermute | solution.py:300
  208.9 4.1 %fold.3 = (bf16[2048,128]{1,0:T(8,128)(2,1)}, f32[2048,128]{1,0:T(8,128)}) custom-call(f32[2048,128]{1,0:T(8,128)} %get-tuple-element.36.keep1_ref, bf16[2048,128]{1,0:T(8,128)(2,1)} %copy-done.11, f32[2048,128]{1,0:T(8,128)} %get-tuple-element.38.keep2_ref, bf16[2048,128]{1,0:T(8,128)(2,1)} %copy-done.9), custom_call_target="tpu_custom_call" | custom-call | flops 2097152 | bytes 4718592 | tf_op jit(solution)/shard_map/fold/pallas_call | solution.py:225
  215.2 4.1 %fold.2 = (bf16[2048,128]{1,0:T(8,128)(2,1)}, f32[2048,128]{1,0:T(8,128)}) custom-call(f32[2048,128]{1,0:T(8,128)} %get-tuple-element.27.keep1_ref, bf16[2048,128]{1,0:T(8,128)(2,1)} %copy-done.12, f32[2048,128]{1,0:T(8,128)} %get-tuple-element.29.keep2_ref, bf16[2048,128]{1,0:T(8,128)(2,1)} %copy-done.10), custom_call_target="tpu_custom_call" | custom-call | flops 2097152 | bytes 4718592 | tf_op jit(solution)/shard_map/fold/pallas_call | solution.py:225
  221.5 17.6 %collective-permute-done.24 = bf16[256,64]{1,0:T(8,128)(2,1)S(1)} collective-permute-done((bf16[256,64]{1,0:T(8,128)(2,1)S(1)}, bf16[256,64]{1,0:T(8,128)(2,1)S(1)}, u32[]{:S(2)}, u32[]{:S(2)}) %collective-permute-start.24) | collective-permute-done | bytes 32800 | tf_op jit(solution)/shard_map/ppermute | solution.py:300
  240.9 4.8 %finish.1 = f32[1,2,2048,128]{3,2,1,0:T(8,128)} custom-call(f32[2048,128]{1,0:T(8,128)} %get-tuple-element.31.own_a_ref, bf16[2048,128]{1,0:T(8,128)(2,1)} %copy-done.8, f32[2048,128]{1,0:T(8,128)} %get-tuple-element.40.own_b_ref, bf16[2048,128]{1,0:T(8,128)(2,1)} %copy-done.7), custom_call_target="tpu_custom_call" | custom-call | tf_op jit(solution)/shard_map/finish/pallas_call | solution.py:261
  (104 shorter events, 37.1 us)
Async XLA Ops:
  8.2 19.9 %collective-permute-start = (bf16[64,64,128]{2,1,0:T(8,128)(2,1)}, bf16[64,64,128]{2,1,0:T(8,128)(2,1)S(1)}, u32[]{:S(2)}, u32[]{:S(2)}) collective-permute-start(bf16[64,64,128]{2,1,0:T(8,128)(2,1)} %get-tuple-element.25.refs_5_), channel_id=1, source_target_pairs={{0,1},{1,2},{2,3},{3,4},{4,5},{5,6},{6,7},{7,8},{8,9},{9,10},{10,1... | collective-permute-start | bytes 3145736 | tf_op jit(solution)/shard_map/ppermute | solution.py:328
  10.2 19.9 %collective-permute-start.1 = (bf16[64,64,128]{2,1,0:T(8,128)(2,1)}, bf16[64,64,128]{2,1,0:T(8,128)(2,1)S(1)}, u32[]{:S(2)}, u32[]{:S(2)}) collective-permute-start(bf16[64,64,128]{2,1,0:T(8,128)(2,1)} %get-tuple-element.25.refs_5_), channel_id=1, source_target_pairs={{1,0},{2,1},{3,2},{4,3},{5,4},{6,5},{7,6},{8,7},{9,8},{10,9},{11,1... | collective-permute-start | bytes 3145736 | tf_op jit(solution)/shard_map/ppermute | solution.py:329
  17.4 46.0 %collective-permute-start.10 = (bf16[64,64,128]{2,1,0:T(8,128)(2,1)}, bf16[64,64,128]{2,1,0:T(8,128)(2,1)S(1)}, u32[]{:S(2)}, u32[]{:S(2)}) collective-permute-start(bf16[64,64,128]{2,1,0:T(8,128)(2,1)} %get-tuple-element.34.refs_5_), channel_id=1, source_target_pairs={{1,0},{2,1},{3,2},{4,3},{5,4},{6,5},{7,6},{8,7},{9,8},{10,9},{11,1... | collective-permute-start | bytes 3145736 | tf_op jit(solution)/shard_map/ppermute | solution.py:329
  19.4 44.1 %collective-permute-start.9 = (bf16[64,64,128]{2,1,0:T(8,128)(2,1)}, bf16[64,64,128]{2,1,0:T(8,128)(2,1)}, u32[]{:S(2)}, u32[]{:S(2)}) collective-permute-start(bf16[64,64,128]{2,1,0:T(8,128)(2,1)} %get-tuple-element.34.refs_5_), channel_id=1, source_target_pairs={{0,1},{1,2},{2,3},{3,4},{4,5},{5,6},{6,7},{7,8},{8,9},{9,10},{10,1... | collective-permute-start | bytes 3145736 | tf_op jit(solution)/shard_map/ppermute | solution.py:328
  54.1 42.7 %collective-permute-start.2 = (bf16[64,64,128]{2,1,0:T(8,128)(2,1)}, bf16[64,64,128]{2,1,0:T(8,128)(2,1)S(1)}, u32[]{:S(2)}, u32[]{:S(2)}) collective-permute-start(bf16[64,64,128]{2,1,0:T(8,128)(2,1)} %sweep.2.refs_5_), channel_id=1, source_target_pairs={{0,1},{1,2},{2,3},{3,4},{4,5},{5,6},{6,7},{7,8},{8,9},{9,10},{10,1... | collective-permute-start | bytes 3145736 | tf_op jit(solution)/shard_map/ppermute | solution.py:328
  56.1 40.8 %collective-permute-start.3 = (bf16[64,64,128]{2,1,0:T(8,128)(2,1)}, bf16[64,64,128]{2,1,0:T(8,128)(2,1)S(1)}, u32[]{:S(2)}, u32[]{:S(2)}) collective-permute-start(bf16[64,64,128]{2,1,0:T(8,128)(2,1)} %sweep.2.refs_5_), channel_id=1, source_target_pairs={{1,0},{2,1},{3,2},{4,3},{5,4},{6,5},{7,6},{8,7},{9,8},{10,9},{11,1... | collective-permute-start | bytes 3145736 | tf_op jit(solution)/shard_map/ppermute | solution.py:329
  87.5 36.5 %collective-permute-start.11 = (bf16[64,64,128]{2,1,0:T(8,128)(2,1)}, bf16[64,64,128]{2,1,0:T(8,128)(2,1)S(1)}, u32[]{:S(2)}, u32[]{:S(2)}) collective-permute-start(bf16[64,64,128]{2,1,0:T(8,128)(2,1)} %sweep.3.refs_5_), channel_id=1, source_target_pairs={{0,1},{1,2},{2,3},{3,4},{4,5},{5,6},{6,7},{7,8},{8,9},{9,10},{10,1... | collective-permute-start | bytes 3145736 | tf_op jit(solution)/shard_map/ppermute | solution.py:328
  89.5 34.6 %collective-permute-start.12 = (bf16[64,64,128]{2,1,0:T(8,128)(2,1)}, bf16[64,64,128]{2,1,0:T(8,128)(2,1)}, u32[]{:S(2)}, u32[]{:S(2)}) collective-permute-start(bf16[64,64,128]{2,1,0:T(8,128)(2,1)} %sweep.3.refs_5_), channel_id=1, source_target_pairs={{1,0},{2,1},{3,2},{4,3},{5,4},{6,5},{7,6},{8,7},{9,8},{10,9},{11,1... | collective-permute-start | bytes 3145736 | tf_op jit(solution)/shard_map/ppermute | solution.py:329
  150.4 7.7 %collective-permute-start.18 = (f32[256,128]{1,0:T(8,128)S(1)}, f32[256,128]{1,0:T(8,128)S(1)}, u32[]{:S(2)}, u32[]{:S(2)}) collective-permute-start(f32[256,128]{1,0:T(8,128)S(1)} %constant_dynamic-update-slice_fusion), channel_id=1, source_target_pairs={{0,1},{1,0},{2,3},{3,2},{4,5},{5,4},{6,7},{7,6},{8,9},{9,8},{10,11... | collective-permute-start | bytes 393224 | tf_op jit(solution)/shard_map/ppermute | solution.py:300
  151.7 17.0 %collective-permute-start.15 = (bf16[2048,128]{1,0:T(8,128)(2,1)S(1)}, bf16[2048,128]{1,0:T(8,128)(2,1)}, u32[]{:S(2)}, u32[]{:S(2)}) collective-permute-start(bf16[2048,128]{1,0:T(8,128)(2,1)S(1)} %bitcast.19), channel_id=1, source_target_pairs={{0,96},{16,112},{32,64},{48,80},{64,32},{80,48},{96,0},{112,16},{1... | collective-permute-start | bytes 1572872 | tf_op jit(solution)/shard_map/ppermute | solution.py:300
  155.8 17.1 %collective-permute-start.13 = (bf16[2048,128]{1,0:T(8,128)(2,1)S(1)}, bf16[2048,128]{1,0:T(8,128)(2,1)}, u32[]{:S(2)}, u32[]{:S(2)}) collective-permute-start(bf16[2048,128]{1,0:T(8,128)(2,1)S(1)} %bitcast.18), channel_id=1, source_target_pairs={{0,32},{16,48},{32,0},{48,16},{64,96},{80,112},{96,64},{112,80},{1... | collective-permute-start | bytes 1572872 | tf_op jit(solution)/shard_map/ppermute | solution.py:300
  155.9 24.5 %collective-permute-start.6 = (bf16[2048,128]{1,0:T(8,128)(2,1)S(1)}, bf16[2048,128]{1,0:T(8,128)(2,1)}, u32[]{:S(2)}, u32[]{:S(2)}) collective-permute-start(bf16[2048,128]{1,0:T(8,128)(2,1)S(1)} %bitcast.17), channel_id=1, source_target_pairs={{0,96},{16,112},{32,64},{48,80},{64,32},{80,48},{96,0},{112,16},{1... | collective-permute-start | bytes 1572872 | tf_op jit(solution)/shard_map/ppermute | solution.py:300
  156.5 29.6 %collective-permute-start.4 = (bf16[2048,128]{1,0:T(8,128)(2,1)S(1)}, bf16[2048,128]{1,0:T(8,128)(2,1)}, u32[]{:S(2)}, u32[]{:S(2)}) collective-permute-start(bf16[2048,128]{1,0:T(8,128)(2,1)S(1)} %bitcast.16), channel_id=1, source_target_pairs={{0,32},{16,48},{32,0},{48,16},{64,96},{80,112},{96,64},{112,80},{1... | collective-permute-start | bytes 1572872 | tf_op jit(solution)/shard_map/ppermute | solution.py:300
  163.3 27.9 %collective-permute-start.20 = (f32[256,128]{1,0:T(8,128)S(1)}, f32[256,128]{1,0:T(8,128)S(1)}, u32[]{:S(2)}, u32[]{:S(2)}) collective-permute-start(f32[256,128]{1,0:T(8,128)S(1)} %add.178), channel_id=1, source_target_pairs={{0,4},{1,5},{2,6},{3,7},{4,0},{5,1},{6,2},{7,3},{8,12},{9,13},{10,... | collective-permute-start | bytes 393224 | tf_op jit(solution)/shard_map/ppermute | solution.py:300
  172.9 35.0 %collective-permute-start.16 = (bf16[2048,128]{1,0:T(8,128)(2,1)}, bf16[2048,128]{1,0:T(8,128)(2,1)S(1)}, u32[]{:S(2)}, u32[]{:S(2)}) collective-permute-start(bf16[2048,128]{1,0:T(8,128)(2,1)} %get-tuple-element.39), channel_id=1, source_target_pairs={{0,32},{16,48},{32,0},{48,16},{64,96},{80,112},{96,64},{112,80},{1... | collective-permute-start | bytes 1572872 | tf_op jit(solution)/shard_map/ppermute | solution.py:300
  177.1 30.8 %collective-permute-start.14 = (bf16[2048,128]{1,0:T(8,128)(2,1)}, bf16[2048,128]{1,0:T(8,128)(2,1)S(1)}, u32[]{:S(2)}, u32[]{:S(2)}) collective-permute-start(bf16[2048,128]{1,0:T(8,128)(2,1)} %get-tuple-element.37), channel_id=1, source_target_pairs={{0,96},{16,112},{32,64},{48,80},{64,32},{80,48},{96,0},{112,16},{1... | collective-permute-start | bytes 1572872 | tf_op jit(solution)/shard_map/ppermute | solution.py:300
  184.6 29.5 %collective-permute-start.7 = (bf16[2048,128]{1,0:T(8,128)(2,1)}, bf16[2048,128]{1,0:T(8,128)(2,1)S(1)}, u32[]{:S(2)}, u32[]{:S(2)}) collective-permute-start(bf16[2048,128]{1,0:T(8,128)(2,1)} %get-tuple-element.30), channel_id=1, source_target_pairs={{0,32},{16,48},{32,0},{48,16},{64,96},{80,112},{96,64},{112,80},{1... | collective-permute-start | bytes 1572872 | tf_op jit(solution)/shard_map/ppermute | solution.py:300
  190.2 24.0 %collective-permute-start.5 = (bf16[2048,128]{1,0:T(8,128)(2,1)}, bf16[2048,128]{1,0:T(8,128)(2,1)S(1)}, u32[]{:S(2)}, u32[]{:S(2)}) collective-permute-start(bf16[2048,128]{1,0:T(8,128)(2,1)} %get-tuple-element.28), channel_id=1, source_target_pairs={{0,96},{16,112},{32,64},{48,80},{64,32},{80,48},{96,0},{112,16},{1... | collective-permute-start | bytes 1572872 | tf_op jit(solution)/shard_map/ppermute | solution.py:300
  191.2 6.6 %collective-permute-start.21 = (f32[256,128]{1,0:T(8,128)S(1)}, f32[256,128]{1,0:T(8,128)S(1)}, u32[]{:S(2)}, u32[]{:S(2)}) collective-permute-start(f32[256,128]{1,0:T(8,128)S(1)} %add.179), channel_id=1, source_target_pairs={{0,8},{1,9},{2,10},{3,11},{4,12},{5,13},{6,14},{7,15},{8,0},{9,1},... | collective-permute-start | bytes 393224 | tf_op jit(solution)/shard_map/ppermute | solution.py:300
  197.8 7.2 %collective-permute-start.22 = (bf16[256,128]{1,0:T(8,128)(2,1)S(1)}, bf16[256,128]{1,0:T(8,128)(2,1)S(1)}, u32[]{:S(2)}, u32[]{:S(2)}) collective-permute-start(bf16[256,128]{1,0:T(8,128)(2,1)S(1)} %add_convert_fusion.own_ref), channel_id=1, source_target_pairs={{0,32},{16,48},{32,0},{48,16},{64,96},{80,112},{96,64},{112,80},{1... | collective-permute-start | bytes 196616 | tf_op jit(solution)/shard_map/ppermute | solution.py:300
  207.6 12.6 %collective-permute-start.23 = (bf16[256,128]{1,0:T(8,128)(2,1)}, bf16[256,128]{1,0:T(8,128)(2,1)S(1)}, u32[]{:S(2)}, u32[]{:S(2)}) collective-permute-start(bf16[256,128]{1,0:T(8,128)(2,1)} %get-tuple-element.45), channel_id=1, source_target_pairs={{0,96},{16,112},{32,64},{48,80},{64,32},{80,48},{96,0},{112,16},{1... | collective-permute-start | bytes 196616 | tf_op jit(solution)/shard_map/ppermute | solution.py:300
  213.0 27.0 %collective-permute-start.17 = (bf16[2048,128]{1,0:T(8,128)(2,1)}, bf16[2048,128]{1,0:T(8,128)(2,1)S(1)}, u32[]{:S(2)}, u32[]{:S(2)}) collective-permute-start(bf16[2048,128]{1,0:T(8,128)(2,1)} %get-tuple-element.41), channel_id=1, source_target_pairs={{0,16},{16,0},{32,48},{48,32},{64,80},{80,64},{96,112},{112,96},{1... | collective-permute-start | bytes 1572872 | tf_op jit(solution)/shard_map/ppermute | solution.py:300
  219.3 20.7 %collective-permute-start.8 = (bf16[2048,128]{1,0:T(8,128)(2,1)}, bf16[2048,128]{1,0:T(8,128)(2,1)S(1)}, u32[]{:S(2)}, u32[]{:S(2)}) collective-permute-start(bf16[2048,128]{1,0:T(8,128)(2,1)} %get-tuple-element.32), channel_id=1, source_target_pairs={{0,16},{16,0},{32,48},{48,32},{64,80},{80,64},{96,112},{112,96},{1... | collective-permute-start | bytes 1572872 | tf_op jit(solution)/shard_map/ppermute | solution.py:300
  220.2 18.8 %collective-permute-start.24 = (bf16[256,64]{1,0:T(8,128)(2,1)S(1)}, bf16[256,64]{1,0:T(8,128)(2,1)S(1)}, u32[]{:S(2)}, u32[]{:S(2)}) collective-permute-start(bf16[256,64]{1,0:T(8,128)(2,1)S(1)} %slice.47), channel_id=1, source_target_pairs={{0,16},{16,0},{32,48},{48,32},{64,80},{80,64},{96,112},{112,96},{1... | collective-permute-start | bytes 98312 | tf_op jit(solution)/shard_map/ppermute | solution.py:300
  (19 other events, 80.9 us)

commit v2 on v1

--- a/solution.py
+++ b/solution.py
@@ -79,6 +79,7 @@
         ],
         out_specs=[out_spec] * 4,
         out_shape=[block] * 4,
+        compiler_params=pltpu.CompilerParams(vmem_limit_bytes=8 << 20),
         name="initial",
     )(rhs, precond, jnp.asarray(unit_lanes(), BF16))
 
@@ -92,12 +93,13 @@
 
 def sweep_kernel(
     last, index_ref, ham_ref, pre_ref, rhs_ref, z_ref, local_ref, before_ref, after_ref, x_ref,
-    out_ref, *rest
+    out_ref, *rest,
 ):
     if last:
-        gram_ref, held, sems = rest
+        second_ref, gram_ref, held, sems, fresh = rest
     else:
         held, sems = rest
+        fresh = out_ref
     step = pl.program_id(0)
 
     @pl.when(step == 0)
@@ -116,38 +118,61 @@
 
     zreal = z_ref[0:1, :]
     zimag = z_ref[1:2, :]
+    totals = []
     for b in range(STEP):
         row = step * STEP + b
-        total = jnp.zeros((BS, LANES), F32)
-        for g in range(SLOTS // 4):
-            right = jnp.concatenate(
-                [held[index_ref[row * SLOTS + g * 4 + s]] for s in range(4)], axis=0
-            )
-            left = ham_ref[b, :, g * 4 * BS : (g + 1) * 4 * BS]
-            total = total + jnp.dot(left, right, preferred_element_type=F32)
-        current = held[RB + row].astype(F32)
+        right = jnp.concatenate(
+            [held[index_ref[row * SLOTS + s]] for s in range(SLOTS)], axis=0
+        )
+        totals.append(jnp.dot(ham_ref[b], right, preferred_element_type=F32))
+    rights = []
+    for b in range(STEP):
+        current = held[RB + step * STEP + b].astype(F32)
         shifted = zreal * current + zimag * rotate_lanes(current)
-        resid = (rhs_ref[b].astype(F32) - (shifted - total)).astype(BF16).astype(F32)
-        right = split_points(resid, rotate_lanes(resid)).astype(BF16)
+        resid = (rhs_ref[b].astype(F32) - (shifted - totals[b])).astype(BF16).astype(F32)
+        rights.append(split_points(resid, rotate_lanes(resid)).astype(BF16))
+    for b in range(STEP):
+        current = held[RB + step * STEP + b].astype(F32)
         left = jnp.concatenate([pre_ref[0, b], pre_ref[1, b]], axis=1)
-        out_ref[b] = (current + jnp.dot(left, right, preferred_element_type=F32)).astype(BF16)
+        fresh[b] = (current + jnp.dot(left, rights[b], preferred_element_type=F32)).astype(BF16)
     if last:
         gram_ref[...] += lax.dot_general(
             x_ref[...],
-            out_ref[...].reshape(STEP * BS, LANES),
+            fresh[...].reshape(STEP * BS, LANES),
             (((0,), (0,)), ((), ())),
             preferred_element_type=F32,
         )
+        steps = pl.num_programs(0)
+
+        @pl.when(step < steps // 2)
+        def _():
+            out_ref[...] = fresh[...]
+
+        @pl.when(step >= steps // 2)
+        def _():
+            second_ref[...] = fresh[...]
 
 
 def sweep(index, ham, precond, rhs_unit, z, local, before, after, rhs, last):
     block = pl.BlockSpec((STEP, BS, LANES), lambda i, n: (i, 0, 0))
     anywhere = pl.BlockSpec(memory_space=pl.ANY)
-    out_specs = [block]
-    out_shape = [jax.ShapeDtypeStruct((RB, BS, LANES), BF16)]
+    scratch = [
+        pltpu.VMEM((3 * RB + 1, BS, LANES), BF16),
+        pltpu.SemaphoreType.DMA((3,)),
+    ]
     if last:
-        out_specs.append(pl.BlockSpec((LANES, LANES), lambda i, n: (0, 0)))
+        half = RB // STEP // 2
+        out_specs = [
+            pl.BlockSpec((STEP, BS, LANES), lambda i, n: (jnp.minimum(i, half - 1), 0, 0)),
+            pl.BlockSpec((STEP, BS, LANES), lambda i, n: (jnp.maximum(i - half, 0), 0, 0)),
+            pl.BlockSpec((LANES, LANES), lambda i, n: (0, 0)),
+        ]
+        out_shape = [jax.ShapeDtypeStruct((RB // 2, BS, LANES), BF16)] * 2
         out_shape.append(jax.ShapeDtypeStruct((LANES, LANES), F32))
+        scratch.append(pltpu.VMEM((STEP, BS, LANES), BF16))
+    else:
+        out_specs = [block]
+        out_shape = [jax.ShapeDtypeStruct((RB, BS, LANES), BF16)]
 
     def kernel(*refs):
         sweep_kernel(last, *refs)
@@ -168,47 +193,43 @@
                 pl.BlockSpec((STEP * BS, LANES), lambda i, n: (i, 0)),
             ],
             out_specs=out_specs,
-            scratch_shapes=[
-                pltpu.VMEM((3 * RB + 1, BS, LANES), BF16),
-                pltpu.SemaphoreType.DMA((3,)),
-            ],
+            scratch_shapes=scratch,
         ),
         out_shape=out_shape,
         cost_estimate=pl.CostEstimate(
             flops=2 * RB * BS * SLOTS * BS * LANES, bytes_accessed=20 << 20, transcendentals=0
         ),
+        compiler_params=pltpu.CompilerParams(vmem_limit_bytes=14 << 20),
         name="sweep_last" if last else "sweep",
     )(index, ham, precond, rhs_unit, z, local, before, after, rhs)
 
 
-def combine_kernel(own_ref, peer_ref, hi_ref, lo_ref, send_ref, keep_ref):
-    both = jnp.concatenate([own_ref[...], peer_ref[...]], axis=1)
-    out = jnp.dot(both, hi_ref[...], preferred_element_type=F32)
-    out = out + jnp.dot(both, lo_ref[...], preferred_element_type=F32)
+def combine_kernel(own_ref, peer_ref, weight_ref, send_ref, keep_ref):
+    own, peer = own_ref[...], peer_ref[...]
+    both = jnp.concatenate([own, peer, own, peer], axis=1)
+    out = jnp.dot(both, weight_ref[...], preferred_element_type=F32)
     send_ref[...] = out[:, :LANES].astype(BF16)
     keep_ref[...] = out[:, LANES:]
 
 
-def combine(own, peer, weights, rows_step, offset):
+def combine(own, peer, weights, rows_step):
     rows = peer.shape[0]
-    hi, lo = weights
-    base = offset // rows_step
     row_spec = pl.BlockSpec((rows_step, LANES), lambda i: (i, 0))
-    mat = pl.BlockSpec((2 * LANES, 2 * LANES), lambda i: (0, 0))
     return pl.pallas_call(
         combine_kernel,
         grid=(rows // rows_step,),
-        in_specs=[pl.BlockSpec((rows_step, LANES), lambda i: (i + base, 0)), row_spec, mat, mat],
+        in_specs=[row_spec, row_spec, pl.BlockSpec((4 * LANES, 2 * LANES), lambda i: (0, 0))],
         out_specs=[row_spec, row_spec],
         out_shape=[
             jax.ShapeDtypeStruct((rows, LANES), BF16),
             jax.ShapeDtypeStruct((rows, LANES), F32),
         ],
+        compiler_params=pltpu.CompilerParams(vmem_limit_bytes=8 << 20),
         cost_estimate=pl.CostEstimate(
             flops=2 * rows * 256 * 512, bytes_accessed=rows * LANES * 12, transcendentals=0
         ),
         name="combine",
-    )(own, peer, hi, lo)
+    )(own, peer, weights)
 
 
 def fold_kernel(keep1_ref, got1_ref, keep2_ref, got2_ref, send_ref, own_ref):
@@ -234,6 +255,7 @@
         cost_estimate=pl.CostEstimate(
             flops=rows * LANES * 8, bytes_accessed=rows * LANES * 18, transcendentals=0
         ),
+        compiler_params=pltpu.CompilerParams(vmem_limit_bytes=10 << 20),
         name="fold",
     )(keep1, got1, keep2, got2)
 
@@ -264,6 +286,7 @@
         in_specs=[spec] * 4,
         out_specs=pl.BlockSpec((1, 2, rows_step, LANES), lambda i: (0, 0, i, 0)),
         out_shape=jax.ShapeDtypeStruct((1, 2, rows, LANES), F32),
+        compiler_params=pltpu.CompilerParams(vmem_limit_bytes=10 << 20),
         name="finish",
     )(own_a, got_a, own_b, got_b)
 
@@ -287,7 +310,7 @@
     value = jnp.where(part_in == part_out, jnp.cos(phase), sine) / POINTS
     value = jnp.where(r % HALF == c % HALF, value, 0.0)
     high = lax.reduce_precision(value, 8, 7)
-    return high.astype(BF16), (value - high).astype(BF16)
+    return jnp.concatenate([high.astype(BF16), (value - high).astype(BF16)], axis=0)
 
 
 def shards(hamiltonian, columns, counts, precond, rhs):
@@ -333,7 +356,8 @@
             )
             units[unit] = got[0]
             if last:
-                grams[unit] = got[1]
+                units[unit] = got[:2]
+                grams[unit] = got[2]
 
     mine, other = quad_index, quad_index ^ 1
     pair, mirror = by_pair(quad_index), by_mirror(quad_index)
@@ -343,21 +367,21 @@
     half_rows = RB * BS // 2
     sums = []
     for unit in range(2):
-        flat = units[unit].reshape(RB * BS, LANES)
-        got1 = swap(flat[:half_rows], "quad", by_pair)
-        got2 = swap(flat[half_rows:], "quad", by_mirror)
-        send1, keep1 = combine(flat, got1, w_pair, 512, 0)
-        send2, keep2 = combine(flat, got2, w_mirror, 512, half_rows)
+        top, bottom = (part.reshape(half_rows, LANES) for part in units[unit])
+        got1 = swap(top, "quad", by_pair)
+        got2 = swap(bottom, "quad", by_mirror)
+        send1, keep1 = combine(top, got1, w_pair, 1024)
+        send2, keep2 = combine(bottom, got2, w_mirror, 1024)
         back1 = swap(send1, "quad", by_mirror)
         back2 = swap(send2, "quad", by_pair)
-        send3, own = fold(keep1, back1, keep2, back2, 512)
+        send3, own = fold(keep1, back1, keep2, back2, 1024)
         sums.append((send3, own))
 
     gram = jnp.concatenate(grams, axis=0)
     for bit in (1, 2, 4, 8):
         gram = gram + swap(gram, "row", lambda i, bit=bit: i ^ bit)
     gram = gram.astype(BF16)
-    send_g, keep_g = combine(gram, swap(gram, "quad", by_pair), w_pair, 256, 0)
+    send_g, keep_g = combine(gram, swap(gram, "quad", by_pair), w_pair, 256)
     gram_sum = keep_g + swap(send_g, "quad", by_mirror).astype(F32)
     gram_got = swap(gram_sum[:, GROUP:].astype(BF16), "quad", by_x)
     blocks = gram_sum[:, :GROUP] + gram_got.astype(F32)

time: 247 us -> 194 us (0.79)
  Pallas kernels: 134 us -> 58.6 us
  waiting for transfers between devices: 43.2 us -> 61.9 us
  local copies, waits for them, and re-layouts: 13.4 us -> 18.5 us
    pallas_call x4, Pallas kernels: 95.1 us -> 44.4 us  [sweep(): pl.pallas_call(kernel, grid_spec=pltpu.PrefetchScalarGridSpec(num_scalar_...]
    ppermute x17, waiting for transfers between devices: 36.5 us -> 54 us  [swap(): return lax.ppermute(x, axis, [(i, peer_of(i)) for i in range(size)])]
    pallas_call x5, Pallas kernels: 18.8 us -> 3.77 us  [combine(): pl.pallas_call(combine_kernel, grid=(rows // rows_step,), in_specs=[row_s...]
    unnamed x38 -> x32, local copies, waits for them, and re-layouts: 10 us -> 18.1 us
    pallas_call x2, Pallas kernels: 8.14 us -> 2.28 us  [fold(): pl.pallas_call(fold_kernel, grid=(rows // rows_step,), in_specs=[spec] *...]
  transfers between devices with their start and end apart: 25 -> 25, of which waited for: 7 -> 11; matrix products, arithmetic and copies ran while one was open for 3% -> 3% of each run, Pallas kernels for 40% -> 20%
where the time goes in v2:
time: 194 us; the launch traced here: 193 us
  waiting for transfers between devices  61.9 us (32%)
  Pallas kernels  58.6 us (30%)
  starting transfers between devices  48.6 us (25%)
  local copies, waits for them, and re-layouts  18.5 us (10%)
  other arithmetic  4.22 us (2%)
    ppermute x17, waiting for transfers between devices, swap(): return lax.ppermute(x, axis, [(i, peer_of(i)) for i in range(size)])  54 us
    pallas_call x4, Pallas kernels, sweep(): pl.pallas_call(kernel, grid_spec=pltpu.PrefetchScalarGridSpec(num_scalar_...  44.4 us
    ppermute x4, starting transfers between devices, shards(): after = lax.ppermute(y, 'row', down)  23.9 us
    unnamed x32, local copies, waits for them, and re-layouts  18.1 us
    ppermute x17, starting transfers between devices, swap(): return lax.ppermute(x, axis, [(i, peer_of(i)) for i in range(size)])  16.5 us
    ppermute x4, starting transfers between devices, shards(): before = lax.ppermute(y, 'row', up)  8.16 us
    ppermute x4, waiting for transfers between devices, shards(): before = lax.ppermute(y, 'row', up)  6.09 us
    pallas_call x1, Pallas kernels, initial(): pl.pallas_call(init_kernel, grid=(RB // STEP,), in_specs=[pl.BlockSpec((S...  5.14 us
  transfers between devices with their start and end apart: 25, of which 11 were waited for; matrix products, arithmetic and copies ran while one was open for 3% of the time, Pallas kernels for 20%

profile of v2, /device:TPU:4, one launch (start us, length us, event | category | flops | bytes accessed | tf_op | source)
XLA Modules:
  0.0 192.9 jit_solution(15582274069315996310)
XLA Ops:
  4.4 5.1 %initial.1 = (bf16[64,64,128]{2,1,0:T(8,128)(2,1)S(1)}, bf16[64,64,128]{2,1,0:T(8,128)(2,1)S(1)}, bf16[64,64,128]{2,1,0:T(8,128)(2,1)}, bf16[64,64,128]{2,1,0:T(8,128)(2,1)}) custom-call(bf16[4096,128]{1,0:T(8,128)(2,1)S(1)} %copy-done.4, bf16[2,64,64,128]{3,2,1,0:T(8,128)(2,1)S(1)} %copy-done.2, bf16[128,512]{1,0:T(8,128)(2,1)S(1)} %copy-done.12), custom_call_target="tpu_custom_call" | custom-call | tf_op jit(solution)/shard_map/initial/pallas_call | solution.py:72
  13.4 7.3 %collective-permute-start.1 = (bf16[64,64,128]{2,1,0:T(8,128)(2,1)}, bf16[64,64,128]{2,1,0:T(8,128)(2,1)}, u32[]{:S(2)}, u32[]{:S(2)}) collective-permute-start(bf16[64,64,128]{2,1,0:T(8,128)(2,1)} %get-tuple-element.27.refs_5_), channel_id=1, source_target_pairs={{1,0},{2,1},{3,2},{4,3},{5,4},{6,5},{7,6},{8,7},{9,8},{10,9},{11,1... | collective-permute-start | bytes 3145736 | tf_op jit(solution)/shard_map/ppermute | solution.py:352
  20.7 1.9 collective-permute-start.10
  22.6 2.4 %collective-permute-start.9 = (bf16[64,64,128]{2,1,0:T(8,128)(2,1)}, bf16[64,64,128]{2,1,0:T(8,128)(2,1)}, u32[]{:S(2)}, u32[]{:S(2)}) collective-permute-start(bf16[64,64,128]{2,1,0:T(8,128)(2,1)} %get-tuple-element.37.refs_5_), channel_id=1, source_target_pairs={{0,1},{1,2},{2,3},{3,4},{4,5},{5,6},{6,7},{7,8},{8,9},{9,10},{10,1... | collective-permute-start | bytes 3145736 | tf_op jit(solution)/shard_map/ppermute | solution.py:351
  25.4 6.1 %collective-permute-done.refs_6_ = bf16[64,64,128]{2,1,0:T(8,128)(2,1)} collective-permute-done((bf16[64,64,128]{2,1,0:T(8,128)(2,1)}, bf16[64,64,128]{2,1,0:T(8,128)(2,1)}, u32[]{:S(2)}, u32[]{:S(2)}) %collective-permute-start) | collective-permute-done | bytes 1048608 | tf_op jit(solution)/shard_map/ppermute | solution.py:351
  33.3 4.6 %copy-done = bf16[64,64,1536]{2,1,0:T(8,128)(2,1)S(1)} copy-done((bf16[64,64,1536]{2,1,0:T(8,128)(2,1)S(1)}, bf16[64,64,1536]{2,1,0:T(8,128)(2,1)}, u32[]{:S(2)}) %copy-start) | copy-done | bytes 12582936
  39.1 10.7 %sweep.2.refs_5_ = bf16[64,64,128]{2,1,0:T(8,128)(2,1)} custom-call(s32[1536]{0:T(1024)S(1)} %reshape.123.refs_0_, bf16[64,64,1536]{2,1,0:T(8,128)(2,1)S(1)} %copy-done, bf16[2,64,64,128]{3,2,1,0:T(8,128)(2,1)S(1)} %copy-done.3, bf16[64,64,128]{2,1,0:T(8,128)(2,1)S(1)} %copy-done.10, f32[8,128]{1,0:T(8,128)S(1)} %maximum_maximum_fusion.refs_4_, ...), custom_call_target="tpu_custom_call" | custom-call | flops 1610612736 | bytes 20971520 | tf_op jit(solution)/shard_map/sweep/pallas_call | solution.py:180
  51.7 7.4 %collective-permute-start.3 = (bf16[64,64,128]{2,1,0:T(8,128)(2,1)}, bf16[64,64,128]{2,1,0:T(8,128)(2,1)}, u32[]{:S(2)}, u32[]{:S(2)}) collective-permute-start(bf16[64,64,128]{2,1,0:T(8,128)(2,1)} %sweep.2.refs_5_), channel_id=1, source_target_pairs={{1,0},{2,1},{3,2},{4,3},{5,4},{6,5},{7,6},{8,7},{9,8},{10,9},{11,1... | collective-permute-start | bytes 3145736 | tf_op jit(solution)/shard_map/ppermute | solution.py:352
  59.2 10.7 %sweep.3.refs_5_ = bf16[64,64,128]{2,1,0:T(8,128)(2,1)} custom-call(s32[1536]{0:T(1024)S(1)} %reshape.123.refs_0_, bf16[64,64,1536]{2,1,0:T(8,128)(2,1)S(1)} %copy-done, bf16[2,64,64,128]{3,2,1,0:T(8,128)(2,1)S(1)} %copy-done.3, bf16[64,64,128]{2,1,0:T(8,128)(2,1)S(1)} %copy-done.7, f32[8,128]{1,0:T(8,128)S(1)} %maximum_maximum_fusion.refs_4_, ...), custom_call_target="tpu_custom_call" | custom-call | flops 1610612736 | bytes 20971520 | tf_op jit(solution)/shard_map/sweep/pallas_call | solution.py:180
  69.8 1.9 collective-permute-start.11
  71.8 7.3 %collective-permute-start.12 = (bf16[64,64,128]{2,1,0:T(8,128)(2,1)}, bf16[64,64,128]{2,1,0:T(8,128)(2,1)}, u32[]{:S(2)}, u32[]{:S(2)}) collective-permute-start(bf16[64,64,128]{2,1,0:T(8,128)(2,1)} %sweep.3.refs_5_), channel_id=1, source_target_pairs={{1,0},{2,1},{3,2},{4,3},{5,4},{6,5},{7,6},{8,7},{9,8},{10,9},{11,1... | collective-permute-start | bytes 3145736 | tf_op jit(solution)/shard_map/ppermute | solution.py:352
  79.2 4.6 %copy-done.1 = bf16[64,64,1536]{2,1,0:T(8,128)(2,1)S(1)} copy-done((bf16[64,64,1536]{2,1,0:T(8,128)(2,1)S(1)}, bf16[64,64,1536]{2,1,0:T(8,128)(2,1)}, u32[]{:S(2)}) %copy-start.1) | copy-done | bytes 12582936
  85.0 11.5 %sweep_last.2 = (bf16[32,64,128]{2,1,0:T(8,128)(2,1)S(1)}, bf16[32,64,128]{2,1,0:T(8,128)(2,1)S(1)}, f32[128,128]{1,0:T(8,128)S(1)}) custom-call(s32[1536]{0:T(1024)S(1)} %reshape.123.refs_0_, bf16[64,64,1536]{2,1,0:T(8,128)(2,1)S(1)} %copy-done.1, bf16[2,64,64,128]{3,2,1,0:T(8,128)(2,1)S(1)} %copy-done.3, bf16[64,64,128]{2,1,0:T(8,128)(2,1)S(1)} %copy-done.11, ...), custom_call_target="tpu_custom_call" | custom-call | flops 1610612736 | bytes 20971520 | tf_op jit(solution)/shard_map/sweep_last/pallas_call | solution.py:180
  96.5 11.6 %sweep_last.3 = (bf16[32,64,128]{2,1,0:T(8,128)(2,1)S(1)}, bf16[32,64,128]{2,1,0:T(8,128)(2,1)S(1)}, f32[128,128]{1,0:T(8,128)S(1)}) custom-call(s32[1536]{0:T(1024)S(1)} %reshape.123.refs_0_, bf16[64,64,1536]{2,1,0:T(8,128)(2,1)S(1)} %copy-done.1, bf16[2,64,64,128]{3,2,1,0:T(8,128)(2,1)S(1)} %copy-done.3, bf16[64,64,128]{2,1,0:T(8,128)(2,1)S(1)} %copy-done.8, ...), custom_call_target="tpu_custom_call" | custom-call | flops 1610612736 | bytes 20971520 | tf_op jit(solution)/shard_map/sweep_last/pallas_call | solution.py:180
  108.2 4.1 %collective-permute-start.15 = (bf16[2048,128]{1,0:T(8,128)(2,1)S(1)}, bf16[2048,128]{1,0:T(8,128)(2,1)S(1)}, u32[]{:S(2)}, u32[]{:S(2)}) collective-permute-start(bf16[2048,128]{1,0:T(8,128)(2,1)S(1)} %bitcast.15), channel_id=1, source_target_pairs={{0,96},{16,112},{32,64},{48,80},{64,32},{80,48},{96,0},{112,16},{1... | collective-permute-start | bytes 1572872 | tf_op jit(solution)/shard_map/ppermute | solution.py:323
  114.4 3.9 %reduce-precision_convert_fusion = (bf16[256,256]{1,0:T(8,128)(2,1)S(1)}, bf16[256,256]{1,0:T(8,128)(2,1)S(1)}, bf16[256,256]{1,0:T(8,128)(2,1)S(1)}, bf16[256,256]{1,0:T(8,128)(2,1)S(1)}) fusion(s32[256]{0:T(256)S(1)} %get-tuple-element.64, s32[256]{0:T(256)S(1)} %get-tuple-element.68, pred[256]{0:T(512)(128)(4,1)S(1)} %get-tuple-element.62, ...), kind=kLoop, calls=%fused_computation.25 | loop fusion | flops 6750208 | bytes 533272 | tf_op jit(solution)/shard_map/convert_element_type | solution.py:313
  118.5 4.9 %collective-permute-done.19 = f32[256,128]{1,0:T(8,128)S(1)} collective-permute-done((f32[256,128]{1,0:T(8,128)S(1)}, f32[256,128]{1,0:T(8,128)S(1)}, u32[]{:S(2)}, u32[]{:S(2)}) %collective-permute-start.19) | collective-permute-done | bytes 131104 | tf_op jit(solution)/shard_map/ppermute | solution.py:323
  128.0 2.3 %collective-permute-start.14 = (bf16[2048,128]{1,0:T(8,128)(2,1)S(1)}, bf16[2048,128]{1,0:T(8,128)(2,1)S(1)}, u32[]{:S(2)}, u32[]{:S(2)}) collective-permute-start(bf16[2048,128]{1,0:T(8,128)(2,1)S(1)} %get-tuple-element.40), channel_id=1, source_target_pairs={{0,96},{16,112},{32,64},{48,80},{64,32},{80,48},{96,0},{112,16},{1... | collective-permute-start | bytes 1572872 | tf_op jit(solution)/shard_map/ppermute | solution.py:323
  130.3 6.0 %collective-permute-done.6.peer_ref = bf16[2048,128]{1,0:T(8,128)(2,1)S(1)} collective-permute-done((bf16[2048,128]{1,0:T(8,128)(2,1)S(1)}, bf16[2048,128]{1,0:T(8,128)(2,1)S(1)}, u32[]{:S(2)}, u32[]{:S(2)}) %collective-permute-start.6) | collective-permute-done | bytes 524320 | tf_op jit(solution)/shard_map/ppermute | solution.py:323
  139.3 2.3 %collective-permute-start.5 = (bf16[2048,128]{1,0:T(8,128)(2,1)S(1)}, bf16[2048,128]{1,0:T(8,128)(2,1)S(1)}, u32[]{:S(2)}, u32[]{:S(2)}) collective-permute-start(bf16[2048,128]{1,0:T(8,128)(2,1)S(1)} %get-tuple-element.30), channel_id=1, source_target_pairs={{0,96},{16,112},{32,64},{48,80},{64,32},{80,48},{96,0},{112,16},{1... | collective-permute-start | bytes 1572872 | tf_op jit(solution)/shard_map/ppermute | solution.py:323
  141.7 6.5 %collective-permute-done.21 = f32[256,128]{1,0:T(8,128)S(1)} collective-permute-done((f32[256,128]{1,0:T(8,128)S(1)}, f32[256,128]{1,0:T(8,128)S(1)}, u32[]{:S(2)}, u32[]{:S(2)}) %collective-permute-start.21) | collective-permute-done | bytes 131104 | tf_op jit(solution)/shard_map/ppermute | solution.py:323
  149.8 11.6 %collective-permute-done.22.peer_ref = bf16[256,128]{1,0:T(8,128)(2,1)S(1)} collective-permute-done((bf16[256,128]{1,0:T(8,128)(2,1)S(1)}, bf16[256,128]{1,0:T(8,128)(2,1)S(1)}, u32[]{:S(2)}, u32[]{:S(2)}) %collective-permute-start.22) | collective-permute-done | bytes 65568 | tf_op jit(solution)/shard_map/ppermute | solution.py:323
  168.6 20.4 %collective-permute-done.24 = bf16[256,64]{1,0:T(8,128)(2,1)S(1)} collective-permute-done((bf16[256,64]{1,0:T(8,128)(2,1)S(1)}, bf16[256,64]{1,0:T(8,128)(2,1)S(1)}, u32[]{:S(2)}, u32[]{:S(2)}) %collective-permute-start.24) | collective-permute-done | bytes 32800 | tf_op jit(solution)/shard_map/ppermute | solution.py:323
  189.9 3.0 %finish.1 = f32[1,2,2048,128]{3,2,1,0:T(8,128)} custom-call(f32[2048,128]{1,0:T(8,128)S(1)} %get-tuple-element.34.own_a_ref, bf16[2048,128]{1,0:T(8,128)(2,1)S(1)} %collective-permute-done.8.got_a_ref, f32[2048,128]{1,0:T(8,128)S(1)} %get-tuple-element.44.own_b_ref, bf16[2048,128]{1,0:T(8,128)(2,1)S(1)} %collective-permute-done.17.got_b_ref), custom_call_target="tpu_custom_call" | custom-call | tf_op jit(solution)/shard_map/finish/pallas_call | solution.py:283
  (98 shorter events, 33.7 us)
Async XLA Ops:
  11.5 20.0 %collective-permute-start = (bf16[64,64,128]{2,1,0:T(8,128)(2,1)}, bf16[64,64,128]{2,1,0:T(8,128)(2,1)}, u32[]{:S(2)}, u32[]{:S(2)}) collective-permute-start(bf16[64,64,128]{2,1,0:T(8,128)(2,1)} %get-tuple-element.27.refs_5_), channel_id=1, source_target_pairs={{0,1},{1,2},{2,3},{3,4},{4,5},{5,6},{6,7},{7,8},{8,9},{9,10},{10,1... | collective-permute-start | bytes 3145736 | tf_op jit(solution)/shard_map/ppermute | solution.py:351
  13.4 19.9 %collective-permute-start.1 = (bf16[64,64,128]{2,1,0:T(8,128)(2,1)}, bf16[64,64,128]{2,1,0:T(8,128)(2,1)}, u32[]{:S(2)}, u32[]{:S(2)}) collective-permute-start(bf16[64,64,128]{2,1,0:T(8,128)(2,1)} %get-tuple-element.27.refs_5_), channel_id=1, source_target_pairs={{1,0},{2,1},{3,2},{4,3},{5,4},{6,5},{7,6},{8,7},{9,8},{10,9},{11,1... | collective-permute-start | bytes 3145736 | tf_op jit(solution)/shard_map/ppermute | solution.py:352
  20.7 38.5 %collective-permute-start.10 = (bf16[64,64,128]{2,1,0:T(8,128)(2,1)}, bf16[64,64,128]{2,1,0:T(8,128)(2,1)}, u32[]{:S(2)}, u32[]{:S(2)}) collective-permute-start(bf16[64,64,128]{2,1,0:T(8,128)(2,1)} %get-tuple-element.37.refs_5_), channel_id=1, source_target_pairs={{1,0},{2,1},{3,2},{4,3},{5,4},{6,5},{7,6},{8,7},{9,8},{10,9},{11,1... | collective-permute-start | bytes 3145736 | tf_op jit(solution)/shard_map/ppermute | solution.py:352
  22.6 36.5 %collective-permute-start.9 = (bf16[64,64,128]{2,1,0:T(8,128)(2,1)}, bf16[64,64,128]{2,1,0:T(8,128)(2,1)}, u32[]{:S(2)}, u32[]{:S(2)}) collective-permute-start(bf16[64,64,128]{2,1,0:T(8,128)(2,1)} %get-tuple-element.37.refs_5_), channel_id=1, source_target_pairs={{0,1},{1,2},{2,3},{3,4},{4,5},{5,6},{6,7},{7,8},{8,9},{9,10},{10,1... | collective-permute-start | bytes 3145736 | tf_op jit(solution)/shard_map/ppermute | solution.py:351
  49.8 29.4 %collective-permute-start.2 = (bf16[64,64,128]{2,1,0:T(8,128)(2,1)}, bf16[64,64,128]{2,1,0:T(8,128)(2,1)}, u32[]{:S(2)}, u32[]{:S(2)}) collective-permute-start(bf16[64,64,128]{2,1,0:T(8,128)(2,1)} %sweep.2.refs_5_), channel_id=1, source_target_pairs={{0,1},{1,2},{2,3},{3,4},{4,5},{5,6},{6,7},{7,8},{8,9},{9,10},{10,1... | collective-permute-start | bytes 3145736 | tf_op jit(solution)/shard_map/ppermute | solution.py:351
  51.7 27.4 %collective-permute-start.3 = (bf16[64,64,128]{2,1,0:T(8,128)(2,1)}, bf16[64,64,128]{2,1,0:T(8,128)(2,1)}, u32[]{:S(2)}, u32[]{:S(2)}) collective-permute-start(bf16[64,64,128]{2,1,0:T(8,128)(2,1)} %sweep.2.refs_5_), channel_id=1, source_target_pairs={{1,0},{2,1},{3,2},{4,3},{5,4},{6,5},{7,6},{8,7},{9,8},{10,9},{11,1... | collective-permute-start | bytes 3145736 | tf_op jit(solution)/shard_map/ppermute | solution.py:352
  69.8 26.7 %collective-permute-start.11 = (bf16[64,64,128]{2,1,0:T(8,128)(2,1)}, bf16[64,64,128]{2,1,0:T(8,128)(2,1)}, u32[]{:S(2)}, u32[]{:S(2)}) collective-permute-start(bf16[64,64,128]{2,1,0:T(8,128)(2,1)} %sweep.3.refs_5_), channel_id=1, source_target_pairs={{0,1},{1,2},{2,3},{3,4},{4,5},{5,6},{6,7},{7,8},{8,9},{9,10},{10,1... | collective-permute-start | bytes 3145736 | tf_op jit(solution)/shard_map/ppermute | solution.py:351
  71.8 24.8 %collective-permute-start.12 = (bf16[64,64,128]{2,1,0:T(8,128)(2,1)}, bf16[64,64,128]{2,1,0:T(8,128)(2,1)}, u32[]{:S(2)}, u32[]{:S(2)}) collective-permute-start(bf16[64,64,128]{2,1,0:T(8,128)(2,1)} %sweep.3.refs_5_), channel_id=1, source_target_pairs={{1,0},{2,1},{3,2},{4,3},{5,4},{6,5},{7,6},{8,7},{9,8},{10,9},{11,1... | collective-permute-start | bytes 3145736 | tf_op jit(solution)/shard_map/ppermute | solution.py:352
  108.1 10.2 %collective-permute-start.18 = (f32[256,128]{1,0:T(8,128)S(1)}, f32[256,128]{1,0:T(8,128)S(1)}, u32[]{:S(2)}, u32[]{:S(2)}) collective-permute-start(f32[256,128]{1,0:T(8,128)S(1)} %constant_dynamic-update-slice_fusion), channel_id=1, source_target_pairs={{0,1},{1,0},{2,3},{3,2},{4,5},{5,4},{6,7},{7,6},{8,9},{9,8},{10,11... | collective-permute-start | bytes 393224 | tf_op jit(solution)/shard_map/ppermute | solution.py:323
  108.2 16.9 %collective-permute-start.15 = (bf16[2048,128]{1,0:T(8,128)(2,1)S(1)}, bf16[2048,128]{1,0:T(8,128)(2,1)S(1)}, u32[]{:S(2)}, u32[]{:S(2)}) collective-permute-start(bf16[2048,128]{1,0:T(8,128)(2,1)S(1)} %bitcast.15), channel_id=1, source_target_pairs={{0,96},{16,112},{32,64},{48,80},{64,32},{80,48},{96,0},{112,16},{1... | collective-permute-start | bytes 1572872 | tf_op jit(solution)/shard_map/ppermute | solution.py:323
  112.3 14.8 %collective-permute-start.13 = (bf16[2048,128]{1,0:T(8,128)(2,1)S(1)}, bf16[2048,128]{1,0:T(8,128)(2,1)S(1)}, u32[]{:S(2)}, u32[]{:S(2)}) collective-permute-start(bf16[2048,128]{1,0:T(8,128)(2,1)S(1)} %bitcast.13), channel_id=1, source_target_pairs={{0,32},{16,48},{32,0},{48,16},{64,96},{80,112},{96,64},{112,80},{1... | collective-permute-start | bytes 1572872 | tf_op jit(solution)/shard_map/ppermute | solution.py:323
  112.3 24.0 %collective-permute-start.6 = (bf16[2048,128]{1,0:T(8,128)(2,1)S(1)}, bf16[2048,128]{1,0:T(8,128)(2,1)S(1)}, u32[]{:S(2)}, u32[]{:S(2)}) collective-permute-start(bf16[2048,128]{1,0:T(8,128)(2,1)S(1)} %bitcast.11), channel_id=1, source_target_pairs={{0,96},{16,112},{32,64},{48,80},{64,32},{80,48},{96,0},{112,16},{1... | collective-permute-start | bytes 1572872 | tf_op jit(solution)/shard_map/ppermute | solution.py:323
  112.8 25.5 %collective-permute-start.4 = (bf16[2048,128]{1,0:T(8,128)(2,1)S(1)}, bf16[2048,128]{1,0:T(8,128)(2,1)S(1)}, u32[]{:S(2)}, u32[]{:S(2)}) collective-permute-start(bf16[2048,128]{1,0:T(8,128)(2,1)S(1)} %bitcast.9), channel_id=1, source_target_pairs={{0,32},{16,48},{32,0},{48,16},{64,96},{80,112},{96,64},{112,80},{1... | collective-permute-start | bytes 1572872 | tf_op jit(solution)/shard_map/ppermute | solution.py:323
  123.4 18.2 %collective-permute-start.20 = (f32[256,128]{1,0:T(8,128)S(1)}, f32[256,128]{1,0:T(8,128)S(1)}, u32[]{:S(2)}, u32[]{:S(2)}) collective-permute-start(f32[256,128]{1,0:T(8,128)S(1)} %add.178), channel_id=1, source_target_pairs={{0,4},{1,5},{2,6},{3,7},{4,0},{5,1},{6,2},{7,3},{8,12},{9,13},{10,... | collective-permute-start | bytes 393224 | tf_op jit(solution)/shard_map/ppermute | solution.py:323
  126.0 36.0 %collective-permute-start.16 = (bf16[2048,128]{1,0:T(8,128)(2,1)S(1)}, bf16[2048,128]{1,0:T(8,128)(2,1)S(1)}, u32[]{:S(2)}, u32[]{:S(2)}) collective-permute-start(bf16[2048,128]{1,0:T(8,128)(2,1)S(1)} %get-tuple-element.43), channel_id=1, source_target_pairs={{0,32},{16,48},{32,0},{48,16},{64,96},{80,112},{96,64},{112,80},{1... | collective-permute-start | bytes 1572872 | tf_op jit(solution)/shard_map/ppermute | solution.py:323
  128.0 34.0 %collective-permute-start.14 = (bf16[2048,128]{1,0:T(8,128)(2,1)S(1)}, bf16[2048,128]{1,0:T(8,128)(2,1)S(1)}, u32[]{:S(2)}, u32[]{:S(2)}) collective-permute-start(bf16[2048,128]{1,0:T(8,128)(2,1)S(1)} %get-tuple-element.40), channel_id=1, source_target_pairs={{0,96},{16,112},{32,64},{48,80},{64,32},{80,48},{96,0},{112,16},{1... | collective-permute-start | bytes 1572872 | tf_op jit(solution)/shard_map/ppermute | solution.py:323
  137.2 27.1 %collective-permute-start.7 = (bf16[2048,128]{1,0:T(8,128)(2,1)S(1)}, bf16[2048,128]{1,0:T(8,128)(2,1)S(1)}, u32[]{:S(2)}, u32[]{:S(2)}) collective-permute-start(bf16[2048,128]{1,0:T(8,128)(2,1)S(1)} %get-tuple-element.33), channel_id=1, source_target_pairs={{0,32},{16,48},{32,0},{48,16},{64,96},{80,112},{96,64},{112,80},{1... | collective-permute-start | bytes 1572872 | tf_op jit(solution)/shard_map/ppermute | solution.py:323
  139.3 25.1 %collective-permute-start.5 = (bf16[2048,128]{1,0:T(8,128)(2,1)S(1)}, bf16[2048,128]{1,0:T(8,128)(2,1)S(1)}, u32[]{:S(2)}, u32[]{:S(2)}) collective-permute-start(bf16[2048,128]{1,0:T(8,128)(2,1)S(1)} %get-tuple-element.30), channel_id=1, source_target_pairs={{0,96},{16,112},{32,64},{48,80},{64,32},{80,48},{96,0},{112,16},{1... | collective-permute-start | bytes 1572872 | tf_op jit(solution)/shard_map/ppermute | solution.py:323
  141.6 6.6 %collective-permute-start.21 = (f32[256,128]{1,0:T(8,128)S(1)}, f32[256,128]{1,0:T(8,128)S(1)}, u32[]{:S(2)}, u32[]{:S(2)}) collective-permute-start(f32[256,128]{1,0:T(8,128)S(1)} %add.179), channel_id=1, source_target_pairs={{0,8},{1,9},{2,10},{3,11},{4,12},{5,13},{6,14},{7,15},{8,0},{9,1},... | collective-permute-start | bytes 393224 | tf_op jit(solution)/shard_map/ppermute | solution.py:323
  148.1 13.3 %collective-permute-start.22 = (bf16[256,128]{1,0:T(8,128)(2,1)S(1)}, bf16[256,128]{1,0:T(8,128)(2,1)S(1)}, u32[]{:S(2)}, u32[]{:S(2)}) collective-permute-start(bf16[256,128]{1,0:T(8,128)(2,1)S(1)} %add_convert_fusion.own_ref), channel_id=1, source_target_pairs={{0,32},{16,48},{32,0},{48,16},{64,96},{80,112},{96,64},{112,80},{1... | collective-permute-start | bytes 196616 | tf_op jit(solution)/shard_map/ppermute | solution.py:323
  161.6 5.6 %collective-permute-start.23 = (bf16[256,128]{1,0:T(8,128)(2,1)S(1)}, bf16[256,128]{1,0:T(8,128)(2,1)S(1)}, u32[]{:S(2)}, u32[]{:S(2)}) collective-permute-start(bf16[256,128]{1,0:T(8,128)(2,1)S(1)} %get-tuple-element.49), channel_id=1, source_target_pairs={{0,96},{16,112},{32,64},{48,80},{64,32},{80,48},{96,0},{112,16},{1... | collective-permute-start | bytes 196616 | tf_op jit(solution)/shard_map/ppermute | solution.py:323
  163.1 26.8 %collective-permute-start.17 = (bf16[2048,128]{1,0:T(8,128)(2,1)}, bf16[2048,128]{1,0:T(8,128)(2,1)S(1)}, u32[]{:S(2)}, u32[]{:S(2)}) collective-permute-start(bf16[2048,128]{1,0:T(8,128)(2,1)} %get-tuple-element.45), channel_id=1, source_target_pairs={{0,16},{16,0},{32,48},{48,32},{64,80},{80,64},{96,112},{112,96},{1... | collective-permute-start | bytes 1572872 | tf_op jit(solution)/shard_map/ppermute | solution.py:323
  165.5 24.4 %collective-permute-start.8 = (bf16[2048,128]{1,0:T(8,128)(2,1)}, bf16[2048,128]{1,0:T(8,128)(2,1)S(1)}, u32[]{:S(2)}, u32[]{:S(2)}) collective-permute-start(bf16[2048,128]{1,0:T(8,128)(2,1)} %get-tuple-element.35), channel_id=1, source_target_pairs={{0,16},{16,0},{32,48},{48,32},{64,80},{80,64},{96,112},{112,96},{1... | collective-permute-start | bytes 1572872 | tf_op jit(solution)/shard_map/ppermute | solution.py:323
  167.3 21.7 %collective-permute-start.24 = (bf16[256,64]{1,0:T(8,128)(2,1)S(1)}, bf16[256,64]{1,0:T(8,128)(2,1)S(1)}, u32[]{:S(2)}, u32[]{:S(2)}) collective-permute-start(bf16[256,64]{1,0:T(8,128)(2,1)S(1)} %slice.15), channel_id=1, source_target_pairs={{0,16},{16,0},{32,48},{48,32},{64,80},{80,64},{96,112},{112,96},{1... | collective-permute-start | bytes 98312 | tf_op jit(solution)/shard_map/ppermute | solution.py:323
  (16 other events, 153.2 us)

commit v3 on v2

v3 whole, which is shorter than its diff:
```python
import math

import jax
import jax.numpy as jnp
import numpy as np
from jax import lax
from jax.experimental import pallas as pl
from jax.experimental.pallas import tpu as pltpu
from jax.sharding import PartitionSpec as P

ITERS = 2
POINTS = 16
BS = 64
SLOTS = 24
RB = 64
LANES = 128
GROUP = 64
HALF = 32
STEP = 8
F32 = jnp.float32
BF16 = jnp.bfloat16


def unit_lanes(points):
    table = np.zeros((points * LANES, 2 * LANES), np.float32)
    for unit in range(2):
        for lane in range(LANES):
            point, part, col = lane // GROUP, (lane // HALF) % 2, lane % HALF
            src = (point % points) * LANES + part * GROUP + unit * HALF + col
            table[src, unit * LANES + lane] = 1.0
    return table


def lane_ids(shape):
    return lax.broadcasted_iota(jnp.int32, shape, len(shape) - 1)


def split_points(top, bottom):
    lane = lane_ids(top.shape) % LANES
    first = lane < GROUP
    zero = jnp.zeros_like(top)
    return jnp.concatenate(
        [
            jnp.where(first, top, zero),
            jnp.where(first, bottom, zero),
            jnp.where(first, zero, top),
            jnp.where(first, zero, bottom),
        ],
        axis=0,
    )


def init_kernel(x_ref, pre_ref, map_ref, y_a_ref, y_b_ref):
    firsts, seconds = [], []
    for b in range(STEP):
        x = x_ref[b * BS : (b + 1) * BS].astype(F32)
        turned = pltpu.roll(x, GROUP, axis=1)
        turned = jnp.where(lane_ids(x.shape) < GROUP, -turned, turned)
        right = jnp.concatenate([x, turned], axis=0).astype(BF16)
        left = jnp.concatenate([pre_ref[0, b], pre_ref[1, b]], axis=0)
        out = jnp.dot(left, right, preferred_element_type=F32).astype(BF16)
        firsts.append(out[:BS])
        seconds.append(out[BS:])
    both = jnp.concatenate(
        [jnp.concatenate(firsts, axis=0), jnp.concatenate(seconds, axis=0)], axis=1
    )
    out = jnp.dot(both, map_ref[...], preferred_element_type=F32).astype(BF16)
    y_a_ref[...] = out[:, :LANES].reshape(STEP, BS, LANES)
    y_b_ref[...] = out[:, LANES:].reshape(STEP, BS, LANES)


def initial(rhs, precond):
    block = jax.ShapeDtypeStruct((RB, BS, LANES), BF16)
    out_spec = pl.BlockSpec((STEP, BS, LANES), lambda i: (i, 0, 0))
    return pl.pallas_call(
        init_kernel,
        grid=(RB // STEP,),
        in_specs=[
            pl.BlockSpec((STEP * BS, LANES), lambda i: (i, 0)),
            pl.BlockSpec((2, STEP, BS, LANES), lambda i: (0, i, 0, 0)),
            pl.BlockSpec((2 * LANES, 2 * LANES), lambda i: (0, 0)),
        ],
        out_specs=[out_spec] * 2,
        out_shape=[block] * 2,
        name="initial",
    )(rhs, precond, jnp.asarray(unit_lanes(2), BF16))


def spread_kernel(x_ref, map_ref, coef_ref, rhs_a_ref, rhs_b_ref, weight_ref):
    out = jnp.dot(x_ref[...], map_ref[...], preferred_element_type=F32).astype(BF16)
    rhs_a_ref[...] = out[:, :LANES].reshape(rhs_a_ref.shape)
    rhs_b_ref[...] = out[:, LANES:].reshape(rhs_b_ref.shape)
    shape = (GROUP, 2 * LANES)
    r = lax.broadcasted_iota(jnp.int32, shape, 0)
    c = lax.broadcasted_iota(jnp.int32, shape, 1)
    same = r % HALF == c % HALF
    straight = same & ((r // HALF) == (c // HALF) % 2)
    crossed = same & ((r // HALF) != (c // HALF) % 2)
    for point in range(4):
        rows = coef_ref[0, point * 8 : point * 8 + 8]
        cosine, sine = rows[0:1, :], rows[1:2, :]
        value = jnp.where(straight, cosine, jnp.where(crossed, sine, 0.0))
        high = value.astype(BF16)
        weight_ref[0, point * GROUP : (point + 1) * GROUP] = high
        weight_ref[0, (4 + point) * GROUP : (5 + point) * GROUP] = (
            value - high.astype(F32)
        ).astype(BF16)


def spread(rhs, coefs):
    block = jax.ShapeDtypeStruct((RB, BS, LANES), BF16)
    out_spec = pl.BlockSpec((RB // 4, BS, LANES), lambda i: (i, 0, 0))
    return pl.pallas_call(
        spread_kernel,
        grid=(4,),
        in_specs=[
            pl.BlockSpec((RB // 4 * BS, LANES), lambda i: (i, 0)),
            pl.BlockSpec((LANES, 2 * LANES), lambda i: (0, 0)),
            pl.BlockSpec((1, 32, 2 * LANES), lambda i: (i, 0, 0)),
        ],
        out_specs=[out_spec, out_spec, pl.BlockSpec((1, 512, 256), lambda i: (i, 0, 0))],
        out_shape=[block, block, jax.ShapeDtypeStruct((4, 512, 256), BF16)],
        compiler_params=pltpu.CompilerParams(vmem_limit_bytes=14 << 20),
        cost_estimate=pl.CostEstimate(
            flops=2 * RB * BS * LANES * 256, bytes_accessed=3 << 20, transcendentals=0
        ),
        name="spread",
    )(rhs, jnp.asarray(unit_lanes(1), BF16), coefs)


def rotate_lanes(x):
    lane = lane_ids(x.shape) % GROUP
    up = pltpu.roll(x, LANES - HALF, axis=x.ndim - 1)
    down = pltpu.roll(x, HALF, axis=x.ndim - 1)
    return jnp.where(lane < HALF, -up, down)


def sweep_kernel(
    last, index_ref, ham_ref, pre_ref, rhs_ref, z_ref, local_ref, near_ref, far_ref, x_ref,
    out_ref, *rest,
):
    if last:
        second_ref, gram_ref, held, sems, ham_buf, pre_buf, fresh = rest
    else:
        held, sems, ham_buf, pre_buf = rest
        fresh = out_ref
    step = pl.program_id(0)
    steps = pl.num_programs(0)
    slot = step % 2

    def fetch(at, to):
        blocks = pl.ds(pl.multiple_of(at * STEP, STEP), STEP)
        return (
            pltpu.make_async_copy(ham_ref.at[blocks], ham_buf.at[to], sems.at[3 + to]),
            pltpu.make_async_copy(pre_ref.at[:, blocks], pre_buf.at[to], sems.at[5 + to]),
        )

    @pl.when(step == 0)
    def _():
        copies = []
        near_at = index_ref[RB * SLOTS]
        places = (near_at, RB, 2 * RB - near_at)
        for n, ref in enumerate((near_ref, local_ref, far_ref)):
            place = pl.multiple_of(places[n], RB)
            copies.append(pltpu.make_async_copy(ref, held.at[pl.ds(place, RB)], sems.at[n]))
            copies[-1].start()
        for copy in fetch(0, 0):
            copy.start()
        held[3 * RB] = jnp.zeros((BS, LANES), BF16)
        if last:
            gram_ref[...] = jnp.zeros_like(gram_ref)
        for copy in copies:
            copy.wait()

    @pl.when(step + 1 < steps)
    def _():
        for copy in fetch(step + 1, 1 - slot):
            copy.start()

    for copy in fetch(step, slot):
        copy.wait()

    zreal = z_ref[0:1, :]
    zimag = z_ref[1:2, :]
    totals = []
    for b in range(STEP):
        row = step * STEP + b
        right = jnp.concatenate(
            [held[index_ref[row * SLOTS + s]] for s in range(SLOTS)], axis=0
        )
        totals.append(jnp.dot(ham_buf[slot, b], right, preferred_element_type=F32))
    rights = []
    for b in range(STEP):
        current = held[RB + step * STEP + b].astype(F32)
        shifted = zreal * current + zimag * rotate_lanes(current)
        resid = (rhs_ref[b].astype(F32) - (shifted - totals[b])).astype(BF16).astype(F32)
        rights.append(split_points(resid, rotate_lanes(resid)).astype(BF16))
    for b in range(STEP):
        current = held[RB + step * STEP + b].astype(F32)
        left = jnp.concatenate([pre_buf[slot, 0, b], pre_buf[slot, 1, b]], axis=1)
        fresh[b] = (current + jnp.dot(left, rights[b], preferred_element_type=F32)).astype(BF16)
    if last:
        gram_ref[...] += lax.dot_general(
            x_ref[...],
            fresh[...].reshape(STEP * BS, LANES),
            (((0,), (0,)), ((), ())),
            preferred_element_type=F32,
        )

        @pl.when(step < steps // 2)
        def _():
            out_ref[...] = fresh[...]

        @pl.when(step >= steps // 2)
        def _():
            second_ref[...] = fresh[...]


def sweep(index, ham, precond, rhs_unit, z, local, near, far, rhs, last):
    block = pl.BlockSpec((STEP, BS, LANES), lambda i, n: (i, 0, 0))
    anywhere = pl.BlockSpec(memory_space=pl.ANY)
    in_hbm = pl.BlockSpec(memory_space=pltpu.MemorySpace.HBM)
    scratch = [
        pltpu.VMEM((3 * RB + 1, BS, LANES), BF16),
        pltpu.SemaphoreType.DMA((7,)),
        pltpu.VMEM((2, STEP, BS, SLOTS * BS), BF16),
        pltpu.VMEM((2, 2, STEP, BS, LANES), BF16),
    ]
    if last:
        half = RB // STEP // 2
        out_specs = [
            pl.BlockSpec((STEP, BS, LANES), lambda i, n: (jnp.minimum(i, half - 1), 0, 0)),
            pl.BlockSpec((STEP, BS, LANES), lambda i, n: (jnp.maximum(i - half, 0), 0, 0)),
            pl.BlockSpec((LANES, LANES), lambda i, n: (0, 0)),
        ]
        out_shape = [jax.ShapeDtypeStruct((RB // 2, BS, LANES), BF16)] * 2
        out_shape.append(jax.ShapeDtypeStruct((LANES, LANES), F32))
        scratch.append(pltpu.VMEM((STEP, BS, LANES), BF16))
    else:
        out_specs = [block]
        out_shape = [jax.ShapeDtypeStruct((RB, BS, LANES), BF16)]

    def kernel(*refs):
        sweep_kernel(last, *refs)

    return pl.pallas_call(
        kernel,
        grid_spec=pltpu.PrefetchScalarGridSpec(
            num_scalar_prefetch=1,
            grid=(RB // STEP,),
            in_specs=[
                in_hbm,
                in_hbm,
                block,
                pl.BlockSpec((8, LANES), lambda i, n: (0, 0)),
                anywhere,
                anywhere,
                anywhere,
                pl.BlockSpec((STEP * BS, LANES), lambda i, n: (i, 0)),
            ],
            out_specs=out_specs,
            scratch_shapes=scratch,
        ),
        out_shape=out_shape,
        cost_estimate=pl.CostEstimate(
            flops=2 * RB * BS * SLOTS * BS * LANES, bytes_accessed=20 << 20, transcendentals=0
        ),
        compiler_params=pltpu.CompilerParams(vmem_limit_bytes=48 << 20),
        name="sweep_last" if last else "sweep",
    )(index, ham, precond, rhs_unit, z, local, near, far, rhs)


def combine_kernel(own_ref, peer_ref, weight_ref, send_ref, keep_ref):
    own, peer = own_ref[...], peer_ref[...]
    both = jnp.concatenate([own, peer, own, peer], axis=1)
    out = jnp.dot(both, weight_ref[0], preferred_element_type=F32)
    send_ref[...] = out[:, :LANES].astype(BF16)
    keep_ref[...] = out[:, LANES:]


def combine(own, peer, weights, which, rows_step):
    rows = peer.shape[0]
    row_spec = pl.BlockSpec((rows_step, LANES), lambda i: (i, 0))
    return pl.pallas_call(
        combine_kernel,
        grid=(rows // rows_step,),
        in_specs=[row_spec, row_spec, pl.BlockSpec((1, 4 * LANES, 2 * LANES), lambda i: (which, 0, 0))],
        out_specs=[row_spec, row_spec],
        out_shape=[
            jax.ShapeDtypeStruct((rows, LANES), BF16),
            jax.ShapeDtypeStruct((rows, LANES), F32),
        ],
        compiler_params=pltpu.CompilerParams(vmem_limit_bytes=8 << 20),
        cost_estimate=pl.CostEstimate(
            flops=2 * rows * 256 * 512, bytes_accessed=rows * LANES * 12, transcendentals=0
        ),
        name="combine",
    )(own, peer, weights)


def fold_kernel(keep1_ref, got1_ref, keep2_ref, got2_ref, send_ref, own_ref):
    top = keep1_ref[...] + got1_ref[...].astype(F32)
    bottom = keep2_ref[...] + got2_ref[...].astype(F32)
    first = lane_ids(top.shape) < GROUP
    send_ref[...] = jnp.where(first, pltpu.roll(top, GROUP, axis=1), bottom).astype(BF16)
    own_ref[...] = jnp.where(first, top, pltpu.roll(bottom, GROUP, axis=1))


def fold(keep1, got1, keep2, got2, rows, shift):
    step = 1024
    spec = pl.BlockSpec((step, LANES), lambda i: (i, 0))
    late = pl.BlockSpec((step, LANES), lambda i: (i + shift // step, 0))
    return pl.pallas_call(
        fold_kernel,
        grid=(rows // step,),
        in_specs=[spec, spec, late, late],
        out_specs=[spec, spec],
        out_shape=[
            jax.ShapeDtypeStruct((rows, LANES), BF16),
            jax.ShapeDtypeStruct((rows, LANES), F32),
        ],
        compiler_params=pltpu.CompilerParams(vmem_limit_bytes=10 << 20),
        cost_estimate=pl.CostEstimate(
            flops=rows * LANES * 8, bytes_accessed=rows * LANES * 18, transcendentals=0
        ),
        name="fold",
    )(keep1, got1, keep2, got2)


def finish_kernel(own1_ref, got1_ref, own2_ref, got2_ref, own_b_ref, got_b_ref, out_ref):
    def turn(x, shift):
        return pltpu.roll(x, shift, axis=1)

    late = pl.program_id(0) >= pl.num_programs(0) // 2
    top_a = own1_ref[...] + got1_ref[...].astype(F32)
    top_a = jnp.where(late, turn(top_a, GROUP), top_a)
    bottom_a = own2_ref[...] + got2_ref[...].astype(F32)
    bottom_a = jnp.where(late, turn(bottom_a, GROUP), bottom_a)
    unit_b = own_b_ref[...] + got_b_ref[...].astype(F32)
    quarter = lane_ids(unit_b.shape) // HALF

    def merge(first, second, third, fourth):
        low = jnp.where(quarter == 0, first, second)
        high = jnp.where(quarter == 2, third, fourth)
        return jnp.where(quarter < 2, low, high)

    out_ref[0, 0] = merge(top_a, turn(unit_b, HALF), turn(top_a, HALF), turn(unit_b, GROUP))
    out_ref[0, 1] = merge(bottom_a, turn(unit_b, 96), turn(bottom_a, HALF), unit_b)


def finish(own1, got1, own2, got2, own_b, got_b, step):
    rows = own_b.shape[0]
    half = rows // 2 // step
    spec = pl.BlockSpec((step, LANES), lambda i: (i, 0))
    spec_a = pl.BlockSpec((step, LANES), lambda i: (i % half, 0))
    return pl.pallas_call(
        finish_kernel,
        grid=(rows // step,),
        in_specs=[spec_a] * 4 + [spec] * 2,
        out_specs=pl.BlockSpec((1, 2, step, LANES), lambda i: (0, 0, i, 0)),
        out_shape=jax.ShapeDtypeStruct((1, 2, rows, LANES), F32),
        compiler_params=pltpu.CompilerParams(vmem_limit_bytes=10 << 20),
        name="finish",
    )(own1, got1, own2, got2, own_b, got_b)


def moment_coefs(plans):
    lane = lax.broadcasted_iota(jnp.int32, (1, 32, 2 * LANES), 2)
    line = lax.broadcasted_iota(jnp.int32, (1, 32, 2 * LANES), 1)
    slot, point, kind = lane // GROUP, line // 8, line % 8
    tables = []
    for owners, orders in plans:
        owner = jnp.where(point < 2, owners[0], owners[1])
        low = jnp.where(slot == 0, orders[0], orders[1])
        high = jnp.where(slot == 2, orders[2], orders[3])
        order = jnp.where(slot < 2, low, high)
        turns = ((order + 1) * (2 * (owner * 2 + point % 2) + 1)) % (2 * POINTS)
        sign = jnp.where((lane // HALF) % 2 == 0, -1.0, 1.0)
        phase = turns.astype(F32) * (math.pi / POINTS)
        quarter = jnp.where(kind == 0, math.pi / 2, 0.0)
        tables.append(jnp.where(kind == 0, 1.0, sign) * jnp.sin(phase + quarter) / POINTS)
    return jnp.concatenate(tables, axis=0)


def step(hamiltonian, columns, counts, precond, rhs):
    row_index = lax.axis_index("row")
    quad_index = lax.axis_index("quad")

    def swap(x, axis, peer_of):
        peers = [(i, peer_of(i)) for i in range(lax.axis_size(axis))]
        return lax.ppermute(x, axis, [(i, j) for i, j in peers if 0 <= j < len(peers)])

    def by_pair(i):
        return (((i // 2) ^ 1) * 2) + i % 2

    def by_mirror(i):
        return ((3 - i // 2) * 2) + i % 2

    def by_x(i):
        return i ^ 1

    def near_row(i):
        return i ^ 1

    def far_row(i):
        return i + 1 if i % 2 else i - 1

    units = list(initial(rhs, precond))

    live = jnp.arange(SLOTS)[None, :] < counts[:, None]
    index = jnp.where(live, columns - (row_index - 1) * RB, 3 * RB).reshape(RB * SLOTS)
    near_at = jnp.where(row_index % 2 == 1, 0, 2 * RB)
    index = jnp.concatenate([index, jnp.full((LANES,), near_at, jnp.int32)])
    lane = jnp.arange(LANES)[None, :]
    theta = 2.0 * jnp.pi * ((quad_index * 2 + lane // GROUP).astype(F32) + 0.5) / POINTS
    z = jnp.concatenate([jnp.cos(theta), jnp.sin(theta), jnp.zeros((6, LANES), F32)], axis=0)

    mine, other = quad_index, quad_index ^ 1
    pair, mirror = by_pair(quad_index), by_mirror(quad_index)
    coefs = moment_coefs(
        (
            ((mine, pair), (other, mirror ^ 1, mine, mirror)),
            ((mine, mirror), (other, pair ^ 1, mine, pair)),
            ((mine, pair), (mirror, mirror ^ 1, mine, other)),
            ((mine, mirror), (pair, pair ^ 1, mine, other)),
        ),
    )
    *rhs_units, weights = spread(rhs, coefs)

    grams = [None, None]
    for it in range(ITERS):
        for unit in range(2):
            y = units[unit]
            far = swap(y, "row", far_row)
            near = swap(y, "row", near_row)
            last = it == ITERS - 1
            got = sweep(index, hamiltonian, precond, rhs_units[unit], z, y, near, far, rhs, last)
            units[unit] = got[0]
            if last:
                units[unit] = got[:2]
                grams[unit] = got[2]

    half_rows = RB * BS // 2

    def first_stage(unit):
        top, bottom = (part.reshape(half_rows, LANES) for part in units[unit])
        got1 = swap(top, "quad", by_pair)
        got2 = swap(bottom, "quad", by_mirror)
        out1 = combine(top, got1, weights, 2 * unit, 1024)
        return out1 + combine(bottom, got2, weights, 2 * unit + 1, 1024)

    send_a1, keep_a1, send_a2, keep_a2 = first_stage(0)
    got_a1 = swap(send_a1, "quad", by_x)
    got_a2 = swap(send_a2, "quad", by_x)
    quarter = half_rows // 2
    send_a1, own_a1 = fold(keep_a1, got_a1, keep_a1, got_a1, quarter, quarter)
    send_a2, own_a2 = fold(keep_a2, got_a2, keep_a2, got_a2, quarter, quarter)

    send_b1, keep_b1, send_b2, keep_b2 = first_stage(1)
    got_b1 = swap(send_b1, "quad", by_mirror)
    got_b2 = swap(send_b2, "quad", by_pair)
    send_b, own_b = fold(keep_b1, got_b1, keep_b2, got_b2, half_rows, 0)

    gram = jnp.concatenate(grams, axis=0)
    for bit in (1, 2, 4, 8):
        gram = gram + swap(gram, "row", lambda i, bit=bit: i ^ bit)
    gram = gram.astype(BF16)
    send_g, keep_g = combine(gram, swap(gram, "quad", by_pair), weights, 2, 256)
    gram_sum = keep_g + swap(send_g, "quad", by_mirror).astype(F32)
    gram_got = swap(gram_sum[:, GROUP:].astype(BF16), "quad", by_x)
    blocks = gram_sum[:, :GROUP] + gram_got.astype(F32)
    blocks = blocks.reshape(2, LANES, 2, HALF).transpose(1, 2, 0, 3).reshape(1, LANES, LANES)
    blocks = blocks * (1.0 / math.sqrt(RB * BS * 16))

    got_a1 = swap(send_a1, "quad", by_mirror)
    got_a2 = swap(send_a2, "quad", by_pair)
    got_b = swap(send_b, "quad", by_x)
    moments = finish(own_a1, got_a1, own_a2, got_a2, own_b, got_b, 512)
    return moments.reshape(1, RB * BS, LANES), blocks


def solution(mesh):
    return jax.shard_map(
        step,
        mesh=mesh,
        in_specs=(
            P("row", None, None),
            P("row", None),
            P("row"),
            P("quad", "row", None, None),
            P("row", None),
        ),
        out_specs=(P("quad", "row", None), P("quad", None, None)),
        check_vma=False,
    )
```

time: 194 us -> 158 us (0.81)
  waiting for transfers between devices: 61.9 us -> 39.7 us
  local copies, waits for them, and re-layouts: 18.5 us -> 2.69 us
  Pallas kernels: 58.6 us -> 70.7 us
  starting transfers between devices: 48.6 us -> 41.9 us
  other arithmetic: 4.22 us -> 0.88 us
    ppermute x25 -> x26, waiting for transfers between devices: 61.9 us -> 39.7 us  [swap(): lax.ppermute(x, axis, [(i, j) for i, j in peers if 0 <= j < len(peers)])]
    unnamed x32 -> x14, local copies, waits for them, and re-layouts: 18.1 us -> 0.76 us
    pallas_call x4, Pallas kernels: 44.4 us -> 52.4 us  [sweep(): pl.pallas_call(kernel, grid_spec=pltpu.PrefetchScalarGridSpec(num_scalar_...]
    ppermute x25 -> x26, starting transfers between devices: 48.6 us -> 41.9 us  [swap(): lax.ppermute(x, axis, [(i, j) for i, j in peers if 0 <= j < len(peers)])]
    convert_element_type x2 -> x1, other arithmetic: 3.94 us -> 0.02 us  [step(): gram = gram.astype(BF16)]
    pallas_call x1, Pallas kernels: 5.14 us -> 7.71 us  [initial(): pl.pallas_call(init_kernel, grid=(RB // STEP,), in_specs=[pl.BlockSpec((S...]
    pallas_call x3 -> x5, Pallas kernels: 5.3 us -> 6.73 us  [the longest x1 3.26 us: finish(): pl.pallas_call(finish_kernel, grid=(rows // step,), in_specs=[spec_a] * 4...]
  transfers between devices with their start and end apart: 25 -> 26, of which waited for: 11 -> 9; matrix products, arithmetic and copies ran while one was open for 3% -> 2% of each run, Pallas kernels for 20% -> 38%
where the time goes in v3:
time: 158 us; the launch traced here: 157 us
  Pallas kernels  70.7 us (45%)
  starting transfers between devices  41.9 us (27%)
  waiting for transfers between devices  39.7 us (25%)
  local copies, waits for them, and re-layouts  2.69 us (2%)
    pallas_call x4, Pallas kernels, sweep(): pl.pallas_call(kernel, grid_spec=pltpu.PrefetchScalarGridSpec(num_scalar_...  52.4 us
    ppermute x26, starting transfers between devices, swap(): lax.ppermute(x, axis, [(i, j) for i, j in peers if 0 <= j < len(peers)])  41.9 us
    ppermute x26, waiting for transfers between devices, swap(): lax.ppermute(x, axis, [(i, j) for i, j in peers if 0 <= j < len(peers)])  39.7 us
    pallas_call x1, Pallas kernels, initial(): pl.pallas_call(init_kernel, grid=(RB // STEP,), in_specs=[pl.BlockSpec((S...  7.71 us
    pallas_call x5, Pallas kernels, combine(): pl.pallas_call(combine_kernel, grid=(rows // rows_step,), in_specs=[row_s...  3.79 us
    pallas_call x1, Pallas kernels, finish(): pl.pallas_call(finish_kernel, grid=(rows // step,), in_specs=[spec_a] * 4...  3.26 us
  transfers between devices with their start and end apart: 26, of which 9 were waited for; matrix products, arithmetic and copies ran while one was open for 2% of the time, Pallas kernels for 38%

profile of v3, /device:TPU:4, one launch (start us, length us, event | category | flops | bytes accessed | tf_op | source)
XLA Modules:
  0.0 157.0 jit_solution(7046755523373308865)
XLA Ops:
  0.7 7.7 %initial.1 = (bf16[64,64,128]{2,1,0:T(8,128)(2,1)}, bf16[64,64,128]{2,1,0:T(8,128)(2,1)}) custom-call(bf16[4096,128]{1,0:T(8,128)(2,1)} %refs_8_.7, bf16[2,64,64,128]{3,2,1,0:T(8,128)(2,1)} %refs_2_.7, bf16[256,256]{1,0:T(8,128)(2,1)} %constant.210.clone.map_ref), custom_call_target="tpu_custom_call" | custom-call | tf_op jit(solution)/shard_map/initial/pallas_call | solution.py:75
  8.4 5.0 %collective-permute-start.11 = (bf16[64,64,128]{2,1,0:T(8,128)(2,1)}, bf16[64,64,128]{2,1,0:T(8,128)(2,1)}, u32[]{:S(2)}, u32[]{:S(2)}) collective-permute-start(bf16[64,64,128]{2,1,0:T(8,128)(2,1)} %get-tuple-element.43.refs_5_), channel_id=1, source_target_pairs={{1,2},{2,1},{3,4},{4,3},{5,6},{6,5},{7,8},{8,7},{9,10},{10,9},{11,... | collective-permute-start | bytes 3145736 | tf_op jit(solution)/shard_map/ppermute | solution.py:391
  13.5 4.2 %collective-permute-start.1 = (bf16[64,64,128]{2,1,0:T(8,128)(2,1)}, bf16[64,64,128]{2,1,0:T(8,128)(2,1)S(1)}, u32[]{:S(2)}, u32[]{:S(2)}) collective-permute-start(bf16[64,64,128]{2,1,0:T(8,128)(2,1)} %get-tuple-element.30.refs_5_), channel_id=1, source_target_pairs={{1,2},{2,1},{3,4},{4,3},{5,6},{6,5},{7,8},{8,7},{9,10},{10,9},{11,... | collective-permute-start | bytes 3145736 | tf_op jit(solution)/shard_map/ppermute | solution.py:391
  20.1 8.3 %collective-permute-done.11.refs_7_ = bf16[64,64,128]{2,1,0:T(8,128)(2,1)} collective-permute-done((bf16[64,64,128]{2,1,0:T(8,128)(2,1)}, bf16[64,64,128]{2,1,0:T(8,128)(2,1)}, u32[]{:S(2)}, u32[]{:S(2)}) %collective-permute-start.11) | collective-permute-done | bytes 1048608 | tf_op jit(solution)/shard_map/ppermute | solution.py:391
  28.4 13.1 %sweep.3.refs_5_ = bf16[64,64,128]{2,1,0:T(8,128)(2,1)S(1)} custom-call(s32[1664]{0:T(1024)S(1)} %concatenate.12.refs_0_, bf16[64,64,1536]{2,1,0:T(8,128)(2,1)} %refs_1_.7, bf16[2,64,64,128]{3,2,1,0:T(8,128)(2,1)} %refs_2_.7, bf16[64,64,128]{2,1,0:T(8,128)(2,1)S(1)} %get-tuple-element.42.refs_3_, f32[8,128]{1,0:T(8,128)S(1)} %maximum_maximum_fusion.refs_4_, ...), custom_call_target="tpu_custom_call" | custom-call | flops 1610612736 | bytes 20971520 | tf_op jit(solution)/shard_map/sweep/pallas_call | solution.py:246
  41.6 5.0 %collective-permute-start.13 = (bf16[64,64,128]{2,1,0:T(8,128)(2,1)S(1)}, bf16[64,64,128]{2,1,0:T(8,128)(2,1)S(1)}, u32[]{:S(2)}, u32[]{:S(2)}) collective-permute-start(bf16[64,64,128]{2,1,0:T(8,128)(2,1)S(1)} %sweep.3.refs_5_), channel_id=1, source_target_pairs={{1,2},{2,1},{3,4},{4,3},{5,6},{6,5},{7,8},{8,7},{9,10},{10,9},{11,... | collective-permute-start | bytes 3145736 | tf_op jit(solution)/shard_map/ppermute | solution.py:391
  46.6 12.6 %sweep.2.refs_5_ = bf16[64,64,128]{2,1,0:T(8,128)(2,1)S(1)} custom-call(s32[1664]{0:T(1024)S(1)} %concatenate.12.refs_0_, bf16[64,64,1536]{2,1,0:T(8,128)(2,1)} %refs_1_.7, bf16[2,64,64,128]{3,2,1,0:T(8,128)(2,1)} %refs_2_.7, bf16[64,64,128]{2,1,0:T(8,128)(2,1)S(1)} %get-tuple-element.29.refs_3_, f32[8,128]{1,0:T(8,128)S(1)} %maximum_maximum_fusion.refs_4_, ...), custom_call_target="tpu_custom_call" | custom-call | flops 1610612736 | bytes 20971520 | tf_op jit(solution)/shard_map/sweep/pallas_call | solution.py:246
  59.4 4.2 %collective-permute-start.3 = (bf16[64,64,128]{2,1,0:T(8,128)(2,1)S(1)}, bf16[64,64,128]{2,1,0:T(8,128)(2,1)S(1)}, u32[]{:S(2)}, u32[]{:S(2)}) collective-permute-start(bf16[64,64,128]{2,1,0:T(8,128)(2,1)S(1)} %sweep.2.refs_5_), channel_id=1, source_target_pairs={{1,2},{2,1},{3,4},{4,3},{5,6},{6,5},{7,8},{8,7},{9,10},{10,9},{11,... | collective-permute-start | bytes 3145736 | tf_op jit(solution)/shard_map/ppermute | solution.py:391
  63.6 13.4 %sweep_last.3 = (bf16[32,64,128]{2,1,0:T(8,128)(2,1)S(1)}, bf16[32,64,128]{2,1,0:T(8,128)(2,1)S(1)}, f32[128,128]{1,0:T(8,128)S(1)}) custom-call(s32[1664]{0:T(1024)S(1)} %concatenate.12.refs_0_, bf16[64,64,1536]{2,1,0:T(8,128)(2,1)} %refs_1_.7, bf16[2,64,64,128]{3,2,1,0:T(8,128)(2,1)} %refs_2_.7, bf16[64,64,128]{2,1,0:T(8,128)(2,1)S(1)} %get-tuple-element.42.refs_3_, ...), custom_call_target="tpu_custom_call" | custom-call | flops 1610612736 | bytes 20971520 | tf_op jit(solution)/shard_map/sweep_last/pallas_call | solution.py:246
  77.0 4.1 %collective-permute-start.16 = (bf16[2048,128]{1,0:T(8,128)(2,1)S(1)}, bf16[2048,128]{1,0:T(8,128)(2,1)S(1)}, u32[]{:S(2)}, u32[]{:S(2)}) collective-permute-start(bf16[2048,128]{1,0:T(8,128)(2,1)S(1)} %bitcast.15), channel_id=1, source_target_pairs={{0,96},{16,112},{32,64},{48,80},{64,32},{80,48},{96,0},{112,16},{1... | collective-permute-start | bytes 1572872 | tf_op jit(solution)/shard_map/ppermute | solution.py:391
  81.1 13.4 %sweep_last.2 = (bf16[32,64,128]{2,1,0:T(8,128)(2,1)S(1)}, bf16[32,64,128]{2,1,0:T(8,128)(2,1)S(1)}, f32[128,128]{1,0:T(8,128)S(1)}) custom-call(s32[1664]{0:T(1024)S(1)} %concatenate.12.refs_0_, bf16[64,64,1536]{2,1,0:T(8,128)(2,1)} %refs_1_.7, bf16[2,64,64,128]{3,2,1,0:T(8,128)(2,1)} %refs_2_.7, bf16[64,64,128]{2,1,0:T(8,128)(2,1)S(1)} %get-tuple-element.29.refs_3_, ...), custom_call_target="tpu_custom_call" | custom-call | flops 1610612736 | bytes 20971520 | tf_op jit(solution)/shard_map/sweep_last/pallas_call | solution.py:246
  94.5 2.1 %collective-permute-start.7 = (bf16[2048,128]{1,0:T(8,128)(2,1)S(1)}, bf16[2048,128]{1,0:T(8,128)(2,1)S(1)}, u32[]{:S(2)}, u32[]{:S(2)}) collective-permute-start(bf16[2048,128]{1,0:T(8,128)(2,1)S(1)} %bitcast.11), channel_id=1, source_target_pairs={{0,96},{16,112},{32,64},{48,80},{64,32},{80,48},{96,0},{112,16},{1... | collective-permute-start | bytes 1572872 | tf_op jit(solution)/shard_map/ppermute | solution.py:391
  98.2 5.5 %collective-permute-done.20 = f32[256,128]{1,0:T(8,128)S(1)} collective-permute-done((f32[256,128]{1,0:T(8,128)S(1)}, f32[256,128]{1,0:T(8,128)S(1)}, u32[]{:S(2)}, u32[]{:S(2)}) %collective-permute-start.20) | collective-permute-done | bytes 131104 | tf_op jit(solution)/shard_map/ppermute | solution.py:391
  104.8 2.0 %collective-permute-start.17 = (bf16[2048,128]{1,0:T(8,128)(2,1)S(1)}, bf16[2048,128]{1,0:T(8,128)(2,1)S(1)}, u32[]{:S(2)}, u32[]{:S(2)}) collective-permute-start(bf16[2048,128]{1,0:T(8,128)(2,1)S(1)} %get-tuple-element.49), channel_id=1, source_target_pairs={{0,32},{16,48},{32,0},{48,16},{64,96},{80,112},{96,64},{112,80},{1... | collective-permute-start | bytes 1572872 | tf_op jit(solution)/shard_map/ppermute | solution.py:391
  110.3 1.5 collective-permute-start.22
  112.7 2.2 %collective-permute-start.8 = (bf16[2048,128]{1,0:T(8,128)(2,1)S(1)}, bf16[2048,128]{1,0:T(8,128)(2,1)S(1)}, u32[]{:S(2)}, u32[]{:S(2)}) collective-permute-start(bf16[2048,128]{1,0:T(8,128)(2,1)S(1)} %get-tuple-element.39), channel_id=1, source_target_pairs={{0,16},{16,0},{32,48},{48,32},{64,80},{80,64},{96,112},{112,96},{1... | collective-permute-start | bytes 1572872 | tf_op jit(solution)/shard_map/ppermute | solution.py:391
  115.9 2.4 %collective-permute-done.22 = f32[256,128]{1,0:T(8,128)S(1)} collective-permute-done((f32[256,128]{1,0:T(8,128)S(1)}, f32[256,128]{1,0:T(8,128)S(1)}, u32[]{:S(2)}, u32[]{:S(2)}) %collective-permute-start.22) | collective-permute-done | bytes 131104 | tf_op jit(solution)/shard_map/ppermute | solution.py:391
  118.3 2.2 %collective-permute-start.23 = (bf16[256,128]{1,0:T(8,128)(2,1)S(1)}, bf16[256,128]{1,0:T(8,128)(2,1)S(1)}, u32[]{:S(2)}, u32[]{:S(2)}) collective-permute-start(bf16[256,128]{1,0:T(8,128)(2,1)S(1)} %add_convert_fusion.own_ref), channel_id=1, source_target_pairs={{0,32},{16,48},{32,0},{48,16},{64,96},{80,112},{96,64},{112,80},{1... | collective-permute-start | bytes 196616 | tf_op jit(solution)/shard_map/ppermute | solution.py:391
  120.5 2.3 %collective-permute-done.23.peer_ref = bf16[256,128]{1,0:T(8,128)(2,1)S(1)} collective-permute-done((bf16[256,128]{1,0:T(8,128)(2,1)S(1)}, bf16[256,128]{1,0:T(8,128)(2,1)S(1)}, u32[]{:S(2)}, u32[]{:S(2)}) %collective-permute-start.23) | collective-permute-done | bytes 65568 | tf_op jit(solution)/shard_map/ppermute | solution.py:391
  123.1 2.6 %collective-permute-start.24 = (bf16[256,128]{1,0:T(8,128)(2,1)S(1)}, bf16[256,128]{1,0:T(8,128)(2,1)S(1)}, u32[]{:S(2)}, u32[]{:S(2)}) collective-permute-start(bf16[256,128]{1,0:T(8,128)(2,1)S(1)} %get-tuple-element.55), channel_id=1, source_target_pairs={{0,96},{16,112},{32,64},{48,80},{64,32},{80,48},{96,0},{112,16},{1... | collective-permute-start | bytes 196616 | tf_op jit(solution)/shard_map/ppermute | solution.py:391
  128.7 2.1 %collective-permute-start.25 = (bf16[256,64]{1,0:T(8,128)(2,1)S(1)}, bf16[256,64]{1,0:T(8,128)(2,1)S(1)}, u32[]{:S(2)}, u32[]{:S(2)}) collective-permute-start(bf16[256,64]{1,0:T(8,128)(2,1)S(1)} %slice.15), channel_id=1, source_target_pairs={{0,16},{16,0},{32,48},{48,32},{64,80},{80,64},{96,112},{112,96},{1... | collective-permute-start | bytes 98312 | tf_op jit(solution)/shard_map/ppermute | solution.py:391
  132.0 8.7 %collective-permute-done.5.got1_ref.got2_ref = bf16[2048,128]{1,0:T(8,128)(2,1)S(1)} collective-permute-done((bf16[2048,128]{1,0:T(8,128)(2,1)S(1)}, bf16[2048,128]{1,0:T(8,128)(2,1)S(1)}, u32[]{:S(2)}, u32[]{:S(2)}) %collective-permute-start.5) | collective-permute-done | bytes 524320 | tf_op jit(solution)/shard_map/ppermute | solution.py:391
  142.2 9.1 %collective-permute-done.25 = bf16[256,64]{1,0:T(8,128)(2,1)S(1)} collective-permute-done((bf16[256,64]{1,0:T(8,128)(2,1)S(1)}, bf16[256,64]{1,0:T(8,128)(2,1)S(1)}, u32[]{:S(2)}, u32[]{:S(2)}) %collective-permute-start.25) | collective-permute-done | bytes 32800 | tf_op jit(solution)/shard_map/ppermute | solution.py:391
  153.7 3.3 %finish.1 = f32[1,2,2048,128]{3,2,1,0:T(8,128)} custom-call(f32[1024,128]{1,0:T(8,128)S(1)} %get-tuple-element.35.own1_ref, bf16[1024,128]{1,0:T(8,128)(2,1)S(1)} %collective-permute-done.6.got1_ref, f32[1024,128]{1,0:T(8,128)S(1)} %get-tuple-element.40.own2_ref, bf16[1024,128]{1,0:T(8,128)(2,1)S(1)} %collective-permute-done.9.got2_ref, ...), custom_call_target="tpu_custom_call" | custom-call | tf_op jit(solution)/shard_map/finish/pallas_call | solution.py:356
  (84 shorter events, 18.8 us)
Async XLA Ops:
  8.4 11.7 %collective-permute-start.10 = (bf16[64,64,128]{2,1,0:T(8,128)(2,1)}, bf16[64,64,128]{2,1,0:T(8,128)(2,1)}, u32[]{:S(2)}, u32[]{:S(2)}) collective-permute-start(bf16[64,64,128]{2,1,0:T(8,128)(2,1)} %get-tuple-element.43.refs_5_), channel_id=1, source_target_pairs={{0,1},{1,0},{2,3},{3,2},{4,5},{5,4},{6,7},{7,6},{8,9},{9,8},{10,11... | collective-permute-start | bytes 3145736 | tf_op jit(solution)/shard_map/ppermute | solution.py:391
  8.4 20.0 %collective-permute-start.11 = (bf16[64,64,128]{2,1,0:T(8,128)(2,1)}, bf16[64,64,128]{2,1,0:T(8,128)(2,1)}, u32[]{:S(2)}, u32[]{:S(2)}) collective-permute-start(bf16[64,64,128]{2,1,0:T(8,128)(2,1)} %get-tuple-element.43.refs_5_), channel_id=1, source_target_pairs={{1,2},{2,1},{3,4},{4,3},{5,6},{6,5},{7,8},{8,7},{9,10},{10,9},{11,... | collective-permute-start | bytes 3145736 | tf_op jit(solution)/shard_map/ppermute | solution.py:391
  13.4 33.3 %collective-permute-start = (bf16[64,64,128]{2,1,0:T(8,128)(2,1)}, bf16[64,64,128]{2,1,0:T(8,128)(2,1)S(1)}, u32[]{:S(2)}, u32[]{:S(2)}) collective-permute-start(bf16[64,64,128]{2,1,0:T(8,128)(2,1)} %get-tuple-element.30.refs_5_), channel_id=1, source_target_pairs={{0,1},{1,0},{2,3},{3,2},{4,5},{5,4},{6,7},{7,6},{8,9},{9,8},{10,11... | collective-permute-start | bytes 3145736 | tf_op jit(solution)/shard_map/ppermute | solution.py:391
  13.5 33.2 %collective-permute-start.1 = (bf16[64,64,128]{2,1,0:T(8,128)(2,1)}, bf16[64,64,128]{2,1,0:T(8,128)(2,1)S(1)}, u32[]{:S(2)}, u32[]{:S(2)}) collective-permute-start(bf16[64,64,128]{2,1,0:T(8,128)(2,1)} %get-tuple-element.30.refs_5_), channel_id=1, source_target_pairs={{1,2},{2,1},{3,4},{4,3},{5,6},{6,5},{7,8},{8,7},{9,10},{10,9},{11,... | collective-permute-start | bytes 3145736 | tf_op jit(solution)/shard_map/ppermute | solution.py:391
  41.5 22.0 %collective-permute-start.12 = (bf16[64,64,128]{2,1,0:T(8,128)(2,1)S(1)}, bf16[64,64,128]{2,1,0:T(8,128)(2,1)S(1)}, u32[]{:S(2)}, u32[]{:S(2)}) collective-permute-start(bf16[64,64,128]{2,1,0:T(8,128)(2,1)S(1)} %sweep.3.refs_5_), channel_id=1, source_target_pairs={{0,1},{1,0},{2,3},{3,2},{4,5},{5,4},{6,7},{7,6},{8,9},{9,8},{10,11... | collective-permute-start | bytes 3145736 | tf_op jit(solution)/shard_map/ppermute | solution.py:391
  41.6 22.0 %collective-permute-start.13 = (bf16[64,64,128]{2,1,0:T(8,128)(2,1)S(1)}, bf16[64,64,128]{2,1,0:T(8,128)(2,1)S(1)}, u32[]{:S(2)}, u32[]{:S(2)}) collective-permute-start(bf16[64,64,128]{2,1,0:T(8,128)(2,1)S(1)} %sweep.3.refs_5_), channel_id=1, source_target_pairs={{1,2},{2,1},{3,4},{4,3},{5,6},{6,5},{7,8},{8,7},{9,10},{10,9},{11,... | collective-permute-start | bytes 3145736 | tf_op jit(solution)/shard_map/ppermute | solution.py:391
  59.3 21.8 %collective-permute-start.2 = (bf16[64,64,128]{2,1,0:T(8,128)(2,1)S(1)}, bf16[64,64,128]{2,1,0:T(8,128)(2,1)S(1)}, u32[]{:S(2)}, u32[]{:S(2)}) collective-permute-start(bf16[64,64,128]{2,1,0:T(8,128)(2,1)S(1)} %sweep.2.refs_5_), channel_id=1, source_target_pairs={{0,1},{1,0},{2,3},{3,2},{4,5},{5,4},{6,7},{7,6},{8,9},{9,8},{10,11... | collective-permute-start | bytes 3145736 | tf_op jit(solution)/shard_map/ppermute | solution.py:391
  59.4 21.7 %collective-permute-start.3 = (bf16[64,64,128]{2,1,0:T(8,128)(2,1)S(1)}, bf16[64,64,128]{2,1,0:T(8,128)(2,1)S(1)}, u32[]{:S(2)}, u32[]{:S(2)}) collective-permute-start(bf16[64,64,128]{2,1,0:T(8,128)(2,1)S(1)} %sweep.2.refs_5_), channel_id=1, source_target_pairs={{1,2},{2,1},{3,4},{4,3},{5,6},{6,5},{7,8},{8,7},{9,10},{10,9},{11,... | collective-permute-start | bytes 3145736 | tf_op jit(solution)/shard_map/ppermute | solution.py:391
  77.0 26.9 %collective-permute-start.16 = (bf16[2048,128]{1,0:T(8,128)(2,1)S(1)}, bf16[2048,128]{1,0:T(8,128)(2,1)S(1)}, u32[]{:S(2)}, u32[]{:S(2)}) collective-permute-start(bf16[2048,128]{1,0:T(8,128)(2,1)S(1)} %bitcast.15), channel_id=1, source_target_pairs={{0,96},{16,112},{32,64},{48,80},{64,32},{80,48},{96,0},{112,16},{1... | collective-permute-start | bytes 1572872 | tf_op jit(solution)/shard_map/ppermute | solution.py:391
  81.1 25.7 %collective-permute-start.14 = (bf16[2048,128]{1,0:T(8,128)(2,1)S(1)}, bf16[2048,128]{1,0:T(8,128)(2,1)S(1)}, u32[]{:S(2)}, u32[]{:S(2)}) collective-permute-start(bf16[2048,128]{1,0:T(8,128)(2,1)S(1)} %bitcast.13), channel_id=1, source_target_pairs={{0,32},{16,48},{32,0},{48,16},{64,96},{80,112},{96,64},{112,80},{1... | collective-permute-start | bytes 1572872 | tf_op jit(solution)/shard_map/ppermute | solution.py:391
  94.5 17.4 %collective-permute-start.7 = (bf16[2048,128]{1,0:T(8,128)(2,1)S(1)}, bf16[2048,128]{1,0:T(8,128)(2,1)S(1)}, u32[]{:S(2)}, u32[]{:S(2)}) collective-permute-start(bf16[2048,128]{1,0:T(8,128)(2,1)S(1)} %bitcast.11), channel_id=1, source_target_pairs={{0,96},{16,112},{32,64},{48,80},{64,32},{80,48},{96,0},{112,16},{1... | collective-permute-start | bytes 1572872 | tf_op jit(solution)/shard_map/ppermute | solution.py:391
  96.6 18.3 %collective-permute-start.4 = (bf16[2048,128]{1,0:T(8,128)(2,1)S(1)}, bf16[2048,128]{1,0:T(8,128)(2,1)S(1)}, u32[]{:S(2)}, u32[]{:S(2)}) collective-permute-start(bf16[2048,128]{1,0:T(8,128)(2,1)S(1)} %bitcast.9), channel_id=1, source_target_pairs={{0,32},{16,48},{32,0},{48,16},{64,96},{80,112},{96,64},{112,80},{1... | collective-permute-start | bytes 1572872 | tf_op jit(solution)/shard_map/ppermute | solution.py:391
  98.1 5.6 %collective-permute-start.20 = (f32[256,128]{1,0:T(8,128)S(1)}, f32[256,128]{1,0:T(8,128)S(1)}, u32[]{:S(2)}, u32[]{:S(2)}) collective-permute-start(f32[256,128]{1,0:T(8,128)S(1)} %add.407), channel_id=1, source_target_pairs={{0,2},{1,3},{2,0},{3,1},{4,6},{5,7},{6,4},{7,5},{8,10},{9,11},{10,... | collective-permute-start | bytes 393224 | tf_op jit(solution)/shard_map/ppermute | solution.py:391
  103.8 6.6 %collective-permute-start.21 = (f32[256,128]{1,0:T(8,128)S(1)}, f32[256,128]{1,0:T(8,128)S(1)}, u32[]{:S(2)}, u32[]{:S(2)}) collective-permute-start(f32[256,128]{1,0:T(8,128)S(1)} %add.408), channel_id=1, source_target_pairs={{0,4},{1,5},{2,6},{3,7},{4,0},{5,1},{6,2},{7,3},{8,12},{9,13},{10,... | collective-permute-start | bytes 393224 | tf_op jit(solution)/shard_map/ppermute | solution.py:391
  104.8 20.9 %collective-permute-start.17 = (bf16[2048,128]{1,0:T(8,128)(2,1)S(1)}, bf16[2048,128]{1,0:T(8,128)(2,1)S(1)}, u32[]{:S(2)}, u32[]{:S(2)}) collective-permute-start(bf16[2048,128]{1,0:T(8,128)(2,1)S(1)} %get-tuple-element.49), channel_id=1, source_target_pairs={{0,32},{16,48},{32,0},{48,16},{64,96},{80,112},{96,64},{112,80},{1... | collective-permute-start | bytes 1572872 | tf_op jit(solution)/shard_map/ppermute | solution.py:391
  107.7 18.0 %collective-permute-start.15 = (bf16[2048,128]{1,0:T(8,128)(2,1)S(1)}, bf16[2048,128]{1,0:T(8,128)(2,1)S(1)}, u32[]{:S(2)}, u32[]{:S(2)}) collective-permute-start(bf16[2048,128]{1,0:T(8,128)(2,1)S(1)} %get-tuple-element.46), channel_id=1, source_target_pairs={{0,96},{16,112},{32,64},{48,80},{64,32},{80,48},{96,0},{112,16},{1... | collective-permute-start | bytes 1572872 | tf_op jit(solution)/shard_map/ppermute | solution.py:391
  110.3 8.0 %collective-permute-start.22 = (f32[256,128]{1,0:T(8,128)S(1)}, f32[256,128]{1,0:T(8,128)S(1)}, u32[]{:S(2)}, u32[]{:S(2)}) collective-permute-start(f32[256,128]{1,0:T(8,128)S(1)} %add.409), channel_id=1, source_target_pairs={{0,8},{1,9},{2,10},{3,11},{4,12},{5,13},{6,14},{7,15},{8,0},{9,1},... | collective-permute-start | bytes 393224 | tf_op jit(solution)/shard_map/ppermute | solution.py:391
  112.7 18.1 %collective-permute-start.8 = (bf16[2048,128]{1,0:T(8,128)(2,1)S(1)}, bf16[2048,128]{1,0:T(8,128)(2,1)S(1)}, u32[]{:S(2)}, u32[]{:S(2)}) collective-permute-start(bf16[2048,128]{1,0:T(8,128)(2,1)S(1)} %get-tuple-element.39), channel_id=1, source_target_pairs={{0,16},{16,0},{32,48},{48,32},{64,80},{80,64},{96,112},{112,96},{1... | collective-permute-start | bytes 1572872 | tf_op jit(solution)/shard_map/ppermute | solution.py:391
  115.8 24.9 %collective-permute-start.5 = (bf16[2048,128]{1,0:T(8,128)(2,1)S(1)}, bf16[2048,128]{1,0:T(8,128)(2,1)S(1)}, u32[]{:S(2)}, u32[]{:S(2)}) collective-permute-start(bf16[2048,128]{1,0:T(8,128)(2,1)S(1)} %get-tuple-element.34), channel_id=1, source_target_pairs={{0,16},{16,0},{32,48},{48,32},{64,80},{80,64},{96,112},{112,96},{1... | collective-permute-start | bytes 1572872 | tf_op jit(solution)/shard_map/ppermute | solution.py:391
  123.1 5.6 %collective-permute-start.24 = (bf16[256,128]{1,0:T(8,128)(2,1)S(1)}, bf16[256,128]{1,0:T(8,128)(2,1)S(1)}, u32[]{:S(2)}, u32[]{:S(2)}) collective-permute-start(bf16[256,128]{1,0:T(8,128)(2,1)S(1)} %get-tuple-element.55), channel_id=1, source_target_pairs={{0,96},{16,112},{32,64},{48,80},{64,32},{80,48},{96,0},{112,16},{1... | collective-permute-start | bytes 196616 | tf_op jit(solution)/shard_map/ppermute | solution.py:391
  126.8 26.9 %collective-permute-start.18 = (bf16[2048,128]{1,0:T(8,128)(2,1)}, bf16[2048,128]{1,0:T(8,128)(2,1)S(1)}, u32[]{:S(2)}, u32[]{:S(2)}) collective-permute-start(bf16[2048,128]{1,0:T(8,128)(2,1)} %get-tuple-element.51), channel_id=1, source_target_pairs={{0,16},{16,0},{32,48},{48,32},{64,80},{80,64},{96,112},{112,96},{1... | collective-permute-start | bytes 1572872 | tf_op jit(solution)/shard_map/ppermute | solution.py:391
  128.7 22.6 %collective-permute-start.25 = (bf16[256,64]{1,0:T(8,128)(2,1)S(1)}, bf16[256,64]{1,0:T(8,128)(2,1)S(1)}, u32[]{:S(2)}, u32[]{:S(2)}) collective-permute-start(bf16[256,64]{1,0:T(8,128)(2,1)S(1)} %slice.15), channel_id=1, source_target_pairs={{0,16},{16,0},{32,48},{48,32},{64,80},{80,64},{96,112},{112,96},{1... | collective-permute-start | bytes 98312 | tf_op jit(solution)/shard_map/ppermute | solution.py:391
  131.1 22.6 %collective-permute-start.9 = (bf16[1024,128]{1,0:T(8,128)(2,1)S(1)}, bf16[1024,128]{1,0:T(8,128)(2,1)S(1)}, u32[]{:S(2)}, u32[]{:S(2)}) collective-permute-start(bf16[1024,128]{1,0:T(8,128)(2,1)S(1)} %get-tuple-element.41), channel_id=1, source_target_pairs={{0,32},{16,48},{32,0},{48,16},{64,96},{80,112},{96,64},{112,80},{1... | collective-permute-start | bytes 786440 | tf_op jit(solution)/shard_map/ppermute | solution.py:391
  141.6 12.1 %collective-permute-start.6 = (bf16[1024,128]{1,0:T(8,128)(2,1)}, bf16[1024,128]{1,0:T(8,128)(2,1)S(1)}, u32[]{:S(2)}, u32[]{:S(2)}) collective-permute-start(bf16[1024,128]{1,0:T(8,128)(2,1)} %get-tuple-element.36), channel_id=1, source_target_pairs={{0,96},{16,112},{32,64},{48,80},{64,32},{80,48},{96,0},{112,16},{1... | collective-permute-start | bytes 786440 | tf_op jit(solution)/shard_map/ppermute | solution.py:391
  (8 other events, 104.9 us)

commit v4 on v3

--- a/solution.py
+++ b/solution.py
@@ -51,16 +51,19 @@
 
 
 def init_kernel(x_ref, pre_ref, map_ref, y_a_ref, y_b_ref):
-    firsts, seconds = [], []
+    rights = []
     for b in range(STEP):
         x = x_ref[b * BS : (b + 1) * BS].astype(F32)
         turned = pltpu.roll(x, GROUP, axis=1)
         turned = jnp.where(lane_ids(x.shape) < GROUP, -turned, turned)
-        right = jnp.concatenate([x, turned], axis=0).astype(BF16)
+        rights.append(jnp.concatenate([x, turned], axis=0).astype(BF16))
+    outs = []
+    for b in range(STEP):
         left = jnp.concatenate([pre_ref[0, b], pre_ref[1, b]], axis=0)
-        out = jnp.dot(left, right, preferred_element_type=F32).astype(BF16)
-        firsts.append(out[:BS])
-        seconds.append(out[BS:])
+        outs.append(jnp.dot(left, rights[b], preferred_element_type=F32))
+    outs = [out.astype(BF16) for out in outs]
+    firsts = [out[:BS] for out in outs]
+    seconds = [out[BS:] for out in outs]
     both = jnp.concatenate(
         [jnp.concatenate(firsts, axis=0), jnp.concatenate(seconds, axis=0)], axis=1
     )
@@ -136,11 +139,11 @@
 
 
 def sweep_kernel(
-    last, index_ref, ham_ref, pre_ref, rhs_ref, z_ref, local_ref, near_ref, far_ref, x_ref,
+    last, index_ref, ham_ref, pre_ref, rhs_ref, z_ref, local_ref, near_ref, far_ref,
     out_ref, *rest,
 ):
     if last:
-        second_ref, gram_ref, held, sems, ham_buf, pre_buf, fresh = rest
+        second_ref, held, sems, ham_buf, pre_buf, fresh = rest
     else:
         held, sems, ham_buf, pre_buf = rest
         fresh = out_ref
@@ -167,8 +170,6 @@
         for copy in fetch(0, 0):
             copy.start()
         held[3 * RB] = jnp.zeros((BS, LANES), BF16)
-        if last:
-            gram_ref[...] = jnp.zeros_like(gram_ref)
         for copy in copies:
             copy.wait()
 
@@ -200,12 +201,6 @@
         left = jnp.concatenate([pre_buf[slot, 0, b], pre_buf[slot, 1, b]], axis=1)
         fresh[b] = (current + jnp.dot(left, rights[b], preferred_element_type=F32)).astype(BF16)
     if last:
-        gram_ref[...] += lax.dot_general(
-            x_ref[...],
-            fresh[...].reshape(STEP * BS, LANES),
-            (((0,), (0,)), ((), ())),
-            preferred_element_type=F32,
-        )
 
         @pl.when(step < steps // 2)
         def _():
@@ -216,7 +211,7 @@
             second_ref[...] = fresh[...]
 
 
-def sweep(index, ham, precond, rhs_unit, z, local, near, far, rhs, last):
+def sweep(index, ham, precond, rhs_unit, z, local, near, far, last):
     block = pl.BlockSpec((STEP, BS, LANES), lambda i, n: (i, 0, 0))
     anywhere = pl.BlockSpec(memory_space=pl.ANY)
     in_hbm = pl.BlockSpec(memory_space=pltpu.MemorySpace.HBM)
@@ -231,10 +226,8 @@
         out_specs = [
             pl.BlockSpec((STEP, BS, LANES), lambda i, n: (jnp.minimum(i, half - 1), 0, 0)),
             pl.BlockSpec((STEP, BS, LANES), lambda i, n: (jnp.maximum(i - half, 0), 0, 0)),
-            pl.BlockSpec((LANES, LANES), lambda i, n: (0, 0)),
         ]
         out_shape = [jax.ShapeDtypeStruct((RB // 2, BS, LANES), BF16)] * 2
-        out_shape.append(jax.ShapeDtypeStruct((LANES, LANES), F32))
         scratch.append(pltpu.VMEM((STEP, BS, LANES), BF16))
     else:
         out_specs = [block]
@@ -256,7 +249,6 @@
                 anywhere,
                 anywhere,
                 anywhere,
-                pl.BlockSpec((STEP * BS, LANES), lambda i, n: (i, 0)),
             ],
             out_specs=out_specs,
             scratch_shapes=scratch,
@@ -265,9 +257,9 @@
         cost_estimate=pl.CostEstimate(
             flops=2 * RB * BS * SLOTS * BS * LANES, bytes_accessed=20 << 20, transcendentals=0
         ),
-        compiler_params=pltpu.CompilerParams(vmem_limit_bytes=48 << 20),
+        compiler_params=pltpu.CompilerParams(vmem_limit_bytes=47 << 20),
         name="sweep_last" if last else "sweep",
-    )(index, ham, precond, rhs_unit, z, local, near, far, rhs)
+    )(index, ham, precond, rhs_unit, z, local, near, far)
 
 
 def combine_kernel(own_ref, peer_ref, weight_ref, send_ref, keep_ref):
@@ -434,11 +426,18 @@
             far = swap(y, "row", far_row)
             near = swap(y, "row", near_row)
             last = it == ITERS - 1
-            got = sweep(index, hamiltonian, precond, rhs_units[unit], z, y, near, far, rhs, last)
+            got = sweep(
+                index, hamiltonian, precond, rhs_units[unit], z, y, near, far, last
+            )
             units[unit] = got[0]
             if last:
                 units[unit] = got[:2]
-                grams[unit] = got[2]
+                both = (part.reshape(-1, LANES) for part in got)
+                parts = zip((rhs[: RB * BS // 2], rhs[RB * BS // 2 :]), both, strict=True)
+                grams[unit] = sum(
+                    lax.dot_general(x, part, (((0,), (0,)), ((), ())), preferred_element_type=F32)
+                    for x, part in parts
+                )
 
     half_rows = RB * BS // 2
 
@@ -462,15 +461,18 @@
     send_b, own_b = fold(keep_b1, got_b1, keep_b2, got_b2, half_rows, 0)
 
     gram = jnp.concatenate(grams, axis=0)
-    for bit in (1, 2, 4, 8):
+    gram = lax.reduce_precision(gram, 8, 7)
+    gram = gram + swap(gram.astype(BF16), "row", lambda i: i ^ 8).astype(F32)
+    for bit in (4, 2, 1):
         gram = gram + swap(gram, "row", lambda i, bit=bit: i ^ bit)
     gram = gram.astype(BF16)
-    send_g, keep_g = combine(gram, swap(gram, "quad", by_pair), weights, 2, 256)
+    peer = swap(gram, "quad", by_pair)
+    send_g, keep_g = combine(gram, peer, weights, 2, 256)
     gram_sum = keep_g + swap(send_g, "quad", by_mirror).astype(F32)
     gram_got = swap(gram_sum[:, GROUP:].astype(BF16), "quad", by_x)
     blocks = gram_sum[:, :GROUP] + gram_got.astype(F32)
+    blocks = blocks * (1.0 / math.sqrt(RB * BS * 16))
     blocks = blocks.reshape(2, LANES, 2, HALF).transpose(1, 2, 0, 3).reshape(1, LANES, LANES)
-    blocks = blocks * (1.0 / math.sqrt(RB * BS * 16))
 
     got_a1 = swap(send_a1, "quad", by_mirror)
     got_a2 = swap(send_a2, "quad", by_pair)

time: 158 us -> 157 us (level)
  Pallas kernels: 70.7 us -> 65.4 us
  starting transfers between devices: 41.9 us -> 43.9 us
    pallas_call x4, Pallas kernels: 52.4 us -> 47.1 us  [sweep(): pl.pallas_call(kernel, grid_spec=pltpu.PrefetchScalarGridSpec(num_scalar_...]
    ppermute x26, starting transfers between devices: 41.9 us -> 43.9 us  [swap(): lax.ppermute(x, axis, [(i, j) for i, j in peers if 0 <= j < len(peers)])]
  transfers between devices with their start and end apart: 26 -> 26, of which waited for: 9 -> 6; matrix products, arithmetic and copies ran while one was open for 2% -> 3% of each run, Pallas kernels for 38% -> 35%
where the time goes in v4:
time: 157 us; the launch traced here: 155 us
  Pallas kernels  65.4 us (42%)
  starting transfers between devices  43.9 us (28%)
  waiting for transfers between devices  38.5 us (25%)
  local copies, waits for them, and re-layouts  3.9 us (2%)
    pallas_call x4, Pallas kernels, sweep(): pl.pallas_call(kernel, grid_spec=pltpu.PrefetchScalarGridSpec(num_scalar_...  47.1 us
    ppermute x26, starting transfers between devices, swap(): lax.ppermute(x, axis, [(i, j) for i, j in peers if 0 <= j < len(peers)])  43.9 us
    ppermute x26, waiting for transfers between devices, swap(): lax.ppermute(x, axis, [(i, j) for i, j in peers if 0 <= j < len(peers)])  38.5 us
    pallas_call x1, Pallas kernels, initial(): pl.pallas_call(init_kernel, grid=(RB // STEP,), in_specs=[pl.BlockSpec((S...  7.71 us
    pallas_call x5, Pallas kernels, combine(): pl.pallas_call(combine_kernel, grid=(rows // rows_step,), in_specs=[row_s...  3.8 us
    pallas_call x1, Pallas kernels, finish(): pl.pallas_call(finish_kernel, grid=(rows // step,), in_specs=[spec_a] * 4...  3.26 us
  transfers between devices with their start and end apart: 26, of which 6 were waited for; matrix products, arithmetic and copies ran while one was open for 3% of the time, Pallas kernels for 35%

profile of v4, /device:TPU:4, one launch (start us, length us, event | category | flops | bytes accessed | tf_op | source)
XLA Modules:
  0.0 155.2 jit_solution(16643139892742335756)
XLA Ops:
  0.7 7.7 %initial.1 = (bf16[64,64,128]{2,1,0:T(8,128)(2,1)}, bf16[64,64,128]{2,1,0:T(8,128)(2,1)}) custom-call(bf16[4096,128]{1,0:T(8,128)(2,1)} %x_ref.3, bf16[2,64,64,128]{3,2,1,0:T(8,128)(2,1)} %refs_2_.7, bf16[256,256]{1,0:T(8,128)(2,1)} %constant.210.clone.map_ref), custom_call_target="tpu_custom_call" | custom-call | tf_op jit(solution)/shard_map/initial/pallas_call | solution.py:78
  8.4 5.0 %collective-permute-start.11 = (bf16[64,64,128]{2,1,0:T(8,128)(2,1)}, bf16[64,64,128]{2,1,0:T(8,128)(2,1)}, u32[]{:S(2)}, u32[]{:S(2)}) collective-permute-start(bf16[64,64,128]{2,1,0:T(8,128)(2,1)} %get-tuple-element.41.refs_5_), channel_id=1, source_target_pairs={{1,2},{2,1},{3,4},{4,3},{5,6},{6,5},{7,8},{8,7},{9,10},{10,9},{11,... | collective-permute-start | bytes 3145736 | tf_op jit(solution)/shard_map/ppermute | solution.py:383
  13.5 4.2 %collective-permute-start.1 = (bf16[64,64,128]{2,1,0:T(8,128)(2,1)}, bf16[64,64,128]{2,1,0:T(8,128)(2,1)S(1)}, u32[]{:S(2)}, u32[]{:S(2)}) collective-permute-start(bf16[64,64,128]{2,1,0:T(8,128)(2,1)} %get-tuple-element.28.refs_5_), channel_id=1, source_target_pairs={{1,2},{2,1},{3,4},{4,3},{5,6},{6,5},{7,8},{8,7},{9,10},{10,9},{11,... | collective-permute-start | bytes 3145736 | tf_op jit(solution)/shard_map/ppermute | solution.py:383
  20.0 8.4 %collective-permute-done.11.refs_7_ = bf16[64,64,128]{2,1,0:T(8,128)(2,1)} collective-permute-done((bf16[64,64,128]{2,1,0:T(8,128)(2,1)}, bf16[64,64,128]{2,1,0:T(8,128)(2,1)}, u32[]{:S(2)}, u32[]{:S(2)}) %collective-permute-start.11) | collective-permute-done | bytes 1048608 | tf_op jit(solution)/shard_map/ppermute | solution.py:383
  29.7 12.1 %sweep.3.refs_5_ = bf16[64,64,128]{2,1,0:T(8,128)(2,1)S(1)} custom-call(s32[1664]{0:T(1024)S(1)} %concatenate.12.refs_0_, bf16[64,64,1536]{2,1,0:T(8,128)(2,1)} %refs_1_.7, bf16[2,64,64,128]{3,2,1,0:T(8,128)(2,1)} %refs_2_.7, bf16[64,64,128]{2,1,0:T(8,128)(2,1)S(1)} %get-tuple-element.40.refs_3_, f32[8,128]{1,0:T(8,128)S(1)} %maximum_maximum_fusion.refs_4_, ...), custom_call_target="tpu_custom_call" | custom-call | flops 1610612736 | bytes 20971520 | tf_op jit(solution)/shard_map/sweep/pallas_call | solution.py:239
  41.9 5.0 %collective-permute-start.13 = (bf16[64,64,128]{2,1,0:T(8,128)(2,1)S(1)}, bf16[64,64,128]{2,1,0:T(8,128)(2,1)S(1)}, u32[]{:S(2)}, u32[]{:S(2)}) collective-permute-start(bf16[64,64,128]{2,1,0:T(8,128)(2,1)S(1)} %sweep.3.refs_5_), channel_id=1, source_target_pairs={{1,2},{2,1},{3,4},{4,3},{5,6},{6,5},{7,8},{8,7},{9,10},{10,9},{11,... | collective-permute-start | bytes 3145736 | tf_op jit(solution)/shard_map/ppermute | solution.py:383
  46.9 11.6 %sweep.2.refs_5_ = bf16[64,64,128]{2,1,0:T(8,128)(2,1)S(1)} custom-call(s32[1664]{0:T(1024)S(1)} %concatenate.12.refs_0_, bf16[64,64,1536]{2,1,0:T(8,128)(2,1)} %refs_1_.7, bf16[2,64,64,128]{3,2,1,0:T(8,128)(2,1)} %refs_2_.7, bf16[64,64,128]{2,1,0:T(8,128)(2,1)S(1)} %get-tuple-element.27.refs_3_, f32[8,128]{1,0:T(8,128)S(1)} %maximum_maximum_fusion.refs_4_, ...), custom_call_target="tpu_custom_call" | custom-call | flops 1610612736 | bytes 20971520 | tf_op jit(solution)/shard_map/sweep/pallas_call | solution.py:239
  58.6 4.2 %collective-permute-start.3 = (bf16[64,64,128]{2,1,0:T(8,128)(2,1)S(1)}, bf16[64,64,128]{2,1,0:T(8,128)(2,1)S(1)}, u32[]{:S(2)}, u32[]{:S(2)}) collective-permute-start(bf16[64,64,128]{2,1,0:T(8,128)(2,1)S(1)} %sweep.2.refs_5_), channel_id=1, source_target_pairs={{1,2},{2,1},{3,4},{4,3},{5,6},{6,5},{7,8},{8,7},{9,10},{10,9},{11,... | collective-permute-start | bytes 3145736 | tf_op jit(solution)/shard_map/ppermute | solution.py:383
  62.8 11.7 %sweep_last.3 = (bf16[32,64,128]{2,1,0:T(8,128)(2,1)S(1)}, bf16[32,64,128]{2,1,0:T(8,128)(2,1)S(1)}) custom-call(s32[1664]{0:T(1024)S(1)} %concatenate.12.refs_0_, bf16[64,64,1536]{2,1,0:T(8,128)(2,1)} %refs_1_.7, bf16[2,64,64,128]{3,2,1,0:T(8,128)(2,1)} %refs_2_.7, bf16[64,64,128]{2,1,0:T(8,128)(2,1)S(1)} %get-tuple-element.40.refs_3_, ...), custom_call_target="tpu_custom_call" | custom-call | flops 1610612736 | bytes 20971520 | tf_op jit(solution)/shard_map/sweep_last/pallas_call | solution.py:239
  74.5 4.1 %collective-permute-start.16 = (bf16[2048,128]{1,0:T(8,128)(2,1)S(1)}, bf16[2048,128]{1,0:T(8,128)(2,1)S(1)}, u32[]{:S(2)}, u32[]{:S(2)}) collective-permute-start(bf16[2048,128]{1,0:T(8,128)(2,1)S(1)} %bitcast.26), channel_id=1, source_target_pairs={{0,96},{16,112},{32,64},{48,80},{64,32},{80,48},{96,0},{112,16},{1... | collective-permute-start | bytes 1572872 | tf_op jit(solution)/shard_map/ppermute | solution.py:383
  79.4 11.7 %sweep_last.2 = (bf16[32,64,128]{2,1,0:T(8,128)(2,1)S(1)}, bf16[32,64,128]{2,1,0:T(8,128)(2,1)S(1)}) custom-call(s32[1664]{0:T(1024)S(1)} %concatenate.12.refs_0_, bf16[64,64,1536]{2,1,0:T(8,128)(2,1)} %refs_1_.7, bf16[2,64,64,128]{3,2,1,0:T(8,128)(2,1)} %refs_2_.7, bf16[64,64,128]{2,1,0:T(8,128)(2,1)S(1)} %get-tuple-element.27.refs_3_, ...), custom_call_target="tpu_custom_call" | custom-call | flops 1610612736 | bytes 20971520 | tf_op jit(solution)/shard_map/sweep_last/pallas_call | solution.py:239
  91.9 3.0 %collective-permute-start.7 = (bf16[2048,128]{1,0:T(8,128)(2,1)S(1)}, bf16[2048,128]{1,0:T(8,128)(2,1)S(1)}, u32[]{:S(2)}, u32[]{:S(2)}) collective-permute-start(bf16[2048,128]{1,0:T(8,128)(2,1)S(1)} %bitcast.24), channel_id=1, source_target_pairs={{0,96},{16,112},{32,64},{48,80},{64,32},{80,48},{96,0},{112,16},{1... | collective-permute-start | bytes 1572872 | tf_op jit(solution)/shard_map/ppermute | solution.py:383
  95.0 2.7 %collective-permute-done.19 = bf16[256,128]{1,0:T(8,128)(2,1)S(1)} collective-permute-done((bf16[256,128]{1,0:T(8,128)(2,1)S(1)}, bf16[256,128]{1,0:T(8,128)(2,1)S(1)}, u32[]{:S(2)}, u32[]{:S(2)}) %collective-permute-start.19) | collective-permute-done | bytes 65568 | tf_op jit(solution)/shard_map/ppermute | solution.py:383
  97.8 6.5 %collective-permute-done.20 = f32[256,128]{1,0:T(8,128)S(1)} collective-permute-done((f32[256,128]{1,0:T(8,128)S(1)}, f32[256,128]{1,0:T(8,128)S(1)}, u32[]{:S(2)}, u32[]{:S(2)}) %collective-permute-start.20) | collective-permute-done | bytes 131104 | tf_op jit(solution)/shard_map/ppermute | solution.py:383
  105.3 2.1 %collective-permute-start.17 = (bf16[2048,128]{1,0:T(8,128)(2,1)S(1)}, bf16[2048,128]{1,0:T(8,128)(2,1)S(1)}, u32[]{:S(2)}, u32[]{:S(2)}) collective-permute-start(bf16[2048,128]{1,0:T(8,128)(2,1)S(1)} %get-tuple-element.47), channel_id=1, source_target_pairs={{0,32},{16,48},{32,0},{48,16},{64,96},{80,112},{96,64},{112,80},{1... | collective-permute-start | bytes 1572872 | tf_op jit(solution)/shard_map/ppermute | solution.py:383
  110.7 2.3 %collective-permute-start.8 = (bf16[2048,128]{1,0:T(8,128)(2,1)S(1)}, bf16[2048,128]{1,0:T(8,128)(2,1)S(1)}, u32[]{:S(2)}, u32[]{:S(2)}) collective-permute-start(bf16[2048,128]{1,0:T(8,128)(2,1)S(1)} %get-tuple-element.37), channel_id=1, source_target_pairs={{0,16},{16,0},{32,48},{48,32},{64,80},{80,64},{96,112},{112,96},{1... | collective-permute-start | bytes 1572872 | tf_op jit(solution)/shard_map/ppermute | solution.py:383
  115.7 2.7 %collective-permute-done.23.peer_ref = bf16[256,128]{1,0:T(8,128)(2,1)S(1)} collective-permute-done((bf16[256,128]{1,0:T(8,128)(2,1)S(1)}, bf16[256,128]{1,0:T(8,128)(2,1)S(1)}, u32[]{:S(2)}, u32[]{:S(2)}) %collective-permute-start.23) | collective-permute-done | bytes 65568 | tf_op jit(solution)/shard_map/ppermute | solution.py:383
  118.7 2.8 %collective-permute-start.24 = (bf16[256,128]{1,0:T(8,128)(2,1)S(1)}, bf16[256,128]{1,0:T(8,128)(2,1)S(1)}, u32[]{:S(2)}, u32[]{:S(2)}) collective-permute-start(bf16[256,128]{1,0:T(8,128)(2,1)S(1)} %get-tuple-element.51), channel_id=1, source_target_pairs={{0,96},{16,112},{32,64},{48,80},{64,32},{80,48},{96,0},{112,16},{1... | collective-permute-start | bytes 196616 | tf_op jit(solution)/shard_map/ppermute | solution.py:383
  122.6 2.0 %collective-permute-start.18 = (bf16[2048,128]{1,0:T(8,128)(2,1)}, bf16[2048,128]{1,0:T(8,128)(2,1)S(1)}, u32[]{:S(2)}, u32[]{:S(2)}) collective-permute-start(bf16[2048,128]{1,0:T(8,128)(2,1)} %get-tuple-element.49), channel_id=1, source_target_pairs={{0,16},{16,0},{32,48},{48,32},{64,80},{80,64},{96,112},{112,96},{1... | collective-permute-start | bytes 1572872 | tf_op jit(solution)/shard_map/ppermute | solution.py:383
  124.7 1.7 %collective-permute-start.25 = (bf16[256,64]{1,0:T(8,128)(2,1)S(1)}, bf16[256,64]{1,0:T(8,128)(2,1)S(1)}, u32[]{:S(2)}, u32[]{:S(2)}) collective-permute-start(bf16[256,64]{1,0:T(8,128)(2,1)S(1)} %slice.33), channel_id=1, source_target_pairs={{0,16},{16,0},{32,48},{48,32},{64,80},{80,64},{96,112},{112,96},{1... | collective-permute-start | bytes 98312 | tf_op jit(solution)/shard_map/ppermute | solution.py:383
  127.8 9.3 %collective-permute-done.5.got1_ref.got2_ref = bf16[2048,128]{1,0:T(8,128)(2,1)S(1)} collective-permute-done((bf16[2048,128]{1,0:T(8,128)(2,1)S(1)}, bf16[2048,128]{1,0:T(8,128)(2,1)S(1)}, u32[]{:S(2)}, u32[]{:S(2)}) %collective-permute-start.5) | collective-permute-done | bytes 524320 | tf_op jit(solution)/shard_map/ppermute | solution.py:383
  137.9 2.7 %collective-permute-start.6 = (bf16[1024,128]{1,0:T(8,128)(2,1)}, bf16[1024,128]{1,0:T(8,128)(2,1)S(1)}, u32[]{:S(2)}, u32[]{:S(2)}) collective-permute-start(bf16[1024,128]{1,0:T(8,128)(2,1)} %get-tuple-element.34), channel_id=1, source_target_pairs={{0,96},{16,112},{32,64},{48,80},{64,32},{80,48},{96,0},{112,16},{1... | collective-permute-start | bytes 786440 | tf_op jit(solution)/shard_map/ppermute | solution.py:383
  140.6 8.9 %collective-permute-done.25 = bf16[256,64]{1,0:T(8,128)(2,1)S(1)} collective-permute-done((bf16[256,64]{1,0:T(8,128)(2,1)S(1)}, bf16[256,64]{1,0:T(8,128)(2,1)S(1)}, u32[]{:S(2)}, u32[]{:S(2)}) %collective-permute-start.25) | collective-permute-done | bytes 32800 | tf_op jit(solution)/shard_map/ppermute | solution.py:383
  151.9 3.3 %finish.1 = f32[1,2,2048,128]{3,2,1,0:T(8,128)} custom-call(f32[1024,128]{1,0:T(8,128)S(1)} %get-tuple-element.33.own1_ref, bf16[1024,128]{1,0:T(8,128)(2,1)S(1)} %collective-permute-done.6.got1_ref, f32[1024,128]{1,0:T(8,128)S(1)} %get-tuple-element.38.own2_ref, bf16[1024,128]{1,0:T(8,128)(2,1)S(1)} %collective-permute-done.9.got2_ref, ...), custom_call_target="tpu_custom_call" | custom-call | tf_op jit(solution)/shard_map/finish/pallas_call | solution.py:348
  (87 shorter events, 18.3 us)
Async XLA Ops:
  8.4 11.7 %collective-permute-start.10 = (bf16[64,64,128]{2,1,0:T(8,128)(2,1)}, bf16[64,64,128]{2,1,0:T(8,128)(2,1)}, u32[]{:S(2)}, u32[]{:S(2)}) collective-permute-start(bf16[64,64,128]{2,1,0:T(8,128)(2,1)} %get-tuple-element.41.refs_5_), channel_id=1, source_target_pairs={{0,1},{1,0},{2,3},{3,2},{4,5},{5,4},{6,7},{7,6},{8,9},{9,8},{10,11... | collective-permute-start | bytes 3145736 | tf_op jit(solution)/shard_map/ppermute | solution.py:383
  8.4 20.0 %collective-permute-start.11 = (bf16[64,64,128]{2,1,0:T(8,128)(2,1)}, bf16[64,64,128]{2,1,0:T(8,128)(2,1)}, u32[]{:S(2)}, u32[]{:S(2)}) collective-permute-start(bf16[64,64,128]{2,1,0:T(8,128)(2,1)} %get-tuple-element.41.refs_5_), channel_id=1, source_target_pairs={{1,2},{2,1},{3,4},{4,3},{5,6},{6,5},{7,8},{8,7},{9,10},{10,9},{11,... | collective-permute-start | bytes 3145736 | tf_op jit(solution)/shard_map/ppermute | solution.py:383
  13.4 33.5 %collective-permute-start = (bf16[64,64,128]{2,1,0:T(8,128)(2,1)}, bf16[64,64,128]{2,1,0:T(8,128)(2,1)S(1)}, u32[]{:S(2)}, u32[]{:S(2)}) collective-permute-start(bf16[64,64,128]{2,1,0:T(8,128)(2,1)} %get-tuple-element.28.refs_5_), channel_id=1, source_target_pairs={{0,1},{1,0},{2,3},{3,2},{4,5},{5,4},{6,7},{7,6},{8,9},{9,8},{10,11... | collective-permute-start | bytes 3145736 | tf_op jit(solution)/shard_map/ppermute | solution.py:383
  13.5 33.4 %collective-permute-start.1 = (bf16[64,64,128]{2,1,0:T(8,128)(2,1)}, bf16[64,64,128]{2,1,0:T(8,128)(2,1)S(1)}, u32[]{:S(2)}, u32[]{:S(2)}) collective-permute-start(bf16[64,64,128]{2,1,0:T(8,128)(2,1)} %get-tuple-element.28.refs_5_), channel_id=1, source_target_pairs={{1,2},{2,1},{3,4},{4,3},{5,6},{6,5},{7,8},{8,7},{9,10},{10,9},{11,... | collective-permute-start | bytes 3145736 | tf_op jit(solution)/shard_map/ppermute | solution.py:383
  41.8 21.0 %collective-permute-start.12 = (bf16[64,64,128]{2,1,0:T(8,128)(2,1)S(1)}, bf16[64,64,128]{2,1,0:T(8,128)(2,1)S(1)}, u32[]{:S(2)}, u32[]{:S(2)}) collective-permute-start(bf16[64,64,128]{2,1,0:T(8,128)(2,1)S(1)} %sweep.3.refs_5_), channel_id=1, source_target_pairs={{0,1},{1,0},{2,3},{3,2},{4,5},{5,4},{6,7},{7,6},{8,9},{9,8},{10,11... | collective-permute-start | bytes 3145736 | tf_op jit(solution)/shard_map/ppermute | solution.py:383
  41.9 20.9 %collective-permute-start.13 = (bf16[64,64,128]{2,1,0:T(8,128)(2,1)S(1)}, bf16[64,64,128]{2,1,0:T(8,128)(2,1)S(1)}, u32[]{:S(2)}, u32[]{:S(2)}) collective-permute-start(bf16[64,64,128]{2,1,0:T(8,128)(2,1)S(1)} %sweep.3.refs_5_), channel_id=1, source_target_pairs={{1,2},{2,1},{3,4},{4,3},{5,6},{6,5},{7,8},{8,7},{9,10},{10,9},{11,... | collective-permute-start | bytes 3145736 | tf_op jit(solution)/shard_map/ppermute | solution.py:383
  58.5 20.9 %collective-permute-start.2 = (bf16[64,64,128]{2,1,0:T(8,128)(2,1)S(1)}, bf16[64,64,128]{2,1,0:T(8,128)(2,1)S(1)}, u32[]{:S(2)}, u32[]{:S(2)}) collective-permute-start(bf16[64,64,128]{2,1,0:T(8,128)(2,1)S(1)} %sweep.2.refs_5_), channel_id=1, source_target_pairs={{0,1},{1,0},{2,3},{3,2},{4,5},{5,4},{6,7},{7,6},{8,9},{9,8},{10,11... | collective-permute-start | bytes 3145736 | tf_op jit(solution)/shard_map/ppermute | solution.py:383
  58.6 20.8 %collective-permute-start.3 = (bf16[64,64,128]{2,1,0:T(8,128)(2,1)S(1)}, bf16[64,64,128]{2,1,0:T(8,128)(2,1)S(1)}, u32[]{:S(2)}, u32[]{:S(2)}) collective-permute-start(bf16[64,64,128]{2,1,0:T(8,128)(2,1)S(1)} %sweep.2.refs_5_), channel_id=1, source_target_pairs={{1,2},{2,1},{3,4},{4,3},{5,6},{6,5},{7,8},{8,7},{9,10},{10,9},{11,... | collective-permute-start | bytes 3145736 | tf_op jit(solution)/shard_map/ppermute | solution.py:383
  74.5 29.8 %collective-permute-start.16 = (bf16[2048,128]{1,0:T(8,128)(2,1)S(1)}, bf16[2048,128]{1,0:T(8,128)(2,1)S(1)}, u32[]{:S(2)}, u32[]{:S(2)}) collective-permute-start(bf16[2048,128]{1,0:T(8,128)(2,1)S(1)} %bitcast.26), channel_id=1, source_target_pairs={{0,96},{16,112},{32,64},{48,80},{64,32},{80,48},{96,0},{112,16},{1... | collective-permute-start | bytes 1572872 | tf_op jit(solution)/shard_map/ppermute | solution.py:383
  78.7 28.7 %collective-permute-start.14 = (bf16[2048,128]{1,0:T(8,128)(2,1)S(1)}, bf16[2048,128]{1,0:T(8,128)(2,1)S(1)}, u32[]{:S(2)}, u32[]{:S(2)}) collective-permute-start(bf16[2048,128]{1,0:T(8,128)(2,1)S(1)} %bitcast.20), channel_id=1, source_target_pairs={{0,32},{16,48},{32,0},{48,16},{64,96},{80,112},{96,64},{112,80},{1... | collective-permute-start | bytes 1572872 | tf_op jit(solution)/shard_map/ppermute | solution.py:383
  91.8 5.8 %collective-permute-start.19 = (bf16[256,128]{1,0:T(8,128)(2,1)S(1)}, bf16[256,128]{1,0:T(8,128)(2,1)S(1)}, u32[]{:S(2)}, u32[]{:S(2)}) collective-permute-start(bf16[256,128]{1,0:T(8,128)(2,1)S(1)} %fusion.9), channel_id=1, source_target_pairs={{0,8},{1,9},{2,10},{3,11},{4,12},{5,13},{6,14},{7,15},{8,0},{9,1},... | collective-permute-start | bytes 196616 | tf_op jit(solution)/shard_map/ppermute | solution.py:383
  91.9 17.9 %collective-permute-start.7 = (bf16[2048,128]{1,0:T(8,128)(2,1)S(1)}, bf16[2048,128]{1,0:T(8,128)(2,1)S(1)}, u32[]{:S(2)}, u32[]{:S(2)}) collective-permute-start(bf16[2048,128]{1,0:T(8,128)(2,1)S(1)} %bitcast.24), channel_id=1, source_target_pairs={{0,96},{16,112},{32,64},{48,80},{64,32},{80,48},{96,0},{112,16},{1... | collective-permute-start | bytes 1572872 | tf_op jit(solution)/shard_map/ppermute | solution.py:383
  95.0 18.1 %collective-permute-start.4 = (bf16[2048,128]{1,0:T(8,128)(2,1)S(1)}, bf16[2048,128]{1,0:T(8,128)(2,1)S(1)}, u32[]{:S(2)}, u32[]{:S(2)}) collective-permute-start(bf16[2048,128]{1,0:T(8,128)(2,1)S(1)} %bitcast.18), channel_id=1, source_target_pairs={{0,32},{16,48},{32,0},{48,16},{64,96},{80,112},{96,64},{112,80},{1... | collective-permute-start | bytes 1572872 | tf_op jit(solution)/shard_map/ppermute | solution.py:383
  97.7 6.6 %collective-permute-start.20 = (f32[256,128]{1,0:T(8,128)S(1)}, f32[256,128]{1,0:T(8,128)S(1)}, u32[]{:S(2)}, u32[]{:S(2)}) collective-permute-start(f32[256,128]{1,0:T(8,128)S(1)} %convert_add_fusion.1), channel_id=1, source_target_pairs={{0,4},{1,5},{2,6},{3,7},{4,0},{5,1},{6,2},{7,3},{8,12},{9,13},{10,... | collective-permute-start | bytes 393224 | tf_op jit(solution)/shard_map/ppermute | solution.py:383
  104.3 5.4 %collective-permute-start.21 = (f32[256,128]{1,0:T(8,128)S(1)}, f32[256,128]{1,0:T(8,128)S(1)}, u32[]{:S(2)}, u32[]{:S(2)}) collective-permute-start(f32[256,128]{1,0:T(8,128)S(1)} %add.424), channel_id=1, source_target_pairs={{0,2},{1,3},{2,0},{3,1},{4,6},{5,7},{6,4},{7,5},{8,10},{9,11},{10,... | collective-permute-start | bytes 393224 | tf_op jit(solution)/shard_map/ppermute | solution.py:383
  105.3 16.2 %collective-permute-start.17 = (bf16[2048,128]{1,0:T(8,128)(2,1)S(1)}, bf16[2048,128]{1,0:T(8,128)(2,1)S(1)}, u32[]{:S(2)}, u32[]{:S(2)}) collective-permute-start(bf16[2048,128]{1,0:T(8,128)(2,1)S(1)} %get-tuple-element.47), channel_id=1, source_target_pairs={{0,32},{16,48},{32,0},{48,16},{64,96},{80,112},{96,64},{112,80},{1... | collective-permute-start | bytes 1572872 | tf_op jit(solution)/shard_map/ppermute | solution.py:383
  108.3 13.2 %collective-permute-start.15 = (bf16[2048,128]{1,0:T(8,128)(2,1)S(1)}, bf16[2048,128]{1,0:T(8,128)(2,1)S(1)}, u32[]{:S(2)}, u32[]{:S(2)}) collective-permute-start(bf16[2048,128]{1,0:T(8,128)(2,1)S(1)} %get-tuple-element.44), channel_id=1, source_target_pairs={{0,96},{16,112},{32,64},{48,80},{64,32},{80,48},{96,0},{112,16},{1... | collective-permute-start | bytes 1572872 | tf_op jit(solution)/shard_map/ppermute | solution.py:383
  110.7 15.7 %collective-permute-start.8 = (bf16[2048,128]{1,0:T(8,128)(2,1)S(1)}, bf16[2048,128]{1,0:T(8,128)(2,1)S(1)}, u32[]{:S(2)}, u32[]{:S(2)}) collective-permute-start(bf16[2048,128]{1,0:T(8,128)(2,1)S(1)} %get-tuple-element.37), channel_id=1, source_target_pairs={{0,16},{16,0},{32,48},{48,32},{64,80},{80,64},{96,112},{112,96},{1... | collective-permute-start | bytes 1572872 | tf_op jit(solution)/shard_map/ppermute | solution.py:383
  114.0 23.1 %collective-permute-start.5 = (bf16[2048,128]{1,0:T(8,128)(2,1)S(1)}, bf16[2048,128]{1,0:T(8,128)(2,1)S(1)}, u32[]{:S(2)}, u32[]{:S(2)}) collective-permute-start(bf16[2048,128]{1,0:T(8,128)(2,1)S(1)} %get-tuple-element.32), channel_id=1, source_target_pairs={{0,16},{16,0},{32,48},{48,32},{64,80},{80,64},{96,112},{112,96},{1... | collective-permute-start | bytes 1572872 | tf_op jit(solution)/shard_map/ppermute | solution.py:383
  118.7 5.9 %collective-permute-start.24 = (bf16[256,128]{1,0:T(8,128)(2,1)S(1)}, bf16[256,128]{1,0:T(8,128)(2,1)S(1)}, u32[]{:S(2)}, u32[]{:S(2)}) collective-permute-start(bf16[256,128]{1,0:T(8,128)(2,1)S(1)} %get-tuple-element.51), channel_id=1, source_target_pairs={{0,96},{16,112},{32,64},{48,80},{64,32},{80,48},{96,0},{112,16},{1... | collective-permute-start | bytes 196616 | tf_op jit(solution)/shard_map/ppermute | solution.py:383
  122.6 29.3 %collective-permute-start.18 = (bf16[2048,128]{1,0:T(8,128)(2,1)}, bf16[2048,128]{1,0:T(8,128)(2,1)S(1)}, u32[]{:S(2)}, u32[]{:S(2)}) collective-permute-start(bf16[2048,128]{1,0:T(8,128)(2,1)} %get-tuple-element.49), channel_id=1, source_target_pairs={{0,16},{16,0},{32,48},{48,32},{64,80},{80,64},{96,112},{112,96},{1... | collective-permute-start | bytes 1572872 | tf_op jit(solution)/shard_map/ppermute | solution.py:383
  124.7 24.8 %collective-permute-start.25 = (bf16[256,64]{1,0:T(8,128)(2,1)S(1)}, bf16[256,64]{1,0:T(8,128)(2,1)S(1)}, u32[]{:S(2)}, u32[]{:S(2)}) collective-permute-start(bf16[256,64]{1,0:T(8,128)(2,1)S(1)} %slice.33), channel_id=1, source_target_pairs={{0,16},{16,0},{32,48},{48,32},{64,80},{80,64},{96,112},{112,96},{1... | collective-permute-start | bytes 98312 | tf_op jit(solution)/shard_map/ppermute | solution.py:383
  126.7 25.2 %collective-permute-start.9 = (bf16[1024,128]{1,0:T(8,128)(2,1)S(1)}, bf16[1024,128]{1,0:T(8,128)(2,1)S(1)}, u32[]{:S(2)}, u32[]{:S(2)}) collective-permute-start(bf16[1024,128]{1,0:T(8,128)(2,1)S(1)} %get-tuple-element.39), channel_id=1, source_target_pairs={{0,32},{16,48},{32,0},{48,16},{64,96},{80,112},{96,64},{112,80},{1... | collective-permute-start | bytes 786440 | tf_op jit(solution)/shard_map/ppermute | solution.py:383
  137.9 14.0 %collective-permute-start.6 = (bf16[1024,128]{1,0:T(8,128)(2,1)}, bf16[1024,128]{1,0:T(8,128)(2,1)S(1)}, u32[]{:S(2)}, u32[]{:S(2)}) collective-permute-start(bf16[1024,128]{1,0:T(8,128)(2,1)} %get-tuple-element.34), channel_id=1, source_target_pairs={{0,96},{16,112},{32,64},{48,80},{64,32},{80,48},{96,0},{112,16},{1... | collective-permute-start | bytes 786440 | tf_op jit(solution)/shard_map/ppermute | solution.py:383
  (8 other events, 97.6 us)

commit v5 on v4

--- a/solution.py
+++ b/solution.py
@@ -97,8 +97,8 @@
     r = lax.broadcasted_iota(jnp.int32, shape, 0)
     c = lax.broadcasted_iota(jnp.int32, shape, 1)
     same = r % HALF == c % HALF
-    straight = same & ((r // HALF) == (c // HALF) % 2)
-    crossed = same & ((r // HALF) != (c // HALF) % 2)
+    straight = same & ((r // HALF) == (c // GROUP) % 2)
+    crossed = same & ((r // HALF) != (c // GROUP) % 2)
     for point in range(4):
         rows = coef_ref[0, point * 8 : point * 8 + 8]
         cosine, sine = rows[0:1, :], rows[1:2, :]
@@ -290,20 +290,35 @@
     )(own, peer, weights)
 
 
-def fold_kernel(keep1_ref, got1_ref, keep2_ref, got2_ref, send_ref, own_ref):
+def own_lanes(shape, unit):
+    return (lane_ids(shape) // HALF) % 2 == unit
+
+
+def to_own(x, unit):
+    return pltpu.roll(x, HALF if unit else LANES - HALF, axis=1)
+
+
+def from_own(x, unit):
+    return pltpu.roll(x, LANES - HALF if unit else HALF, axis=1)
+
+
+def fold_kernel(unit, keep1_ref, got1_ref, keep2_ref, got2_ref, send_ref, own_ref):
     top = keep1_ref[...] + got1_ref[...].astype(F32)
     bottom = keep2_ref[...] + got2_ref[...].astype(F32)
-    first = lane_ids(top.shape) < GROUP
-    send_ref[...] = jnp.where(first, pltpu.roll(top, GROUP, axis=1), bottom).astype(BF16)
-    own_ref[...] = jnp.where(first, top, pltpu.roll(bottom, GROUP, axis=1))
-
-
-def fold(keep1, got1, keep2, got2, rows, shift):
+    own = own_lanes(top.shape, unit)
+    send_ref[...] = jnp.where(own, to_own(top, unit), bottom).astype(BF16)
+    own_ref[...] = jnp.where(own, top, from_own(bottom, unit))
+
+
+def fold(unit, keep1, got1, keep2, got2, rows, shift):
+    def kernel(*refs):
+        fold_kernel(unit, *refs)
+
     step = 1024
     spec = pl.BlockSpec((step, LANES), lambda i: (i, 0))
     late = pl.BlockSpec((step, LANES), lambda i: (i + shift // step, 0))
     return pl.pallas_call(
-        fold_kernel,
+        kernel,
         grid=(rows // step,),
         in_specs=[spec, spec, late, late],
         out_specs=[spec, spec],
@@ -320,24 +335,23 @@
 
 
 def finish_kernel(own1_ref, got1_ref, own2_ref, got2_ref, own_b_ref, got_b_ref, out_ref):
-    def turn(x, shift):
-        return pltpu.roll(x, shift, axis=1)
-
-    late = pl.program_id(0) >= pl.num_programs(0) // 2
-    top_a = own1_ref[...] + got1_ref[...].astype(F32)
-    top_a = jnp.where(late, turn(top_a, GROUP), top_a)
-    bottom_a = own2_ref[...] + got2_ref[...].astype(F32)
-    bottom_a = jnp.where(late, turn(bottom_a, GROUP), bottom_a)
     unit_b = own_b_ref[...] + got_b_ref[...].astype(F32)
-    quarter = lane_ids(unit_b.shape) // HALF
-
-    def merge(first, second, third, fourth):
-        low = jnp.where(quarter == 0, first, second)
-        high = jnp.where(quarter == 2, third, fourth)
-        return jnp.where(quarter < 2, low, high)
-
-    out_ref[0, 0] = merge(top_a, turn(unit_b, HALF), turn(top_a, HALF), turn(unit_b, GROUP))
-    out_ref[0, 1] = merge(bottom_a, turn(unit_b, 96), turn(bottom_a, HALF), unit_b)
+    first = own_lanes(unit_b.shape, 0)
+    halves = pl.num_programs(0) // 2
+
+    def store(place):
+        top_a = place(own1_ref[...] + got1_ref[...].astype(F32))
+        bottom_a = place(own2_ref[...] + got2_ref[...].astype(F32))
+        out_ref[0, 0] = jnp.where(first, top_a, unit_b)
+        out_ref[0, 1] = jnp.where(first, bottom_a, to_own(unit_b, 1))
+
+    @pl.when(pl.program_id(0) < halves)
+    def _():
+        store(lambda x: x)
+
+    @pl.when(pl.program_id(0) >= halves)
+    def _():
+        store(lambda x: to_own(x, 0))
 
 
 def finish(own1, got1, own2, got2, own_b, got_b, step):
@@ -359,15 +373,16 @@
 def moment_coefs(plans):
     lane = lax.broadcasted_iota(jnp.int32, (1, 32, 2 * LANES), 2)
     line = lax.broadcasted_iota(jnp.int32, (1, 32, 2 * LANES), 1)
-    slot, point, kind = lane // GROUP, line // 8, line % 8
+    point, kind = line // 8, line % 8
     tables = []
-    for owners, orders in plans:
+    for unit, owners, orders in plans:
+        slot = lane // LANES * 2 + ((lane // HALF) % 2 ^ unit)
         owner = jnp.where(point < 2, owners[0], owners[1])
         low = jnp.where(slot == 0, orders[0], orders[1])
         high = jnp.where(slot == 2, orders[2], orders[3])
         order = jnp.where(slot < 2, low, high)
         turns = ((order + 1) * (2 * (owner * 2 + point % 2) + 1)) % (2 * POINTS)
-        sign = jnp.where((lane // HALF) % 2 == 0, -1.0, 1.0)
+        sign = jnp.where((lane // GROUP) % 2 == 0, -1.0, 1.0)
         phase = turns.astype(F32) * (math.pi / POINTS)
         quarter = jnp.where(kind == 0, math.pi / 2, 0.0)
         tables.append(jnp.where(kind == 0, 1.0, sign) * jnp.sin(phase + quarter) / POINTS)
@@ -411,10 +426,10 @@
     pair, mirror = by_pair(quad_index), by_mirror(quad_index)
     coefs = moment_coefs(
         (
-            ((mine, pair), (other, mirror ^ 1, mine, mirror)),
-            ((mine, mirror), (other, pair ^ 1, mine, pair)),
-            ((mine, pair), (mirror, mirror ^ 1, mine, other)),
-            ((mine, mirror), (pair, pair ^ 1, mine, other)),
+            (0, (mine, pair), (other, mirror ^ 1, mine, mirror)),
+            (0, (mine, mirror), (other, pair ^ 1, mine, pair)),
+            (1, (mine, pair), (mirror, mirror ^ 1, mine, other)),
+            (1, (mine, mirror), (pair, pair ^ 1, mine, other)),
         ),
     )
     *rhs_units, weights = spread(rhs, coefs)
@@ -452,27 +467,36 @@
     got_a1 = swap(send_a1, "quad", by_x)
     got_a2 = swap(send_a2, "quad", by_x)
     quarter = half_rows // 2
-    send_a1, own_a1 = fold(keep_a1, got_a1, keep_a1, got_a1, quarter, quarter)
-    send_a2, own_a2 = fold(keep_a2, got_a2, keep_a2, got_a2, quarter, quarter)
+    send_a1, own_a1 = fold(0, keep_a1, got_a1, keep_a1, got_a1, quarter, quarter)
+    send_a2, own_a2 = fold(0, keep_a2, got_a2, keep_a2, got_a2, quarter, quarter)
 
     send_b1, keep_b1, send_b2, keep_b2 = first_stage(1)
     got_b1 = swap(send_b1, "quad", by_mirror)
     got_b2 = swap(send_b2, "quad", by_pair)
-    send_b, own_b = fold(keep_b1, got_b1, keep_b2, got_b2, half_rows, 0)
-
-    gram = jnp.concatenate(grams, axis=0)
-    gram = lax.reduce_precision(gram, 8, 7)
-    gram = gram + swap(gram.astype(BF16), "row", lambda i: i ^ 8).astype(F32)
-    for bit in (4, 2, 1):
-        gram = gram + swap(gram, "row", lambda i, bit=bit: i ^ bit)
+    send_b, own_b = fold(1, keep_b1, got_b1, keep_b2, got_b2, half_rows, 0)
+
+    def rounded(x):
+        return lax.reduce_precision(x, 8, 7)
+
+    even = row_index % 2 == 0
+    gram = jnp.where(even, grams[0], grams[1])
+    gram = gram + swap(jnp.where(even, grams[1], grams[0]), "row", near_row)
+    for bit in (8, 4, 2):
+        gram = rounded(gram)
+        peer = swap(gram.astype(BF16), "row", lambda i, bit=bit: i ^ bit)
+        gram = gram + peer.astype(F32)
     gram = gram.astype(BF16)
     peer = swap(gram, "quad", by_pair)
-    send_g, keep_g = combine(gram, peer, weights, 2, 256)
+    send_g, keep_g = combine(gram, peer, weights, 2, LANES)
     gram_sum = keep_g + swap(send_g, "quad", by_mirror).astype(F32)
-    gram_got = swap(gram_sum[:, GROUP:].astype(BF16), "quad", by_x)
-    blocks = gram_sum[:, :GROUP] + gram_got.astype(F32)
-    blocks = blocks * (1.0 / math.sqrt(RB * BS * 16))
-    blocks = blocks.reshape(2, LANES, 2, HALF).transpose(1, 2, 0, 3).reshape(1, LANES, LANES)
+    gram_got = swap(gram_sum.astype(BF16), "quad", by_x)
+    gram_own = gram_sum + jnp.roll(gram_got, HALF, axis=1).astype(F32)
+    gram_other = swap(gram_own, "row", near_row)
+    gram_a = jnp.where(even, gram_own, gram_other)
+    gram_b = jnp.where(even, gram_other, gram_own)
+    first = own_lanes((LANES, LANES), 0)
+    blocks = jnp.where(first, jnp.roll(gram_a, -HALF, axis=1), gram_b)
+    blocks = (blocks * (1.0 / math.sqrt(RB * BS * 16)))[None]
 
     got_a1 = swap(send_a1, "quad", by_mirror)
     got_a2 = swap(send_a2, "quad", by_pair)

time: 157 us -> 185 us (1.18)
  waiting for transfers between devices: 38.5 us -> 62.6 us
  Pallas kernels: 65.4 us -> 72 us
  starting transfers between devices: 43.9 us -> 38.4 us
  matrix products: 1.39 us -> 3.45 us
    ppermute x26 -> x27, waiting for transfers between devices: 38.5 us -> 62.6 us  [swap(): lax.ppermute(x, axis, [(i, j) for i, j in peers if 0 <= j < len(peers)])]
    ppermute x26 -> x27, starting transfers between devices: 43.9 us -> 38.4 us  [swap(): lax.ppermute(x, axis, [(i, j) for i, j in peers if 0 <= j < len(peers)])]
    pallas_call x4, Pallas kernels: 47.1 us -> 51.8 us  [sweep(): pl.pallas_call(kernel, grid_spec=pltpu.PrefetchScalarGridSpec(num_scalar_...]
    pallas_call x5, Pallas kernels: 3.8 us -> 6.71 us  [combine(): pl.pallas_call(combine_kernel, grid=(rows // rows_step,), in_specs=[row_s...]
    dot_general x4, matrix products: 1.39 us -> 3.45 us  [step(): lax.dot_general(x, part, (((0,), (0,)), ((), ())), preferred_element_type...]
  transfers between devices with their start and end apart: 26 -> 27, of which waited for: 6 -> 10; matrix products, arithmetic and copies ran while one was open for 3% -> 2% of each run, Pallas kernels for 35% -> 27%
where the time goes in v5:
time: 185 us; the launch traced here: 183 us
  Pallas kernels  72 us (39%)
  waiting for transfers between devices  62.6 us (34%)
  starting transfers between devices  38.4 us (21%)
  local copies, waits for them, and re-layouts  3.66 us (2%)
  matrix products  3.45 us (2%)
    ppermute x27, waiting for transfers between devices, swap(): lax.ppermute(x, axis, [(i, j) for i, j in peers if 0 <= j < len(peers)])  62.6 us
    pallas_call x4, Pallas kernels, sweep(): pl.pallas_call(kernel, grid_spec=pltpu.PrefetchScalarGridSpec(num_scalar_...  51.8 us
    ppermute x27, starting transfers between devices, swap(): lax.ppermute(x, axis, [(i, j) for i, j in peers if 0 <= j < len(peers)])  38.4 us
    pallas_call x1, Pallas kernels, initial(): pl.pallas_call(init_kernel, grid=(RB // STEP,), in_specs=[pl.BlockSpec((S...  7.65 us
    pallas_call x5, Pallas kernels, combine(): pl.pallas_call(combine_kernel, grid=(rows // rows_step,), in_specs=[row_s...  6.71 us
  transfers between devices with their start and end apart: 27, of which 10 were waited for; matrix products, arithmetic and copies ran while one was open for 2% of the time, Pallas kernels for 27%

profile of v5, /device:TPU:4, one launch (start us, length us, event | category | flops | bytes accessed | tf_op | source)
XLA Modules:
  0.0 182.8 jit_solution(12289125301181022500)
XLA Ops:
  0.7 7.7 %initial.1 = (bf16[64,64,128]{2,1,0:T(8,128)(2,1)}, bf16[64,64,128]{2,1,0:T(8,128)(2,1)}) custom-call(bf16[4096,128]{1,0:T(8,128)(2,1)} %x_ref.3, bf16[2,64,64,128]{3,2,1,0:T(8,128)(2,1)} %refs_2_.7, bf16[256,256]{1,0:T(8,128)(2,1)} %constant.271.clone.map_ref), custom_call_target="tpu_custom_call" | custom-call | tf_op jit(solution)/shard_map/initial/pallas_call | solution.py:78
  8.3 5.0 %collective-permute-start.11 = (bf16[64,64,128]{2,1,0:T(8,128)(2,1)}, bf16[64,64,128]{2,1,0:T(8,128)(2,1)}, u32[]{:S(2)}, u32[]{:S(2)}) collective-permute-start(bf16[64,64,128]{2,1,0:T(8,128)(2,1)} %get-tuple-element.41.refs_5_), channel_id=1, source_target_pairs={{1,2},{2,1},{3,4},{4,3},{5,6},{6,5},{7,8},{8,7},{9,10},{10,9},{11,... | collective-permute-start | bytes 3145736 | tf_op jit(solution)/shard_map/ppermute | solution.py:398
  13.4 4.2 %collective-permute-start.1 = (bf16[64,64,128]{2,1,0:T(8,128)(2,1)}, bf16[64,64,128]{2,1,0:T(8,128)(2,1)}, u32[]{:S(2)}, u32[]{:S(2)}) collective-permute-start(bf16[64,64,128]{2,1,0:T(8,128)(2,1)} %get-tuple-element.28.refs_5_), channel_id=1, source_target_pairs={{1,2},{2,1},{3,4},{4,3},{5,6},{6,5},{7,8},{8,7},{9,10},{10,9},{11,... | collective-permute-start | bytes 3145736 | tf_op jit(solution)/shard_map/ppermute | solution.py:398
  21.6 6.8 %collective-permute-done.11.refs_7_ = bf16[64,64,128]{2,1,0:T(8,128)(2,1)} collective-permute-done((bf16[64,64,128]{2,1,0:T(8,128)(2,1)}, bf16[64,64,128]{2,1,0:T(8,128)(2,1)}, u32[]{:S(2)}, u32[]{:S(2)}) %collective-permute-start.11) | collective-permute-done | bytes 1048608 | tf_op jit(solution)/shard_map/ppermute | solution.py:398
  29.6 12.9 %sweep.3.refs_5_ = bf16[64,64,128]{2,1,0:T(8,128)(2,1)} custom-call(s32[1664]{0:T(1024)S(1)} %concatenate.17.refs_0_, bf16[64,64,1536]{2,1,0:T(8,128)(2,1)} %refs_1_.7, bf16[2,64,64,128]{3,2,1,0:T(8,128)(2,1)} %refs_2_.7, bf16[64,64,128]{2,1,0:T(8,128)(2,1)S(1)} %get-tuple-element.40.refs_3_, f32[8,128]{1,0:T(8,128)S(1)} %maximum_maximum_fusion.refs_4_, ...), custom_call_target="tpu_custom_call" | custom-call | flops 1610612736 | bytes 20971520 | tf_op jit(solution)/shard_map/sweep/pallas_call | solution.py:239
  42.6 5.0 %collective-permute-start.13 = (bf16[64,64,128]{2,1,0:T(8,128)(2,1)}, bf16[64,64,128]{2,1,0:T(8,128)(2,1)}, u32[]{:S(2)}, u32[]{:S(2)}) collective-permute-start(bf16[64,64,128]{2,1,0:T(8,128)(2,1)} %sweep.3.refs_5_), channel_id=1, source_target_pairs={{1,2},{2,1},{3,4},{4,3},{5,6},{6,5},{7,8},{8,7},{9,10},{10,9},{11,... | collective-permute-start | bytes 3145736 | tf_op jit(solution)/shard_map/ppermute | solution.py:398
  47.6 13.0 %sweep.2.refs_5_ = bf16[64,64,128]{2,1,0:T(8,128)(2,1)} custom-call(s32[1664]{0:T(1024)S(1)} %concatenate.17.refs_0_, bf16[64,64,1536]{2,1,0:T(8,128)(2,1)} %refs_1_.7, bf16[2,64,64,128]{3,2,1,0:T(8,128)(2,1)} %refs_2_.7, bf16[64,64,128]{2,1,0:T(8,128)(2,1)S(1)} %get-tuple-element.27.refs_3_, f32[8,128]{1,0:T(8,128)S(1)} %maximum_maximum_fusion.refs_4_, ...), custom_call_target="tpu_custom_call" | custom-call | flops 1610612736 | bytes 20971520 | tf_op jit(solution)/shard_map/sweep/pallas_call | solution.py:239
  60.7 4.2 %collective-permute-start.3 = (bf16[64,64,128]{2,1,0:T(8,128)(2,1)}, bf16[64,64,128]{2,1,0:T(8,128)(2,1)}, u32[]{:S(2)}, u32[]{:S(2)}) collective-permute-start(bf16[64,64,128]{2,1,0:T(8,128)(2,1)} %sweep.2.refs_5_), channel_id=1, source_target_pairs={{1,2},{2,1},{3,4},{4,3},{5,6},{6,5},{7,8},{8,7},{9,10},{10,9},{11,... | collective-permute-start | bytes 3145736 | tf_op jit(solution)/shard_map/ppermute | solution.py:398
  65.0 13.3 %sweep_last.3 = (bf16[32,64,128]{2,1,0:T(8,128)(2,1)}, bf16[32,64,128]{2,1,0:T(8,128)(2,1)}) custom-call(s32[1664]{0:T(1024)S(1)} %concatenate.17.refs_0_, bf16[64,64,1536]{2,1,0:T(8,128)(2,1)} %refs_1_.7, bf16[2,64,64,128]{3,2,1,0:T(8,128)(2,1)} %refs_2_.7, bf16[64,64,128]{2,1,0:T(8,128)(2,1)S(1)} %get-tuple-element.40.refs_3_, ...), custom_call_target="tpu_custom_call" | custom-call | flops 1610612736 | bytes 20971520 | tf_op jit(solution)/shard_map/sweep_last/pallas_call | solution.py:239
  80.8 12.5 %sweep_last.2 = (bf16[32,64,128]{2,1,0:T(8,128)(2,1)S(1)}, bf16[32,64,128]{2,1,0:T(8,128)(2,1)S(1)}) custom-call(s32[1664]{0:T(1024)S(1)} %concatenate.17.refs_0_, bf16[64,64,1536]{2,1,0:T(8,128)(2,1)} %refs_1_.7, bf16[2,64,64,128]{3,2,1,0:T(8,128)(2,1)} %refs_2_.7, bf16[64,64,128]{2,1,0:T(8,128)(2,1)S(1)} %get-tuple-element.27.refs_3_, ...), custom_call_target="tpu_custom_call" | custom-call | flops 1610612736 | bytes 20971520 | tf_op jit(solution)/shard_map/sweep_last/pallas_call | solution.py:239
  96.8 5.4 %collective-permute-done.20 = bf16[128,128]{1,0:T(8,128)(2,1)S(1)} collective-permute-done((bf16[128,128]{1,0:T(8,128)(2,1)S(1)}, bf16[128,128]{1,0:T(8,128)(2,1)S(1)}, u32[]{:S(2)}, u32[]{:S(2)}) %collective-permute-start.20) | collective-permute-done | bytes 32800 | tf_op jit(solution)/shard_map/ppermute | solution.py:398
  102.3 4.1 %collective-permute-start.16 = (bf16[2048,128]{1,0:T(8,128)(2,1)}, bf16[2048,128]{1,0:T(8,128)(2,1)S(1)}, u32[]{:S(2)}, u32[]{:S(2)}) collective-permute-start(bf16[2048,128]{1,0:T(8,128)(2,1)} %bitcast.3.own_ref), channel_id=1, source_target_pairs={{0,96},{16,112},{32,64},{48,80},{64,32},{80,48},{96,0},{112,16},{1... | collective-permute-start | bytes 1572872 | tf_op jit(solution)/shard_map/ppermute | solution.py:398
  108.7 3.8 %collective-permute-done.22 = bf16[128,128]{1,0:T(8,128)(2,1)S(1)} collective-permute-done((bf16[128,128]{1,0:T(8,128)(2,1)S(1)}, bf16[128,128]{1,0:T(8,128)(2,1)S(1)}, u32[]{:S(2)}, u32[]{:S(2)}) %collective-permute-start.22) | collective-permute-done | bytes 32800 | tf_op jit(solution)/shard_map/ppermute | solution.py:398
  113.8 17.4 %collective-permute-done.23.peer_ref = bf16[128,128]{1,0:T(8,128)(2,1)S(1)} collective-permute-done((bf16[128,128]{1,0:T(8,128)(2,1)S(1)}, bf16[128,128]{1,0:T(8,128)(2,1)S(1)}, u32[]{:S(2)}, u32[]{:S(2)}) %collective-permute-start.23) | collective-permute-done | bytes 32800 | tf_op jit(solution)/shard_map/ppermute | solution.py:398
  132.0 1.9 %combine.8 = (bf16[2048,128]{1,0:T(8,128)(2,1)S(1)}, f32[2048,128]{1,0:T(8,128)S(1)}) custom-call(bf16[2048,128]{1,0:T(8,128)(2,1)} %bitcast.3.own_ref, bf16[2048,128]{1,0:T(8,128)(2,1)S(1)} %collective-permute-done.16.peer_ref, bf16[4,512,256]{2,1,0:T(8,128)(2,1)S(1)} %get-tuple-element.30.weight_ref), custom_call_target="tpu_custom_call" | custom-call | flops 536870912 | bytes 3145728 | tf_op jit(solution)/shard_map/combine/pallas_call | solution.py:276
  134.2 1.9 %combine.7 = (bf16[2048,128]{1,0:T(8,128)(2,1)S(1)}, f32[2048,128]{1,0:T(8,128)S(1)}) custom-call(bf16[2048,128]{1,0:T(8,128)(2,1)} %bitcast.2.own_ref, bf16[2048,128]{1,0:T(8,128)(2,1)} %collective-permute-done.14.peer_ref, bf16[4,512,256]{2,1,0:T(8,128)(2,1)S(1)} %get-tuple-element.30.weight_ref), custom_call_target="tpu_custom_call" | custom-call | flops 536870912 | bytes 3145728 | tf_op jit(solution)/shard_map/combine/pallas_call | solution.py:276
  136.1 2.9 %collective-permute-start.15 = (bf16[2048,128]{1,0:T(8,128)(2,1)S(1)}, bf16[2048,128]{1,0:T(8,128)(2,1)S(1)}, u32[]{:S(2)}, u32[]{:S(2)}) collective-permute-start(bf16[2048,128]{1,0:T(8,128)(2,1)S(1)} %get-tuple-element.44), channel_id=1, source_target_pairs={{0,96},{16,112},{32,64},{48,80},{64,32},{80,48},{96,0},{112,16},{1... | collective-permute-start | bytes 1572872 | tf_op jit(solution)/shard_map/ppermute | solution.py:398
  139.1 1.9 %combine.6 = (bf16[2048,128]{1,0:T(8,128)(2,1)S(1)}, f32[2048,128]{1,0:T(8,128)S(1)}) custom-call(bf16[2048,128]{1,0:T(8,128)(2,1)S(1)} %bitcast.23, bf16[2048,128]{1,0:T(8,128)(2,1)} %collective-permute-done.7.peer_ref, bf16[4,512,256]{2,1,0:T(8,128)(2,1)S(1)} %get-tuple-element.30.weight_ref), custom_call_target="tpu_custom_call" | custom-call | flops 536870912 | bytes 3145728 | tf_op jit(solution)/shard_map/combine/pallas_call | solution.py:276
  140.9 2.2 %collective-permute-start.8 = (bf16[2048,128]{1,0:T(8,128)(2,1)S(1)}, bf16[2048,128]{1,0:T(8,128)(2,1)S(1)}, u32[]{:S(2)}, u32[]{:S(2)}) collective-permute-start(bf16[2048,128]{1,0:T(8,128)(2,1)S(1)} %get-tuple-element.37), channel_id=1, source_target_pairs={{0,16},{16,0},{32,48},{48,32},{64,80},{80,64},{96,112},{112,96},{1... | collective-permute-start | bytes 1572872 | tf_op jit(solution)/shard_map/ppermute | solution.py:398
  144.1 2.1 %collective-permute-start.25 = (bf16[128,128]{0,1:T(8,128)(2,1)S(1)}, bf16[128,128]{0,1:T(8,128)(2,1)S(1)}, u32[]{:S(2)}, u32[]{:S(2)}) collective-permute-start(bf16[128,128]{0,1:T(8,128)(2,1)S(1)} %fusion.11), channel_id=1, source_target_pairs={{0,16},{16,0},{32,48},{48,32},{64,80},{80,64},{96,112},{112,96},{1... | collective-permute-start | bytes 98312 | tf_op jit(solution)/shard_map/ppermute | solution.py:398
  146.2 18.3 %collective-permute-done.25 = bf16[128,128]{0,1:T(8,128)(2,1)S(1)} collective-permute-done((bf16[128,128]{0,1:T(8,128)(2,1)S(1)}, bf16[128,128]{0,1:T(8,128)(2,1)S(1)}, u32[]{:S(2)}, u32[]{:S(2)}) %collective-permute-start.25) | collective-permute-done | bytes 32800 | tf_op jit(solution)/shard_map/ppermute | solution.py:398
  171.7 4.6 %collective-permute-done.9.got2_ref = bf16[1024,128]{1,0:T(8,128)(2,1)S(1)} collective-permute-done((bf16[1024,128]{1,0:T(8,128)(2,1)S(1)}, bf16[1024,128]{1,0:T(8,128)(2,1)S(1)}, u32[]{:S(2)}, u32[]{:S(2)}) %collective-permute-start.9) | collective-permute-done | bytes 262176 | tf_op jit(solution)/shard_map/ppermute | solution.py:398
  176.4 3.1 %collective-permute-done.6.got1_ref = bf16[1024,128]{1,0:T(8,128)(2,1)S(1)} collective-permute-done((bf16[1024,128]{1,0:T(8,128)(2,1)}, bf16[1024,128]{1,0:T(8,128)(2,1)S(1)}, u32[]{:S(2)}, u32[]{:S(2)}) %collective-permute-start.6) | collective-permute-done | bytes 262176 | tf_op jit(solution)/shard_map/ppermute | solution.py:398
  180.4 2.4 %finish.1 = f32[1,2,2048,128]{3,2,1,0:T(8,128)} custom-call(f32[1024,128]{1,0:T(8,128)S(1)} %get-tuple-element.33.own1_ref, bf16[1024,128]{1,0:T(8,128)(2,1)S(1)} %collective-permute-done.6.got1_ref, f32[1024,128]{1,0:T(8,128)S(1)} %get-tuple-element.38.own2_ref, bf16[1024,128]{1,0:T(8,128)(2,1)S(1)} %collective-permute-done.9.got2_ref, ...), custom_call_target="tpu_custom_call" | custom-call | tf_op jit(solution)/shard_map/finish/pallas_call | solution.py:362
  (102 shorter events, 25.0 us)
Async XLA Ops:
  8.3 13.3 %collective-permute-start.10 = (bf16[64,64,128]{2,1,0:T(8,128)(2,1)}, bf16[64,64,128]{2,1,0:T(8,128)(2,1)}, u32[]{:S(2)}, u32[]{:S(2)}) collective-permute-start(bf16[64,64,128]{2,1,0:T(8,128)(2,1)} %get-tuple-element.41.refs_5_), channel_id=1, source_target_pairs={{0,1},{1,0},{2,3},{3,2},{4,5},{5,4},{6,7},{7,6},{8,9},{9,8},{10,11... | collective-permute-start | bytes 3145736 | tf_op jit(solution)/shard_map/ppermute | solution.py:398
  8.3 20.0 %collective-permute-start.11 = (bf16[64,64,128]{2,1,0:T(8,128)(2,1)}, bf16[64,64,128]{2,1,0:T(8,128)(2,1)}, u32[]{:S(2)}, u32[]{:S(2)}) collective-permute-start(bf16[64,64,128]{2,1,0:T(8,128)(2,1)} %get-tuple-element.41.refs_5_), channel_id=1, source_target_pairs={{1,2},{2,1},{3,4},{4,3},{5,6},{6,5},{7,8},{8,7},{9,10},{10,9},{11,... | collective-permute-start | bytes 3145736 | tf_op jit(solution)/shard_map/ppermute | solution.py:398
  13.3 34.3 %collective-permute-start = (bf16[64,64,128]{2,1,0:T(8,128)(2,1)}, bf16[64,64,128]{2,1,0:T(8,128)(2,1)}, u32[]{:S(2)}, u32[]{:S(2)}) collective-permute-start(bf16[64,64,128]{2,1,0:T(8,128)(2,1)} %get-tuple-element.28.refs_5_), channel_id=1, source_target_pairs={{0,1},{1,0},{2,3},{3,2},{4,5},{5,4},{6,7},{7,6},{8,9},{9,8},{10,11... | collective-permute-start | bytes 3145736 | tf_op jit(solution)/shard_map/ppermute | solution.py:398
  13.4 34.2 %collective-permute-start.1 = (bf16[64,64,128]{2,1,0:T(8,128)(2,1)}, bf16[64,64,128]{2,1,0:T(8,128)(2,1)}, u32[]{:S(2)}, u32[]{:S(2)}) collective-permute-start(bf16[64,64,128]{2,1,0:T(8,128)(2,1)} %get-tuple-element.28.refs_5_), channel_id=1, source_target_pairs={{1,2},{2,1},{3,4},{4,3},{5,6},{6,5},{7,8},{8,7},{9,10},{10,9},{11,... | collective-permute-start | bytes 3145736 | tf_op jit(solution)/shard_map/ppermute | solution.py:398
  42.5 22.4 %collective-permute-start.12 = (bf16[64,64,128]{2,1,0:T(8,128)(2,1)}, bf16[64,64,128]{2,1,0:T(8,128)(2,1)}, u32[]{:S(2)}, u32[]{:S(2)}) collective-permute-start(bf16[64,64,128]{2,1,0:T(8,128)(2,1)} %sweep.3.refs_5_), channel_id=1, source_target_pairs={{0,1},{1,0},{2,3},{3,2},{4,5},{5,4},{6,7},{7,6},{8,9},{9,8},{10,11... | collective-permute-start | bytes 3145736 | tf_op jit(solution)/shard_map/ppermute | solution.py:398
  42.6 22.3 %collective-permute-start.13 = (bf16[64,64,128]{2,1,0:T(8,128)(2,1)}, bf16[64,64,128]{2,1,0:T(8,128)(2,1)}, u32[]{:S(2)}, u32[]{:S(2)}) collective-permute-start(bf16[64,64,128]{2,1,0:T(8,128)(2,1)} %sweep.3.refs_5_), channel_id=1, source_target_pairs={{1,2},{2,1},{3,4},{4,3},{5,6},{6,5},{7,8},{8,7},{9,10},{10,9},{11,... | collective-permute-start | bytes 3145736 | tf_op jit(solution)/shard_map/ppermute | solution.py:398
  60.6 19.1 %collective-permute-start.2 = (bf16[64,64,128]{2,1,0:T(8,128)(2,1)}, bf16[64,64,128]{2,1,0:T(8,128)(2,1)}, u32[]{:S(2)}, u32[]{:S(2)}) collective-permute-start(bf16[64,64,128]{2,1,0:T(8,128)(2,1)} %sweep.2.refs_5_), channel_id=1, source_target_pairs={{0,1},{1,0},{2,3},{3,2},{4,5},{5,4},{6,7},{7,6},{8,9},{9,8},{10,11... | collective-permute-start | bytes 3145736 | tf_op jit(solution)/shard_map/ppermute | solution.py:398
  60.7 20.0 %collective-permute-start.3 = (bf16[64,64,128]{2,1,0:T(8,128)(2,1)}, bf16[64,64,128]{2,1,0:T(8,128)(2,1)}, u32[]{:S(2)}, u32[]{:S(2)}) collective-permute-start(bf16[64,64,128]{2,1,0:T(8,128)(2,1)} %sweep.2.refs_5_), channel_id=1, source_target_pairs={{1,2},{2,1},{3,4},{4,3},{5,6},{6,5},{7,8},{8,7},{9,10},{10,9},{11,... | collective-permute-start | bytes 3145736 | tf_op jit(solution)/shard_map/ppermute | solution.py:398
  102.3 6.2 %collective-permute-start.21 = (bf16[128,128]{1,0:T(8,128)(2,1)S(1)}, bf16[128,128]{1,0:T(8,128)(2,1)S(1)}, u32[]{:S(2)}, u32[]{:S(2)}) collective-permute-start(bf16[128,128]{1,0:T(8,128)(2,1)S(1)} %fusion.12), channel_id=1, source_target_pairs={{0,4},{1,5},{2,6},{3,7},{4,0},{5,1},{6,2},{7,3},{8,12},{9,13},{10,... | collective-permute-start | bytes 98312 | tf_op jit(solution)/shard_map/ppermute | solution.py:398
  102.3 29.7 %collective-permute-start.16 = (bf16[2048,128]{1,0:T(8,128)(2,1)}, bf16[2048,128]{1,0:T(8,128)(2,1)S(1)}, u32[]{:S(2)}, u32[]{:S(2)}) collective-permute-start(bf16[2048,128]{1,0:T(8,128)(2,1)} %bitcast.3.own_ref), channel_id=1, source_target_pairs={{0,96},{16,112},{32,64},{48,80},{64,32},{80,48},{96,0},{112,16},{1... | collective-permute-start | bytes 1572872 | tf_op jit(solution)/shard_map/ppermute | solution.py:398
  106.5 27.7 %collective-permute-start.14 = (bf16[2048,128]{1,0:T(8,128)(2,1)}, bf16[2048,128]{1,0:T(8,128)(2,1)}, u32[]{:S(2)}, u32[]{:S(2)}) collective-permute-start(bf16[2048,128]{1,0:T(8,128)(2,1)} %bitcast.2.own_ref), channel_id=1, source_target_pairs={{0,32},{16,48},{32,0},{48,16},{64,96},{80,112},{96,64},{112,80},{1... | collective-permute-start | bytes 1572872 | tf_op jit(solution)/shard_map/ppermute | solution.py:398
  106.5 32.6 %collective-permute-start.7 = (bf16[2048,128]{1,0:T(8,128)(2,1)S(1)}, bf16[2048,128]{1,0:T(8,128)(2,1)}, u32[]{:S(2)}, u32[]{:S(2)}) collective-permute-start(bf16[2048,128]{1,0:T(8,128)(2,1)S(1)} %bitcast.22), channel_id=1, source_target_pairs={{0,96},{16,112},{32,64},{48,80},{64,32},{80,48},{96,0},{112,16},{1... | collective-permute-start | bytes 1572872 | tf_op jit(solution)/shard_map/ppermute | solution.py:398
  107.0 36.1 %collective-permute-start.4 = (bf16[2048,128]{1,0:T(8,128)(2,1)S(1)}, bf16[2048,128]{1,0:T(8,128)(2,1)S(1)}, u32[]{:S(2)}, u32[]{:S(2)}) collective-permute-start(bf16[2048,128]{1,0:T(8,128)(2,1)S(1)} %bitcast.19), channel_id=1, source_target_pairs={{0,32},{16,48},{32,0},{48,16},{64,96},{80,112},{96,64},{112,80},{1... | collective-permute-start | bytes 1572872 | tf_op jit(solution)/shard_map/ppermute | solution.py:398
  112.5 18.6 %collective-permute-start.23 = (bf16[128,128]{1,0:T(8,128)(2,1)S(1)}, bf16[128,128]{1,0:T(8,128)(2,1)S(1)}, u32[]{:S(2)}, u32[]{:S(2)}) collective-permute-start(bf16[128,128]{1,0:T(8,128)(2,1)S(1)} %add_convert_fusion.own_ref), channel_id=1, source_target_pairs={{0,32},{16,48},{32,0},{48,16},{64,96},{80,112},{96,64},{112,80},{1... | collective-permute-start | bytes 98312 | tf_op jit(solution)/shard_map/ppermute | solution.py:398
  131.5 12.6 %collective-permute-start.24 = (bf16[128,128]{0,1:T(8,128)(2,1)S(1)}, bf16[128,128]{0,1:T(8,128)(2,1)S(1)}, u32[]{:S(2)}, u32[]{:S(2)}) collective-permute-start(bf16[128,128]{0,1:T(8,128)(2,1)S(1)} %copy.21), channel_id=1, source_target_pairs={{0,96},{16,112},{32,64},{48,80},{64,32},{80,48},{96,0},{112,16},{1... | collective-permute-start | bytes 98312 | tf_op jit(solution)/shard_map/ppermute | solution.py:398
  133.9 30.8 %collective-permute-start.17 = (bf16[2048,128]{1,0:T(8,128)(2,1)S(1)}, bf16[2048,128]{1,0:T(8,128)(2,1)S(1)}, u32[]{:S(2)}, u32[]{:S(2)}) collective-permute-start(bf16[2048,128]{1,0:T(8,128)(2,1)S(1)} %get-tuple-element.47), channel_id=1, source_target_pairs={{0,32},{16,48},{32,0},{48,16},{64,96},{80,112},{96,64},{112,80},{1... | collective-permute-start | bytes 1572872 | tf_op jit(solution)/shard_map/ppermute | solution.py:398
  136.1 28.6 %collective-permute-start.15 = (bf16[2048,128]{1,0:T(8,128)(2,1)S(1)}, bf16[2048,128]{1,0:T(8,128)(2,1)S(1)}, u32[]{:S(2)}, u32[]{:S(2)}) collective-permute-start(bf16[2048,128]{1,0:T(8,128)(2,1)S(1)} %get-tuple-element.44), channel_id=1, source_target_pairs={{0,96},{16,112},{32,64},{48,80},{64,32},{80,48},{96,0},{112,16},{1... | collective-permute-start | bytes 1572872 | tf_op jit(solution)/shard_map/ppermute | solution.py:398
  140.9 26.7 %collective-permute-start.8 = (bf16[2048,128]{1,0:T(8,128)(2,1)S(1)}, bf16[2048,128]{1,0:T(8,128)(2,1)S(1)}, u32[]{:S(2)}, u32[]{:S(2)}) collective-permute-start(bf16[2048,128]{1,0:T(8,128)(2,1)S(1)} %get-tuple-element.37), channel_id=1, source_target_pairs={{0,16},{16,0},{32,48},{48,32},{64,80},{80,64},{96,112},{112,96},{1... | collective-permute-start | bytes 1572872 | tf_op jit(solution)/shard_map/ppermute | solution.py:398
  144.0 25.1 %collective-permute-start.5 = (bf16[2048,128]{1,0:T(8,128)(2,1)S(1)}, bf16[2048,128]{1,0:T(8,128)(2,1)S(1)}, u32[]{:S(2)}, u32[]{:S(2)}) collective-permute-start(bf16[2048,128]{1,0:T(8,128)(2,1)S(1)} %get-tuple-element.32), channel_id=1, source_target_pairs={{0,16},{16,0},{32,48},{48,32},{64,80},{80,64},{96,112},{112,96},{1... | collective-permute-start | bytes 1572872 | tf_op jit(solution)/shard_map/ppermute | solution.py:398
  144.1 20.4 %collective-permute-start.25 = (bf16[128,128]{0,1:T(8,128)(2,1)S(1)}, bf16[128,128]{0,1:T(8,128)(2,1)S(1)}, u32[]{:S(2)}, u32[]{:S(2)}) collective-permute-start(bf16[128,128]{0,1:T(8,128)(2,1)S(1)} %fusion.11), channel_id=1, source_target_pairs={{0,16},{16,0},{32,48},{48,32},{64,80},{80,64},{96,112},{112,96},{1... | collective-permute-start | bytes 98312 | tf_op jit(solution)/shard_map/ppermute | solution.py:398
  164.6 6.3 %collective-permute-start.26 = (f32[128,128]{0,1:T(8,128)S(1)}, f32[128,128]{0,1:T(8,128)S(1)}, u32[]{:S(2)}, u32[]{:S(2)}) collective-permute-start(f32[128,128]{0,1:T(8,128)S(1)} %convert_add_fusion), channel_id=1, source_target_pairs={{0,1},{1,0},{2,3},{3,2},{4,5},{5,4},{6,7},{7,6},{8,9},{9,8},{10,11... | collective-permute-start | bytes 196616 | tf_op jit(solution)/shard_map/ppermute | solution.py:398
  165.9 14.5 %collective-permute-start.18 = (bf16[2048,128]{1,0:T(8,128)(2,1)}, bf16[2048,128]{1,0:T(8,128)(2,1)S(1)}, u32[]{:S(2)}, u32[]{:S(2)}) collective-permute-start(bf16[2048,128]{1,0:T(8,128)(2,1)} %get-tuple-element.49), channel_id=1, source_target_pairs={{0,16},{16,0},{32,48},{48,32},{64,80},{80,64},{96,112},{112,96},{1... | collective-permute-start | bytes 1572872 | tf_op jit(solution)/shard_map/ppermute | solution.py:398
  167.9 8.5 %collective-permute-start.9 = (bf16[1024,128]{1,0:T(8,128)(2,1)S(1)}, bf16[1024,128]{1,0:T(8,128)(2,1)S(1)}, u32[]{:S(2)}, u32[]{:S(2)}) collective-permute-start(bf16[1024,128]{1,0:T(8,128)(2,1)S(1)} %get-tuple-element.39), channel_id=1, source_target_pairs={{0,32},{16,48},{32,0},{48,16},{64,96},{80,112},{96,64},{112,80},{1... | collective-permute-start | bytes 786440 | tf_op jit(solution)/shard_map/ppermute | solution.py:398
  169.9 9.5 %collective-permute-start.6 = (bf16[1024,128]{1,0:T(8,128)(2,1)}, bf16[1024,128]{1,0:T(8,128)(2,1)S(1)}, u32[]{:S(2)}, u32[]{:S(2)}) collective-permute-start(bf16[1024,128]{1,0:T(8,128)(2,1)} %get-tuple-element.34), channel_id=1, source_target_pairs={{0,96},{16,112},{32,64},{48,80},{64,32},{80,48},{96,0},{112,16},{1... | collective-permute-start | bytes 786440 | tf_op jit(solution)/shard_map/ppermute | solution.py:398
  (10 other events, 97.3 us)

commit v6 on v5

--- a/solution.py
+++ b/solution.py
@@ -16,7 +16,8 @@
 LANES = 128
 GROUP = 64
 HALF = 32
-STEP = 8
+STEP = 16
+FIRST = 32
 F32 = jnp.float32
 BF16 = jnp.bfloat16
 
@@ -52,13 +53,13 @@
 
 def init_kernel(x_ref, pre_ref, map_ref, y_a_ref, y_b_ref):
     rights = []
-    for b in range(STEP):
+    for b in range(FIRST):
         x = x_ref[b * BS : (b + 1) * BS].astype(F32)
         turned = pltpu.roll(x, GROUP, axis=1)
         turned = jnp.where(lane_ids(x.shape) < GROUP, -turned, turned)
         rights.append(jnp.concatenate([x, turned], axis=0).astype(BF16))
     outs = []
-    for b in range(STEP):
+    for b in range(FIRST):
         left = jnp.concatenate([pre_ref[0, b], pre_ref[1, b]], axis=0)
         outs.append(jnp.dot(left, rights[b], preferred_element_type=F32))
     outs = [out.astype(BF16) for out in outs]
@@ -68,19 +69,19 @@
         [jnp.concatenate(firsts, axis=0), jnp.concatenate(seconds, axis=0)], axis=1
     )
     out = jnp.dot(both, map_ref[...], preferred_element_type=F32).astype(BF16)
-    y_a_ref[...] = out[:, :LANES].reshape(STEP, BS, LANES)
-    y_b_ref[...] = out[:, LANES:].reshape(STEP, BS, LANES)
+    y_a_ref[...] = out[:, :LANES].reshape(FIRST, BS, LANES)
+    y_b_ref[...] = out[:, LANES:].reshape(FIRST, BS, LANES)
 
 
 def initial(rhs, precond):
     block = jax.ShapeDtypeStruct((RB, BS, LANES), BF16)
-    out_spec = pl.BlockSpec((STEP, BS, LANES), lambda i: (i, 0, 0))
+    out_spec = pl.BlockSpec((FIRST, BS, LANES), lambda i: (i, 0, 0))
     return pl.pallas_call(
         init_kernel,
-        grid=(RB // STEP,),
+        grid=(RB // FIRST,),
         in_specs=[
-            pl.BlockSpec((STEP * BS, LANES), lambda i: (i, 0)),
-            pl.BlockSpec((2, STEP, BS, LANES), lambda i: (0, i, 0, 0)),
+            pl.BlockSpec((FIRST * BS, LANES), lambda i: (i, 0)),
+            pl.BlockSpec((2, FIRST, BS, LANES), lambda i: (0, i, 0, 0)),
             pl.BlockSpec((2 * LANES, 2 * LANES), lambda i: (0, 0)),
         ],
         out_specs=[out_spec] * 2,
@@ -257,34 +258,37 @@
         cost_estimate=pl.CostEstimate(
             flops=2 * RB * BS * SLOTS * BS * LANES, bytes_accessed=20 << 20, transcendentals=0
         ),
-        compiler_params=pltpu.CompilerParams(vmem_limit_bytes=47 << 20),
+        compiler_params=pltpu.CompilerParams(vmem_limit_bytes=48 << 20),
         name="sweep_last" if last else "sweep",
     )(index, ham, precond, rhs_unit, z, local, near, far)
 
 
-def combine_kernel(own_ref, peer_ref, weight_ref, send_ref, keep_ref):
+def weighted(own_ref, peer_ref, weight_ref):
     own, peer = own_ref[...], peer_ref[...]
     both = jnp.concatenate([own, peer, own, peer], axis=1)
-    out = jnp.dot(both, weight_ref[0], preferred_element_type=F32)
-    send_ref[...] = out[:, :LANES].astype(BF16)
-    keep_ref[...] = out[:, LANES:]
-
-
-def combine(own, peer, weights, which, rows_step):
+    return jnp.dot(both, weight_ref[0], preferred_element_type=F32)
+
+
+def combine_kernel(own_ref, peer_ref, weight_ref, send_ref):
+    send_ref[...] = weighted(own_ref, peer_ref, weight_ref).astype(send_ref.dtype)
+
+
+def combine(own, peer, weights, which, part, rows_step, kind=BF16):
     rows = peer.shape[0]
     row_spec = pl.BlockSpec((rows_step, LANES), lambda i: (i, 0))
     return pl.pallas_call(
         combine_kernel,
         grid=(rows // rows_step,),
-        in_specs=[row_spec, row_spec, pl.BlockSpec((1, 4 * LANES, 2 * LANES), lambda i: (which, 0, 0))],
-        out_specs=[row_spec, row_spec],
-        out_shape=[
-            jax.ShapeDtypeStruct((rows, LANES), BF16),
-            jax.ShapeDtypeStruct((rows, LANES), F32),
+        in_specs=[
+            row_spec,
+            row_spec,
+            pl.BlockSpec((1, 4 * LANES, LANES), lambda i: (which, 0, part)),
         ],
+        out_specs=row_spec,
+        out_shape=jax.ShapeDtypeStruct((rows, LANES), kind),
         compiler_params=pltpu.CompilerParams(vmem_limit_bytes=8 << 20),
         cost_estimate=pl.CostEstimate(
-            flops=2 * rows * 256 * 512, bytes_accessed=rows * LANES * 12, transcendentals=0
+            flops=2 * rows * 128 * 512, bytes_accessed=rows * LANES * 6, transcendentals=0
         ),
         name="combine",
     )(own, peer, weights)
@@ -302,36 +306,40 @@
     return pltpu.roll(x, LANES - HALF if unit else HALF, axis=1)
 
 
-def fold_kernel(unit, keep1_ref, got1_ref, keep2_ref, got2_ref, send_ref, own_ref):
-    top = keep1_ref[...] + got1_ref[...].astype(F32)
-    bottom = keep2_ref[...] + got2_ref[...].astype(F32)
+def fold_kernel(unit, own1, peer1, got1, weight1, own2, peer2, got2, weight2, send_ref, own_ref):
+    top = weighted(own1, peer1, weight1) + got1[...].astype(F32)
+    bottom = weighted(own2, peer2, weight2) + got2[...].astype(F32)
     own = own_lanes(top.shape, unit)
     send_ref[...] = jnp.where(own, to_own(top, unit), bottom).astype(BF16)
     own_ref[...] = jnp.where(own, top, from_own(bottom, unit))
 
 
-def fold(unit, keep1, got1, keep2, got2, rows, shift):
+def fold(unit, first, second, weights, rows, shift):
     def kernel(*refs):
         fold_kernel(unit, *refs)
 
     step = 1024
     spec = pl.BlockSpec((step, LANES), lambda i: (i, 0))
     late = pl.BlockSpec((step, LANES), lambda i: (i + shift // step, 0))
+
+    def weight_spec(which):
+        return pl.BlockSpec((1, 4 * LANES, LANES), lambda i: (which, 0, 1))
+
     return pl.pallas_call(
         kernel,
         grid=(rows // step,),
-        in_specs=[spec, spec, late, late],
+        in_specs=[spec] * 3 + [weight_spec(first[3])] + [late] * 3 + [weight_spec(second[3])],
         out_specs=[spec, spec],
         out_shape=[
             jax.ShapeDtypeStruct((rows, LANES), BF16),
             jax.ShapeDtypeStruct((rows, LANES), F32),
         ],
-        compiler_params=pltpu.CompilerParams(vmem_limit_bytes=10 << 20),
+        compiler_params=pltpu.CompilerParams(vmem_limit_bytes=12 << 20),
         cost_estimate=pl.CostEstimate(
-            flops=rows * LANES * 8, bytes_accessed=rows * LANES * 18, transcendentals=0
+            flops=rows * LANES * 2048, bytes_accessed=rows * LANES * 18, transcendentals=0
         ),
         name="fold",
-    )(keep1, got1, keep2, got2)
+    )(*first[:3], weights, *second[:3], weights)
 
 
 def finish_kernel(own1_ref, got1_ref, own2_ref, got2_ref, own_b_ref, got_b_ref, out_ref):
@@ -460,20 +468,24 @@
         top, bottom = (part.reshape(half_rows, LANES) for part in units[unit])
         got1 = swap(top, "quad", by_pair)
         got2 = swap(bottom, "quad", by_mirror)
-        out1 = combine(top, got1, weights, 2 * unit, 1024)
-        return out1 + combine(bottom, got2, weights, 2 * unit + 1, 1024)
-
-    send_a1, keep_a1, send_a2, keep_a2 = first_stage(0)
+        send1 = combine(top, got1, weights, 2 * unit, 0, 1024)
+        send2 = combine(bottom, got2, weights, 2 * unit + 1, 0, 1024)
+        return (top, got1), (bottom, got2), send1, send2
+
+    pair_a1, pair_a2, send_a1, send_a2 = first_stage(0)
     got_a1 = swap(send_a1, "quad", by_x)
     got_a2 = swap(send_a2, "quad", by_x)
     quarter = half_rows // 2
-    send_a1, own_a1 = fold(0, keep_a1, got_a1, keep_a1, got_a1, quarter, quarter)
-    send_a2, own_a2 = fold(0, keep_a2, got_a2, keep_a2, got_a2, quarter, quarter)
-
-    send_b1, keep_b1, send_b2, keep_b2 = first_stage(1)
+    half = (*pair_a1, got_a1, 0)
+    send_a1, own_a1 = fold(0, half, half, weights, quarter, quarter)
+    half = (*pair_a2, got_a2, 1)
+    send_a2, own_a2 = fold(0, half, half, weights, quarter, quarter)
+
+    pair_b1, pair_b2, send_b1, send_b2 = first_stage(1)
     got_b1 = swap(send_b1, "quad", by_mirror)
     got_b2 = swap(send_b2, "quad", by_pair)
-    send_b, own_b = fold(1, keep_b1, got_b1, keep_b2, got_b2, half_rows, 0)
+    halves = (*pair_b1, got_b1, 2), (*pair_b2, got_b2, 3)
+    send_b, own_b = fold(1, *halves, weights, half_rows, 0)
 
     def rounded(x):
         return lax.reduce_precision(x, 8, 7)
@@ -487,7 +499,8 @@
         gram = gram + peer.astype(F32)
     gram = gram.astype(BF16)
     peer = swap(gram, "quad", by_pair)
-    send_g, keep_g = combine(gram, peer, weights, 2, LANES)
+    send_g = combine(gram, peer, weights, 2, 0, LANES)
+    keep_g = combine(gram, peer, weights, 2, 1, LANES, F32)
     gram_sum = keep_g + swap(send_g, "quad", by_mirror).astype(F32)
     gram_got = swap(gram_sum.astype(BF16), "quad", by_x)
     gram_own = gram_sum + jnp.roll(gram_got, HALF, axis=1).astype(F32)

time: 185 us -> 172 us (0.930)
  Pallas kernels: 72 us -> 61.5 us
  waiting for transfers between devices: 62.6 us -> 56.5 us
  starting transfers between devices: 38.4 us -> 41.4 us
  local copies, waits for them, and re-layouts: 3.66 us -> 5.94 us
    pallas_call x4, Pallas kernels: 51.8 us -> 41.2 us  [sweep(): pl.pallas_call(kernel, grid_spec=pltpu.PrefetchScalarGridSpec(num_scalar_...]
    ppermute x27, waiting for transfers between devices: 62.6 us -> 56.5 us  [swap(): lax.ppermute(x, axis, [(i, j) for i, j in peers if 0 <= j < len(peers)])]
    ppermute x27, starting transfers between devices: 38.4 us -> 41.4 us  [swap(): lax.ppermute(x, axis, [(i, j) for i, j in peers if 0 <= j < len(peers)])]
    unnamed x15 -> x23, local copies, waits for them, and re-layouts: 3.2 us -> 5.47 us
    pallas_call x5 -> x6, Pallas kernels: 6.71 us -> 6.1 us  [combine(): pl.pallas_call(combine_kernel, grid=(rows // rows_step,), in_specs=[row_s...]
  transfers between devices with their start and end apart: 27 -> 27, of which waited for: 10 -> 12; matrix products, arithmetic and copies ran while one was open for 2% -> 2% of each run, Pallas kernels for 27% -> 26%
where the time goes in v6:
time: 172 us
  Pallas kernels  61.5 us (36%)
  waiting for transfers between devices  56.5 us (33%)
  starting transfers between devices  41.4 us (24%)
  local copies, waits for them, and re-layouts  5.94 us (3%)
  matrix products  3.46 us (2%)
    ppermute x27, waiting for transfers between devices, swap(): lax.ppermute(x, axis, [(i, j) for i, j in peers if 0 <= j < len(peers)])  56.5 us
    ppermute x27, starting transfers between devices, swap(): lax.ppermute(x, axis, [(i, j) for i, j in peers if 0 <= j < len(peers)])  41.4 us
    pallas_call x4, Pallas kernels, sweep(): pl.pallas_call(kernel, grid_spec=pltpu.PrefetchScalarGridSpec(num_scalar_...  41.2 us
    pallas_call x6, Pallas kernels, combine(): pl.pallas_call(combine_kernel, grid=(rows // rows_step,), in_specs=[row_s...  6.1 us
    unnamed x23, local copies, waits for them, and re-layouts  5.47 us
    pallas_call x3, Pallas kernels, fold(): pl.pallas_call(kernel, grid=(rows // step,), in_specs=[spec] * 3 + [weigh...  5.11 us
    pallas_call x1, Pallas kernels, initial(): pl.pallas_call(init_kernel, grid=(RB // FIRST,), in_specs=[pl.BlockSpec((...  4.05 us
    pallas_call x1, Pallas kernels, finish(): pl.pallas_call(finish_kernel, grid=(rows // step,), in_specs=[spec_a] * 4...  3.89 us
  transfers between devices with their start and end apart: 27, of which 12 were waited for; matrix products, arithmetic and copies ran while one was open for 2% of the time, Pallas kernels for 26%

profile of v6, /device:TPU:4, one launch (start us, length us, event | category | flops | bytes accessed | tf_op | source)
XLA Modules:
  0.0 171.5 jit_solution(8657914862288991462)
XLA Ops:
  0.7 4.0 %initial.1 = (bf16[64,64,128]{2,1,0:T(8,128)(2,1)}, bf16[64,64,128]{2,1,0:T(8,128)(2,1)}) custom-call(bf16[4096,128]{1,0:T(8,128)(2,1)} %x_ref.3, bf16[2,64,64,128]{3,2,1,0:T(8,128)(2,1)} %refs_2_.7, bf16[256,256]{1,0:T(8,128)(2,1)} %constant.271.clone.map_ref), custom_call_target="tpu_custom_call" | custom-call | tf_op jit(solution)/shard_map/initial/pallas_call | solution.py:79
  4.7 5.0 %collective-permute-start.11 = (bf16[64,64,128]{2,1,0:T(8,128)(2,1)}, bf16[64,64,128]{2,1,0:T(8,128)(2,1)}, u32[]{:S(2)}, u32[]{:S(2)}) collective-permute-start(bf16[64,64,128]{2,1,0:T(8,128)(2,1)} %get-tuple-element.27.refs_5_), channel_id=1, source_target_pairs={{1,2},{2,1},{3,4},{4,3},{5,6},{6,5},{7,8},{8,7},{9,10},{10,9},{11,... | collective-permute-start | bytes 3145736 | tf_op jit(solution)/shard_map/ppermute | solution.py:406
  9.8 4.2 %collective-permute-start.1 = (bf16[64,64,128]{2,1,0:T(8,128)(2,1)}, bf16[64,64,128]{2,1,0:T(8,128)(2,1)}, u32[]{:S(2)}, u32[]{:S(2)}) collective-permute-start(bf16[64,64,128]{2,1,0:T(8,128)(2,1)} %get-tuple-element.18.refs_5_), channel_id=1, source_target_pairs={{1,2},{2,1},{3,4},{4,3},{5,6},{6,5},{7,8},{8,7},{9,10},{10,9},{11,... | collective-permute-start | bytes 3145736 | tf_op jit(solution)/shard_map/ppermute | solution.py:406
  18.0 6.8 %collective-permute-done.11.refs_7_ = bf16[64,64,128]{2,1,0:T(8,128)(2,1)} collective-permute-done((bf16[64,64,128]{2,1,0:T(8,128)(2,1)}, bf16[64,64,128]{2,1,0:T(8,128)(2,1)}, u32[]{:S(2)}, u32[]{:S(2)}) %collective-permute-start.11) | collective-permute-done | bytes 1048608 | tf_op jit(solution)/shard_map/ppermute | solution.py:406
  26.0 10.3 %sweep.3.refs_5_ = bf16[64,64,128]{2,1,0:T(8,128)(2,1)} custom-call(s32[1664]{0:T(1024)S(1)} %concatenate.17.refs_0_, bf16[64,64,1536]{2,1,0:T(8,128)(2,1)} %refs_1_.7, bf16[2,64,64,128]{3,2,1,0:T(8,128)(2,1)} %refs_2_.7, bf16[64,64,128]{2,1,0:T(8,128)(2,1)S(1)} %get-tuple-element.26.refs_3_, f32[8,128]{1,0:T(8,128)S(1)} %maximum_maximum_fusion.refs_4_, ...), custom_call_target="tpu_custom_call" | custom-call | flops 1610612736 | bytes 20971520 | tf_op jit(solution)/shard_map/sweep/pallas_call | solution.py:240
  36.4 5.0 %collective-permute-start.13 = (bf16[64,64,128]{2,1,0:T(8,128)(2,1)}, bf16[64,64,128]{2,1,0:T(8,128)(2,1)}, u32[]{:S(2)}, u32[]{:S(2)}) collective-permute-start(bf16[64,64,128]{2,1,0:T(8,128)(2,1)} %sweep.3.refs_5_), channel_id=1, source_target_pairs={{1,2},{2,1},{3,4},{4,3},{5,6},{6,5},{7,8},{8,7},{9,10},{10,9},{11,... | collective-permute-start | bytes 3145736 | tf_op jit(solution)/shard_map/ppermute | solution.py:406
  41.4 10.3 %sweep.2.refs_5_ = bf16[64,64,128]{2,1,0:T(8,128)(2,1)} custom-call(s32[1664]{0:T(1024)S(1)} %concatenate.17.refs_0_, bf16[64,64,1536]{2,1,0:T(8,128)(2,1)} %refs_1_.7, bf16[2,64,64,128]{3,2,1,0:T(8,128)(2,1)} %refs_2_.7, bf16[64,64,128]{2,1,0:T(8,128)(2,1)S(1)} %get-tuple-element.17.refs_3_, f32[8,128]{1,0:T(8,128)S(1)} %maximum_maximum_fusion.refs_4_, ...), custom_call_target="tpu_custom_call" | custom-call | flops 1610612736 | bytes 20971520 | tf_op jit(solution)/shard_map/sweep/pallas_call | solution.py:240
  51.9 4.2 %collective-permute-start.3 = (bf16[64,64,128]{2,1,0:T(8,128)(2,1)}, bf16[64,64,128]{2,1,0:T(8,128)(2,1)}, u32[]{:S(2)}, u32[]{:S(2)}) collective-permute-start(bf16[64,64,128]{2,1,0:T(8,128)(2,1)} %sweep.2.refs_5_), channel_id=1, source_target_pairs={{1,2},{2,1},{3,4},{4,3},{5,6},{6,5},{7,8},{8,7},{9,10},{10,9},{11,... | collective-permute-start | bytes 3145736 | tf_op jit(solution)/shard_map/ppermute | solution.py:406
  56.4 10.7 %sweep_last.3 = (bf16[32,64,128]{2,1,0:T(8,128)(2,1)}, bf16[32,64,128]{2,1,0:T(8,128)(2,1)}) custom-call(s32[1664]{0:T(1024)S(1)} %concatenate.17.refs_0_, bf16[64,64,1536]{2,1,0:T(8,128)(2,1)} %refs_1_.7, bf16[2,64,64,128]{3,2,1,0:T(8,128)(2,1)} %refs_2_.7, bf16[64,64,128]{2,1,0:T(8,128)(2,1)S(1)} %get-tuple-element.26.refs_3_, ...), custom_call_target="tpu_custom_call" | custom-call | flops 1610612736 | bytes 20971520 | tf_op jit(solution)/shard_map/sweep_last/pallas_call | solution.py:240
  68.6 3.3 %collective-permute-done.3.refs_7_ = bf16[64,64,128]{2,1,0:T(8,128)(2,1)} collective-permute-done((bf16[64,64,128]{2,1,0:T(8,128)(2,1)}, bf16[64,64,128]{2,1,0:T(8,128)(2,1)}, u32[]{:S(2)}, u32[]{:S(2)}) %collective-permute-start.3) | collective-permute-done | bytes 1048608 | tf_op jit(solution)/shard_map/ppermute | solution.py:406
  71.9 9.8 %sweep_last.2 = (bf16[32,64,128]{2,1,0:T(8,128)(2,1)S(1)}, bf16[32,64,128]{2,1,0:T(8,128)(2,1)S(1)}) custom-call(s32[1664]{0:T(1024)S(1)} %concatenate.17.refs_0_, bf16[64,64,1536]{2,1,0:T(8,128)(2,1)} %refs_1_.7, bf16[2,64,64,128]{3,2,1,0:T(8,128)(2,1)} %refs_2_.7, bf16[64,64,128]{2,1,0:T(8,128)(2,1)S(1)} %get-tuple-element.17.refs_3_, ...), custom_call_target="tpu_custom_call" | custom-call | flops 1610612736 | bytes 20971520 | tf_op jit(solution)/shard_map/sweep_last/pallas_call | solution.py:240
  85.3 5.4 %collective-permute-done.20 = bf16[128,128]{1,0:T(8,128)(2,1)S(1)} collective-permute-done((bf16[128,128]{1,0:T(8,128)(2,1)S(1)}, bf16[128,128]{1,0:T(8,128)(2,1)S(1)}, u32[]{:S(2)}, u32[]{:S(2)}) %collective-permute-start.20) | collective-permute-done | bytes 32800 | tf_op jit(solution)/shard_map/ppermute | solution.py:406
  90.8 4.1 %collective-permute-start.16 = (bf16[2048,128]{1,0:T(8,128)(2,1)}, bf16[2048,128]{1,0:T(8,128)(2,1)}, u32[]{:S(2)}, u32[]{:S(2)}) collective-permute-start(bf16[2048,128]{1,0:T(8,128)(2,1)} %bitcast.3.own_ref.refs_4_), channel_id=1, source_target_pairs={{0,96},{16,112},{32,64},{48,80},{64,32},{80,48},{96,0},{112,16},{1... | collective-permute-start | bytes 1572872 | tf_op jit(solution)/shard_map/ppermute | solution.py:406
  96.5 4.1 %collective-permute-start.7 = (bf16[2048,128]{1,0:T(8,128)(2,1)S(1)}, bf16[2048,128]{1,0:T(8,128)(2,1)S(1)}, u32[]{:S(2)}, u32[]{:S(2)}) collective-permute-start(bf16[2048,128]{1,0:T(8,128)(2,1)S(1)} %bitcast.24), channel_id=1, source_target_pairs={{0,96},{16,112},{32,64},{48,80},{64,32},{80,48},{96,0},{112,16},{1... | collective-permute-start | bytes 1572872 | tf_op jit(solution)/shard_map/ppermute | solution.py:406
  100.6 2.1 %collective-permute-start.23 = (bf16[128,128]{1,0:T(8,128)(2,1)S(1)}, bf16[128,128]{1,0:T(8,128)(2,1)S(1)}, u32[]{:S(2)}, u32[]{:S(2)}) collective-permute-start(bf16[128,128]{1,0:T(8,128)(2,1)S(1)} %add_convert_fusion.own_ref), channel_id=1, source_target_pairs={{0,32},{16,48},{32,0},{48,16},{64,96},{80,112},{96,64},{112,80},{1... | collective-permute-start | bytes 98312 | tf_op jit(solution)/shard_map/ppermute | solution.py:406
  102.8 16.9 %collective-permute-done.23.peer_ref = bf16[128,128]{1,0:T(8,128)(2,1)S(1)} collective-permute-done((bf16[128,128]{1,0:T(8,128)(2,1)S(1)}, bf16[128,128]{1,0:T(8,128)(2,1)S(1)}, u32[]{:S(2)}, u32[]{:S(2)}) %collective-permute-start.23) | collective-permute-done | bytes 32800 | tf_op jit(solution)/shard_map/ppermute | solution.py:406
  124.7 2.9 %collective-permute-start.15 = (bf16[2048,128]{1,0:T(8,128)(2,1)S(1)}, bf16[2048,128]{1,0:T(8,128)(2,1)S(1)}, u32[]{:S(2)}, u32[]{:S(2)}) collective-permute-start(bf16[2048,128]{1,0:T(8,128)(2,1)S(1)} %combine.8), channel_id=1, source_target_pairs={{0,96},{16,112},{32,64},{48,80},{64,32},{80,48},{96,0},{112,16},{1... | collective-permute-start | bytes 1572872 | tf_op jit(solution)/shard_map/ppermute | solution.py:406
  127.7 2.2 %collective-permute-start.25 = (bf16[128,128]{0,1:T(8,128)(2,1)S(1)}, bf16[128,128]{0,1:T(8,128)(2,1)S(1)}, u32[]{:S(2)}, u32[]{:S(2)}) collective-permute-start(bf16[128,128]{0,1:T(8,128)(2,1)S(1)} %fusion.11), channel_id=1, source_target_pairs={{0,16},{16,0},{32,48},{48,32},{64,80},{80,64},{96,112},{112,96},{1... | collective-permute-start | bytes 98312 | tf_op jit(solution)/shard_map/ppermute | solution.py:406
  134.4 3.3 %collective-permute-done.15.refs_2_ = bf16[2048,128]{1,0:T(8,128)(2,1)S(1)} collective-permute-done((bf16[2048,128]{1,0:T(8,128)(2,1)S(1)}, bf16[2048,128]{1,0:T(8,128)(2,1)S(1)}, u32[]{:S(2)}, u32[]{:S(2)}) %collective-permute-start.15) | collective-permute-done | bytes 524320 | tf_op jit(solution)/shard_map/ppermute | solution.py:406
  137.7 3.5 %fold.5 = (bf16[2048,128]{1,0:T(8,128)(2,1)}, f32[2048,128]{1,0:T(8,128)S(1)}) custom-call(bf16[2048,128]{1,0:T(8,128)(2,1)} %bitcast.2.own_ref.refs_0_, bf16[2048,128]{1,0:T(8,128)(2,1)} %collective-permute-done.14.peer_ref.refs_1_, bf16[2048,128]{1,0:T(8,128)(2,1)S(1)} %collective-permute-done.15.refs_2_, ...), custom_call_target="tpu_custom_call" | custom-call | flops 536870912 | bytes 4718592 | tf_op jit(solution)/shard_map/fold/pallas_call | solution.py:328
  143.3 2.3 %collective-permute-done.8.refs_2_.refs_6_ = bf16[2048,128]{1,0:T(8,128)(2,1)S(1)} collective-permute-done((bf16[2048,128]{1,0:T(8,128)(2,1)S(1)}, bf16[2048,128]{1,0:T(8,128)(2,1)S(1)}, u32[]{:S(2)}, u32[]{:S(2)}) %collective-permute-start.8) | collective-permute-done | bytes 524320 | tf_op jit(solution)/shard_map/ppermute | solution.py:406
  147.9 8.9 %collective-permute-done.5.refs_2_.refs_6_ = bf16[2048,128]{1,0:T(8,128)(2,1)S(1)} collective-permute-done((bf16[2048,128]{1,0:T(8,128)(2,1)S(1)}, bf16[2048,128]{1,0:T(8,128)(2,1)S(1)}, u32[]{:S(2)}, u32[]{:S(2)}) %collective-permute-start.5) | collective-permute-done | bytes 524320 | tf_op jit(solution)/shard_map/ppermute | solution.py:406
  159.1 6.3 %collective-permute-done.6.got1_ref = bf16[1024,128]{1,0:T(8,128)(2,1)S(1)} collective-permute-done((bf16[1024,128]{1,0:T(8,128)(2,1)S(1)}, bf16[1024,128]{1,0:T(8,128)(2,1)S(1)}, u32[]{:S(2)}, u32[]{:S(2)}) %collective-permute-start.6) | collective-permute-done | bytes 262176 | tf_op jit(solution)/shard_map/ppermute | solution.py:406
  167.6 3.9 %finish.1 = f32[1,2,2048,128]{3,2,1,0:T(8,128)} custom-call(f32[1024,128]{1,0:T(8,128)S(1)} %get-tuple-element.21.own1_ref, bf16[1024,128]{1,0:T(8,128)(2,1)S(1)} %collective-permute-done.6.got1_ref, f32[1024,128]{1,0:T(8,128)S(1)} %copy-done.7, bf16[1024,128]{1,0:T(8,128)(2,1)S(1)} %collective-permute-done.9.got2_ref, f32[2048,128]{1,0:T(8,128)S(1)} %copy-done.5, ...), custom_call_target="tpu_custom_call" | custom-call | tf_op jit(solution)/shard_map/finish/pallas_call | solution.py:370
  (111 shorter events, 30.6 us)
Async XLA Ops:
  4.7 13.3 %collective-permute-start.10 = (bf16[64,64,128]{2,1,0:T(8,128)(2,1)}, bf16[64,64,128]{2,1,0:T(8,128)(2,1)}, u32[]{:S(2)}, u32[]{:S(2)}) collective-permute-start(bf16[64,64,128]{2,1,0:T(8,128)(2,1)} %get-tuple-element.27.refs_5_), channel_id=1, source_target_pairs={{0,1},{1,0},{2,3},{3,2},{4,5},{5,4},{6,7},{7,6},{8,9},{9,8},{10,11... | collective-permute-start | bytes 3145736 | tf_op jit(solution)/shard_map/ppermute | solution.py:406
  4.7 20.0 %collective-permute-start.11 = (bf16[64,64,128]{2,1,0:T(8,128)(2,1)}, bf16[64,64,128]{2,1,0:T(8,128)(2,1)}, u32[]{:S(2)}, u32[]{:S(2)}) collective-permute-start(bf16[64,64,128]{2,1,0:T(8,128)(2,1)} %get-tuple-element.27.refs_5_), channel_id=1, source_target_pairs={{1,2},{2,1},{3,4},{4,3},{5,6},{6,5},{7,8},{8,7},{9,10},{10,9},{11,... | collective-permute-start | bytes 3145736 | tf_op jit(solution)/shard_map/ppermute | solution.py:406
  9.7 31.7 %collective-permute-start = (bf16[64,64,128]{2,1,0:T(8,128)(2,1)}, bf16[64,64,128]{2,1,0:T(8,128)(2,1)}, u32[]{:S(2)}, u32[]{:S(2)}) collective-permute-start(bf16[64,64,128]{2,1,0:T(8,128)(2,1)} %get-tuple-element.18.refs_5_), channel_id=1, source_target_pairs={{0,1},{1,0},{2,3},{3,2},{4,5},{5,4},{6,7},{7,6},{8,9},{9,8},{10,11... | collective-permute-start | bytes 3145736 | tf_op jit(solution)/shard_map/ppermute | solution.py:406
  9.8 31.6 %collective-permute-start.1 = (bf16[64,64,128]{2,1,0:T(8,128)(2,1)}, bf16[64,64,128]{2,1,0:T(8,128)(2,1)}, u32[]{:S(2)}, u32[]{:S(2)}) collective-permute-start(bf16[64,64,128]{2,1,0:T(8,128)(2,1)} %get-tuple-element.18.refs_5_), channel_id=1, source_target_pairs={{1,2},{2,1},{3,4},{4,3},{5,6},{6,5},{7,8},{8,7},{9,10},{10,9},{11,... | collective-permute-start | bytes 3145736 | tf_op jit(solution)/shard_map/ppermute | solution.py:406
  36.3 19.8 %collective-permute-start.12 = (bf16[64,64,128]{2,1,0:T(8,128)(2,1)}, bf16[64,64,128]{2,1,0:T(8,128)(2,1)}, u32[]{:S(2)}, u32[]{:S(2)}) collective-permute-start(bf16[64,64,128]{2,1,0:T(8,128)(2,1)} %sweep.3.refs_5_), channel_id=1, source_target_pairs={{0,1},{1,0},{2,3},{3,2},{4,5},{5,4},{6,7},{7,6},{8,9},{9,8},{10,11... | collective-permute-start | bytes 3145736 | tf_op jit(solution)/shard_map/ppermute | solution.py:406
  36.4 20.0 %collective-permute-start.13 = (bf16[64,64,128]{2,1,0:T(8,128)(2,1)}, bf16[64,64,128]{2,1,0:T(8,128)(2,1)}, u32[]{:S(2)}, u32[]{:S(2)}) collective-permute-start(bf16[64,64,128]{2,1,0:T(8,128)(2,1)} %sweep.3.refs_5_), channel_id=1, source_target_pairs={{1,2},{2,1},{3,4},{4,3},{5,6},{6,5},{7,8},{8,7},{9,10},{10,9},{11,... | collective-permute-start | bytes 3145736 | tf_op jit(solution)/shard_map/ppermute | solution.py:406
  51.8 16.8 %collective-permute-start.2 = (bf16[64,64,128]{2,1,0:T(8,128)(2,1)}, bf16[64,64,128]{2,1,0:T(8,128)(2,1)}, u32[]{:S(2)}, u32[]{:S(2)}) collective-permute-start(bf16[64,64,128]{2,1,0:T(8,128)(2,1)} %sweep.2.refs_5_), channel_id=1, source_target_pairs={{0,1},{1,0},{2,3},{3,2},{4,5},{5,4},{6,7},{7,6},{8,9},{9,8},{10,11... | collective-permute-start | bytes 3145736 | tf_op jit(solution)/shard_map/ppermute | solution.py:406
  51.9 20.0 %collective-permute-start.3 = (bf16[64,64,128]{2,1,0:T(8,128)(2,1)}, bf16[64,64,128]{2,1,0:T(8,128)(2,1)}, u32[]{:S(2)}, u32[]{:S(2)}) collective-permute-start(bf16[64,64,128]{2,1,0:T(8,128)(2,1)} %sweep.2.refs_5_), channel_id=1, source_target_pairs={{1,2},{2,1},{3,4},{4,3},{5,6},{6,5},{7,8},{8,7},{9,10},{10,9},{11,... | collective-permute-start | bytes 3145736 | tf_op jit(solution)/shard_map/ppermute | solution.py:406
  85.2 5.5 %collective-permute-start.20 = (bf16[128,128]{1,0:T(8,128)(2,1)S(1)}, bf16[128,128]{1,0:T(8,128)(2,1)S(1)}, u32[]{:S(2)}, u32[]{:S(2)}) collective-permute-start(bf16[128,128]{1,0:T(8,128)(2,1)S(1)} %get-tuple-element.36), channel_id=1, source_target_pairs={{0,8},{1,9},{2,10},{3,11},{4,12},{5,13},{6,14},{7,15},{8,0},{9,1},... | collective-permute-start | bytes 98312 | tf_op jit(solution)/shard_map/ppermute | solution.py:406
  90.8 29.9 %collective-permute-start.16 = (bf16[2048,128]{1,0:T(8,128)(2,1)}, bf16[2048,128]{1,0:T(8,128)(2,1)}, u32[]{:S(2)}, u32[]{:S(2)}) collective-permute-start(bf16[2048,128]{1,0:T(8,128)(2,1)} %bitcast.3.own_ref.refs_4_), channel_id=1, source_target_pairs={{0,96},{16,112},{32,64},{48,80},{64,32},{80,48},{96,0},{112,16},{1... | collective-permute-start | bytes 1572872 | tf_op jit(solution)/shard_map/ppermute | solution.py:406
  94.9 27.8 %collective-permute-start.14 = (bf16[2048,128]{1,0:T(8,128)(2,1)}, bf16[2048,128]{1,0:T(8,128)(2,1)}, u32[]{:S(2)}, u32[]{:S(2)}) collective-permute-start(bf16[2048,128]{1,0:T(8,128)(2,1)} %bitcast.2.own_ref.refs_0_), channel_id=1, source_target_pairs={{0,32},{16,48},{32,0},{48,16},{64,96},{80,112},{96,64},{112,80},{1... | collective-permute-start | bytes 1572872 | tf_op jit(solution)/shard_map/ppermute | solution.py:406
  96.5 33.3 %collective-permute-start.7 = (bf16[2048,128]{1,0:T(8,128)(2,1)S(1)}, bf16[2048,128]{1,0:T(8,128)(2,1)S(1)}, u32[]{:S(2)}, u32[]{:S(2)}) collective-permute-start(bf16[2048,128]{1,0:T(8,128)(2,1)S(1)} %bitcast.24), channel_id=1, source_target_pairs={{0,96},{16,112},{32,64},{48,80},{64,32},{80,48},{96,0},{112,16},{1... | collective-permute-start | bytes 1572872 | tf_op jit(solution)/shard_map/ppermute | solution.py:406
  100.6 30.3 %collective-permute-start.4 = (bf16[2048,128]{1,0:T(8,128)(2,1)S(1)}, bf16[2048,128]{1,0:T(8,128)(2,1)S(1)}, u32[]{:S(2)}, u32[]{:S(2)}) collective-permute-start(bf16[2048,128]{1,0:T(8,128)(2,1)S(1)} %bitcast.19), channel_id=1, source_target_pairs={{0,32},{16,48},{32,0},{48,16},{64,96},{80,112},{96,64},{112,80},{1... | collective-permute-start | bytes 1572872 | tf_op jit(solution)/shard_map/ppermute | solution.py:406
  100.6 19.0 %collective-permute-start.23 = (bf16[128,128]{1,0:T(8,128)(2,1)S(1)}, bf16[128,128]{1,0:T(8,128)(2,1)S(1)}, u32[]{:S(2)}, u32[]{:S(2)}) collective-permute-start(bf16[128,128]{1,0:T(8,128)(2,1)S(1)} %add_convert_fusion.own_ref), channel_id=1, source_target_pairs={{0,32},{16,48},{32,0},{48,16},{64,96},{80,112},{96,64},{112,80},{1... | collective-permute-start | bytes 98312 | tf_op jit(solution)/shard_map/ppermute | solution.py:406
  119.9 7.7 %collective-permute-start.24 = (bf16[128,128]{0,1:T(8,128)(2,1)S(1)}, bf16[128,128]{0,1:T(8,128)(2,1)S(1)}, u32[]{:S(2)}, u32[]{:S(2)}) collective-permute-start(bf16[128,128]{0,1:T(8,128)(2,1)S(1)} %copy.21), channel_id=1, source_target_pairs={{0,96},{16,112},{32,64},{48,80},{64,32},{80,48},{96,0},{112,16},{1... | collective-permute-start | bytes 98312 | tf_op jit(solution)/shard_map/ppermute | solution.py:406
  122.6 11.8 %collective-permute-start.17 = (bf16[2048,128]{1,0:T(8,128)(2,1)S(1)}, bf16[2048,128]{1,0:T(8,128)(2,1)S(1)}, u32[]{:S(2)}, u32[]{:S(2)}) collective-permute-start(bf16[2048,128]{1,0:T(8,128)(2,1)S(1)} %combine.9), channel_id=1, source_target_pairs={{0,32},{16,48},{32,0},{48,16},{64,96},{80,112},{96,64},{112,80},{1... | collective-permute-start | bytes 1572872 | tf_op jit(solution)/shard_map/ppermute | solution.py:406
  124.7 13.0 %collective-permute-start.15 = (bf16[2048,128]{1,0:T(8,128)(2,1)S(1)}, bf16[2048,128]{1,0:T(8,128)(2,1)S(1)}, u32[]{:S(2)}, u32[]{:S(2)}) collective-permute-start(bf16[2048,128]{1,0:T(8,128)(2,1)S(1)} %combine.8), channel_id=1, source_target_pairs={{0,96},{16,112},{32,64},{48,80},{64,32},{80,48},{96,0},{112,16},{1... | collective-permute-start | bytes 1572872 | tf_op jit(solution)/shard_map/ppermute | solution.py:406
  127.7 6.2 %collective-permute-start.25 = (bf16[128,128]{0,1:T(8,128)(2,1)S(1)}, bf16[128,128]{0,1:T(8,128)(2,1)S(1)}, u32[]{:S(2)}, u32[]{:S(2)}) collective-permute-start(bf16[128,128]{0,1:T(8,128)(2,1)S(1)} %fusion.11), channel_id=1, source_target_pairs={{0,16},{16,0},{32,48},{48,32},{64,80},{80,64},{96,112},{112,96},{1... | collective-permute-start | bytes 98312 | tf_op jit(solution)/shard_map/ppermute | solution.py:406
  130.8 14.9 %collective-permute-start.8 = (bf16[2048,128]{1,0:T(8,128)(2,1)S(1)}, bf16[2048,128]{1,0:T(8,128)(2,1)S(1)}, u32[]{:S(2)}, u32[]{:S(2)}) collective-permute-start(bf16[2048,128]{1,0:T(8,128)(2,1)S(1)} %combine.7), channel_id=1, source_target_pairs={{0,16},{16,0},{32,48},{48,32},{64,80},{80,64},{96,112},{112,96},{1... | collective-permute-start | bytes 1572872 | tf_op jit(solution)/shard_map/ppermute | solution.py:406
  131.8 25.1 %collective-permute-start.5 = (bf16[2048,128]{1,0:T(8,128)(2,1)S(1)}, bf16[2048,128]{1,0:T(8,128)(2,1)S(1)}, u32[]{:S(2)}, u32[]{:S(2)}) collective-permute-start(bf16[2048,128]{1,0:T(8,128)(2,1)S(1)} %combine.6), channel_id=1, source_target_pairs={{0,16},{16,0},{32,48},{48,32},{64,80},{80,64},{96,112},{112,96},{1... | collective-permute-start | bytes 1572872 | tf_op jit(solution)/shard_map/ppermute | solution.py:406
  133.9 24.3 %collective-permute-start.26 = (f32[128,128]{0,1:T(8,128)S(1)}, f32[128,128]{0,1:T(8,128)S(1)}, u32[]{:S(2)}, u32[]{:S(2)}) collective-permute-start(f32[128,128]{0,1:T(8,128)S(1)} %convert_add_fusion), channel_id=1, source_target_pairs={{0,1},{1,0},{2,3},{3,2},{4,5},{5,4},{6,7},{7,6},{8,9},{9,8},{10,11... | collective-permute-start | bytes 196616 | tf_op jit(solution)/shard_map/ppermute | solution.py:406
  141.2 24.1 %collective-permute-start.18 = (bf16[2048,128]{1,0:T(8,128)(2,1)}, bf16[2048,128]{1,0:T(8,128)(2,1)}, u32[]{:S(2)}, u32[]{:S(2)}) collective-permute-start(bf16[2048,128]{1,0:T(8,128)(2,1)} %get-tuple-element.31), channel_id=1, source_target_pairs={{0,16},{16,0},{32,48},{48,32},{64,80},{80,64},{96,112},{112,96},{1... | collective-permute-start | bytes 1572872 | tf_op jit(solution)/shard_map/ppermute | solution.py:406
  146.5 12.6 %collective-permute-start.9 = (bf16[1024,128]{1,0:T(8,128)(2,1)S(1)}, bf16[1024,128]{1,0:T(8,128)(2,1)S(1)}, u32[]{:S(2)}, u32[]{:S(2)}) collective-permute-start(bf16[1024,128]{1,0:T(8,128)(2,1)S(1)} %get-tuple-element.25), channel_id=1, source_target_pairs={{0,32},{16,48},{32,0},{48,16},{64,96},{80,112},{96,64},{112,80},{1... | collective-permute-start | bytes 786440 | tf_op jit(solution)/shard_map/ppermute | solution.py:406
  157.7 7.7 %collective-permute-start.6 = (bf16[1024,128]{1,0:T(8,128)(2,1)S(1)}, bf16[1024,128]{1,0:T(8,128)(2,1)S(1)}, u32[]{:S(2)}, u32[]{:S(2)}) collective-permute-start(bf16[1024,128]{1,0:T(8,128)(2,1)S(1)} %get-tuple-element.22), channel_id=1, source_target_pairs={{0,96},{16,112},{32,64},{48,80},{64,32},{80,48},{96,0},{112,16},{1... | collective-permute-start | bytes 786440 | tf_op jit(solution)/shard_map/ppermute | solution.py:406
  (14 other events, 100.7 us)

commit v7 on v6

--- a/solution.py
+++ b/solution.py
@@ -30,6 +30,10 @@
             src = (point % points) * LANES + part * GROUP + unit * HALF + col
             table[src, unit * LANES + lane] = 1.0
     return table
+
+
+def in_hbm(x):
+    return pltpu.with_memory_space_constraint(x, pltpu.MemorySpace.HBM)
 
 
 def lane_ids(shape):
@@ -113,17 +117,17 @@
 
 def spread(rhs, coefs):
     block = jax.ShapeDtypeStruct((RB, BS, LANES), BF16)
-    out_spec = pl.BlockSpec((RB // 4, BS, LANES), lambda i: (i, 0, 0))
+    out_spec = pl.BlockSpec((RB // 8, BS, LANES), lambda i: (i, 0, 0))
     return pl.pallas_call(
         spread_kernel,
-        grid=(4,),
+        grid=(8,),
         in_specs=[
-            pl.BlockSpec((RB // 4 * BS, LANES), lambda i: (i, 0)),
+            pl.BlockSpec((RB // 8 * BS, LANES), lambda i: (i, 0)),
             pl.BlockSpec((LANES, 2 * LANES), lambda i: (0, 0)),
-            pl.BlockSpec((1, 32, 2 * LANES), lambda i: (i, 0, 0)),
+            pl.BlockSpec((1, 32, 2 * LANES), lambda i: (jnp.minimum(i, 4), 0, 0)),
         ],
-        out_specs=[out_spec, out_spec, pl.BlockSpec((1, 512, 256), lambda i: (i, 0, 0))],
-        out_shape=[block, block, jax.ShapeDtypeStruct((4, 512, 256), BF16)],
+        out_specs=[out_spec, out_spec, pl.BlockSpec((1, 512, 256), lambda i: (jnp.minimum(i, 4), 0, 0))],
+        out_shape=[block, block, jax.ShapeDtypeStruct((5, 512, 256), BF16)],
         compiler_params=pltpu.CompilerParams(vmem_limit_bytes=14 << 20),
         cost_estimate=pl.CostEstimate(
             flops=2 * RB * BS * LANES * 256, bytes_accessed=3 << 20, transcendentals=0
@@ -215,7 +219,7 @@
 def sweep(index, ham, precond, rhs_unit, z, local, near, far, last):
     block = pl.BlockSpec((STEP, BS, LANES), lambda i, n: (i, 0, 0))
     anywhere = pl.BlockSpec(memory_space=pl.ANY)
-    in_hbm = pl.BlockSpec(memory_space=pltpu.MemorySpace.HBM)
+    raw = pl.BlockSpec(memory_space=pltpu.MemorySpace.HBM)
     scratch = [
         pltpu.VMEM((3 * RB + 1, BS, LANES), BF16),
         pltpu.SemaphoreType.DMA((7,)),
@@ -243,8 +247,8 @@
             num_scalar_prefetch=1,
             grid=(RB // STEP,),
             in_specs=[
-                in_hbm,
-                in_hbm,
+                raw,
+                raw,
                 block,
                 pl.BlockSpec((8, LANES), lambda i, n: (0, 0)),
                 anywhere,
@@ -258,9 +262,9 @@
         cost_estimate=pl.CostEstimate(
             flops=2 * RB * BS * SLOTS * BS * LANES, bytes_accessed=20 << 20, transcendentals=0
         ),
-        compiler_params=pltpu.CompilerParams(vmem_limit_bytes=48 << 20),
+        compiler_params=pltpu.CompilerParams(vmem_limit_bytes=24 << 20),
         name="sweep_last" if last else "sweep",
-    )(index, ham, precond, rhs_unit, z, local, near, far)
+    )(index, in_hbm(ham), in_hbm(precond), in_hbm(rhs_unit), z, in_hbm(local), near, far)
 
 
 def weighted(own_ref, peer_ref, weight_ref):
@@ -438,6 +442,7 @@
             (0, (mine, mirror), (other, pair ^ 1, mine, pair)),
             (1, (mine, pair), (mirror, mirror ^ 1, mine, other)),
             (1, (mine, mirror), (pair, pair ^ 1, mine, other)),
+            (1, (mine, other), (pair, by_mirror(pair), mine, mirror)),
         ),
     )
     *rhs_units, weights = spread(rhs, coefs)
@@ -498,11 +503,11 @@
         peer = swap(gram.astype(BF16), "row", lambda i, bit=bit: i ^ bit)
         gram = gram + peer.astype(F32)
     gram = gram.astype(BF16)
-    peer = swap(gram, "quad", by_pair)
-    send_g = combine(gram, peer, weights, 2, 0, LANES)
-    keep_g = combine(gram, peer, weights, 2, 1, LANES, F32)
-    gram_sum = keep_g + swap(send_g, "quad", by_mirror).astype(F32)
-    gram_got = swap(gram_sum.astype(BF16), "quad", by_x)
+    peer = swap(gram, "quad", by_x)
+    send_g = combine(gram, peer, weights, 4, 0, LANES)
+    keep_g = combine(gram, peer, weights, 4, 1, LANES, F32)
+    gram_sum = keep_g + swap(send_g, "quad", by_pair).astype(F32)
+    gram_got = swap(gram_sum.astype(BF16), "quad", by_mirror)
     gram_own = gram_sum + jnp.roll(gram_got, HALF, axis=1).astype(F32)
     gram_other = swap(gram_own, "row", near_row)
     gram_a = jnp.where(even, gram_own, gram_other)

time: 172 us -> 170 us (0.988); the launches traced: 172 us -> 167 us
  waiting for transfers between devices: 56.5 us -> 39.7 us
  local copies, waits for them, and re-layouts: 5.94 us -> 10.5 us
  Pallas kernels: 61.5 us -> 65.7 us
  starting transfers between devices: 41.4 us -> 43.5 us
  other arithmetic: 1.36 us -> 3.1 us
    ppermute x27, waiting for transfers between devices: 56.5 us -> 39.7 us  [swap(): lax.ppermute(x, axis, [(i, j) for i, j in peers if 0 <= j < len(peers)])]
    unnamed x23 -> x37, local copies, waits for them, and re-layouts: 5.47 us -> 8.81 us
    pallas_call x4, Pallas kernels: 41.2 us -> 44 us  [sweep(): pl.pallas_call(kernel, grid_spec=pltpu.PrefetchScalarGridSpec(num_scalar_...]
    ppermute x27, starting transfers between devices: 41.4 us -> 43.5 us  [swap(): lax.ppermute(x, axis, [(i, j) for i, j in peers if 0 <= j < len(peers)])]
  transfers between devices with their start and end apart: 27 -> 27, of which waited for: 12 -> 12; matrix products, arithmetic and copies ran while one was open for 2% -> 4% of each run, Pallas kernels for 26% -> 28%
where the time goes in v7:
time: 170 us; the launch traced here: 167 us
  Pallas kernels  65.7 us (39%)
  starting transfers between devices  43.5 us (26%)
  waiting for transfers between devices  39.7 us (23%)
  local copies, waits for them, and re-layouts  10.5 us (6%)
  matrix products  3.49 us (2%)
  other arithmetic  3.1 us (2%)
    pallas_call x4, Pallas kernels, sweep(): pl.pallas_call(kernel, grid_spec=pltpu.PrefetchScalarGridSpec(num_scalar_...  44 us
    ppermute x27, starting transfers between devices, swap(): lax.ppermute(x, axis, [(i, j) for i, j in peers if 0 <= j < len(peers)])  43.5 us
    ppermute x27, waiting for transfers between devices, swap(): lax.ppermute(x, axis, [(i, j) for i, j in peers if 0 <= j < len(peers)])  39.7 us
    unnamed x37, local copies, waits for them, and re-layouts  8.81 us
    pallas_call x6, Pallas kernels, combine(): pl.pallas_call(combine_kernel, grid=(rows // rows_step,), in_specs=[row_s...  6.07 us
    pallas_call x3, Pallas kernels, fold(): pl.pallas_call(kernel, grid=(rows // step,), in_specs=[spec] * 3 + [weigh...  5.83 us
    pallas_call x1, Pallas kernels, initial(): pl.pallas_call(init_kernel, grid=(RB // FIRST,), in_specs=[pl.BlockSpec((...  4.12 us
    pallas_call x1, Pallas kernels, finish(): pl.pallas_call(finish_kernel, grid=(rows // step,), in_specs=[spec_a] * 4...  3.89 us
  transfers between devices with their start and end apart: 27, of which 12 were waited for; matrix products, arithmetic and copies ran while one was open for 4% of the time, Pallas kernels for 28%

profile of v7, /device:TPU:4, one launch (start us, length us, event | category | flops | bytes accessed | tf_op | source)
XLA Modules:
  0.0 167.3 jit_solution(11016535725617864521)
XLA Ops:
  0.7 4.1 %initial.1 = (bf16[64,64,128]{2,1,0:T(8,128)(2,1)}, bf16[64,64,128]{2,1,0:T(8,128)(2,1)}) custom-call(bf16[4096,128]{1,0:T(8,128)(2,1)} %x_ref.3, bf16[2,64,64,128]{3,2,1,0:T(8,128)(2,1)} %refs_2_.7, bf16[256,256]{1,0:T(8,128)(2,1)} %constant.303.clone.map_ref), custom_call_target="tpu_custom_call" | custom-call | tf_op jit(solution)/shard_map/initial/pallas_call | solution.py:83
  4.8 5.0 %collective-permute-start.11 = (bf16[64,64,128]{2,1,0:T(8,128)(2,1)}, bf16[64,64,128]{2,1,0:T(8,128)(2,1)}, u32[]{:S(2)}, u32[]{:S(2)}) collective-permute-start(bf16[64,64,128]{2,1,0:T(8,128)(2,1)} %get-tuple-element.27.refs_5_), channel_id=1, source_target_pairs={{1,2},{2,1},{3,4},{4,3},{5,6},{6,5},{7,8},{8,7},{9,10},{10,9},{11,... | collective-permute-start | bytes 3145736 | tf_op jit(solution)/shard_map/ppermute | solution.py:410
  9.9 4.2 %collective-permute-start.1 = (bf16[64,64,128]{2,1,0:T(8,128)(2,1)}, bf16[64,64,128]{2,1,0:T(8,128)(2,1)}, u32[]{:S(2)}, u32[]{:S(2)}) collective-permute-start(bf16[64,64,128]{2,1,0:T(8,128)(2,1)} %get-tuple-element.18.refs_5_), channel_id=1, source_target_pairs={{1,2},{2,1},{3,4},{4,3},{5,6},{6,5},{7,8},{8,7},{9,10},{10,9},{11,... | collective-permute-start | bytes 3145736 | tf_op jit(solution)/shard_map/ppermute | solution.py:410
  21.3 3.6 %collective-permute-done.11.refs_7_ = bf16[64,64,128]{2,1,0:T(8,128)(2,1)} collective-permute-done((bf16[64,64,128]{2,1,0:T(8,128)(2,1)}, bf16[64,64,128]{2,1,0:T(8,128)(2,1)}, u32[]{:S(2)}, u32[]{:S(2)}) %collective-permute-start.11) | collective-permute-done | bytes 1048608 | tf_op jit(solution)/shard_map/ppermute | solution.py:410
  24.8 10.8 %sweep.3.refs_5_ = bf16[64,64,128]{2,1,0:T(8,128)(2,1)S(1)} custom-call(s32[1664]{0:T(1024)S(1)} %concatenate.17.refs_0_, bf16[64,64,1536]{2,1,0:T(8,128)(2,1)} %refs_1_.7, bf16[2,64,64,128]{3,2,1,0:T(8,128)(2,1)} %refs_2_.7, bf16[64,64,128]{2,1,0:T(8,128)(2,1)} %copy-done.1, f32[8,128]{1,0:T(8,128)S(1)} %maximum_maximum_fusion.refs_4_, ...), custom_call_target="tpu_custom_call" | custom-call | flops 1610612736 | bytes 20971520 | tf_op jit(solution)/shard_map/sweep/pallas_call | solution.py:244
  35.8 5.0 %collective-permute-start.13 = (bf16[64,64,128]{2,1,0:T(8,128)(2,1)S(1)}, bf16[64,64,128]{2,1,0:T(8,128)(2,1)}, u32[]{:S(2)}, u32[]{:S(2)}) collective-permute-start(bf16[64,64,128]{2,1,0:T(8,128)(2,1)S(1)} %sweep.3.refs_5_), channel_id=1, source_target_pairs={{1,2},{2,1},{3,4},{4,3},{5,6},{6,5},{7,8},{8,7},{9,10},{10,9},{11,... | collective-permute-start | bytes 3145736 | tf_op jit(solution)/shard_map/ppermute | solution.py:410
  43.0 10.6 %sweep.2.refs_5_ = bf16[64,64,128]{2,1,0:T(8,128)(2,1)S(1)} custom-call(s32[1664]{0:T(1024)S(1)} %concatenate.17.refs_0_, bf16[64,64,1536]{2,1,0:T(8,128)(2,1)} %refs_1_.7, bf16[2,64,64,128]{3,2,1,0:T(8,128)(2,1)} %refs_2_.7, bf16[64,64,128]{2,1,0:T(8,128)(2,1)} %copy-done, f32[8,128]{1,0:T(8,128)S(1)} %maximum_maximum_fusion.refs_4_, ...), custom_call_target="tpu_custom_call" | custom-call | flops 1610612736 | bytes 20971520 | tf_op jit(solution)/shard_map/sweep/pallas_call | solution.py:244
  53.6 4.2 %collective-permute-start.3 = (bf16[64,64,128]{2,1,0:T(8,128)(2,1)S(1)}, bf16[64,64,128]{2,1,0:T(8,128)(2,1)}, u32[]{:S(2)}, u32[]{:S(2)}) collective-permute-start(bf16[64,64,128]{2,1,0:T(8,128)(2,1)S(1)} %sweep.2.refs_5_), channel_id=1, source_target_pairs={{1,2},{2,1},{3,4},{4,3},{5,6},{6,5},{7,8},{8,7},{9,10},{10,9},{11,... | collective-permute-start | bytes 3145736 | tf_op jit(solution)/shard_map/ppermute | solution.py:410
  57.9 11.7 %sweep_last.3 = (bf16[32,64,128]{2,1,0:T(8,128)(2,1)}, bf16[32,64,128]{2,1,0:T(8,128)(2,1)}) custom-call(s32[1664]{0:T(1024)S(1)} %concatenate.17.refs_0_, bf16[64,64,1536]{2,1,0:T(8,128)(2,1)} %refs_1_.7, bf16[2,64,64,128]{3,2,1,0:T(8,128)(2,1)} %refs_2_.7, bf16[64,64,128]{2,1,0:T(8,128)(2,1)} %copy-done.1, f32[8,128]{1,0:T(8,128)S(1)} %maximum_maximum_fusion.refs_4_, ...), custom_call_target="tpu_custom_call" | custom-call | flops 1610612736 | bytes 20971520 | tf_op jit(solution)/shard_map/sweep_last/pallas_call | solution.py:244
  71.1 2.4 %collective-permute-done.3.refs_7_ = bf16[64,64,128]{2,1,0:T(8,128)(2,1)} collective-permute-done((bf16[64,64,128]{2,1,0:T(8,128)(2,1)S(1)}, bf16[64,64,128]{2,1,0:T(8,128)(2,1)}, u32[]{:S(2)}, u32[]{:S(2)}) %collective-permute-start.3) | collective-permute-done | bytes 1048608 | tf_op jit(solution)/shard_map/ppermute | solution.py:410
  73.5 10.9 %sweep_last.2 = (bf16[32,64,128]{2,1,0:T(8,128)(2,1)S(1)}, bf16[32,64,128]{2,1,0:T(8,128)(2,1)S(1)}) custom-call(s32[1664]{0:T(1024)S(1)} %concatenate.17.refs_0_, bf16[64,64,1536]{2,1,0:T(8,128)(2,1)} %refs_1_.7, bf16[2,64,64,128]{3,2,1,0:T(8,128)(2,1)} %refs_2_.7, bf16[64,64,128]{2,1,0:T(8,128)(2,1)} %copy-done, f32[8,128]{1,0:T(8,128)S(1)} %maximum_maximum_fusion.refs_4_, ...), custom_call_target="tpu_custom_call" | custom-call | flops 1610612736 | bytes 20971520 | tf_op jit(solution)/shard_map/sweep_last/pallas_call | solution.py:244
  87.9 5.4 %collective-permute-done.20 = bf16[128,128]{1,0:T(8,128)(2,1)S(1)} collective-permute-done((bf16[128,128]{1,0:T(8,128)(2,1)S(1)}, bf16[128,128]{1,0:T(8,128)(2,1)S(1)}, u32[]{:S(2)}, u32[]{:S(2)}) %collective-permute-start.20) | collective-permute-done | bytes 32800 | tf_op jit(solution)/shard_map/ppermute | solution.py:410
  93.4 4.1 %collective-permute-start.16 = (bf16[2048,128]{1,0:T(8,128)(2,1)}, bf16[2048,128]{1,0:T(8,128)(2,1)}, u32[]{:S(2)}, u32[]{:S(2)}) collective-permute-start(bf16[2048,128]{1,0:T(8,128)(2,1)} %bitcast.3.own_ref.refs_4_), channel_id=1, source_target_pairs={{0,96},{16,112},{32,64},{48,80},{64,32},{80,48},{96,0},{112,16},{1... | collective-permute-start | bytes 1572872 | tf_op jit(solution)/shard_map/ppermute | solution.py:410
  99.1 4.1 %collective-permute-start.7 = (bf16[2048,128]{1,0:T(8,128)(2,1)S(1)}, bf16[2048,128]{1,0:T(8,128)(2,1)S(1)}, u32[]{:S(2)}, u32[]{:S(2)}) collective-permute-start(bf16[2048,128]{1,0:T(8,128)(2,1)S(1)} %bitcast.24), channel_id=1, source_target_pairs={{0,96},{16,112},{32,64},{48,80},{64,32},{80,48},{96,0},{112,16},{1... | collective-permute-start | bytes 1572872 | tf_op jit(solution)/shard_map/ppermute | solution.py:410
  103.3 2.3 %collective-permute-start.23 = (bf16[128,128]{1,0:T(8,128)(2,1)S(1)}, bf16[128,128]{1,0:T(8,128)(2,1)S(1)}, u32[]{:S(2)}, u32[]{:S(2)}) collective-permute-start(bf16[128,128]{1,0:T(8,128)(2,1)S(1)} %add_convert_fusion.own_ref), channel_id=1, source_target_pairs={{0,16},{16,0},{32,48},{48,32},{64,80},{80,64},{96,112},{112,96},{1... | collective-permute-start | bytes 98312 | tf_op jit(solution)/shard_map/ppermute | solution.py:410
  115.4 3.9 %collective-permute-start.15 = (bf16[2048,128]{1,0:T(8,128)(2,1)S(1)}, bf16[2048,128]{1,0:T(8,128)(2,1)S(1)}, u32[]{:S(2)}, u32[]{:S(2)}) collective-permute-start(bf16[2048,128]{1,0:T(8,128)(2,1)S(1)} %combine.8), channel_id=1, source_target_pairs={{0,96},{16,112},{32,64},{48,80},{64,32},{80,48},{96,0},{112,16},{1... | collective-permute-start | bytes 1572872 | tf_op jit(solution)/shard_map/ppermute | solution.py:410
  119.2 5.4 %collective-permute-done.24 = bf16[128,128]{0,1:T(8,128)(2,1)} collective-permute-done((bf16[128,128]{0,1:T(8,128)(2,1)}, bf16[128,128]{0,1:T(8,128)(2,1)}, u32[]{:S(2)}, u32[]{:S(2)}) %collective-permute-start.24) | collective-permute-done | bytes 32800 | tf_op jit(solution)/shard_map/ppermute | solution.py:410
  129.7 2.3 %collective-permute-done.25 = bf16[128,128]{0,1:T(8,128)(2,1)S(1)} collective-permute-done((bf16[128,128]{0,1:T(8,128)(2,1)S(1)}, bf16[128,128]{0,1:T(8,128)(2,1)S(1)}, u32[]{:S(2)}, u32[]{:S(2)}) %collective-permute-start.25) | collective-permute-done | bytes 32800 | tf_op jit(solution)/shard_map/ppermute | solution.py:410
  133.5 3.5 %fold.5 = (bf16[2048,128]{1,0:T(8,128)(2,1)}, f32[2048,128]{1,0:T(8,128)S(1)}) custom-call(bf16[2048,128]{1,0:T(8,128)(2,1)} %bitcast.2.own_ref.refs_0_, bf16[2048,128]{1,0:T(8,128)(2,1)} %collective-permute-done.14.peer_ref.refs_1_, bf16[2048,128]{1,0:T(8,128)(2,1)S(1)} %collective-permute-done.15.refs_2_, ...), custom_call_target="tpu_custom_call" | custom-call | flops 536870912 | bytes 4718592 | tf_op jit(solution)/shard_map/fold/pallas_call | solution.py:332
  139.1 2.3 %collective-permute-done.8.refs_2_.refs_6_ = bf16[2048,128]{1,0:T(8,128)(2,1)S(1)} collective-permute-done((bf16[2048,128]{1,0:T(8,128)(2,1)S(1)}, bf16[2048,128]{1,0:T(8,128)(2,1)S(1)}, u32[]{:S(2)}, u32[]{:S(2)}) %collective-permute-start.8) | collective-permute-done | bytes 524320 | tf_op jit(solution)/shard_map/ppermute | solution.py:410
  143.0 9.7 %collective-permute-done.5.refs_2_.refs_6_ = bf16[2048,128]{1,0:T(8,128)(2,1)S(1)} collective-permute-done((bf16[2048,128]{1,0:T(8,128)(2,1)S(1)}, bf16[2048,128]{1,0:T(8,128)(2,1)S(1)}, u32[]{:S(2)}, u32[]{:S(2)}) %collective-permute-start.5) | collective-permute-done | bytes 524320 | tf_op jit(solution)/shard_map/ppermute | solution.py:410
  153.5 3.2 %collective-permute-start.6 = (bf16[1024,128]{1,0:T(8,128)(2,1)S(1)}, bf16[1024,128]{1,0:T(8,128)(2,1)S(1)}, u32[]{:S(2)}, u32[]{:S(2)}) collective-permute-start(bf16[1024,128]{1,0:T(8,128)(2,1)S(1)} %get-tuple-element.22), channel_id=1, source_target_pairs={{0,96},{16,112},{32,64},{48,80},{64,32},{80,48},{96,0},{112,16},{1... | collective-permute-start | bytes 786440 | tf_op jit(solution)/shard_map/ppermute | solution.py:410
  157.6 3.5 %collective-permute-done.6.got1_ref = bf16[1024,128]{1,0:T(8,128)(2,1)S(1)} collective-permute-done((bf16[1024,128]{1,0:T(8,128)(2,1)S(1)}, bf16[1024,128]{1,0:T(8,128)(2,1)S(1)}, u32[]{:S(2)}, u32[]{:S(2)}) %collective-permute-start.6) | collective-permute-done | bytes 262176 | tf_op jit(solution)/shard_map/ppermute | solution.py:410
  163.4 3.9 %finish.1 = f32[1,2,2048,128]{3,2,1,0:T(8,128)} custom-call(f32[1024,128]{1,0:T(8,128)S(1)} %get-tuple-element.21.own1_ref, bf16[1024,128]{1,0:T(8,128)(2,1)S(1)} %collective-permute-done.6.got1_ref, f32[1024,128]{1,0:T(8,128)S(1)} %copy-done.11, bf16[1024,128]{1,0:T(8,128)(2,1)S(1)} %collective-permute-done.9.got2_ref, f32[2048,128]{1,0:T(8,128)S(1)} %copy-done.9, ...), custom_call_target="tpu_custom_call" | custom-call | tf_op jit(solution)/shard_map/finish/pallas_call | solution.py:374
  (125 shorter events, 39.9 us)
Async XLA Ops:
  4.8 16.5 %collective-permute-start.10 = (bf16[64,64,128]{2,1,0:T(8,128)(2,1)}, bf16[64,64,128]{2,1,0:T(8,128)(2,1)}, u32[]{:S(2)}, u32[]{:S(2)}) collective-permute-start(bf16[64,64,128]{2,1,0:T(8,128)(2,1)} %get-tuple-element.27.refs_5_), channel_id=1, source_target_pairs={{0,1},{1,0},{2,3},{3,2},{4,5},{5,4},{6,7},{7,6},{8,9},{9,8},{10,11... | collective-permute-start | bytes 3145736 | tf_op jit(solution)/shard_map/ppermute | solution.py:410
  4.8 20.0 %collective-permute-start.11 = (bf16[64,64,128]{2,1,0:T(8,128)(2,1)}, bf16[64,64,128]{2,1,0:T(8,128)(2,1)}, u32[]{:S(2)}, u32[]{:S(2)}) collective-permute-start(bf16[64,64,128]{2,1,0:T(8,128)(2,1)} %get-tuple-element.27.refs_5_), channel_id=1, source_target_pairs={{1,2},{2,1},{3,4},{4,3},{5,6},{6,5},{7,8},{8,7},{9,10},{10,9},{11,... | collective-permute-start | bytes 3145736 | tf_op jit(solution)/shard_map/ppermute | solution.py:410
  9.8 31.0 %collective-permute-start = (bf16[64,64,128]{2,1,0:T(8,128)(2,1)}, bf16[64,64,128]{2,1,0:T(8,128)(2,1)S(1)}, u32[]{:S(2)}, u32[]{:S(2)}) collective-permute-start(bf16[64,64,128]{2,1,0:T(8,128)(2,1)} %get-tuple-element.18.refs_5_), channel_id=1, source_target_pairs={{0,1},{1,0},{2,3},{3,2},{4,5},{5,4},{6,7},{7,6},{8,9},{9,8},{10,11... | collective-permute-start | bytes 3145736 | tf_op jit(solution)/shard_map/ppermute | solution.py:410
  9.9 31.9 %collective-permute-start.1 = (bf16[64,64,128]{2,1,0:T(8,128)(2,1)}, bf16[64,64,128]{2,1,0:T(8,128)(2,1)}, u32[]{:S(2)}, u32[]{:S(2)}) collective-permute-start(bf16[64,64,128]{2,1,0:T(8,128)(2,1)} %get-tuple-element.18.refs_5_), channel_id=1, source_target_pairs={{1,2},{2,1},{3,4},{4,3},{5,6},{6,5},{7,8},{8,7},{9,10},{10,9},{11,... | collective-permute-start | bytes 3145736 | tf_op jit(solution)/shard_map/ppermute | solution.py:410
  35.7 22.2 %collective-permute-start.12 = (bf16[64,64,128]{2,1,0:T(8,128)(2,1)S(1)}, bf16[64,64,128]{2,1,0:T(8,128)(2,1)}, u32[]{:S(2)}, u32[]{:S(2)}) collective-permute-start(bf16[64,64,128]{2,1,0:T(8,128)(2,1)S(1)} %sweep.3.refs_5_), channel_id=1, source_target_pairs={{0,1},{1,0},{2,3},{3,2},{4,5},{5,4},{6,7},{7,6},{8,9},{9,8},{10,11... | collective-permute-start | bytes 3145736 | tf_op jit(solution)/shard_map/ppermute | solution.py:410
  35.8 22.1 %collective-permute-start.13 = (bf16[64,64,128]{2,1,0:T(8,128)(2,1)S(1)}, bf16[64,64,128]{2,1,0:T(8,128)(2,1)}, u32[]{:S(2)}, u32[]{:S(2)}) collective-permute-start(bf16[64,64,128]{2,1,0:T(8,128)(2,1)S(1)} %sweep.3.refs_5_), channel_id=1, source_target_pairs={{1,2},{2,1},{3,4},{4,3},{5,6},{6,5},{7,8},{8,7},{9,10},{10,9},{11,... | collective-permute-start | bytes 3145736 | tf_op jit(solution)/shard_map/ppermute | solution.py:410
  53.6 17.5 %collective-permute-start.2 = (bf16[64,64,128]{2,1,0:T(8,128)(2,1)S(1)}, bf16[64,64,128]{2,1,0:T(8,128)(2,1)}, u32[]{:S(2)}, u32[]{:S(2)}) collective-permute-start(bf16[64,64,128]{2,1,0:T(8,128)(2,1)S(1)} %sweep.2.refs_5_), channel_id=1, source_target_pairs={{0,1},{1,0},{2,3},{3,2},{4,5},{5,4},{6,7},{7,6},{8,9},{9,8},{10,11... | collective-permute-start | bytes 3145736 | tf_op jit(solution)/shard_map/ppermute | solution.py:410
  53.6 19.8 %collective-permute-start.3 = (bf16[64,64,128]{2,1,0:T(8,128)(2,1)S(1)}, bf16[64,64,128]{2,1,0:T(8,128)(2,1)}, u32[]{:S(2)}, u32[]{:S(2)}) collective-permute-start(bf16[64,64,128]{2,1,0:T(8,128)(2,1)S(1)} %sweep.2.refs_5_), channel_id=1, source_target_pairs={{1,2},{2,1},{3,4},{4,3},{5,6},{6,5},{7,8},{8,7},{9,10},{10,9},{11,... | collective-permute-start | bytes 3145736 | tf_op jit(solution)/shard_map/ppermute | solution.py:410
  87.8 5.5 %collective-permute-start.20 = (bf16[128,128]{1,0:T(8,128)(2,1)S(1)}, bf16[128,128]{1,0:T(8,128)(2,1)S(1)}, u32[]{:S(2)}, u32[]{:S(2)}) collective-permute-start(bf16[128,128]{1,0:T(8,128)(2,1)S(1)} %get-tuple-element.36), channel_id=1, source_target_pairs={{0,8},{1,9},{2,10},{3,11},{4,12},{5,13},{6,14},{7,15},{8,0},{9,1},... | collective-permute-start | bytes 98312 | tf_op jit(solution)/shard_map/ppermute | solution.py:410
  93.3 5.5 %collective-permute-start.21 = (bf16[128,128]{1,0:T(8,128)(2,1)S(1)}, bf16[128,128]{1,0:T(8,128)(2,1)S(1)}, u32[]{:S(2)}, u32[]{:S(2)}) collective-permute-start(bf16[128,128]{1,0:T(8,128)(2,1)S(1)} %fusion.12), channel_id=1, source_target_pairs={{0,4},{1,5},{2,6},{3,7},{4,0},{5,1},{6,2},{7,3},{8,12},{9,13},{10,... | collective-permute-start | bytes 98312 | tf_op jit(solution)/shard_map/ppermute | solution.py:410
  93.4 17.9 %collective-permute-start.16 = (bf16[2048,128]{1,0:T(8,128)(2,1)}, bf16[2048,128]{1,0:T(8,128)(2,1)}, u32[]{:S(2)}, u32[]{:S(2)}) collective-permute-start(bf16[2048,128]{1,0:T(8,128)(2,1)} %bitcast.3.own_ref.refs_4_), channel_id=1, source_target_pairs={{0,96},{16,112},{32,64},{48,80},{64,32},{80,48},{96,0},{112,16},{1... | collective-permute-start | bytes 1572872 | tf_op jit(solution)/shard_map/ppermute | solution.py:410
  97.6 15.8 %collective-permute-start.14 = (bf16[2048,128]{1,0:T(8,128)(2,1)}, bf16[2048,128]{1,0:T(8,128)(2,1)}, u32[]{:S(2)}, u32[]{:S(2)}) collective-permute-start(bf16[2048,128]{1,0:T(8,128)(2,1)} %bitcast.2.own_ref.refs_0_), channel_id=1, source_target_pairs={{0,32},{16,48},{32,0},{48,16},{64,96},{80,112},{96,64},{112,80},{1... | collective-permute-start | bytes 1572872 | tf_op jit(solution)/shard_map/ppermute | solution.py:410
  99.1 26.4 %collective-permute-start.7 = (bf16[2048,128]{1,0:T(8,128)(2,1)S(1)}, bf16[2048,128]{1,0:T(8,128)(2,1)S(1)}, u32[]{:S(2)}, u32[]{:S(2)}) collective-permute-start(bf16[2048,128]{1,0:T(8,128)(2,1)S(1)} %bitcast.24), channel_id=1, source_target_pairs={{0,96},{16,112},{32,64},{48,80},{64,32},{80,48},{96,0},{112,16},{1... | collective-permute-start | bytes 1572872 | tf_op jit(solution)/shard_map/ppermute | solution.py:410
  103.3 25.4 %collective-permute-start.4 = (bf16[2048,128]{1,0:T(8,128)(2,1)S(1)}, bf16[2048,128]{1,0:T(8,128)(2,1)S(1)}, u32[]{:S(2)}, u32[]{:S(2)}) collective-permute-start(bf16[2048,128]{1,0:T(8,128)(2,1)S(1)} %bitcast.19), channel_id=1, source_target_pairs={{0,32},{16,48},{32,0},{48,16},{64,96},{80,112},{96,64},{112,80},{1... | collective-permute-start | bytes 1572872 | tf_op jit(solution)/shard_map/ppermute | solution.py:410
  108.4 16.2 %collective-permute-start.24 = (bf16[128,128]{0,1:T(8,128)(2,1)}, bf16[128,128]{0,1:T(8,128)(2,1)}, u32[]{:S(2)}, u32[]{:S(2)}) collective-permute-start(bf16[128,128]{0,1:T(8,128)(2,1)} %copy.21), channel_id=1, source_target_pairs={{0,32},{16,48},{32,0},{48,16},{64,96},{80,112},{96,64},{112,80},{1... | collective-permute-start | bytes 98312 | tf_op jit(solution)/shard_map/ppermute | solution.py:410
  113.3 20.2 %collective-permute-start.17 = (bf16[2048,128]{1,0:T(8,128)(2,1)S(1)}, bf16[2048,128]{1,0:T(8,128)(2,1)S(1)}, u32[]{:S(2)}, u32[]{:S(2)}) collective-permute-start(bf16[2048,128]{1,0:T(8,128)(2,1)S(1)} %combine.9), channel_id=1, source_target_pairs={{0,32},{16,48},{32,0},{48,16},{64,96},{80,112},{96,64},{112,80},{1... | collective-permute-start | bytes 1572872 | tf_op jit(solution)/shard_map/ppermute | solution.py:410
  115.4 18.1 %collective-permute-start.15 = (bf16[2048,128]{1,0:T(8,128)(2,1)S(1)}, bf16[2048,128]{1,0:T(8,128)(2,1)S(1)}, u32[]{:S(2)}, u32[]{:S(2)}) collective-permute-start(bf16[2048,128]{1,0:T(8,128)(2,1)S(1)} %combine.8), channel_id=1, source_target_pairs={{0,96},{16,112},{32,64},{48,80},{64,32},{80,48},{96,0},{112,16},{1... | collective-permute-start | bytes 1572872 | tf_op jit(solution)/shard_map/ppermute | solution.py:410
  125.4 6.7 %collective-permute-start.25 = (bf16[128,128]{0,1:T(8,128)(2,1)S(1)}, bf16[128,128]{0,1:T(8,128)(2,1)S(1)}, u32[]{:S(2)}, u32[]{:S(2)}) collective-permute-start(bf16[128,128]{0,1:T(8,128)(2,1)S(1)} %fusion.11), channel_id=1, source_target_pairs={{0,96},{16,112},{32,64},{48,80},{64,32},{80,48},{96,0},{112,16},{1... | collective-permute-start | bytes 98312 | tf_op jit(solution)/shard_map/ppermute | solution.py:410
  126.5 15.0 %collective-permute-start.8 = (bf16[2048,128]{1,0:T(8,128)(2,1)S(1)}, bf16[2048,128]{1,0:T(8,128)(2,1)S(1)}, u32[]{:S(2)}, u32[]{:S(2)}) collective-permute-start(bf16[2048,128]{1,0:T(8,128)(2,1)S(1)} %combine.7), channel_id=1, source_target_pairs={{0,16},{16,0},{32,48},{48,32},{64,80},{80,64},{96,112},{112,96},{1... | collective-permute-start | bytes 1572872 | tf_op jit(solution)/shard_map/ppermute | solution.py:410
  129.6 23.1 %collective-permute-start.5 = (bf16[2048,128]{1,0:T(8,128)(2,1)S(1)}, bf16[2048,128]{1,0:T(8,128)(2,1)S(1)}, u32[]{:S(2)}, u32[]{:S(2)}) collective-permute-start(bf16[2048,128]{1,0:T(8,128)(2,1)S(1)} %combine.6), channel_id=1, source_target_pairs={{0,16},{16,0},{32,48},{48,32},{64,80},{80,64},{96,112},{112,96},{1... | collective-permute-start | bytes 1572872 | tf_op jit(solution)/shard_map/ppermute | solution.py:410
  132.8 23.9 %collective-permute-start.26 = (f32[128,128]{0,1:T(8,128)S(1)}, f32[128,128]{0,1:T(8,128)S(1)}, u32[]{:S(2)}, u32[]{:S(2)}) collective-permute-start(f32[128,128]{0,1:T(8,128)S(1)} %convert_add_fusion), channel_id=1, source_target_pairs={{0,1},{1,0},{2,3},{3,2},{4,5},{5,4},{6,7},{7,6},{8,9},{9,8},{10,11... | collective-permute-start | bytes 196616 | tf_op jit(solution)/shard_map/ppermute | solution.py:410
  137.0 24.1 %collective-permute-start.18 = (bf16[2048,128]{1,0:T(8,128)(2,1)}, bf16[2048,128]{1,0:T(8,128)(2,1)}, u32[]{:S(2)}, u32[]{:S(2)}) collective-permute-start(bf16[2048,128]{1,0:T(8,128)(2,1)} %get-tuple-element.31), channel_id=1, source_target_pairs={{0,16},{16,0},{32,48},{48,32},{64,80},{80,64},{96,112},{112,96},{1... | collective-permute-start | bytes 1572872 | tf_op jit(solution)/shard_map/ppermute | solution.py:410
  143.0 14.7 %collective-permute-start.9 = (bf16[1024,128]{1,0:T(8,128)(2,1)}, bf16[1024,128]{1,0:T(8,128)(2,1)S(1)}, u32[]{:S(2)}, u32[]{:S(2)}) collective-permute-start(bf16[1024,128]{1,0:T(8,128)(2,1)} %get-tuple-element.25), channel_id=1, source_target_pairs={{0,32},{16,48},{32,0},{48,16},{64,96},{80,112},{96,64},{112,80},{1... | collective-permute-start | bytes 786440 | tf_op jit(solution)/shard_map/ppermute | solution.py:410
  153.5 7.7 %collective-permute-start.6 = (bf16[1024,128]{1,0:T(8,128)(2,1)S(1)}, bf16[1024,128]{1,0:T(8,128)(2,1)S(1)}, u32[]{:S(2)}, u32[]{:S(2)}) collective-permute-start(bf16[1024,128]{1,0:T(8,128)(2,1)S(1)} %get-tuple-element.22), channel_id=1, source_target_pairs={{0,96},{16,112},{32,64},{48,80},{64,32},{80,48},{96,0},{112,16},{1... | collective-permute-start | bytes 786440 | tf_op jit(solution)/shard_map/ppermute | solution.py:410
  (21 other events, 152.2 us)

commit v8 on v7

--- a/solution.py
+++ b/solution.py
@@ -30,10 +30,6 @@
             src = (point % points) * LANES + part * GROUP + unit * HALF + col
             table[src, unit * LANES + lane] = 1.0
     return table
-
-
-def in_hbm(x):
-    return pltpu.with_memory_space_constraint(x, pltpu.MemorySpace.HBM)
 
 
 def lane_ids(shape):
@@ -262,22 +258,20 @@
         cost_estimate=pl.CostEstimate(
             flops=2 * RB * BS * SLOTS * BS * LANES, bytes_accessed=20 << 20, transcendentals=0
         ),
-        compiler_params=pltpu.CompilerParams(vmem_limit_bytes=24 << 20),
+        compiler_params=pltpu.CompilerParams(vmem_limit_bytes=48 << 20),
         name="sweep_last" if last else "sweep",
-    )(index, in_hbm(ham), in_hbm(precond), in_hbm(rhs_unit), z, in_hbm(local), near, far)
-
-
-def weighted(own_ref, peer_ref, weight_ref):
+    )(index, ham, precond, rhs_unit, z, local, near, far)
+
+
+def combine_kernel(own_ref, peer_ref, weight_ref, send_ref, keep_ref):
     own, peer = own_ref[...], peer_ref[...]
     both = jnp.concatenate([own, peer, own, peer], axis=1)
-    return jnp.dot(both, weight_ref[0], preferred_element_type=F32)
-
-
-def combine_kernel(own_ref, peer_ref, weight_ref, send_ref):
-    send_ref[...] = weighted(own_ref, peer_ref, weight_ref).astype(send_ref.dtype)
-
-
-def combine(own, peer, weights, which, part, rows_step, kind=BF16):
+    out = jnp.dot(both, weight_ref[0], preferred_element_type=F32)
+    send_ref[...] = out[:, :LANES].astype(BF16)
+    keep_ref[...] = out[:, LANES:].astype(keep_ref.dtype)
+
+
+def combine(own, peer, weights, which, rows_step, kind=BF16):
     rows = peer.shape[0]
     row_spec = pl.BlockSpec((rows_step, LANES), lambda i: (i, 0))
     return pl.pallas_call(
@@ -286,13 +280,16 @@
         in_specs=[
             row_spec,
             row_spec,
-            pl.BlockSpec((1, 4 * LANES, LANES), lambda i: (which, 0, part)),
+            pl.BlockSpec((1, 4 * LANES, 2 * LANES), lambda i: (which, 0, 0)),
         ],
-        out_specs=row_spec,
-        out_shape=jax.ShapeDtypeStruct((rows, LANES), kind),
+        out_specs=[row_spec, row_spec],
+        out_shape=[
+            jax.ShapeDtypeStruct((rows, LANES), BF16),
+            jax.ShapeDtypeStruct((rows, LANES), kind),
+        ],
         compiler_params=pltpu.CompilerParams(vmem_limit_bytes=8 << 20),
         cost_estimate=pl.CostEstimate(
-            flops=2 * rows * 128 * 512, bytes_accessed=rows * LANES * 6, transcendentals=0
+            flops=2 * rows * 256 * 512, bytes_accessed=rows * LANES * 8, transcendentals=0
         ),
         name="combine",
     )(own, peer, weights)
@@ -310,40 +307,36 @@
     return pltpu.roll(x, LANES - HALF if unit else HALF, axis=1)
 
 
-def fold_kernel(unit, own1, peer1, got1, weight1, own2, peer2, got2, weight2, send_ref, own_ref):
-    top = weighted(own1, peer1, weight1) + got1[...].astype(F32)
-    bottom = weighted(own2, peer2, weight2) + got2[...].astype(F32)
+def fold_kernel(unit, keep1_ref, got1_ref, keep2_ref, got2_ref, send_ref, own_ref):
+    top = keep1_ref[...].astype(F32) + got1_ref[...].astype(F32)
+    bottom = keep2_ref[...].astype(F32) + got2_ref[...].astype(F32)
     own = own_lanes(top.shape, unit)
     send_ref[...] = jnp.where(own, to_own(top, unit), bottom).astype(BF16)
     own_ref[...] = jnp.where(own, top, from_own(bottom, unit))
 
 
-def fold(unit, first, second, weights, rows, shift):
+def fold(unit, first, second, rows, shift):
     def kernel(*refs):
         fold_kernel(unit, *refs)
 
     step = 1024
     spec = pl.BlockSpec((step, LANES), lambda i: (i, 0))
     late = pl.BlockSpec((step, LANES), lambda i: (i + shift // step, 0))
-
-    def weight_spec(which):
-        return pl.BlockSpec((1, 4 * LANES, LANES), lambda i: (which, 0, 1))
-
     return pl.pallas_call(
         kernel,
         grid=(rows // step,),
-        in_specs=[spec] * 3 + [weight_spec(first[3])] + [late] * 3 + [weight_spec(second[3])],
+        in_specs=[spec, spec, late, late],
         out_specs=[spec, spec],
         out_shape=[
             jax.ShapeDtypeStruct((rows, LANES), BF16),
             jax.ShapeDtypeStruct((rows, LANES), F32),
         ],
-        compiler_params=pltpu.CompilerParams(vmem_limit_bytes=12 << 20),
+        compiler_params=pltpu.CompilerParams(vmem_limit_bytes=10 << 20),
         cost_estimate=pl.CostEstimate(
-            flops=rows * LANES * 2048, bytes_accessed=rows * LANES * 18, transcendentals=0
+            flops=rows * LANES * 8, bytes_accessed=rows * LANES * 14, transcendentals=0
         ),
         name="fold",
-    )(*first[:3], weights, *second[:3], weights)
+    )(*first, *second)
 
 
 def finish_kernel(own1_ref, got1_ref, own2_ref, got2_ref, own_b_ref, got_b_ref, out_ref):
@@ -473,24 +466,23 @@
         top, bottom = (part.reshape(half_rows, LANES) for part in units[unit])
         got1 = swap(top, "quad", by_pair)
         got2 = swap(bottom, "quad", by_mirror)
-        send1 = combine(top, got1, weights, 2 * unit, 0, 1024)
-        send2 = combine(bottom, got2, weights, 2 * unit + 1, 0, 1024)
-        return (top, got1), (bottom, got2), send1, send2
-
-    pair_a1, pair_a2, send_a1, send_a2 = first_stage(0)
+        out1 = combine(top, got1, weights, 2 * unit, 1024)
+        out2 = combine(bottom, got2, weights, 2 * unit + 1, 1024)
+        return *out1, *out2
+
+    send_a1, keep_a1, send_a2, keep_a2 = first_stage(0)
     got_a1 = swap(send_a1, "quad", by_x)
     got_a2 = swap(send_a2, "quad", by_x)
     quarter = half_rows // 2
-    half = (*pair_a1, got_a1, 0)
-    send_a1, own_a1 = fold(0, half, half, weights, quarter, quarter)
-    half = (*pair_a2, got_a2, 1)
-    send_a2, own_a2 = fold(0, half, half, weights, quarter, quarter)
-
-    pair_b1, pair_b2, send_b1, send_b2 = first_stage(1)
+    half = (keep_a1, got_a1)
+    send_a1, own_a1 = fold(0, half, half, quarter, quarter)
+    half = (keep_a2, got_a2)
+    send_a2, own_a2 = fold(0, half, half, quarter, quarter)
+
+    send_b1, keep_b1, send_b2, keep_b2 = first_stage(1)
     got_b1 = swap(send_b1, "quad", by_mirror)
     got_b2 = swap(send_b2, "quad", by_pair)
-    halves = (*pair_b1, got_b1, 2), (*pair_b2, got_b2, 3)
-    send_b, own_b = fold(1, *halves, weights, half_rows, 0)
+    send_b, own_b = fold(1, (keep_b1, got_b1), (keep_b2, got_b2), half_rows, 0)
 
     def rounded(x):
         return lax.reduce_precision(x, 8, 7)
@@ -504,8 +496,7 @@
         gram = gram + peer.astype(F32)
     gram = gram.astype(BF16)
     peer = swap(gram, "quad", by_x)
-    send_g = combine(gram, peer, weights, 4, 0, LANES)
-    keep_g = combine(gram, peer, weights, 4, 1, LANES, F32)
+    send_g, keep_g = combine(gram, peer, weights, 4, LANES, F32)
     gram_sum = keep_g + swap(send_g, "quad", by_pair).astype(F32)
     gram_got = swap(gram_sum.astype(BF16), "quad", by_mirror)
     gram_own = gram_sum + jnp.roll(gram_got, HALF, axis=1).astype(F32)

time: 170 us -> 161 us (0.947)
  Pallas kernels: 65.7 us -> 58.5 us
  local copies, waits for them, and re-layouts: 10.5 us -> 7.67 us
    pallas_call x3, Pallas kernels: 5.83 us -> 2.37 us  [fold(): pl.pallas_call(kernel, grid=(rows // step,), in_specs=[spec, spec, late,...]
    pallas_call x4, Pallas kernels: 44 us -> 41.2 us  [sweep(): pl.pallas_call(kernel, grid_spec=pltpu.PrefetchScalarGridSpec(num_scalar_...]
    unnamed x37 -> x23, local copies, waits for them, and re-layouts: 8.81 us -> 6.6 us
    pallas_call x6 -> x5, Pallas kernels: 6.07 us -> 6.7 us  [combine(): pl.pallas_call(combine_kernel, grid=(rows // rows_step,), in_specs=[row_s...]
  transfers between devices with their start and end apart: 27 -> 27, of which waited for: 12 -> 13; matrix products, arithmetic and copies ran while one was open for 4% -> 4% of each run, Pallas kernels for 28% -> 27%
where the time goes in v8:
time: 161 us; the launch traced here: 158 us
  Pallas kernels  58.5 us (36%)
  starting transfers between devices  43.3 us (27%)
  waiting for transfers between devices  41.2 us (26%)
  local copies, waits for them, and re-layouts  7.67 us (5%)
  matrix products  3.46 us (2%)
  other arithmetic  3.11 us (2%)
    ppermute x27, starting transfers between devices, swap(): lax.ppermute(x, axis, [(i, j) for i, j in peers if 0 <= j < len(peers)])  43.3 us
    pallas_call x4, Pallas kernels, sweep(): pl.pallas_call(kernel, grid_spec=pltpu.PrefetchScalarGridSpec(num_scalar_...  41.2 us
    ppermute x27, waiting for transfers between devices, swap(): lax.ppermute(x, axis, [(i, j) for i, j in peers if 0 <= j < len(peers)])  41.2 us
    pallas_call x5, Pallas kernels, combine(): pl.pallas_call(combine_kernel, grid=(rows // rows_step,), in_specs=[row_s...  6.7 us
    unnamed x23, local copies, waits for them, and re-layouts  6.6 us
    pallas_call x1, Pallas kernels, initial(): pl.pallas_call(init_kernel, grid=(RB // FIRST,), in_specs=[pl.BlockSpec((...  4.05 us
    dot_general x4, matrix products, step(): lax.dot_general(x, part, (((0,), (0,)), ((), ())), preferred_element_type...  3.46 us
  transfers between devices with their start and end apart: 27, of which 13 were waited for; matrix products, arithmetic and copies ran while one was open for 4% of the time, Pallas kernels for 27%

profile of v8, /device:TPU:4, one launch (start us, length us, event | category | flops | bytes accessed | tf_op | source)
XLA Modules:
  0.0 158.4 jit_solution(3625597823652082691)
XLA Ops:
  0.7 4.1 %initial.1 = (bf16[64,64,128]{2,1,0:T(8,128)(2,1)}, bf16[64,64,128]{2,1,0:T(8,128)(2,1)}) custom-call(bf16[4096,128]{1,0:T(8,128)(2,1)} %x_ref.3, bf16[2,64,64,128]{3,2,1,0:T(8,128)(2,1)} %refs_2_.7, bf16[256,256]{1,0:T(8,128)(2,1)} %constant.303.clone.map_ref), custom_call_target="tpu_custom_call" | custom-call | tf_op jit(solution)/shard_map/initial/pallas_call | solution.py:79
  4.7 5.0 %collective-permute-start.11 = (bf16[64,64,128]{2,1,0:T(8,128)(2,1)}, bf16[64,64,128]{2,1,0:T(8,128)(2,1)}, u32[]{:S(2)}, u32[]{:S(2)}) collective-permute-start(bf16[64,64,128]{2,1,0:T(8,128)(2,1)} %get-tuple-element.41.refs_5_), channel_id=1, source_target_pairs={{1,2},{2,1},{3,4},{4,3},{5,6},{6,5},{7,8},{8,7},{9,10},{10,9},{11,... | collective-permute-start | bytes 3145736 | tf_op jit(solution)/shard_map/ppermute | solution.py:403
  9.8 4.2 %collective-permute-start.1 = (bf16[64,64,128]{2,1,0:T(8,128)(2,1)}, bf16[64,64,128]{2,1,0:T(8,128)(2,1)}, u32[]{:S(2)}, u32[]{:S(2)}) collective-permute-start(bf16[64,64,128]{2,1,0:T(8,128)(2,1)} %get-tuple-element.28.refs_5_), channel_id=1, source_target_pairs={{1,2},{2,1},{3,4},{4,3},{5,6},{6,5},{7,8},{8,7},{9,10},{10,9},{11,... | collective-permute-start | bytes 3145736 | tf_op jit(solution)/shard_map/ppermute | solution.py:403
  20.4 4.4 %collective-permute-done.11.refs_7_ = bf16[64,64,128]{2,1,0:T(8,128)(2,1)} collective-permute-done((bf16[64,64,128]{2,1,0:T(8,128)(2,1)}, bf16[64,64,128]{2,1,0:T(8,128)(2,1)}, u32[]{:S(2)}, u32[]{:S(2)}) %collective-permute-start.11) | collective-permute-done | bytes 1048608 | tf_op jit(solution)/shard_map/ppermute | solution.py:403
  26.0 10.3 %sweep.3.refs_5_ = bf16[64,64,128]{2,1,0:T(8,128)(2,1)} custom-call(s32[1664]{0:T(1024)S(1)} %concatenate.17.refs_0_, bf16[64,64,1536]{2,1,0:T(8,128)(2,1)} %refs_1_.7, bf16[2,64,64,128]{3,2,1,0:T(8,128)(2,1)} %refs_2_.7, bf16[64,64,128]{2,1,0:T(8,128)(2,1)S(1)} %get-tuple-element.40.refs_3_, f32[8,128]{1,0:T(8,128)S(1)} %maximum_maximum_fusion.refs_4_, ...), custom_call_target="tpu_custom_call" | custom-call | flops 1610612736 | bytes 20971520 | tf_op jit(solution)/shard_map/sweep/pallas_call | solution.py:240
  36.4 5.0 %collective-permute-start.13 = (bf16[64,64,128]{2,1,0:T(8,128)(2,1)}, bf16[64,64,128]{2,1,0:T(8,128)(2,1)}, u32[]{:S(2)}, u32[]{:S(2)}) collective-permute-start(bf16[64,64,128]{2,1,0:T(8,128)(2,1)} %sweep.3.refs_5_), channel_id=1, source_target_pairs={{1,2},{2,1},{3,4},{4,3},{5,6},{6,5},{7,8},{8,7},{9,10},{10,9},{11,... | collective-permute-start | bytes 3145736 | tf_op jit(solution)/shard_map/ppermute | solution.py:403
  41.4 10.3 %sweep.2.refs_5_ = bf16[64,64,128]{2,1,0:T(8,128)(2,1)} custom-call(s32[1664]{0:T(1024)S(1)} %concatenate.17.refs_0_, bf16[64,64,1536]{2,1,0:T(8,128)(2,1)} %refs_1_.7, bf16[2,64,64,128]{3,2,1,0:T(8,128)(2,1)} %refs_2_.7, bf16[64,64,128]{2,1,0:T(8,128)(2,1)S(1)} %get-tuple-element.27.refs_3_, f32[8,128]{1,0:T(8,128)S(1)} %maximum_maximum_fusion.refs_4_, ...), custom_call_target="tpu_custom_call" | custom-call | flops 1610612736 | bytes 20971520 | tf_op jit(solution)/shard_map/sweep/pallas_call | solution.py:240
  51.9 4.2 %collective-permute-start.3 = (bf16[64,64,128]{2,1,0:T(8,128)(2,1)}, bf16[64,64,128]{2,1,0:T(8,128)(2,1)}, u32[]{:S(2)}, u32[]{:S(2)}) collective-permute-start(bf16[64,64,128]{2,1,0:T(8,128)(2,1)} %sweep.2.refs_5_), channel_id=1, source_target_pairs={{1,2},{2,1},{3,4},{4,3},{5,6},{6,5},{7,8},{8,7},{9,10},{10,9},{11,... | collective-permute-start | bytes 3145736 | tf_op jit(solution)/shard_map/ppermute | solution.py:403
  56.5 10.7 %sweep_last.3 = (bf16[32,64,128]{2,1,0:T(8,128)(2,1)}, bf16[32,64,128]{2,1,0:T(8,128)(2,1)}) custom-call(s32[1664]{0:T(1024)S(1)} %concatenate.17.refs_0_, bf16[64,64,1536]{2,1,0:T(8,128)(2,1)} %refs_1_.7, bf16[2,64,64,128]{3,2,1,0:T(8,128)(2,1)} %refs_2_.7, bf16[64,64,128]{2,1,0:T(8,128)(2,1)S(1)} %get-tuple-element.40.refs_3_, ...), custom_call_target="tpu_custom_call" | custom-call | flops 1610612736 | bytes 20971520 | tf_op jit(solution)/shard_map/sweep_last/pallas_call | solution.py:240
  68.6 3.3 %collective-permute-done.3.refs_7_ = bf16[64,64,128]{2,1,0:T(8,128)(2,1)} collective-permute-done((bf16[64,64,128]{2,1,0:T(8,128)(2,1)}, bf16[64,64,128]{2,1,0:T(8,128)(2,1)}, u32[]{:S(2)}, u32[]{:S(2)}) %collective-permute-start.3) | collective-permute-done | bytes 1048608 | tf_op jit(solution)/shard_map/ppermute | solution.py:403
  71.9 9.8 %sweep_last.2 = (bf16[32,64,128]{2,1,0:T(8,128)(2,1)S(1)}, bf16[32,64,128]{2,1,0:T(8,128)(2,1)S(1)}) custom-call(s32[1664]{0:T(1024)S(1)} %concatenate.17.refs_0_, bf16[64,64,1536]{2,1,0:T(8,128)(2,1)} %refs_1_.7, bf16[2,64,64,128]{3,2,1,0:T(8,128)(2,1)} %refs_2_.7, bf16[64,64,128]{2,1,0:T(8,128)(2,1)S(1)} %get-tuple-element.27.refs_3_, ...), custom_call_target="tpu_custom_call" | custom-call | flops 1610612736 | bytes 20971520 | tf_op jit(solution)/shard_map/sweep_last/pallas_call | solution.py:240
  85.3 5.4 %collective-permute-done.20 = bf16[128,128]{1,0:T(8,128)(2,1)S(1)} collective-permute-done((bf16[128,128]{1,0:T(8,128)(2,1)S(1)}, bf16[128,128]{1,0:T(8,128)(2,1)S(1)}, u32[]{:S(2)}, u32[]{:S(2)}) %collective-permute-start.20) | collective-permute-done | bytes 32800 | tf_op jit(solution)/shard_map/ppermute | solution.py:403
  90.8 4.1 %collective-permute-start.16 = (bf16[2048,128]{1,0:T(8,128)(2,1)}, bf16[2048,128]{1,0:T(8,128)(2,1)S(1)}, u32[]{:S(2)}, u32[]{:S(2)}) collective-permute-start(bf16[2048,128]{1,0:T(8,128)(2,1)} %bitcast.3.own_ref), channel_id=1, source_target_pairs={{0,96},{16,112},{32,64},{48,80},{64,32},{80,48},{96,0},{112,16},{1... | collective-permute-start | bytes 1572872 | tf_op jit(solution)/shard_map/ppermute | solution.py:403
  97.2 3.8 %collective-permute-done.22 = bf16[128,128]{1,0:T(8,128)(2,1)S(1)} collective-permute-done((bf16[128,128]{1,0:T(8,128)(2,1)S(1)}, bf16[128,128]{1,0:T(8,128)(2,1)S(1)}, u32[]{:S(2)}, u32[]{:S(2)}) %collective-permute-start.22) | collective-permute-done | bytes 32800 | tf_op jit(solution)/shard_map/ppermute | solution.py:403
  101.0 2.2 %collective-permute-start.23 = (bf16[128,128]{1,0:T(8,128)(2,1)S(1)}, bf16[128,128]{1,0:T(8,128)(2,1)S(1)}, u32[]{:S(2)}, u32[]{:S(2)}) collective-permute-start(bf16[128,128]{1,0:T(8,128)(2,1)S(1)} %add_convert_fusion.own_ref), channel_id=1, source_target_pairs={{0,16},{16,0},{32,48},{48,32},{64,80},{80,64},{96,112},{112,96},{1... | collective-permute-start | bytes 98312 | tf_op jit(solution)/shard_map/ppermute | solution.py:403
  113.8 3.4 %collective-permute-start.15 = (bf16[2048,128]{1,0:T(8,128)(2,1)S(1)}, bf16[2048,128]{1,0:T(8,128)(2,1)S(1)}, u32[]{:S(2)}, u32[]{:S(2)}) collective-permute-start(bf16[2048,128]{1,0:T(8,128)(2,1)S(1)} %get-tuple-element.44), channel_id=1, source_target_pairs={{0,96},{16,112},{32,64},{48,80},{64,32},{80,48},{96,0},{112,16},{1... | collective-permute-start | bytes 1572872 | tf_op jit(solution)/shard_map/ppermute | solution.py:403
  117.2 2.0 %collective-permute-done.7.peer_ref = bf16[2048,128]{1,0:T(8,128)(2,1)} collective-permute-done((bf16[2048,128]{1,0:T(8,128)(2,1)S(1)}, bf16[2048,128]{1,0:T(8,128)(2,1)}, u32[]{:S(2)}, u32[]{:S(2)}) %collective-permute-start.7) | collective-permute-done | bytes 524320 | tf_op jit(solution)/shard_map/ppermute | solution.py:403
  121.1 2.2 %collective-permute-start.8 = (bf16[2048,128]{1,0:T(8,128)(2,1)S(1)}, bf16[2048,128]{1,0:T(8,128)(2,1)S(1)}, u32[]{:S(2)}, u32[]{:S(2)}) collective-permute-start(bf16[2048,128]{1,0:T(8,128)(2,1)S(1)} %get-tuple-element.37), channel_id=1, source_target_pairs={{0,16},{16,0},{32,48},{48,32},{64,80},{80,64},{96,112},{112,96},{1... | collective-permute-start | bytes 1572872 | tf_op jit(solution)/shard_map/ppermute | solution.py:403
  125.1 3.3 %collective-permute-start.25 = (bf16[128,128]{0,1:T(8,128)(2,1)S(1)}, bf16[128,128]{0,1:T(8,128)(2,1)S(1)}, u32[]{:S(2)}, u32[]{:S(2)}) collective-permute-start(bf16[128,128]{0,1:T(8,128)(2,1)S(1)} %fusion.11), channel_id=1, source_target_pairs={{0,96},{16,112},{32,64},{48,80},{64,32},{80,48},{96,0},{112,16},{1... | collective-permute-start | bytes 98312 | tf_op jit(solution)/shard_map/ppermute | solution.py:403
  132.4 2.0 %collective-permute-start.18 = (bf16[2048,128]{1,0:T(8,128)(2,1)}, bf16[2048,128]{1,0:T(8,128)(2,1)S(1)}, u32[]{:S(2)}, u32[]{:S(2)}) collective-permute-start(bf16[2048,128]{1,0:T(8,128)(2,1)} %get-tuple-element.49), channel_id=1, source_target_pairs={{0,16},{16,0},{32,48},{48,32},{64,80},{80,64},{96,112},{112,96},{1... | collective-permute-start | bytes 1572872 | tf_op jit(solution)/shard_map/ppermute | solution.py:403
  136.4 10.9 %collective-permute-done.5.refs_1_.refs_3_ = bf16[2048,128]{1,0:T(8,128)(2,1)S(1)} collective-permute-done((bf16[2048,128]{1,0:T(8,128)(2,1)S(1)}, bf16[2048,128]{1,0:T(8,128)(2,1)S(1)}, u32[]{:S(2)}, u32[]{:S(2)}) %collective-permute-start.5) | collective-permute-done | bytes 524320 | tf_op jit(solution)/shard_map/ppermute | solution.py:403
  148.2 3.2 %collective-permute-start.6 = (bf16[1024,128]{1,0:T(8,128)(2,1)}, bf16[1024,128]{1,0:T(8,128)(2,1)S(1)}, u32[]{:S(2)}, u32[]{:S(2)}) collective-permute-start(bf16[1024,128]{1,0:T(8,128)(2,1)} %get-tuple-element.34), channel_id=1, source_target_pairs={{0,96},{16,112},{32,64},{48,80},{64,32},{80,48},{96,0},{112,16},{1... | collective-permute-start | bytes 786440 | tf_op jit(solution)/shard_map/ppermute | solution.py:403
  152.4 3.7 %collective-permute-done.6.got1_ref = bf16[1024,128]{1,0:T(8,128)(2,1)S(1)} collective-permute-done((bf16[1024,128]{1,0:T(8,128)(2,1)}, bf16[1024,128]{1,0:T(8,128)(2,1)S(1)}, u32[]{:S(2)}, u32[]{:S(2)}) %collective-permute-start.6) | collective-permute-done | bytes 262176 | tf_op jit(solution)/shard_map/ppermute | solution.py:403
  156.0 2.4 %finish.1 = f32[1,2,2048,128]{3,2,1,0:T(8,128)} custom-call(f32[1024,128]{1,0:T(8,128)S(1)} %get-tuple-element.33.own1_ref, bf16[1024,128]{1,0:T(8,128)(2,1)S(1)} %collective-permute-done.6.got1_ref, f32[1024,128]{1,0:T(8,128)S(1)} %get-tuple-element.38.own2_ref, bf16[1024,128]{1,0:T(8,128)(2,1)S(1)} %collective-permute-done.9.got2_ref, ...), custom_call_target="tpu_custom_call" | custom-call | tf_op jit(solution)/shard_map/finish/pallas_call | solution.py:367
  (110 shorter events, 37.4 us)
Async XLA Ops:
  4.7 15.7 %collective-permute-start.10 = (bf16[64,64,128]{2,1,0:T(8,128)(2,1)}, bf16[64,64,128]{2,1,0:T(8,128)(2,1)}, u32[]{:S(2)}, u32[]{:S(2)}) collective-permute-start(bf16[64,64,128]{2,1,0:T(8,128)(2,1)} %get-tuple-element.41.refs_5_), channel_id=1, source_target_pairs={{0,1},{1,0},{2,3},{3,2},{4,5},{5,4},{6,7},{7,6},{8,9},{9,8},{10,11... | collective-permute-start | bytes 3145736 | tf_op jit(solution)/shard_map/ppermute | solution.py:403
  4.7 20.0 %collective-permute-start.11 = (bf16[64,64,128]{2,1,0:T(8,128)(2,1)}, bf16[64,64,128]{2,1,0:T(8,128)(2,1)}, u32[]{:S(2)}, u32[]{:S(2)}) collective-permute-start(bf16[64,64,128]{2,1,0:T(8,128)(2,1)} %get-tuple-element.41.refs_5_), channel_id=1, source_target_pairs={{1,2},{2,1},{3,4},{4,3},{5,6},{6,5},{7,8},{8,7},{9,10},{10,9},{11,... | collective-permute-start | bytes 3145736 | tf_op jit(solution)/shard_map/ppermute | solution.py:403
  9.7 31.7 %collective-permute-start = (bf16[64,64,128]{2,1,0:T(8,128)(2,1)}, bf16[64,64,128]{2,1,0:T(8,128)(2,1)}, u32[]{:S(2)}, u32[]{:S(2)}) collective-permute-start(bf16[64,64,128]{2,1,0:T(8,128)(2,1)} %get-tuple-element.28.refs_5_), channel_id=1, source_target_pairs={{0,1},{1,0},{2,3},{3,2},{4,5},{5,4},{6,7},{7,6},{8,9},{9,8},{10,11... | collective-permute-start | bytes 3145736 | tf_op jit(solution)/shard_map/ppermute | solution.py:403
  9.8 31.6 %collective-permute-start.1 = (bf16[64,64,128]{2,1,0:T(8,128)(2,1)}, bf16[64,64,128]{2,1,0:T(8,128)(2,1)}, u32[]{:S(2)}, u32[]{:S(2)}) collective-permute-start(bf16[64,64,128]{2,1,0:T(8,128)(2,1)} %get-tuple-element.28.refs_5_), channel_id=1, source_target_pairs={{1,2},{2,1},{3,4},{4,3},{5,6},{6,5},{7,8},{8,7},{9,10},{10,9},{11,... | collective-permute-start | bytes 3145736 | tf_op jit(solution)/shard_map/ppermute | solution.py:403
  36.3 19.8 %collective-permute-start.12 = (bf16[64,64,128]{2,1,0:T(8,128)(2,1)}, bf16[64,64,128]{2,1,0:T(8,128)(2,1)}, u32[]{:S(2)}, u32[]{:S(2)}) collective-permute-start(bf16[64,64,128]{2,1,0:T(8,128)(2,1)} %sweep.3.refs_5_), channel_id=1, source_target_pairs={{0,1},{1,0},{2,3},{3,2},{4,5},{5,4},{6,7},{7,6},{8,9},{9,8},{10,11... | collective-permute-start | bytes 3145736 | tf_op jit(solution)/shard_map/ppermute | solution.py:403
  36.4 20.0 %collective-permute-start.13 = (bf16[64,64,128]{2,1,0:T(8,128)(2,1)}, bf16[64,64,128]{2,1,0:T(8,128)(2,1)}, u32[]{:S(2)}, u32[]{:S(2)}) collective-permute-start(bf16[64,64,128]{2,1,0:T(8,128)(2,1)} %sweep.3.refs_5_), channel_id=1, source_target_pairs={{1,2},{2,1},{3,4},{4,3},{5,6},{6,5},{7,8},{8,7},{9,10},{10,9},{11,... | collective-permute-start | bytes 3145736 | tf_op jit(solution)/shard_map/ppermute | solution.py:403
  51.8 16.8 %collective-permute-start.2 = (bf16[64,64,128]{2,1,0:T(8,128)(2,1)}, bf16[64,64,128]{2,1,0:T(8,128)(2,1)}, u32[]{:S(2)}, u32[]{:S(2)}) collective-permute-start(bf16[64,64,128]{2,1,0:T(8,128)(2,1)} %sweep.2.refs_5_), channel_id=1, source_target_pairs={{0,1},{1,0},{2,3},{3,2},{4,5},{5,4},{6,7},{7,6},{8,9},{9,8},{10,11... | collective-permute-start | bytes 3145736 | tf_op jit(solution)/shard_map/ppermute | solution.py:403
  51.9 20.0 %collective-permute-start.3 = (bf16[64,64,128]{2,1,0:T(8,128)(2,1)}, bf16[64,64,128]{2,1,0:T(8,128)(2,1)}, u32[]{:S(2)}, u32[]{:S(2)}) collective-permute-start(bf16[64,64,128]{2,1,0:T(8,128)(2,1)} %sweep.2.refs_5_), channel_id=1, source_target_pairs={{1,2},{2,1},{3,4},{4,3},{5,6},{6,5},{7,8},{8,7},{9,10},{10,9},{11,... | collective-permute-start | bytes 3145736 | tf_op jit(solution)/shard_map/ppermute | solution.py:403
  85.2 5.5 %collective-permute-start.20 = (bf16[128,128]{1,0:T(8,128)(2,1)S(1)}, bf16[128,128]{1,0:T(8,128)(2,1)S(1)}, u32[]{:S(2)}, u32[]{:S(2)}) collective-permute-start(bf16[128,128]{1,0:T(8,128)(2,1)S(1)} %get-tuple-element.56), channel_id=1, source_target_pairs={{0,8},{1,9},{2,10},{3,11},{4,12},{5,13},{6,14},{7,15},{8,0},{9,1},... | collective-permute-start | bytes 98312 | tf_op jit(solution)/shard_map/ppermute | solution.py:403
  90.7 6.2 %collective-permute-start.21 = (bf16[128,128]{1,0:T(8,128)(2,1)S(1)}, bf16[128,128]{1,0:T(8,128)(2,1)S(1)}, u32[]{:S(2)}, u32[]{:S(2)}) collective-permute-start(bf16[128,128]{1,0:T(8,128)(2,1)S(1)} %fusion.12), channel_id=1, source_target_pairs={{0,4},{1,5},{2,6},{3,7},{4,0},{5,1},{6,2},{7,3},{8,12},{9,13},{10,... | collective-permute-start | bytes 98312 | tf_op jit(solution)/shard_map/ppermute | solution.py:403
  90.8 17.1 %collective-permute-start.16 = (bf16[2048,128]{1,0:T(8,128)(2,1)}, bf16[2048,128]{1,0:T(8,128)(2,1)S(1)}, u32[]{:S(2)}, u32[]{:S(2)}) collective-permute-start(bf16[2048,128]{1,0:T(8,128)(2,1)} %bitcast.3.own_ref), channel_id=1, source_target_pairs={{0,96},{16,112},{32,64},{48,80},{64,32},{80,48},{96,0},{112,16},{1... | collective-permute-start | bytes 1572872 | tf_op jit(solution)/shard_map/ppermute | solution.py:403
  94.9 17.0 %collective-permute-start.14 = (bf16[2048,128]{1,0:T(8,128)(2,1)}, bf16[2048,128]{1,0:T(8,128)(2,1)}, u32[]{:S(2)}, u32[]{:S(2)}) collective-permute-start(bf16[2048,128]{1,0:T(8,128)(2,1)} %bitcast.2.own_ref), channel_id=1, source_target_pairs={{0,32},{16,48},{32,0},{48,16},{64,96},{80,112},{96,64},{112,80},{1... | collective-permute-start | bytes 1572872 | tf_op jit(solution)/shard_map/ppermute | solution.py:403
  94.9 24.3 %collective-permute-start.7 = (bf16[2048,128]{1,0:T(8,128)(2,1)S(1)}, bf16[2048,128]{1,0:T(8,128)(2,1)}, u32[]{:S(2)}, u32[]{:S(2)}) collective-permute-start(bf16[2048,128]{1,0:T(8,128)(2,1)S(1)} %bitcast.22), channel_id=1, source_target_pairs={{0,96},{16,112},{32,64},{48,80},{64,32},{80,48},{96,0},{112,16},{1... | collective-permute-start | bytes 1572872 | tf_op jit(solution)/shard_map/ppermute | solution.py:403
  95.4 27.8 %collective-permute-start.4 = (bf16[2048,128]{1,0:T(8,128)(2,1)S(1)}, bf16[2048,128]{1,0:T(8,128)(2,1)S(1)}, u32[]{:S(2)}, u32[]{:S(2)}) collective-permute-start(bf16[2048,128]{1,0:T(8,128)(2,1)S(1)} %bitcast.19), channel_id=1, source_target_pairs={{0,32},{16,48},{32,0},{48,16},{64,96},{80,112},{96,64},{112,80},{1... | collective-permute-start | bytes 1572872 | tf_op jit(solution)/shard_map/ppermute | solution.py:403
  106.0 18.3 %collective-permute-start.24 = (bf16[128,128]{0,1:T(8,128)(2,1)}, bf16[128,128]{0,1:T(8,128)(2,1)}, u32[]{:S(2)}, u32[]{:S(2)}) collective-permute-start(bf16[128,128]{0,1:T(8,128)(2,1)} %copy.21), channel_id=1, source_target_pairs={{0,32},{16,48},{32,0},{48,16},{64,96},{80,112},{96,64},{112,80},{1... | collective-permute-start | bytes 98312 | tf_op jit(solution)/shard_map/ppermute | solution.py:403
  111.6 19.6 %collective-permute-start.17 = (bf16[2048,128]{1,0:T(8,128)(2,1)S(1)}, bf16[2048,128]{1,0:T(8,128)(2,1)S(1)}, u32[]{:S(2)}, u32[]{:S(2)}) collective-permute-start(bf16[2048,128]{1,0:T(8,128)(2,1)S(1)} %get-tuple-element.47), channel_id=1, source_target_pairs={{0,32},{16,48},{32,0},{48,16},{64,96},{80,112},{96,64},{112,80},{1... | collective-permute-start | bytes 1572872 | tf_op jit(solution)/shard_map/ppermute | solution.py:403
  113.8 17.3 %collective-permute-start.15 = (bf16[2048,128]{1,0:T(8,128)(2,1)S(1)}, bf16[2048,128]{1,0:T(8,128)(2,1)S(1)}, u32[]{:S(2)}, u32[]{:S(2)}) collective-permute-start(bf16[2048,128]{1,0:T(8,128)(2,1)S(1)} %get-tuple-element.44), channel_id=1, source_target_pairs={{0,96},{16,112},{32,64},{48,80},{64,32},{80,48},{96,0},{112,16},{1... | collective-permute-start | bytes 1572872 | tf_op jit(solution)/shard_map/ppermute | solution.py:403
  121.1 15.0 %collective-permute-start.8 = (bf16[2048,128]{1,0:T(8,128)(2,1)S(1)}, bf16[2048,128]{1,0:T(8,128)(2,1)S(1)}, u32[]{:S(2)}, u32[]{:S(2)}) collective-permute-start(bf16[2048,128]{1,0:T(8,128)(2,1)S(1)} %get-tuple-element.37), channel_id=1, source_target_pairs={{0,16},{16,0},{32,48},{48,32},{64,80},{80,64},{96,112},{112,96},{1... | collective-permute-start | bytes 1572872 | tf_op jit(solution)/shard_map/ppermute | solution.py:403
  124.2 23.1 %collective-permute-start.5 = (bf16[2048,128]{1,0:T(8,128)(2,1)S(1)}, bf16[2048,128]{1,0:T(8,128)(2,1)S(1)}, u32[]{:S(2)}, u32[]{:S(2)}) collective-permute-start(bf16[2048,128]{1,0:T(8,128)(2,1)S(1)} %get-tuple-element.32), channel_id=1, source_target_pairs={{0,16},{16,0},{32,48},{48,32},{64,80},{80,64},{96,112},{112,96},{1... | collective-permute-start | bytes 1572872 | tf_op jit(solution)/shard_map/ppermute | solution.py:403
  125.1 5.2 %collective-permute-start.25 = (bf16[128,128]{0,1:T(8,128)(2,1)S(1)}, bf16[128,128]{0,1:T(8,128)(2,1)S(1)}, u32[]{:S(2)}, u32[]{:S(2)}) collective-permute-start(bf16[128,128]{0,1:T(8,128)(2,1)S(1)} %fusion.11), channel_id=1, source_target_pairs={{0,96},{16,112},{32,64},{48,80},{64,32},{80,48},{96,0},{112,16},{1... | collective-permute-start | bytes 98312 | tf_op jit(solution)/shard_map/ppermute | solution.py:403
  131.1 20.4 %collective-permute-start.26 = (f32[128,128]{0,1:T(8,128)S(1)}, f32[128,128]{0,1:T(8,128)S(1)}, u32[]{:S(2)}, u32[]{:S(2)}) collective-permute-start(f32[128,128]{0,1:T(8,128)S(1)} %convert_add_fusion), channel_id=1, source_target_pairs={{0,1},{1,0},{2,3},{3,2},{4,5},{5,4},{6,7},{7,6},{8,9},{9,8},{10,11... | collective-permute-start | bytes 196616 | tf_op jit(solution)/shard_map/ppermute | solution.py:403
  132.4 23.6 %collective-permute-start.18 = (bf16[2048,128]{1,0:T(8,128)(2,1)}, bf16[2048,128]{1,0:T(8,128)(2,1)S(1)}, u32[]{:S(2)}, u32[]{:S(2)}) collective-permute-start(bf16[2048,128]{1,0:T(8,128)(2,1)} %get-tuple-element.49), channel_id=1, source_target_pairs={{0,16},{16,0},{32,48},{48,32},{64,80},{80,64},{96,112},{112,96},{1... | collective-permute-start | bytes 1572872 | tf_op jit(solution)/shard_map/ppermute | solution.py:403
  136.3 16.0 %collective-permute-start.9 = (bf16[1024,128]{1,0:T(8,128)(2,1)S(1)}, bf16[1024,128]{1,0:T(8,128)(2,1)S(1)}, u32[]{:S(2)}, u32[]{:S(2)}) collective-permute-start(bf16[1024,128]{1,0:T(8,128)(2,1)S(1)} %get-tuple-element.39), channel_id=1, source_target_pairs={{0,32},{16,48},{32,0},{48,16},{64,96},{80,112},{96,64},{112,80},{1... | collective-permute-start | bytes 786440 | tf_op jit(solution)/shard_map/ppermute | solution.py:403
  148.2 7.8 %collective-permute-start.6 = (bf16[1024,128]{1,0:T(8,128)(2,1)}, bf16[1024,128]{1,0:T(8,128)(2,1)S(1)}, u32[]{:S(2)}, u32[]{:S(2)}) collective-permute-start(bf16[1024,128]{1,0:T(8,128)(2,1)} %get-tuple-element.34), channel_id=1, source_target_pairs={{0,96},{16,112},{32,64},{48,80},{64,32},{80,48},{96,0},{112,16},{1... | collective-permute-start | bytes 786440 | tf_op jit(solution)/shard_map/ppermute | solution.py:403
  (14 other events, 86.4 us)

commit v9 on v8

--- a/solution.py
+++ b/solution.py
@@ -30,6 +30,10 @@
             src = (point % points) * LANES + part * GROUP + unit * HALF + col
             table[src, unit * LANES + lane] = 1.0
     return table
+
+
+def in_hbm(x):
+    return pltpu.with_memory_space_constraint(x, pltpu.MemorySpace.HBM)
 
 
 def lane_ids(shape):
@@ -447,8 +451,9 @@
             far = swap(y, "row", far_row)
             near = swap(y, "row", near_row)
             last = it == ITERS - 1
+            local = y if it else in_hbm(y)
             got = sweep(
-                index, hamiltonian, precond, rhs_units[unit], z, y, near, far, last
+                index, hamiltonian, precond, rhs_units[unit], z, local, near, far, last
             )
             units[unit] = got[0]
             if last:
@@ -471,9 +476,9 @@
         return *out1, *out2
 
     send_a1, keep_a1, send_a2, keep_a2 = first_stage(0)
+    quarter = half_rows // 2
     got_a1 = swap(send_a1, "quad", by_x)
     got_a2 = swap(send_a2, "quad", by_x)
-    quarter = half_rows // 2
     half = (keep_a1, got_a1)
     send_a1, own_a1 = fold(0, half, half, quarter, quarter)
     half = (keep_a2, got_a2)
@@ -510,7 +515,7 @@
     got_a1 = swap(send_a1, "quad", by_mirror)
     got_a2 = swap(send_a2, "quad", by_pair)
     got_b = swap(send_b, "quad", by_x)
-    moments = finish(own_a1, got_a1, own_a2, got_a2, own_b, got_b, 512)
+    moments = finish(own_a1, got_a1, in_hbm(own_a2), got_a2, own_b, got_b, 1024)
     return moments.reshape(1, RB * BS, LANES), blocks
 
 

time: 161 us -> 160 us (level)
    unnamed x23 -> x21, local copies, waits for them, and re-layouts: 6.6 us -> 5.39 us
where the time goes in v9:
time: 160 us; the launch traced here: 158 us
  Pallas kernels  59 us (37%)
  starting transfers between devices  43.3 us (27%)
  waiting for transfers between devices  41.7 us (26%)
  local copies, waits for them, and re-layouts  6.47 us (4%)
  matrix products  3.46 us (2%)
  other arithmetic  3.11 us (2%)
    ppermute x27, starting transfers between devices, swap(): lax.ppermute(x, axis, [(i, j) for i, j in peers if 0 <= j < len(peers)])  43.3 us
    pallas_call x4, Pallas kernels, sweep(): pl.pallas_call(kernel, grid_spec=pltpu.PrefetchScalarGridSpec(num_scalar_...  41.7 us
    ppermute x27, waiting for transfers between devices, swap(): lax.ppermute(x, axis, [(i, j) for i, j in peers if 0 <= j < len(peers)])  41.7 us
    pallas_call x5, Pallas kernels, combine(): pl.pallas_call(combine_kernel, grid=(rows // rows_step,), in_specs=[row_s...  6.71 us
    unnamed x21, local copies, waits for them, and re-layouts  5.39 us
    pallas_call x1, Pallas kernels, initial(): pl.pallas_call(init_kernel, grid=(RB // FIRST,), in_specs=[pl.BlockSpec((...  4.06 us
    dot_general x4, matrix products, step(): lax.dot_general(x, part, (((0,), (0,)), ((), ())), preferred_element_type...  3.46 us
  transfers between devices with their start and end apart: 27, of which 13 were waited for; matrix products, arithmetic and copies ran while one was open for 4% of the time, Pallas kernels for 27%

profile of v9, /device:TPU:4, one launch (start us, length us, event | category | flops | bytes accessed | tf_op | source)
XLA Modules:
  0.0 158.3 jit_solution(9450416735566101511)
XLA Ops:
  0.7 4.1 %initial.1 = (bf16[64,64,128]{2,1,0:T(8,128)(2,1)}, bf16[64,64,128]{2,1,0:T(8,128)(2,1)}) custom-call(bf16[4096,128]{1,0:T(8,128)(2,1)} %x_ref.3, bf16[2,64,64,128]{3,2,1,0:T(8,128)(2,1)} %refs_2_.7, bf16[256,256]{1,0:T(8,128)(2,1)} %constant.303.clone.map_ref), custom_call_target="tpu_custom_call" | custom-call | tf_op jit(solution)/shard_map/initial/pallas_call | solution.py:83
  4.7 5.0 %collective-permute-start.11 = (bf16[64,64,128]{2,1,0:T(8,128)(2,1)}, bf16[64,64,128]{2,1,0:T(8,128)(2,1)}, u32[]{:S(2)}, u32[]{:S(2)}) collective-permute-start(bf16[64,64,128]{2,1,0:T(8,128)(2,1)} %get-tuple-element.41.refs_5_), channel_id=1, source_target_pairs={{1,2},{2,1},{3,4},{4,3},{5,6},{6,5},{7,8},{8,7},{9,10},{10,9},{11,... | collective-permute-start | bytes 3145736 | tf_op jit(solution)/shard_map/ppermute | solution.py:407
  9.8 4.2 %collective-permute-start.1 = (bf16[64,64,128]{2,1,0:T(8,128)(2,1)}, bf16[64,64,128]{2,1,0:T(8,128)(2,1)}, u32[]{:S(2)}, u32[]{:S(2)}) collective-permute-start(bf16[64,64,128]{2,1,0:T(8,128)(2,1)} %get-tuple-element.28.refs_5_), channel_id=1, source_target_pairs={{1,2},{2,1},{3,4},{4,3},{5,6},{6,5},{7,8},{8,7},{9,10},{10,9},{11,... | collective-permute-start | bytes 3145736 | tf_op jit(solution)/shard_map/ppermute | solution.py:407
  20.4 4.3 %collective-permute-done.11.refs_7_ = bf16[64,64,128]{2,1,0:T(8,128)(2,1)} collective-permute-done((bf16[64,64,128]{2,1,0:T(8,128)(2,1)}, bf16[64,64,128]{2,1,0:T(8,128)(2,1)}, u32[]{:S(2)}, u32[]{:S(2)}) %collective-permute-start.11) | collective-permute-done | bytes 1048608 | tf_op jit(solution)/shard_map/ppermute | solution.py:407
  24.8 10.6 %sweep.3.refs_5_ = bf16[64,64,128]{2,1,0:T(8,128)(2,1)} custom-call(s32[1664]{0:T(1024)S(1)} %concatenate.17.refs_0_, bf16[64,64,1536]{2,1,0:T(8,128)(2,1)} %refs_1_.7, bf16[2,64,64,128]{3,2,1,0:T(8,128)(2,1)} %refs_2_.7, bf16[64,64,128]{2,1,0:T(8,128)(2,1)S(1)} %get-tuple-element.40.refs_3_, f32[8,128]{1,0:T(8,128)S(1)} %maximum_maximum_fusion.refs_4_, ...), custom_call_target="tpu_custom_call" | custom-call | flops 1610612736 | bytes 20971520 | tf_op jit(solution)/shard_map/sweep/pallas_call | solution.py:244
  35.5 5.0 %collective-permute-start.13 = (bf16[64,64,128]{2,1,0:T(8,128)(2,1)}, bf16[64,64,128]{2,1,0:T(8,128)(2,1)}, u32[]{:S(2)}, u32[]{:S(2)}) collective-permute-start(bf16[64,64,128]{2,1,0:T(8,128)(2,1)} %sweep.3.refs_5_), channel_id=1, source_target_pairs={{1,2},{2,1},{3,4},{4,3},{5,6},{6,5},{7,8},{8,7},{9,10},{10,9},{11,... | collective-permute-start | bytes 3145736 | tf_op jit(solution)/shard_map/ppermute | solution.py:407
  40.5 10.6 %sweep.2.refs_5_ = bf16[64,64,128]{2,1,0:T(8,128)(2,1)} custom-call(s32[1664]{0:T(1024)S(1)} %concatenate.17.refs_0_, bf16[64,64,1536]{2,1,0:T(8,128)(2,1)} %refs_1_.7, bf16[2,64,64,128]{3,2,1,0:T(8,128)(2,1)} %refs_2_.7, bf16[64,64,128]{2,1,0:T(8,128)(2,1)S(1)} %get-tuple-element.27.refs_3_, f32[8,128]{1,0:T(8,128)S(1)} %maximum_maximum_fusion.refs_4_, ...), custom_call_target="tpu_custom_call" | custom-call | flops 1610612736 | bytes 20971520 | tf_op jit(solution)/shard_map/sweep/pallas_call | solution.py:244
  51.2 4.2 %collective-permute-start.3 = (bf16[64,64,128]{2,1,0:T(8,128)(2,1)}, bf16[64,64,128]{2,1,0:T(8,128)(2,1)}, u32[]{:S(2)}, u32[]{:S(2)}) collective-permute-start(bf16[64,64,128]{2,1,0:T(8,128)(2,1)} %sweep.2.refs_5_), channel_id=1, source_target_pairs={{1,2},{2,1},{3,4},{4,3},{5,6},{6,5},{7,8},{8,7},{9,10},{10,9},{11,... | collective-permute-start | bytes 3145736 | tf_op jit(solution)/shard_map/ppermute | solution.py:407
  55.5 10.7 %sweep_last.3 = (bf16[32,64,128]{2,1,0:T(8,128)(2,1)}, bf16[32,64,128]{2,1,0:T(8,128)(2,1)}) custom-call(s32[1664]{0:T(1024)S(1)} %concatenate.17.refs_0_, bf16[64,64,1536]{2,1,0:T(8,128)(2,1)} %refs_1_.7, bf16[2,64,64,128]{3,2,1,0:T(8,128)(2,1)} %refs_2_.7, bf16[64,64,128]{2,1,0:T(8,128)(2,1)S(1)} %get-tuple-element.40.refs_3_, ...), custom_call_target="tpu_custom_call" | custom-call | flops 1610612736 | bytes 20971520 | tf_op jit(solution)/shard_map/sweep_last/pallas_call | solution.py:244
  67.6 3.6 %collective-permute-done.3.refs_7_ = bf16[64,64,128]{2,1,0:T(8,128)(2,1)} collective-permute-done((bf16[64,64,128]{2,1,0:T(8,128)(2,1)}, bf16[64,64,128]{2,1,0:T(8,128)(2,1)}, u32[]{:S(2)}, u32[]{:S(2)}) %collective-permute-start.3) | collective-permute-done | bytes 1048608 | tf_op jit(solution)/shard_map/ppermute | solution.py:407
  71.3 9.8 %sweep_last.2 = (bf16[32,64,128]{2,1,0:T(8,128)(2,1)S(1)}, bf16[32,64,128]{2,1,0:T(8,128)(2,1)S(1)}) custom-call(s32[1664]{0:T(1024)S(1)} %concatenate.17.refs_0_, bf16[64,64,1536]{2,1,0:T(8,128)(2,1)} %refs_1_.7, bf16[2,64,64,128]{3,2,1,0:T(8,128)(2,1)} %refs_2_.7, bf16[64,64,128]{2,1,0:T(8,128)(2,1)S(1)} %get-tuple-element.27.refs_3_, ...), custom_call_target="tpu_custom_call" | custom-call | flops 1610612736 | bytes 20971520 | tf_op jit(solution)/shard_map/sweep_last/pallas_call | solution.py:244
  84.6 5.4 %collective-permute-done.20 = bf16[128,128]{1,0:T(8,128)(2,1)S(1)} collective-permute-done((bf16[128,128]{1,0:T(8,128)(2,1)S(1)}, bf16[128,128]{1,0:T(8,128)(2,1)S(1)}, u32[]{:S(2)}, u32[]{:S(2)}) %collective-permute-start.20) | collective-permute-done | bytes 32800 | tf_op jit(solution)/shard_map/ppermute | solution.py:407
  90.2 4.1 %collective-permute-start.16 = (bf16[2048,128]{1,0:T(8,128)(2,1)}, bf16[2048,128]{1,0:T(8,128)(2,1)S(1)}, u32[]{:S(2)}, u32[]{:S(2)}) collective-permute-start(bf16[2048,128]{1,0:T(8,128)(2,1)} %bitcast.3.own_ref), channel_id=1, source_target_pairs={{0,96},{16,112},{32,64},{48,80},{64,32},{80,48},{96,0},{112,16},{1... | collective-permute-start | bytes 1572872 | tf_op jit(solution)/shard_map/ppermute | solution.py:407
  96.6 3.8 %collective-permute-done.22 = bf16[128,128]{1,0:T(8,128)(2,1)S(1)} collective-permute-done((bf16[128,128]{1,0:T(8,128)(2,1)S(1)}, bf16[128,128]{1,0:T(8,128)(2,1)S(1)}, u32[]{:S(2)}, u32[]{:S(2)}) %collective-permute-start.22) | collective-permute-done | bytes 32800 | tf_op jit(solution)/shard_map/ppermute | solution.py:407
  100.4 2.2 %collective-permute-start.23 = (bf16[128,128]{1,0:T(8,128)(2,1)S(1)}, bf16[128,128]{1,0:T(8,128)(2,1)S(1)}, u32[]{:S(2)}, u32[]{:S(2)}) collective-permute-start(bf16[128,128]{1,0:T(8,128)(2,1)S(1)} %add_convert_fusion.own_ref), channel_id=1, source_target_pairs={{0,16},{16,0},{32,48},{48,32},{64,80},{80,64},{96,112},{112,96},{1... | collective-permute-start | bytes 98312 | tf_op jit(solution)/shard_map/ppermute | solution.py:407
  113.2 3.4 %collective-permute-start.15 = (bf16[2048,128]{1,0:T(8,128)(2,1)S(1)}, bf16[2048,128]{1,0:T(8,128)(2,1)S(1)}, u32[]{:S(2)}, u32[]{:S(2)}) collective-permute-start(bf16[2048,128]{1,0:T(8,128)(2,1)S(1)} %get-tuple-element.44), channel_id=1, source_target_pairs={{0,96},{16,112},{32,64},{48,80},{64,32},{80,48},{96,0},{112,16},{1... | collective-permute-start | bytes 1572872 | tf_op jit(solution)/shard_map/ppermute | solution.py:407
  120.5 2.2 %collective-permute-start.8 = (bf16[2048,128]{1,0:T(8,128)(2,1)S(1)}, bf16[2048,128]{1,0:T(8,128)(2,1)S(1)}, u32[]{:S(2)}, u32[]{:S(2)}) collective-permute-start(bf16[2048,128]{1,0:T(8,128)(2,1)S(1)} %get-tuple-element.37), channel_id=1, source_target_pairs={{0,16},{16,0},{32,48},{48,32},{64,80},{80,64},{96,112},{112,96},{1... | collective-permute-start | bytes 1572872 | tf_op jit(solution)/shard_map/ppermute | solution.py:407
  124.4 3.3 %collective-permute-start.25 = (bf16[128,128]{0,1:T(8,128)(2,1)S(1)}, bf16[128,128]{0,1:T(8,128)(2,1)S(1)}, u32[]{:S(2)}, u32[]{:S(2)}) collective-permute-start(bf16[128,128]{0,1:T(8,128)(2,1)S(1)} %fusion.11), channel_id=1, source_target_pairs={{0,96},{16,112},{32,64},{48,80},{64,32},{80,48},{96,0},{112,16},{1... | collective-permute-start | bytes 98312 | tf_op jit(solution)/shard_map/ppermute | solution.py:407
  131.1 2.1 %collective-permute-start.18 = (bf16[2048,128]{1,0:T(8,128)(2,1)S(1)}, bf16[2048,128]{1,0:T(8,128)(2,1)S(1)}, u32[]{:S(2)}, u32[]{:S(2)}) collective-permute-start(bf16[2048,128]{1,0:T(8,128)(2,1)S(1)} %get-tuple-element.49), channel_id=1, source_target_pairs={{0,16},{16,0},{32,48},{48,32},{64,80},{80,64},{96,112},{112,96},{1... | collective-permute-start | bytes 1572872 | tf_op jit(solution)/shard_map/ppermute | solution.py:407
  133.2 2.2 %collective-permute-done.8.refs_1_.refs_3_ = bf16[2048,128]{1,0:T(8,128)(2,1)S(1)} collective-permute-done((bf16[2048,128]{1,0:T(8,128)(2,1)S(1)}, bf16[2048,128]{1,0:T(8,128)(2,1)S(1)}, u32[]{:S(2)}, u32[]{:S(2)}) %collective-permute-start.8) | collective-permute-done | bytes 524320 | tf_op jit(solution)/shard_map/ppermute | solution.py:407
  135.8 10.9 %collective-permute-done.5.refs_1_.refs_3_ = bf16[2048,128]{1,0:T(8,128)(2,1)S(1)} collective-permute-done((bf16[2048,128]{1,0:T(8,128)(2,1)S(1)}, bf16[2048,128]{1,0:T(8,128)(2,1)S(1)}, u32[]{:S(2)}, u32[]{:S(2)}) %collective-permute-start.5) | collective-permute-done | bytes 524320 | tf_op jit(solution)/shard_map/ppermute | solution.py:407
  147.6 3.2 %collective-permute-start.6 = (bf16[1024,128]{1,0:T(8,128)(2,1)}, bf16[1024,128]{1,0:T(8,128)(2,1)S(1)}, u32[]{:S(2)}, u32[]{:S(2)}) collective-permute-start(bf16[1024,128]{1,0:T(8,128)(2,1)} %get-tuple-element.34), channel_id=1, source_target_pairs={{0,96},{16,112},{32,64},{48,80},{64,32},{80,48},{96,0},{112,16},{1... | collective-permute-start | bytes 786440 | tf_op jit(solution)/shard_map/ppermute | solution.py:407
  151.7 3.7 %collective-permute-done.6.got1_ref = bf16[1024,128]{1,0:T(8,128)(2,1)S(1)} collective-permute-done((bf16[1024,128]{1,0:T(8,128)(2,1)}, bf16[1024,128]{1,0:T(8,128)(2,1)S(1)}, u32[]{:S(2)}, u32[]{:S(2)}) %collective-permute-start.6) | collective-permute-done | bytes 262176 | tf_op jit(solution)/shard_map/ppermute | solution.py:407
  155.4 2.9 %finish.1 = f32[1,2,2048,128]{3,2,1,0:T(8,128)} custom-call(f32[1024,128]{1,0:T(8,128)S(1)} %get-tuple-element.33.own1_ref, bf16[1024,128]{1,0:T(8,128)(2,1)S(1)} %collective-permute-done.6.got1_ref, f32[1024,128]{1,0:T(8,128)} %copy-done.2, bf16[1024,128]{1,0:T(8,128)(2,1)S(1)} %collective-permute-done.9.got2_ref, ...), custom_call_target="tpu_custom_call" | custom-call | tf_op jit(solution)/shard_map/finish/pallas_call | solution.py:371
  (108 shorter events, 35.6 us)
Async XLA Ops:
  4.7 15.7 %collective-permute-start.10 = (bf16[64,64,128]{2,1,0:T(8,128)(2,1)}, bf16[64,64,128]{2,1,0:T(8,128)(2,1)}, u32[]{:S(2)}, u32[]{:S(2)}) collective-permute-start(bf16[64,64,128]{2,1,0:T(8,128)(2,1)} %get-tuple-element.41.refs_5_), channel_id=1, source_target_pairs={{0,1},{1,0},{2,3},{3,2},{4,5},{5,4},{6,7},{7,6},{8,9},{9,8},{10,11... | collective-permute-start | bytes 3145736 | tf_op jit(solution)/shard_map/ppermute | solution.py:407
  4.7 20.0 %collective-permute-start.11 = (bf16[64,64,128]{2,1,0:T(8,128)(2,1)}, bf16[64,64,128]{2,1,0:T(8,128)(2,1)}, u32[]{:S(2)}, u32[]{:S(2)}) collective-permute-start(bf16[64,64,128]{2,1,0:T(8,128)(2,1)} %get-tuple-element.41.refs_5_), channel_id=1, source_target_pairs={{1,2},{2,1},{3,4},{4,3},{5,6},{6,5},{7,8},{8,7},{9,10},{10,9},{11,... | collective-permute-start | bytes 3145736 | tf_op jit(solution)/shard_map/ppermute | solution.py:407
  9.7 30.8 %collective-permute-start = (bf16[64,64,128]{2,1,0:T(8,128)(2,1)}, bf16[64,64,128]{2,1,0:T(8,128)(2,1)}, u32[]{:S(2)}, u32[]{:S(2)}) collective-permute-start(bf16[64,64,128]{2,1,0:T(8,128)(2,1)} %get-tuple-element.28.refs_5_), channel_id=1, source_target_pairs={{0,1},{1,0},{2,3},{3,2},{4,5},{5,4},{6,7},{7,6},{8,9},{9,8},{10,11... | collective-permute-start | bytes 3145736 | tf_op jit(solution)/shard_map/ppermute | solution.py:407
  9.8 30.7 %collective-permute-start.1 = (bf16[64,64,128]{2,1,0:T(8,128)(2,1)}, bf16[64,64,128]{2,1,0:T(8,128)(2,1)}, u32[]{:S(2)}, u32[]{:S(2)}) collective-permute-start(bf16[64,64,128]{2,1,0:T(8,128)(2,1)} %get-tuple-element.28.refs_5_), channel_id=1, source_target_pairs={{1,2},{2,1},{3,4},{4,3},{5,6},{6,5},{7,8},{8,7},{9,10},{10,9},{11,... | collective-permute-start | bytes 3145736 | tf_op jit(solution)/shard_map/ppermute | solution.py:407
  35.4 20.1 %collective-permute-start.12 = (bf16[64,64,128]{2,1,0:T(8,128)(2,1)}, bf16[64,64,128]{2,1,0:T(8,128)(2,1)}, u32[]{:S(2)}, u32[]{:S(2)}) collective-permute-start(bf16[64,64,128]{2,1,0:T(8,128)(2,1)} %sweep.3.refs_5_), channel_id=1, source_target_pairs={{0,1},{1,0},{2,3},{3,2},{4,5},{5,4},{6,7},{7,6},{8,9},{9,8},{10,11... | collective-permute-start | bytes 3145736 | tf_op jit(solution)/shard_map/ppermute | solution.py:407
  35.5 20.0 %collective-permute-start.13 = (bf16[64,64,128]{2,1,0:T(8,128)(2,1)}, bf16[64,64,128]{2,1,0:T(8,128)(2,1)}, u32[]{:S(2)}, u32[]{:S(2)}) collective-permute-start(bf16[64,64,128]{2,1,0:T(8,128)(2,1)} %sweep.3.refs_5_), channel_id=1, source_target_pairs={{1,2},{2,1},{3,4},{4,3},{5,6},{6,5},{7,8},{8,7},{9,10},{10,9},{11,... | collective-permute-start | bytes 3145736 | tf_op jit(solution)/shard_map/ppermute | solution.py:407
  51.1 16.5 %collective-permute-start.2 = (bf16[64,64,128]{2,1,0:T(8,128)(2,1)}, bf16[64,64,128]{2,1,0:T(8,128)(2,1)}, u32[]{:S(2)}, u32[]{:S(2)}) collective-permute-start(bf16[64,64,128]{2,1,0:T(8,128)(2,1)} %sweep.2.refs_5_), channel_id=1, source_target_pairs={{0,1},{1,0},{2,3},{3,2},{4,5},{5,4},{6,7},{7,6},{8,9},{9,8},{10,11... | collective-permute-start | bytes 3145736 | tf_op jit(solution)/shard_map/ppermute | solution.py:407
  51.2 20.0 %collective-permute-start.3 = (bf16[64,64,128]{2,1,0:T(8,128)(2,1)}, bf16[64,64,128]{2,1,0:T(8,128)(2,1)}, u32[]{:S(2)}, u32[]{:S(2)}) collective-permute-start(bf16[64,64,128]{2,1,0:T(8,128)(2,1)} %sweep.2.refs_5_), channel_id=1, source_target_pairs={{1,2},{2,1},{3,4},{4,3},{5,6},{6,5},{7,8},{8,7},{9,10},{10,9},{11,... | collective-permute-start | bytes 3145736 | tf_op jit(solution)/shard_map/ppermute | solution.py:407
  84.6 5.5 %collective-permute-start.20 = (bf16[128,128]{1,0:T(8,128)(2,1)S(1)}, bf16[128,128]{1,0:T(8,128)(2,1)S(1)}, u32[]{:S(2)}, u32[]{:S(2)}) collective-permute-start(bf16[128,128]{1,0:T(8,128)(2,1)S(1)} %get-tuple-element.56), channel_id=1, source_target_pairs={{0,8},{1,9},{2,10},{3,11},{4,12},{5,13},{6,14},{7,15},{8,0},{9,1},... | collective-permute-start | bytes 98312 | tf_op jit(solution)/shard_map/ppermute | solution.py:407
  90.1 6.2 %collective-permute-start.21 = (bf16[128,128]{1,0:T(8,128)(2,1)S(1)}, bf16[128,128]{1,0:T(8,128)(2,1)S(1)}, u32[]{:S(2)}, u32[]{:S(2)}) collective-permute-start(bf16[128,128]{1,0:T(8,128)(2,1)S(1)} %fusion.12), channel_id=1, source_target_pairs={{0,4},{1,5},{2,6},{3,7},{4,0},{5,1},{6,2},{7,3},{8,12},{9,13},{10,... | collective-permute-start | bytes 98312 | tf_op jit(solution)/shard_map/ppermute | solution.py:407
  90.2 17.1 %collective-permute-start.16 = (bf16[2048,128]{1,0:T(8,128)(2,1)}, bf16[2048,128]{1,0:T(8,128)(2,1)S(1)}, u32[]{:S(2)}, u32[]{:S(2)}) collective-permute-start(bf16[2048,128]{1,0:T(8,128)(2,1)} %bitcast.3.own_ref), channel_id=1, source_target_pairs={{0,96},{16,112},{32,64},{48,80},{64,32},{80,48},{96,0},{112,16},{1... | collective-permute-start | bytes 1572872 | tf_op jit(solution)/shard_map/ppermute | solution.py:407
  94.3 17.0 %collective-permute-start.14 = (bf16[2048,128]{1,0:T(8,128)(2,1)}, bf16[2048,128]{1,0:T(8,128)(2,1)}, u32[]{:S(2)}, u32[]{:S(2)}) collective-permute-start(bf16[2048,128]{1,0:T(8,128)(2,1)} %bitcast.2.own_ref), channel_id=1, source_target_pairs={{0,32},{16,48},{32,0},{48,16},{64,96},{80,112},{96,64},{112,80},{1... | collective-permute-start | bytes 1572872 | tf_op jit(solution)/shard_map/ppermute | solution.py:407
  94.3 24.3 %collective-permute-start.7 = (bf16[2048,128]{1,0:T(8,128)(2,1)S(1)}, bf16[2048,128]{1,0:T(8,128)(2,1)}, u32[]{:S(2)}, u32[]{:S(2)}) collective-permute-start(bf16[2048,128]{1,0:T(8,128)(2,1)S(1)} %bitcast.22), channel_id=1, source_target_pairs={{0,96},{16,112},{32,64},{48,80},{64,32},{80,48},{96,0},{112,16},{1... | collective-permute-start | bytes 1572872 | tf_op jit(solution)/shard_map/ppermute | solution.py:407
  94.8 27.9 %collective-permute-start.4 = (bf16[2048,128]{1,0:T(8,128)(2,1)S(1)}, bf16[2048,128]{1,0:T(8,128)(2,1)S(1)}, u32[]{:S(2)}, u32[]{:S(2)}) collective-permute-start(bf16[2048,128]{1,0:T(8,128)(2,1)S(1)} %bitcast.19), channel_id=1, source_target_pairs={{0,32},{16,48},{32,0},{48,16},{64,96},{80,112},{96,64},{112,80},{1... | collective-permute-start | bytes 1572872 | tf_op jit(solution)/shard_map/ppermute | solution.py:407
  105.4 18.3 %collective-permute-start.24 = (bf16[128,128]{0,1:T(8,128)(2,1)}, bf16[128,128]{0,1:T(8,128)(2,1)}, u32[]{:S(2)}, u32[]{:S(2)}) collective-permute-start(bf16[128,128]{0,1:T(8,128)(2,1)} %copy.21), channel_id=1, source_target_pairs={{0,32},{16,48},{32,0},{48,16},{64,96},{80,112},{96,64},{112,80},{1... | collective-permute-start | bytes 98312 | tf_op jit(solution)/shard_map/ppermute | solution.py:407
  111.0 19.6 %collective-permute-start.17 = (bf16[2048,128]{1,0:T(8,128)(2,1)S(1)}, bf16[2048,128]{1,0:T(8,128)(2,1)S(1)}, u32[]{:S(2)}, u32[]{:S(2)}) collective-permute-start(bf16[2048,128]{1,0:T(8,128)(2,1)S(1)} %get-tuple-element.47), channel_id=1, source_target_pairs={{0,32},{16,48},{32,0},{48,16},{64,96},{80,112},{96,64},{112,80},{1... | collective-permute-start | bytes 1572872 | tf_op jit(solution)/shard_map/ppermute | solution.py:407
  113.2 17.3 %collective-permute-start.15 = (bf16[2048,128]{1,0:T(8,128)(2,1)S(1)}, bf16[2048,128]{1,0:T(8,128)(2,1)S(1)}, u32[]{:S(2)}, u32[]{:S(2)}) collective-permute-start(bf16[2048,128]{1,0:T(8,128)(2,1)S(1)} %get-tuple-element.44), channel_id=1, source_target_pairs={{0,96},{16,112},{32,64},{48,80},{64,32},{80,48},{96,0},{112,16},{1... | collective-permute-start | bytes 1572872 | tf_op jit(solution)/shard_map/ppermute | solution.py:407
  120.5 15.0 %collective-permute-start.8 = (bf16[2048,128]{1,0:T(8,128)(2,1)S(1)}, bf16[2048,128]{1,0:T(8,128)(2,1)S(1)}, u32[]{:S(2)}, u32[]{:S(2)}) collective-permute-start(bf16[2048,128]{1,0:T(8,128)(2,1)S(1)} %get-tuple-element.37), channel_id=1, source_target_pairs={{0,16},{16,0},{32,48},{48,32},{64,80},{80,64},{96,112},{112,96},{1... | collective-permute-start | bytes 1572872 | tf_op jit(solution)/shard_map/ppermute | solution.py:407
  123.5 23.1 %collective-permute-start.5 = (bf16[2048,128]{1,0:T(8,128)(2,1)S(1)}, bf16[2048,128]{1,0:T(8,128)(2,1)S(1)}, u32[]{:S(2)}, u32[]{:S(2)}) collective-permute-start(bf16[2048,128]{1,0:T(8,128)(2,1)S(1)} %get-tuple-element.32), channel_id=1, source_target_pairs={{0,16},{16,0},{32,48},{48,32},{64,80},{80,64},{96,112},{112,96},{1... | collective-permute-start | bytes 1572872 | tf_op jit(solution)/shard_map/ppermute | solution.py:407
  124.4 5.2 %collective-permute-start.25 = (bf16[128,128]{0,1:T(8,128)(2,1)S(1)}, bf16[128,128]{0,1:T(8,128)(2,1)S(1)}, u32[]{:S(2)}, u32[]{:S(2)}) collective-permute-start(bf16[128,128]{0,1:T(8,128)(2,1)S(1)} %fusion.11), channel_id=1, source_target_pairs={{0,96},{16,112},{32,64},{48,80},{64,32},{80,48},{96,0},{112,16},{1... | collective-permute-start | bytes 98312 | tf_op jit(solution)/shard_map/ppermute | solution.py:407
  130.4 20.4 %collective-permute-start.26 = (f32[128,128]{0,1:T(8,128)S(1)}, f32[128,128]{0,1:T(8,128)S(1)}, u32[]{:S(2)}, u32[]{:S(2)}) collective-permute-start(f32[128,128]{0,1:T(8,128)S(1)} %convert_add_fusion), channel_id=1, source_target_pairs={{0,1},{1,0},{2,3},{3,2},{4,5},{5,4},{6,7},{7,6},{8,9},{9,8},{10,11... | collective-permute-start | bytes 196616 | tf_op jit(solution)/shard_map/ppermute | solution.py:407
  131.1 24.2 %collective-permute-start.18 = (bf16[2048,128]{1,0:T(8,128)(2,1)S(1)}, bf16[2048,128]{1,0:T(8,128)(2,1)S(1)}, u32[]{:S(2)}, u32[]{:S(2)}) collective-permute-start(bf16[2048,128]{1,0:T(8,128)(2,1)S(1)} %get-tuple-element.49), channel_id=1, source_target_pairs={{0,16},{16,0},{32,48},{48,32},{64,80},{80,64},{96,112},{112,96},{1... | collective-permute-start | bytes 1572872 | tf_op jit(solution)/shard_map/ppermute | solution.py:407
  135.7 16.0 %collective-permute-start.9 = (bf16[1024,128]{1,0:T(8,128)(2,1)S(1)}, bf16[1024,128]{1,0:T(8,128)(2,1)S(1)}, u32[]{:S(2)}, u32[]{:S(2)}) collective-permute-start(bf16[1024,128]{1,0:T(8,128)(2,1)S(1)} %get-tuple-element.39), channel_id=1, source_target_pairs={{0,32},{16,48},{32,0},{48,16},{64,96},{80,112},{96,64},{112,80},{1... | collective-permute-start | bytes 786440 | tf_op jit(solution)/shard_map/ppermute | solution.py:407
  147.6 7.8 %collective-permute-start.6 = (bf16[1024,128]{1,0:T(8,128)(2,1)}, bf16[1024,128]{1,0:T(8,128)(2,1)S(1)}, u32[]{:S(2)}, u32[]{:S(2)}) collective-permute-start(bf16[1024,128]{1,0:T(8,128)(2,1)} %get-tuple-element.34), channel_id=1, source_target_pairs={{0,96},{16,112},{32,64},{48,80},{64,32},{80,48},{96,0},{112,16},{1... | collective-permute-start | bytes 786440 | tf_op jit(solution)/shard_map/ppermute | solution.py:407
  (13 other events, 81.4 us)

commit v10 on v9

--- a/solution.py
+++ b/solution.py
@@ -439,7 +439,7 @@
             (0, (mine, mirror), (other, pair ^ 1, mine, pair)),
             (1, (mine, pair), (mirror, mirror ^ 1, mine, other)),
             (1, (mine, mirror), (pair, pair ^ 1, mine, other)),
-            (1, (mine, other), (pair, by_mirror(pair), mine, mirror)),
+            (1, (mine, other), (mirror, by_pair(mirror), mine, pair)),
         ),
     )
     *rhs_units, weights = spread(rhs, coefs)
@@ -502,8 +502,8 @@
     gram = gram.astype(BF16)
     peer = swap(gram, "quad", by_x)
     send_g, keep_g = combine(gram, peer, weights, 4, LANES, F32)
-    gram_sum = keep_g + swap(send_g, "quad", by_pair).astype(F32)
-    gram_got = swap(gram_sum.astype(BF16), "quad", by_mirror)
+    gram_sum = keep_g + swap(send_g, "quad", by_mirror).astype(F32)
+    gram_got = swap(gram_sum.astype(BF16), "quad", by_pair)
     gram_own = gram_sum + jnp.roll(gram_got, HALF, axis=1).astype(F32)
     gram_other = swap(gram_own, "row", near_row)
     gram_a = jnp.where(even, gram_own, gram_other)

time: 160 us -> 160 us (level)
  starting transfers between devices: 43.3 us -> 40.6 us
  waiting for transfers between devices: 41.7 us -> 44.4 us
    ppermute x27, starting transfers between devices: 43.3 us -> 40.6 us  [swap(): lax.ppermute(x, axis, [(i, j) for i, j in peers if 0 <= j < len(peers)])]
    ppermute x27, waiting for transfers between devices: 41.7 us -> 44.4 us  [swap(): lax.ppermute(x, axis, [(i, j) for i, j in peers if 0 <= j < len(peers)])]
  transfers between devices with their start and end apart: 27 -> 27, of which waited for: 13 -> 12; matrix products, arithmetic and copies ran while one was open for 4% -> 4% of each run, Pallas kernels for 27% -> 27%
where the time goes in v10:
time: 160 us; the launch traced here: 158 us
  Pallas kernels  59 us (37%)
  waiting for transfers between devices  44.4 us (28%)
  starting transfers between devices  40.6 us (25%)
  local copies, waits for them, and re-layouts  6.46 us (4%)
  matrix products  3.46 us (2%)
  other arithmetic  3.11 us (2%)
    ppermute x27, waiting for transfers between devices, swap(): lax.ppermute(x, axis, [(i, j) for i, j in peers if 0 <= j < len(peers)])  44.4 us
    pallas_call x4, Pallas kernels, sweep(): pl.pallas_call(kernel, grid_spec=pltpu.PrefetchScalarGridSpec(num_scalar_...  41.7 us
    ppermute x27, starting transfers between devices, swap(): lax.ppermute(x, axis, [(i, j) for i, j in peers if 0 <= j < len(peers)])  40.6 us
    pallas_call x5, Pallas kernels, combine(): pl.pallas_call(combine_kernel, grid=(rows // rows_step,), in_specs=[row_s...  6.73 us
    unnamed x21, local copies, waits for them, and re-layouts  5.39 us
    pallas_call x1, Pallas kernels, initial(): pl.pallas_call(init_kernel, grid=(RB // FIRST,), in_specs=[pl.BlockSpec((...  4.06 us
    dot_general x4, matrix products, step(): lax.dot_general(x, part, (((0,), (0,)), ((), ())), preferred_element_type...  3.46 us
  transfers between devices with their start and end apart: 27, of which 12 were waited for; matrix products, arithmetic and copies ran while one was open for 4% of the time, Pallas kernels for 27%

profile of v10, /device:TPU:4, one launch (start us, length us, event | category | flops | bytes accessed | tf_op | source)
XLA Modules:
  0.0 158.3 jit_solution(4031940333103873423)
XLA Ops:
  0.7 4.1 %initial.1 = (bf16[64,64,128]{2,1,0:T(8,128)(2,1)}, bf16[64,64,128]{2,1,0:T(8,128)(2,1)}) custom-call(bf16[4096,128]{1,0:T(8,128)(2,1)} %x_ref.3, bf16[2,64,64,128]{3,2,1,0:T(8,128)(2,1)} %refs_2_.7, bf16[256,256]{1,0:T(8,128)(2,1)} %constant.303.clone.map_ref), custom_call_target="tpu_custom_call" | custom-call | tf_op jit(solution)/shard_map/initial/pallas_call | solution.py:83
  4.7 5.0 %collective-permute-start.11 = (bf16[64,64,128]{2,1,0:T(8,128)(2,1)}, bf16[64,64,128]{2,1,0:T(8,128)(2,1)}, u32[]{:S(2)}, u32[]{:S(2)}) collective-permute-start(bf16[64,64,128]{2,1,0:T(8,128)(2,1)} %get-tuple-element.41.refs_5_), channel_id=1, source_target_pairs={{1,2},{2,1},{3,4},{4,3},{5,6},{6,5},{7,8},{8,7},{9,10},{10,9},{11,... | collective-permute-start | bytes 3145736 | tf_op jit(solution)/shard_map/ppermute | solution.py:407
  9.8 4.2 %collective-permute-start.1 = (bf16[64,64,128]{2,1,0:T(8,128)(2,1)}, bf16[64,64,128]{2,1,0:T(8,128)(2,1)}, u32[]{:S(2)}, u32[]{:S(2)}) collective-permute-start(bf16[64,64,128]{2,1,0:T(8,128)(2,1)} %get-tuple-element.28.refs_5_), channel_id=1, source_target_pairs={{1,2},{2,1},{3,4},{4,3},{5,6},{6,5},{7,8},{8,7},{9,10},{10,9},{11,... | collective-permute-start | bytes 3145736 | tf_op jit(solution)/shard_map/ppermute | solution.py:407
  20.4 4.3 %collective-permute-done.11.refs_7_ = bf16[64,64,128]{2,1,0:T(8,128)(2,1)} collective-permute-done((bf16[64,64,128]{2,1,0:T(8,128)(2,1)}, bf16[64,64,128]{2,1,0:T(8,128)(2,1)}, u32[]{:S(2)}, u32[]{:S(2)}) %collective-permute-start.11) | collective-permute-done | bytes 1048608 | tf_op jit(solution)/shard_map/ppermute | solution.py:407
  24.8 10.6 %sweep.3.refs_5_ = bf16[64,64,128]{2,1,0:T(8,128)(2,1)} custom-call(s32[1664]{0:T(1024)S(1)} %concatenate.17.refs_0_, bf16[64,64,1536]{2,1,0:T(8,128)(2,1)} %refs_1_.7, bf16[2,64,64,128]{3,2,1,0:T(8,128)(2,1)} %refs_2_.7, bf16[64,64,128]{2,1,0:T(8,128)(2,1)S(1)} %get-tuple-element.40.refs_3_, f32[8,128]{1,0:T(8,128)S(1)} %maximum_maximum_fusion.refs_4_, ...), custom_call_target="tpu_custom_call" | custom-call | flops 1610612736 | bytes 20971520 | tf_op jit(solution)/shard_map/sweep/pallas_call | solution.py:244
  35.5 5.0 %collective-permute-start.13 = (bf16[64,64,128]{2,1,0:T(8,128)(2,1)}, bf16[64,64,128]{2,1,0:T(8,128)(2,1)}, u32[]{:S(2)}, u32[]{:S(2)}) collective-permute-start(bf16[64,64,128]{2,1,0:T(8,128)(2,1)} %sweep.3.refs_5_), channel_id=1, source_target_pairs={{1,2},{2,1},{3,4},{4,3},{5,6},{6,5},{7,8},{8,7},{9,10},{10,9},{11,... | collective-permute-start | bytes 3145736 | tf_op jit(solution)/shard_map/ppermute | solution.py:407
  40.5 10.6 %sweep.2.refs_5_ = bf16[64,64,128]{2,1,0:T(8,128)(2,1)} custom-call(s32[1664]{0:T(1024)S(1)} %concatenate.17.refs_0_, bf16[64,64,1536]{2,1,0:T(8,128)(2,1)} %refs_1_.7, bf16[2,64,64,128]{3,2,1,0:T(8,128)(2,1)} %refs_2_.7, bf16[64,64,128]{2,1,0:T(8,128)(2,1)S(1)} %get-tuple-element.27.refs_3_, f32[8,128]{1,0:T(8,128)S(1)} %maximum_maximum_fusion.refs_4_, ...), custom_call_target="tpu_custom_call" | custom-call | flops 1610612736 | bytes 20971520 | tf_op jit(solution)/shard_map/sweep/pallas_call | solution.py:244
  51.2 4.2 %collective-permute-start.3 = (bf16[64,64,128]{2,1,0:T(8,128)(2,1)}, bf16[64,64,128]{2,1,0:T(8,128)(2,1)}, u32[]{:S(2)}, u32[]{:S(2)}) collective-permute-start(bf16[64,64,128]{2,1,0:T(8,128)(2,1)} %sweep.2.refs_5_), channel_id=1, source_target_pairs={{1,2},{2,1},{3,4},{4,3},{5,6},{6,5},{7,8},{8,7},{9,10},{10,9},{11,... | collective-permute-start | bytes 3145736 | tf_op jit(solution)/shard_map/ppermute | solution.py:407
  55.5 10.7 %sweep_last.3 = (bf16[32,64,128]{2,1,0:T(8,128)(2,1)}, bf16[32,64,128]{2,1,0:T(8,128)(2,1)}) custom-call(s32[1664]{0:T(1024)S(1)} %concatenate.17.refs_0_, bf16[64,64,1536]{2,1,0:T(8,128)(2,1)} %refs_1_.7, bf16[2,64,64,128]{3,2,1,0:T(8,128)(2,1)} %refs_2_.7, bf16[64,64,128]{2,1,0:T(8,128)(2,1)S(1)} %get-tuple-element.40.refs_3_, ...), custom_call_target="tpu_custom_call" | custom-call | flops 1610612736 | bytes 20971520 | tf_op jit(solution)/shard_map/sweep_last/pallas_call | solution.py:244
  67.6 3.6 %collective-permute-done.3.refs_7_ = bf16[64,64,128]{2,1,0:T(8,128)(2,1)} collective-permute-done((bf16[64,64,128]{2,1,0:T(8,128)(2,1)}, bf16[64,64,128]{2,1,0:T(8,128)(2,1)}, u32[]{:S(2)}, u32[]{:S(2)}) %collective-permute-start.3) | collective-permute-done | bytes 1048608 | tf_op jit(solution)/shard_map/ppermute | solution.py:407
  71.3 9.8 %sweep_last.2 = (bf16[32,64,128]{2,1,0:T(8,128)(2,1)S(1)}, bf16[32,64,128]{2,1,0:T(8,128)(2,1)S(1)}) custom-call(s32[1664]{0:T(1024)S(1)} %concatenate.17.refs_0_, bf16[64,64,1536]{2,1,0:T(8,128)(2,1)} %refs_1_.7, bf16[2,64,64,128]{3,2,1,0:T(8,128)(2,1)} %refs_2_.7, bf16[64,64,128]{2,1,0:T(8,128)(2,1)S(1)} %get-tuple-element.27.refs_3_, ...), custom_call_target="tpu_custom_call" | custom-call | flops 1610612736 | bytes 20971520 | tf_op jit(solution)/shard_map/sweep_last/pallas_call | solution.py:244
  84.6 5.4 %collective-permute-done.20 = bf16[128,128]{1,0:T(8,128)(2,1)S(1)} collective-permute-done((bf16[128,128]{1,0:T(8,128)(2,1)S(1)}, bf16[128,128]{1,0:T(8,128)(2,1)S(1)}, u32[]{:S(2)}, u32[]{:S(2)}) %collective-permute-start.20) | collective-permute-done | bytes 32800 | tf_op jit(solution)/shard_map/ppermute | solution.py:407
  90.2 4.1 %collective-permute-start.16 = (bf16[2048,128]{1,0:T(8,128)(2,1)}, bf16[2048,128]{1,0:T(8,128)(2,1)S(1)}, u32[]{:S(2)}, u32[]{:S(2)}) collective-permute-start(bf16[2048,128]{1,0:T(8,128)(2,1)} %bitcast.3.own_ref), channel_id=1, source_target_pairs={{0,96},{16,112},{32,64},{48,80},{64,32},{80,48},{96,0},{112,16},{1... | collective-permute-start | bytes 1572872 | tf_op jit(solution)/shard_map/ppermute | solution.py:407
  96.6 3.8 %collective-permute-done.22 = bf16[128,128]{1,0:T(8,128)(2,1)S(1)} collective-permute-done((bf16[128,128]{1,0:T(8,128)(2,1)S(1)}, bf16[128,128]{1,0:T(8,128)(2,1)S(1)}, u32[]{:S(2)}, u32[]{:S(2)}) %collective-permute-start.22) | collective-permute-done | bytes 32800 | tf_op jit(solution)/shard_map/ppermute | solution.py:407
  100.4 2.2 %collective-permute-start.23 = (bf16[128,128]{1,0:T(8,128)(2,1)S(1)}, bf16[128,128]{1,0:T(8,128)(2,1)S(1)}, u32[]{:S(2)}, u32[]{:S(2)}) collective-permute-start(bf16[128,128]{1,0:T(8,128)(2,1)S(1)} %add_convert_fusion.own_ref), channel_id=1, source_target_pairs={{0,16},{16,0},{32,48},{48,32},{64,80},{80,64},{96,112},{112,96},{1... | collective-permute-start | bytes 98312 | tf_op jit(solution)/shard_map/ppermute | solution.py:407
  105.4 3.3 %collective-permute-start.24 = (bf16[128,128]{0,1:T(8,128)(2,1)}, bf16[128,128]{0,1:T(8,128)(2,1)}, u32[]{:S(2)}, u32[]{:S(2)}) collective-permute-start(bf16[128,128]{0,1:T(8,128)(2,1)} %copy.21), channel_id=1, source_target_pairs={{0,96},{16,112},{32,64},{48,80},{64,32},{80,48},{96,0},{112,16},{1... | collective-permute-start | bytes 98312 | tf_op jit(solution)/shard_map/ppermute | solution.py:407
  116.3 2.3 %collective-permute-done.7.peer_ref = bf16[2048,128]{1,0:T(8,128)(2,1)} collective-permute-done((bf16[2048,128]{1,0:T(8,128)(2,1)S(1)}, bf16[2048,128]{1,0:T(8,128)(2,1)}, u32[]{:S(2)}, u32[]{:S(2)}) %collective-permute-start.7) | collective-permute-done | bytes 524320 | tf_op jit(solution)/shard_map/ppermute | solution.py:407
  120.5 2.2 %collective-permute-start.8 = (bf16[2048,128]{1,0:T(8,128)(2,1)S(1)}, bf16[2048,128]{1,0:T(8,128)(2,1)S(1)}, u32[]{:S(2)}, u32[]{:S(2)}) collective-permute-start(bf16[2048,128]{1,0:T(8,128)(2,1)S(1)} %get-tuple-element.37), channel_id=1, source_target_pairs={{0,16},{16,0},{32,48},{48,32},{64,80},{80,64},{96,112},{112,96},{1... | collective-permute-start | bytes 1572872 | tf_op jit(solution)/shard_map/ppermute | solution.py:407
  124.5 5.7 %collective-permute-done.25 = bf16[128,128]{0,1:T(8,128)(2,1)S(1)} collective-permute-done((bf16[128,128]{0,1:T(8,128)(2,1)S(1)}, bf16[128,128]{0,1:T(8,128)(2,1)S(1)}, u32[]{:S(2)}, u32[]{:S(2)}) %collective-permute-start.25) | collective-permute-done | bytes 32800 | tf_op jit(solution)/shard_map/ppermute | solution.py:407
  131.7 2.2 %collective-permute-start.18 = (bf16[2048,128]{1,0:T(8,128)(2,1)S(1)}, bf16[2048,128]{1,0:T(8,128)(2,1)S(1)}, u32[]{:S(2)}, u32[]{:S(2)}) collective-permute-start(bf16[2048,128]{1,0:T(8,128)(2,1)S(1)} %get-tuple-element.49), channel_id=1, source_target_pairs={{0,16},{16,0},{32,48},{48,32},{64,80},{80,64},{96,112},{112,96},{1... | collective-permute-start | bytes 1572872 | tf_op jit(solution)/shard_map/ppermute | solution.py:407
  135.8 10.9 %collective-permute-done.5.refs_1_.refs_3_ = bf16[2048,128]{1,0:T(8,128)(2,1)S(1)} collective-permute-done((bf16[2048,128]{1,0:T(8,128)(2,1)S(1)}, bf16[2048,128]{1,0:T(8,128)(2,1)S(1)}, u32[]{:S(2)}, u32[]{:S(2)}) %collective-permute-start.5) | collective-permute-done | bytes 524320 | tf_op jit(solution)/shard_map/ppermute | solution.py:407
  147.6 3.2 %collective-permute-start.6 = (bf16[1024,128]{1,0:T(8,128)(2,1)}, bf16[1024,128]{1,0:T(8,128)(2,1)S(1)}, u32[]{:S(2)}, u32[]{:S(2)}) collective-permute-start(bf16[1024,128]{1,0:T(8,128)(2,1)} %get-tuple-element.34), channel_id=1, source_target_pairs={{0,96},{16,112},{32,64},{48,80},{64,32},{80,48},{96,0},{112,16},{1... | collective-permute-start | bytes 786440 | tf_op jit(solution)/shard_map/ppermute | solution.py:407
  151.7 3.7 %collective-permute-done.6.got1_ref = bf16[1024,128]{1,0:T(8,128)(2,1)S(1)} collective-permute-done((bf16[1024,128]{1,0:T(8,128)(2,1)}, bf16[1024,128]{1,0:T(8,128)(2,1)S(1)}, u32[]{:S(2)}, u32[]{:S(2)}) %collective-permute-start.6) | collective-permute-done | bytes 262176 | tf_op jit(solution)/shard_map/ppermute | solution.py:407
  155.4 2.9 %finish.1 = f32[1,2,2048,128]{3,2,1,0:T(8,128)} custom-call(f32[1024,128]{1,0:T(8,128)S(1)} %get-tuple-element.33.own1_ref, bf16[1024,128]{1,0:T(8,128)(2,1)S(1)} %collective-permute-done.6.got1_ref, f32[1024,128]{1,0:T(8,128)} %copy-done.2, bf16[1024,128]{1,0:T(8,128)(2,1)S(1)} %collective-permute-done.9.got2_ref, ...), custom_call_target="tpu_custom_call" | custom-call | tf_op jit(solution)/shard_map/finish/pallas_call | solution.py:371
  (108 shorter events, 33.1 us)
Async XLA Ops:
  4.7 15.7 %collective-permute-start.10 = (bf16[64,64,128]{2,1,0:T(8,128)(2,1)}, bf16[64,64,128]{2,1,0:T(8,128)(2,1)}, u32[]{:S(2)}, u32[]{:S(2)}) collective-permute-start(bf16[64,64,128]{2,1,0:T(8,128)(2,1)} %get-tuple-element.41.refs_5_), channel_id=1, source_target_pairs={{0,1},{1,0},{2,3},{3,2},{4,5},{5,4},{6,7},{7,6},{8,9},{9,8},{10,11... | collective-permute-start | bytes 3145736 | tf_op jit(solution)/shard_map/ppermute | solution.py:407
  4.7 20.0 %collective-permute-start.11 = (bf16[64,64,128]{2,1,0:T(8,128)(2,1)}, bf16[64,64,128]{2,1,0:T(8,128)(2,1)}, u32[]{:S(2)}, u32[]{:S(2)}) collective-permute-start(bf16[64,64,128]{2,1,0:T(8,128)(2,1)} %get-tuple-element.41.refs_5_), channel_id=1, source_target_pairs={{1,2},{2,1},{3,4},{4,3},{5,6},{6,5},{7,8},{8,7},{9,10},{10,9},{11,... | collective-permute-start | bytes 3145736 | tf_op jit(solution)/shard_map/ppermute | solution.py:407
  9.7 30.8 %collective-permute-start = (bf16[64,64,128]{2,1,0:T(8,128)(2,1)}, bf16[64,64,128]{2,1,0:T(8,128)(2,1)}, u32[]{:S(2)}, u32[]{:S(2)}) collective-permute-start(bf16[64,64,128]{2,1,0:T(8,128)(2,1)} %get-tuple-element.28.refs_5_), channel_id=1, source_target_pairs={{0,1},{1,0},{2,3},{3,2},{4,5},{5,4},{6,7},{7,6},{8,9},{9,8},{10,11... | collective-permute-start | bytes 3145736 | tf_op jit(solution)/shard_map/ppermute | solution.py:407
  9.8 30.7 %collective-permute-start.1 = (bf16[64,64,128]{2,1,0:T(8,128)(2,1)}, bf16[64,64,128]{2,1,0:T(8,128)(2,1)}, u32[]{:S(2)}, u32[]{:S(2)}) collective-permute-start(bf16[64,64,128]{2,1,0:T(8,128)(2,1)} %get-tuple-element.28.refs_5_), channel_id=1, source_target_pairs={{1,2},{2,1},{3,4},{4,3},{5,6},{6,5},{7,8},{8,7},{9,10},{10,9},{11,... | collective-permute-start | bytes 3145736 | tf_op jit(solution)/shard_map/ppermute | solution.py:407
  35.4 20.1 %collective-permute-start.12 = (bf16[64,64,128]{2,1,0:T(8,128)(2,1)}, bf16[64,64,128]{2,1,0:T(8,128)(2,1)}, u32[]{:S(2)}, u32[]{:S(2)}) collective-permute-start(bf16[64,64,128]{2,1,0:T(8,128)(2,1)} %sweep.3.refs_5_), channel_id=1, source_target_pairs={{0,1},{1,0},{2,3},{3,2},{4,5},{5,4},{6,7},{7,6},{8,9},{9,8},{10,11... | collective-permute-start | bytes 3145736 | tf_op jit(solution)/shard_map/ppermute | solution.py:407
  35.5 20.0 %collective-permute-start.13 = (bf16[64,64,128]{2,1,0:T(8,128)(2,1)}, bf16[64,64,128]{2,1,0:T(8,128)(2,1)}, u32[]{:S(2)}, u32[]{:S(2)}) collective-permute-start(bf16[64,64,128]{2,1,0:T(8,128)(2,1)} %sweep.3.refs_5_), channel_id=1, source_target_pairs={{1,2},{2,1},{3,4},{4,3},{5,6},{6,5},{7,8},{8,7},{9,10},{10,9},{11,... | collective-permute-start | bytes 3145736 | tf_op jit(solution)/shard_map/ppermute | solution.py:407
  51.1 16.5 %collective-permute-start.2 = (bf16[64,64,128]{2,1,0:T(8,128)(2,1)}, bf16[64,64,128]{2,1,0:T(8,128)(2,1)}, u32[]{:S(2)}, u32[]{:S(2)}) collective-permute-start(bf16[64,64,128]{2,1,0:T(8,128)(2,1)} %sweep.2.refs_5_), channel_id=1, source_target_pairs={{0,1},{1,0},{2,3},{3,2},{4,5},{5,4},{6,7},{7,6},{8,9},{9,8},{10,11... | collective-permute-start | bytes 3145736 | tf_op jit(solution)/shard_map/ppermute | solution.py:407
  51.2 20.0 %collective-permute-start.3 = (bf16[64,64,128]{2,1,0:T(8,128)(2,1)}, bf16[64,64,128]{2,1,0:T(8,128)(2,1)}, u32[]{:S(2)}, u32[]{:S(2)}) collective-permute-start(bf16[64,64,128]{2,1,0:T(8,128)(2,1)} %sweep.2.refs_5_), channel_id=1, source_target_pairs={{1,2},{2,1},{3,4},{4,3},{5,6},{6,5},{7,8},{8,7},{9,10},{10,9},{11,... | collective-permute-start | bytes 3145736 | tf_op jit(solution)/shard_map/ppermute | solution.py:407
  84.6 5.5 %collective-permute-start.20 = (bf16[128,128]{1,0:T(8,128)(2,1)S(1)}, bf16[128,128]{1,0:T(8,128)(2,1)S(1)}, u32[]{:S(2)}, u32[]{:S(2)}) collective-permute-start(bf16[128,128]{1,0:T(8,128)(2,1)S(1)} %get-tuple-element.56), channel_id=1, source_target_pairs={{0,8},{1,9},{2,10},{3,11},{4,12},{5,13},{6,14},{7,15},{8,0},{9,1},... | collective-permute-start | bytes 98312 | tf_op jit(solution)/shard_map/ppermute | solution.py:407
  90.1 6.2 %collective-permute-start.21 = (bf16[128,128]{1,0:T(8,128)(2,1)S(1)}, bf16[128,128]{1,0:T(8,128)(2,1)S(1)}, u32[]{:S(2)}, u32[]{:S(2)}) collective-permute-start(bf16[128,128]{1,0:T(8,128)(2,1)S(1)} %fusion.12), channel_id=1, source_target_pairs={{0,4},{1,5},{2,6},{3,7},{4,0},{5,1},{6,2},{7,3},{8,12},{9,13},{10,... | collective-permute-start | bytes 98312 | tf_op jit(solution)/shard_map/ppermute | solution.py:407
  90.2 18.6 %collective-permute-start.16 = (bf16[2048,128]{1,0:T(8,128)(2,1)}, bf16[2048,128]{1,0:T(8,128)(2,1)S(1)}, u32[]{:S(2)}, u32[]{:S(2)}) collective-permute-start(bf16[2048,128]{1,0:T(8,128)(2,1)} %bitcast.3.own_ref), channel_id=1, source_target_pairs={{0,96},{16,112},{32,64},{48,80},{64,32},{80,48},{96,0},{112,16},{1... | collective-permute-start | bytes 1572872 | tf_op jit(solution)/shard_map/ppermute | solution.py:407
  94.3 18.3 %collective-permute-start.14 = (bf16[2048,128]{1,0:T(8,128)(2,1)}, bf16[2048,128]{1,0:T(8,128)(2,1)}, u32[]{:S(2)}, u32[]{:S(2)}) collective-permute-start(bf16[2048,128]{1,0:T(8,128)(2,1)} %bitcast.2.own_ref), channel_id=1, source_target_pairs={{0,32},{16,48},{32,0},{48,16},{64,96},{80,112},{96,64},{112,80},{1... | collective-permute-start | bytes 1572872 | tf_op jit(solution)/shard_map/ppermute | solution.py:407
  94.3 24.3 %collective-permute-start.7 = (bf16[2048,128]{1,0:T(8,128)(2,1)S(1)}, bf16[2048,128]{1,0:T(8,128)(2,1)}, u32[]{:S(2)}, u32[]{:S(2)}) collective-permute-start(bf16[2048,128]{1,0:T(8,128)(2,1)S(1)} %bitcast.22), channel_id=1, source_target_pairs={{0,96},{16,112},{32,64},{48,80},{64,32},{80,48},{96,0},{112,16},{1... | collective-permute-start | bytes 1572872 | tf_op jit(solution)/shard_map/ppermute | solution.py:407
  94.8 27.9 %collective-permute-start.4 = (bf16[2048,128]{1,0:T(8,128)(2,1)S(1)}, bf16[2048,128]{1,0:T(8,128)(2,1)S(1)}, u32[]{:S(2)}, u32[]{:S(2)}) collective-permute-start(bf16[2048,128]{1,0:T(8,128)(2,1)S(1)} %bitcast.19), channel_id=1, source_target_pairs={{0,32},{16,48},{32,0},{48,16},{64,96},{80,112},{96,64},{112,80},{1... | collective-permute-start | bytes 1572872 | tf_op jit(solution)/shard_map/ppermute | solution.py:407
  105.4 18.3 %collective-permute-start.24 = (bf16[128,128]{0,1:T(8,128)(2,1)}, bf16[128,128]{0,1:T(8,128)(2,1)}, u32[]{:S(2)}, u32[]{:S(2)}) collective-permute-start(bf16[128,128]{0,1:T(8,128)(2,1)} %copy.21), channel_id=1, source_target_pairs={{0,96},{16,112},{32,64},{48,80},{64,32},{80,48},{96,0},{112,16},{1... | collective-permute-start | bytes 98312 | tf_op jit(solution)/shard_map/ppermute | solution.py:407
  112.4 18.6 %collective-permute-start.17 = (bf16[2048,128]{1,0:T(8,128)(2,1)S(1)}, bf16[2048,128]{1,0:T(8,128)(2,1)S(1)}, u32[]{:S(2)}, u32[]{:S(2)}) collective-permute-start(bf16[2048,128]{1,0:T(8,128)(2,1)S(1)} %get-tuple-element.47), channel_id=1, source_target_pairs={{0,32},{16,48},{32,0},{48,16},{64,96},{80,112},{96,64},{112,80},{1... | collective-permute-start | bytes 1572872 | tf_op jit(solution)/shard_map/ppermute | solution.py:407
  114.5 16.6 %collective-permute-start.15 = (bf16[2048,128]{1,0:T(8,128)(2,1)S(1)}, bf16[2048,128]{1,0:T(8,128)(2,1)S(1)}, u32[]{:S(2)}, u32[]{:S(2)}) collective-permute-start(bf16[2048,128]{1,0:T(8,128)(2,1)S(1)} %get-tuple-element.44), channel_id=1, source_target_pairs={{0,96},{16,112},{32,64},{48,80},{64,32},{80,48},{96,0},{112,16},{1... | collective-permute-start | bytes 1572872 | tf_op jit(solution)/shard_map/ppermute | solution.py:407
  120.5 15.0 %collective-permute-start.8 = (bf16[2048,128]{1,0:T(8,128)(2,1)S(1)}, bf16[2048,128]{1,0:T(8,128)(2,1)S(1)}, u32[]{:S(2)}, u32[]{:S(2)}) collective-permute-start(bf16[2048,128]{1,0:T(8,128)(2,1)S(1)} %get-tuple-element.37), channel_id=1, source_target_pairs={{0,16},{16,0},{32,48},{48,32},{64,80},{80,64},{96,112},{112,96},{1... | collective-permute-start | bytes 1572872 | tf_op jit(solution)/shard_map/ppermute | solution.py:407
  123.5 23.1 %collective-permute-start.5 = (bf16[2048,128]{1,0:T(8,128)(2,1)S(1)}, bf16[2048,128]{1,0:T(8,128)(2,1)S(1)}, u32[]{:S(2)}, u32[]{:S(2)}) collective-permute-start(bf16[2048,128]{1,0:T(8,128)(2,1)S(1)} %get-tuple-element.32), channel_id=1, source_target_pairs={{0,16},{16,0},{32,48},{48,32},{64,80},{80,64},{96,112},{112,96},{1... | collective-permute-start | bytes 1572872 | tf_op jit(solution)/shard_map/ppermute | solution.py:407
  124.4 5.8 %collective-permute-start.25 = (bf16[128,128]{0,1:T(8,128)(2,1)S(1)}, bf16[128,128]{0,1:T(8,128)(2,1)S(1)}, u32[]{:S(2)}, u32[]{:S(2)}) collective-permute-start(bf16[128,128]{0,1:T(8,128)(2,1)S(1)} %fusion.11), channel_id=1, source_target_pairs={{0,32},{16,48},{32,0},{48,16},{64,96},{80,112},{96,64},{112,80},{1... | collective-permute-start | bytes 98312 | tf_op jit(solution)/shard_map/ppermute | solution.py:407
  131.0 19.8 %collective-permute-start.26 = (f32[128,128]{0,1:T(8,128)S(1)}, f32[128,128]{0,1:T(8,128)S(1)}, u32[]{:S(2)}, u32[]{:S(2)}) collective-permute-start(f32[128,128]{0,1:T(8,128)S(1)} %convert_add_fusion), channel_id=1, source_target_pairs={{0,1},{1,0},{2,3},{3,2},{4,5},{5,4},{6,7},{7,6},{8,9},{9,8},{10,11... | collective-permute-start | bytes 196616 | tf_op jit(solution)/shard_map/ppermute | solution.py:407
  131.7 23.6 %collective-permute-start.18 = (bf16[2048,128]{1,0:T(8,128)(2,1)S(1)}, bf16[2048,128]{1,0:T(8,128)(2,1)S(1)}, u32[]{:S(2)}, u32[]{:S(2)}) collective-permute-start(bf16[2048,128]{1,0:T(8,128)(2,1)S(1)} %get-tuple-element.49), channel_id=1, source_target_pairs={{0,16},{16,0},{32,48},{48,32},{64,80},{80,64},{96,112},{112,96},{1... | collective-permute-start | bytes 1572872 | tf_op jit(solution)/shard_map/ppermute | solution.py:407
  135.7 16.0 %collective-permute-start.9 = (bf16[1024,128]{1,0:T(8,128)(2,1)S(1)}, bf16[1024,128]{1,0:T(8,128)(2,1)S(1)}, u32[]{:S(2)}, u32[]{:S(2)}) collective-permute-start(bf16[1024,128]{1,0:T(8,128)(2,1)S(1)} %get-tuple-element.39), channel_id=1, source_target_pairs={{0,32},{16,48},{32,0},{48,16},{64,96},{80,112},{96,64},{112,80},{1... | collective-permute-start | bytes 786440 | tf_op jit(solution)/shard_map/ppermute | solution.py:407
  147.6 7.8 %collective-permute-start.6 = (bf16[1024,128]{1,0:T(8,128)(2,1)}, bf16[1024,128]{1,0:T(8,128)(2,1)S(1)}, u32[]{:S(2)}, u32[]{:S(2)}) collective-permute-start(bf16[1024,128]{1,0:T(8,128)(2,1)} %get-tuple-element.34), channel_id=1, source_target_pairs={{0,96},{16,112},{32,64},{48,80},{64,32},{80,48},{96,0},{112,16},{1... | collective-permute-start | bytes 786440 | tf_op jit(solution)/shard_map/ppermute | solution.py:407
  (13 other events, 81.4 us)
